TPU v7x, 512 devices: a whole 4x8x8 slice. The times are simulated.
512 devices in a mesh: rows: 64 (over y, z_hi, core), rep: 8 (over x, z_lo).
Axes of the slice: x: 4, y: 8, z: 8 (z_hi: 4, z_lo: 2; z = z_hi * 2 + z_lo), core: 2. Of those that a mesh axis runs over, the one named last changes fastest.
Arguments:
- features: bfloat16 [32768, 128], P('rows'), may hold values from -6 to 6
- degree: int32 [32768], P('rows'), may hold values from 32 to 320
- tile_block: int32 [256, 64, 8], P('rows', 'rep'), may hold values from 0 to 3
- edge_count: int32 [256, 64, 8], P('rows', 'rep'), may hold values from 0 to 128, as said below
- edge_code: int32 [256, 64, 8, 128], P('rows', 'rep'), may hold values from 0 to 16368
- weight: bfloat16 [128, 256], replicated, may hold values from -3 to 3
- bias: float32 [256], replicated, may hold values from -3 to 3
- cotangent: bfloat16 [32768, 256], P(('rows', 'rep')), may hold values from -0.03125 to 0.03125
Outputs:
- activated: bfloat16 [32768, 256], P(('rows', 'rep'))
- grad_weight: float32 [128, 256], replicated
- grad_bias: float32 [256], replicated
Inputs may be any that keep to these rules, and one draw needn't show every extreme that they name: Only the first edge_count entries of a tile's edge codes are live; some tiles hold 128 live edges.
All inputs are finite; a program needn't handle non-finite values.
Results may differ from a plain program's by a relative error of at most 0.0063.
Values may be sent and summed in bfloat16 or wider, within the bound.
No kernel may reach another device: no remote copies, remote signals or barrier semaphores. Data moves between devices by JAX's collectives and lax.ppermute only.
A program may use at most 64 MiB of HBM per device.

v0:
```python
import jax
import jax.numpy as jnp
from jax import lax
from jax.sharding import PartitionSpec as P


def from_behind(value, axis, steps):
    count = lax.axis_size(axis)
    pairs = [(source, (source + steps) % count) for source in range(count)]
    return lax.ppermute(value, axis, pairs)


def gelu_tanh(values):
    return jax.nn.gelu(values, approximate=True)


def tile_sums(buffer, offset, tile_block, edge_count, edge_code):
    block_ids = lax.dynamic_index_in_dim(tile_block, offset, 1, keepdims=False)
    live_count = lax.dynamic_index_in_dim(edge_count, offset, 1, keepdims=False)
    codes = lax.dynamic_index_in_dim(edge_code, offset, 1, keepdims=False)
    block_total, slot_count, edge_cap = codes.shape
    feat_width = buffer.shape[1]
    far_node = block_ids[:, :, None] * 128 + codes % 128
    picked = jnp.take(buffer, far_node.reshape(-1), axis=0).reshape(
        block_total, slot_count, edge_cap, feat_width
    )
    is_live = lax.broadcasted_iota(jnp.int32, codes.shape, 2) < live_count[:, :, None]
    target = jnp.where(is_live, codes // 128, -1)
    row_iota = lax.broadcasted_iota(jnp.int32, (1, 1, 128, 1), 2)
    onehot = (target[:, :, None, :] == row_iota).astype(jnp.bfloat16)
    summed = jnp.einsum("bkre,bkef->brf", onehot, picked, preferred_element_type=jnp.float32)
    return summed.reshape(block_total * 128, feat_width)


def local(features, degree, tile_block, edge_count, edge_code, weight, bias, cotangent):
    step_count = tile_block.shape[1]
    replicas = lax.axis_size("rep")
    replica = lax.axis_index("rep")
    inv_deg = lax.rsqrt(degree.astype(jnp.float32))
    scaled = (features.astype(jnp.float32) * inv_deg[:, None]).astype(jnp.bfloat16)

    def local_sums(buffer, offset):
        return tile_sums(buffer, offset, tile_block, edge_count, edge_code)

    buffer = scaled
    for bit_index in range(replicas.bit_length() - 1):
        shifted = from_behind(buffer, "rows", -(step_count << bit_index))
        select = replica // (1 << bit_index) % 2 == 1
        buffer = jnp.where(select, shifted, buffer)
    partial_total = local_sums(buffer, 0)

    def advance(step_index, loop_state):
        current, running = loop_state
        current = from_behind(current, "rows", -1)
        return (current, running + local_sums(current, step_index))

    buffer, partial_total = lax.fori_loop(1, step_count, advance, (buffer, partial_total))
    edge_sums = lax.psum_scatter(partial_total, "rep", scatter_dimension=0, tiled=True)
    share_rows = edge_sums.shape[0]
    share_start = replica * share_rows
    own_rows = lax.dynamic_slice_in_dim(scaled, share_start, share_rows, 0).astype(jnp.float32)
    own_inv = lax.dynamic_slice_in_dim(inv_deg, share_start, share_rows, 0)
    aggregate = (own_inv[:, None] * (edge_sums + own_rows)).astype(jnp.bfloat16)
    pre_act = jnp.dot(aggregate, weight, preferred_element_type=jnp.float32) + bias
    activated, pull_back = jax.vjp(gelu_tanh, pre_act)
    delta_bf = pull_back(cotangent.astype(jnp.float32))[0].astype(jnp.bfloat16)
    local_weight = lax.dot_general(
        aggregate, delta_bf, (((0,), (0,)), ((), ())), preferred_element_type=jnp.float32
    )
    local_bias = jnp.sum(delta_bf.astype(jnp.float32), axis=0)
    grad_weight, grad_bias = lax.psum((local_weight, local_bias), ("rows", "rep"))
    return (activated.astype(jnp.bfloat16), grad_weight, grad_bias)


def solution(mesh):
    in_specs = (
        P("rows", None),
        P("rows"),
        P("rows", "rep", None),
        P("rows", "rep", None),
        P("rows", "rep", None, None),
        P(),
        P(),
        P(("rows", "rep"), None),
    )
    out_specs = (P(("rows", "rep"), None), P(), P())
    return jax.shard_map(local, mesh=mesh, in_specs=in_specs, out_specs=out_specs, check_vma=False)
```

profile of v0, /device:TPU:6, one launch (start us, length us, event | category | flops | bytes accessed | tf_op | source)
XLA Modules:
  0.0 556.4 jit_solution(3029872089114882890)
XLA Ops:
  8.0 1.0 multiply_convert_fusion
  9.0 5.4 collective-permute-start.1
  15.9 0.8 broadcast_clamp_fusion.1
  17.1 1.0 broadcast_select_fusion.2
  18.2 5.2 collective-permute-start.2
  23.4 0.8 fusion.21
  24.1 3.2 collective-permute-done.2
  27.4 7.6 %collective-permute-start.3 = (bf16[512,128]{1,0:T(8,128)(2,1)S(1)}, bf16[512,128]{1,0:T(8,128)(2,1)S(1)}, u32[]{:S(2)}, u32[]{:S(2)}) collective-permute-start(bf16[512,128]{1,0:T(8,128)(2,1)S(1)} %broadcast_select_fusion.3), channel_id=1, source_target_pairs={{0,256},{8,264},{16,272},{24,280},{32,288},{40,296},{48,304},{56,3... | collective-permute-start | bytes 393224 | tf_op jit(solution)/shard_map/ppermute | solution.py:10
  35.1 4.4 collective-permute-done.3
  39.5 12.1 %gather_fusion.1 = bf16[4096,128]{1,0:T(8,128)(2,1)S(1)} fusion(bf16[512,128]{1,0:T(8,128)(2,1)S(1)} %broadcast_select_fusion.4, s32[4096]{0:T(1024)S(1)} %broadcast_clamp_fusion.1), kind=kCustom, calls=%fused_computation.1.clone | custom fusion | bytes 2113536 | tf_op jit(solution)/shard_map/jit(_take)/gather | solution.py:24
  51.6 2.1 broadcast_select_fusion.1
  54.3 186.2 %while.19 = (s32[]{:T(128)}, bf16[512,128]{1,0:T(8,128)(2,1)S(1)}, f32[512,128]{1,0:T(8,128)S(1)}, s32[4,8,8]{2,1,0:T(8,128)}, s32[4,8,8,128]{3,2,1,0:T(8,128)S(...) while((s32[]{:T(128)}, bf16[512,128]{1,0:T(8,128)(2,1)S(1)}, f32[512,128]{1,0:T(8,128)S(1)}, ...), condition=%wide.region_1.3_spmd, body=%wide.region_0.2_spmd.sunk | while | flops 135540768 | bytes 7202103 | solution.py:57
  54.3 13.9 %collective-permute-start = (bf16[512,128]{1,0:T(8,128)(2,1)S(1)}, bf16[512,128]{1,0:T(8,128)(2,1)S(1)}, u32[]{:S(2)}, u32[]{:S(2)}) collective-permute-start(bf16[512,128]{1,0:T(8,128)(2,1)S(1)} %get-tuple-element.281), channel_id=1, source_target_pairs={{0,504},{8,0},{16,8},{24,16},{32,24},{40,32},{48,40},{56,48},{64,5... | collective-permute-start | bytes 393224 | tf_op jit(solution)/shard_map/while/body/eval_jaxpr/ppermute | solution.py:10
  68.2 0.7 constant_dynamic-slice_fusion.3
  69.2 1.5 collective-permute-done
  70.7 12.1 %gather_fusion = bf16[4096,128]{1,0:T(8,128)(2,1)S(1)} fusion(bf16[512,128]{1,0:T(8,128)(2,1)S(1)} %collective-permute-done, s32[4096]{0:T(1024)S(1)} %broadcast_clamp_fusion.3), kind=kCustom, calls=%fused_computation.clone.clone.1 | custom fusion | bytes 2113536 | tf_op jit(solution)/shard_map/while/body/eval_jaxpr/jit(_take)/gather | solution.py:24
  82.8 2.1 broadcast_select_fusion.6
  85.5 8.5 %collective-permute-start = (bf16[512,128]{1,0:T(8,128)(2,1)S(1)}, bf16[512,128]{1,0:T(8,128)(2,1)S(1)}, u32[]{:S(2)}, u32[]{:S(2)}) collective-permute-start(bf16[512,128]{1,0:T(8,128)(2,1)S(1)} %get-tuple-element.281), channel_id=1, source_target_pairs={{0,504},{8,0},{16,8},{24,16},{32,24},{40,32},{48,40},{56,48},{64,5... | collective-permute-start | bytes 393224 | tf_op jit(solution)/shard_map/while/body/eval_jaxpr/ppermute | solution.py:10
  95.0 1.5 collective-permute-done
  96.5 12.1 %gather_fusion = bf16[4096,128]{1,0:T(8,128)(2,1)S(1)} fusion(bf16[512,128]{1,0:T(8,128)(2,1)S(1)} %collective-permute-done, s32[4096]{0:T(1024)S(1)} %broadcast_clamp_fusion.3), kind=kCustom, calls=%fused_computation.clone.clone.1 | custom fusion | bytes 2113536 | tf_op jit(solution)/shard_map/while/body/eval_jaxpr/jit(_take)/gather | solution.py:24
  108.7 2.1 broadcast_select_fusion.6
  111.4 8.5 %collective-permute-start = (bf16[512,128]{1,0:T(8,128)(2,1)S(1)}, bf16[512,128]{1,0:T(8,128)(2,1)S(1)}, u32[]{:S(2)}, u32[]{:S(2)}) collective-permute-start(bf16[512,128]{1,0:T(8,128)(2,1)S(1)} %get-tuple-element.281), channel_id=1, source_target_pairs={{0,504},{8,0},{16,8},{24,16},{32,24},{40,32},{48,40},{56,48},{64,5... | collective-permute-start | bytes 393224 | tf_op jit(solution)/shard_map/while/body/eval_jaxpr/ppermute | solution.py:10
  120.9 1.5 collective-permute-done
  122.4 12.1 %gather_fusion = bf16[4096,128]{1,0:T(8,128)(2,1)S(1)} fusion(bf16[512,128]{1,0:T(8,128)(2,1)S(1)} %collective-permute-done, s32[4096]{0:T(1024)S(1)} %broadcast_clamp_fusion.3), kind=kCustom, calls=%fused_computation.clone.clone.1 | custom fusion | bytes 2113536 | tf_op jit(solution)/shard_map/while/body/eval_jaxpr/jit(_take)/gather | solution.py:24
  134.5 2.1 broadcast_select_fusion.6
  137.2 8.5 %collective-permute-start = (bf16[512,128]{1,0:T(8,128)(2,1)S(1)}, bf16[512,128]{1,0:T(8,128)(2,1)S(1)}, u32[]{:S(2)}, u32[]{:S(2)}) collective-permute-start(bf16[512,128]{1,0:T(8,128)(2,1)S(1)} %get-tuple-element.281), channel_id=1, source_target_pairs={{0,504},{8,0},{16,8},{24,16},{32,24},{40,32},{48,40},{56,48},{64,5... | collective-permute-start | bytes 393224 | tf_op jit(solution)/shard_map/while/body/eval_jaxpr/ppermute | solution.py:10
  146.7 1.5 collective-permute-done
  148.2 12.1 %gather_fusion = bf16[4096,128]{1,0:T(8,128)(2,1)S(1)} fusion(bf16[512,128]{1,0:T(8,128)(2,1)S(1)} %collective-permute-done, s32[4096]{0:T(1024)S(1)} %broadcast_clamp_fusion.3), kind=kCustom, calls=%fused_computation.clone.clone.1 | custom fusion | bytes 2113536 | tf_op jit(solution)/shard_map/while/body/eval_jaxpr/jit(_take)/gather | solution.py:24
  160.4 2.1 broadcast_select_fusion.6
  163.1 8.5 %collective-permute-start = (bf16[512,128]{1,0:T(8,128)(2,1)S(1)}, bf16[512,128]{1,0:T(8,128)(2,1)S(1)}, u32[]{:S(2)}, u32[]{:S(2)}) collective-permute-start(bf16[512,128]{1,0:T(8,128)(2,1)S(1)} %get-tuple-element.281), channel_id=1, source_target_pairs={{0,504},{8,0},{16,8},{24,16},{32,24},{40,32},{48,40},{56,48},{64,5... | collective-permute-start | bytes 393224 | tf_op jit(solution)/shard_map/while/body/eval_jaxpr/ppermute | solution.py:10
  172.5 1.5 collective-permute-done
  174.0 12.1 %gather_fusion = bf16[4096,128]{1,0:T(8,128)(2,1)S(1)} fusion(bf16[512,128]{1,0:T(8,128)(2,1)S(1)} %collective-permute-done, s32[4096]{0:T(1024)S(1)} %broadcast_clamp_fusion.3), kind=kCustom, calls=%fused_computation.clone.clone.1 | custom fusion | bytes 2113536 | tf_op jit(solution)/shard_map/while/body/eval_jaxpr/jit(_take)/gather | solution.py:24
  186.2 2.1 broadcast_select_fusion.6
  188.9 8.5 %collective-permute-start = (bf16[512,128]{1,0:T(8,128)(2,1)S(1)}, bf16[512,128]{1,0:T(8,128)(2,1)S(1)}, u32[]{:S(2)}, u32[]{:S(2)}) collective-permute-start(bf16[512,128]{1,0:T(8,128)(2,1)S(1)} %get-tuple-element.281), channel_id=1, source_target_pairs={{0,504},{8,0},{16,8},{24,16},{32,24},{40,32},{48,40},{56,48},{64,5... | collective-permute-start | bytes 393224 | tf_op jit(solution)/shard_map/while/body/eval_jaxpr/ppermute | solution.py:10
  198.3 1.5 collective-permute-done
  199.9 12.1 %gather_fusion = bf16[4096,128]{1,0:T(8,128)(2,1)S(1)} fusion(bf16[512,128]{1,0:T(8,128)(2,1)S(1)} %collective-permute-done, s32[4096]{0:T(1024)S(1)} %broadcast_clamp_fusion.3), kind=kCustom, calls=%fused_computation.clone.clone.1 | custom fusion | bytes 2113536 | tf_op jit(solution)/shard_map/while/body/eval_jaxpr/jit(_take)/gather | solution.py:24
  212.0 2.1 broadcast_select_fusion.6
  214.7 8.5 %collective-permute-start = (bf16[512,128]{1,0:T(8,128)(2,1)S(1)}, bf16[512,128]{1,0:T(8,128)(2,1)S(1)}, u32[]{:S(2)}, u32[]{:S(2)}) collective-permute-start(bf16[512,128]{1,0:T(8,128)(2,1)S(1)} %get-tuple-element.281), channel_id=1, source_target_pairs={{0,504},{8,0},{16,8},{24,16},{32,24},{40,32},{48,40},{56,48},{64,5... | collective-permute-start | bytes 393224 | tf_op jit(solution)/shard_map/while/body/eval_jaxpr/ppermute | solution.py:10
  224.1 1.5 collective-permute-done
  225.7 12.1 %gather_fusion = bf16[4096,128]{1,0:T(8,128)(2,1)S(1)} fusion(bf16[512,128]{1,0:T(8,128)(2,1)S(1)} %collective-permute-done, s32[4096]{0:T(1024)S(1)} %broadcast_clamp_fusion.3), kind=kCustom, calls=%fused_computation.clone.clone.1 | custom fusion | bytes 2113536 | tf_op jit(solution)/shard_map/while/body/eval_jaxpr/jit(_take)/gather | solution.py:24
  237.8 2.1 broadcast_select_fusion.6
  241.4 38.0 %reduce-scatter.2.cloned.1.call-done = f32[64,128]{1,0:T(8,128)} async-done(((f32[512,128]{1,0:T(8,128)}), f32[64,128]{1,0:T(8,128)}) %reduce-scatter.2.cloned.1.call-update) | async-done | bytes 32784 | tf_op jit(solution)/shard_map/reduce_scatter | solution.py:58
  279.3 0.8 multiply_convert_fusion.2
  280.2 0.8 convert_reduce_fusion
  281.0 0.9 fusion.27
  281.9 98.0 %psum.15 = f32[256]{0:T(256)} all-reduce(f32[256]{0:T(256)S(1)} %get-tuple-element.225), channel_id=1, replica_groups=mesh['rows'=64,'rep'=8] {'rows','rep'}, use_global_device_ids=true, to_apply=%region_5.7 | all-reduce | flops 256 | bytes 2048 | tf_op jit(solution)/shard_map/psum | solution.py:71
  379.9 168.2 %all-reduce.2.cloned.1.call-done = f32[128,256]{1,0:T(8,128)} async-done(((f32[128,256]{1,0:T(8,128)}), f32[128,256]{1,0:T(8,128)}) %all-reduce.2.cloned.1.call-update) | async-done | bytes 131088 | tf_op jit(solution)/shard_map/psum | solution.py:71
  548.0 1.6 copy.29
  (78 shorter events, 13.8 us)
Async XLA Ops:
  7.2 273.0 %copy-start = (bf16[128,256]{1,0:T(8,128)(2,1)S(1)}, bf16[128,256]{1,0:T(8,128)(2,1)}, u32[]{:S(2)}) copy-start(bf16[128,256]{1,0:T(8,128)(2,1)} %param.17) | copy-start | bytes 196612
  7.2 27.8 %copy-start.2 = (s32[4,8,8,128]{3,2,1,0:T(8,128)S(1)}, s32[4,8,8,128]{3,2,1,0:T(8,128)}, u32[]{:S(2)}) copy-start(s32[4,8,8,128]{3,2,1,0:T(8,128)} %param.16) | copy-start | bytes 393220
  7.2 272.1 %reduce-scatter.2.cloned.1.call-start = ((), (), s32[]{:S(2)}) async-start(), calls=%async_computation.1 | async-start | bytes 294912 | tf_op jit(solution)/shard_map/reduce_scatter | solution.py:58
  9.0 8.1 %collective-permute-start.1 = (bf16[512,128]{1,0:T(8,128)(2,1)S(1)}, bf16[512,128]{1,0:T(8,128)(2,1)S(1)}, u32[]{:S(2)}, u32[]{:S(2)}) collective-permute-start(bf16[512,128]{1,0:T(8,128)(2,1)S(1)} %multiply_convert_fusion), channel_id=1, source_target_pairs={{0,448},{8,456},{16,464},{24,472},{32,480},{40,488},{48,496},{56,5... | collective-permute-start | bytes 393224 | tf_op jit(solution)/shard_map/ppermute | solution.py:10
  18.2 9.2 %collective-permute-start.2 = (bf16[512,128]{1,0:T(8,128)(2,1)S(1)}, bf16[512,128]{1,0:T(8,128)(2,1)S(1)}, u32[]{:S(2)}, u32[]{:S(2)}) collective-permute-start(bf16[512,128]{1,0:T(8,128)(2,1)S(1)} %broadcast_select_fusion.2), channel_id=1, source_target_pairs={{0,384},{8,392},{16,400},{24,408},{32,416},{40,424},{48,432},{56,4... | collective-permute-start | bytes 393224 | tf_op jit(solution)/shard_map/ppermute | solution.py:10
  27.4 12.1 %collective-permute-start.3 = (bf16[512,128]{1,0:T(8,128)(2,1)S(1)}, bf16[512,128]{1,0:T(8,128)(2,1)S(1)}, u32[]{:S(2)}, u32[]{:S(2)}) collective-permute-start(bf16[512,128]{1,0:T(8,128)(2,1)S(1)} %broadcast_select_fusion.3), channel_id=1, source_target_pairs={{0,256},{8,264},{16,272},{24,280},{32,288},{40,296},{48,304},{56,3... | collective-permute-start | bytes 393224 | tf_op jit(solution)/shard_map/ppermute | solution.py:10
  54.3 225.9 %copy-start.3 = (bf16[64,256]{1,0:T(8,128)(2,1)S(1)}, bf16[64,256]{1,0:T(8,128)(2,1)}, u32[]{:S(2)}) copy-start(bf16[64,256]{1,0:T(8,128)(2,1)} %param.19) | copy-start | bytes 98308
  54.3 225.9 %copy-start.4 = (f32[256]{0:T(256)S(1)}, f32[256]{0:T(256)}, u32[]{:S(2)}) copy-start(f32[256]{0:T(256)} %param.18) | copy-start | bytes 3076
  54.3 16.4 %collective-permute-start = (bf16[512,128]{1,0:T(8,128)(2,1)S(1)}, bf16[512,128]{1,0:T(8,128)(2,1)S(1)}, u32[]{:S(2)}, u32[]{:S(2)}) collective-permute-start(bf16[512,128]{1,0:T(8,128)(2,1)S(1)} %get-tuple-element.281), channel_id=1, source_target_pairs={{0,504},{8,0},{16,8},{24,16},{32,24},{40,32},{48,40},{56,48},{64,5... | collective-permute-start | bytes 393224 | tf_op jit(solution)/shard_map/while/body/eval_jaxpr/ppermute | solution.py:10
  85.5 11.0 %collective-permute-start = (bf16[512,128]{1,0:T(8,128)(2,1)S(1)}, bf16[512,128]{1,0:T(8,128)(2,1)S(1)}, u32[]{:S(2)}, u32[]{:S(2)}) collective-permute-start(bf16[512,128]{1,0:T(8,128)(2,1)S(1)} %get-tuple-element.281), channel_id=1, source_target_pairs={{0,504},{8,0},{16,8},{24,16},{32,24},{40,32},{48,40},{56,48},{64,5... | collective-permute-start | bytes 393224 | tf_op jit(solution)/shard_map/while/body/eval_jaxpr/ppermute | solution.py:10
  111.4 11.0 %collective-permute-start = (bf16[512,128]{1,0:T(8,128)(2,1)S(1)}, bf16[512,128]{1,0:T(8,128)(2,1)S(1)}, u32[]{:S(2)}, u32[]{:S(2)}) collective-permute-start(bf16[512,128]{1,0:T(8,128)(2,1)S(1)} %get-tuple-element.281), channel_id=1, source_target_pairs={{0,504},{8,0},{16,8},{24,16},{32,24},{40,32},{48,40},{56,48},{64,5... | collective-permute-start | bytes 393224 | tf_op jit(solution)/shard_map/while/body/eval_jaxpr/ppermute | solution.py:10
  137.2 11.0 %collective-permute-start = (bf16[512,128]{1,0:T(8,128)(2,1)S(1)}, bf16[512,128]{1,0:T(8,128)(2,1)S(1)}, u32[]{:S(2)}, u32[]{:S(2)}) collective-permute-start(bf16[512,128]{1,0:T(8,128)(2,1)S(1)} %get-tuple-element.281), channel_id=1, source_target_pairs={{0,504},{8,0},{16,8},{24,16},{32,24},{40,32},{48,40},{56,48},{64,5... | collective-permute-start | bytes 393224 | tf_op jit(solution)/shard_map/while/body/eval_jaxpr/ppermute | solution.py:10
  163.1 11.0 %collective-permute-start = (bf16[512,128]{1,0:T(8,128)(2,1)S(1)}, bf16[512,128]{1,0:T(8,128)(2,1)S(1)}, u32[]{:S(2)}, u32[]{:S(2)}) collective-permute-start(bf16[512,128]{1,0:T(8,128)(2,1)S(1)} %get-tuple-element.281), channel_id=1, source_target_pairs={{0,504},{8,0},{16,8},{24,16},{32,24},{40,32},{48,40},{56,48},{64,5... | collective-permute-start | bytes 393224 | tf_op jit(solution)/shard_map/while/body/eval_jaxpr/ppermute | solution.py:10
  188.9 11.0 %collective-permute-start = (bf16[512,128]{1,0:T(8,128)(2,1)S(1)}, bf16[512,128]{1,0:T(8,128)(2,1)S(1)}, u32[]{:S(2)}, u32[]{:S(2)}) collective-permute-start(bf16[512,128]{1,0:T(8,128)(2,1)S(1)} %get-tuple-element.281), channel_id=1, source_target_pairs={{0,504},{8,0},{16,8},{24,16},{32,24},{40,32},{48,40},{56,48},{64,5... | collective-permute-start | bytes 393224 | tf_op jit(solution)/shard_map/while/body/eval_jaxpr/ppermute | solution.py:10
  214.7 11.0 %collective-permute-start = (bf16[512,128]{1,0:T(8,128)(2,1)S(1)}, bf16[512,128]{1,0:T(8,128)(2,1)S(1)}, u32[]{:S(2)}, u32[]{:S(2)}) collective-permute-start(bf16[512,128]{1,0:T(8,128)(2,1)S(1)} %get-tuple-element.281), channel_id=1, source_target_pairs={{0,504},{8,0},{16,8},{24,16},{32,24},{40,32},{48,40},{56,48},{64,5... | collective-permute-start | bytes 393224 | tf_op jit(solution)/shard_map/while/body/eval_jaxpr/ppermute | solution.py:10
  240.5 0.7 copy-start.1
  241.2 306.8 %all-reduce.2.cloned.1.call-start = ((), (), s32[]{:S(2)}) async-start(), calls=%async_computation.2 | async-start | bytes 262144 | tf_op jit(solution)/shard_map/psum | solution.py:71
Sparse Core Ops, SparseCore 0:
  241.3 37.9 reduce-scatter.1
  284.9 263.1 all-reduce.1
where the time goes:
time: 562 us; the launch traced here: 556 us
  waiting for transfers between devices  225 us (40%)
  local copies, waits for them, and re-layouts  105 us (19%)
  blocking collectives  98 us (17%)
  starting transfers between devices  83.1 us (15%)
  other arithmetic  25.2 us (4%)
  between operations  14.2 us (3%)
    psum x1, waiting for transfers between devices, local(): lax.psum((local_weight, local_bias), ('rows', 'rep'))  168 us
    psum x1, blocking collectives, local(): lax.psum((local_weight, local_bias), ('rows', 'rep'))  98 us
    gather x8, local copies, waits for them, and re-layouts, tile_sums(): jnp.take(buffer, far_node.reshape(-1), axis=0)  97 us
    ppermute x10, starting transfers between devices, from_behind(): return lax.ppermute(value, axis, pairs)  83 us
    reduce_scatter x1, waiting for transfers between devices, local(): lax.psum_scatter(partial_total, 'rep', scatter_dimension=0, tiled=True)  38 us
    ppermute x10, waiting for transfers between devices, from_behind(): return lax.ppermute(value, axis, pairs)  18.6 us
    select_n x8, other arithmetic, tile_sums(): jnp.take(buffer, far_node.reshape(-1), axis=0)  17.2 us
  transfers between devices with their start and end apart: 12, of which 12 were waited for; matrix products, arithmetic and copies ran while one was open for 2% of the time, Pallas kernels for 0%

commit v1 on v0

--- a/solution.py
+++ b/solution.py
@@ -2,12 +2,39 @@
 import jax.numpy as jnp
 from jax import lax
 from jax.sharding import PartitionSpec as P
+
+BFLY_BITS = (3, 0, 1, 6, 4, 2, 7, 5, 8)
 
 
 def from_behind(value, axis, steps):
     count = lax.axis_size(axis)
     pairs = [(source, (source + steps) % count) for source in range(count)]
     return lax.ppermute(value, axis, pairs)
+
+
+def butterfly_sum(value, axes, count):
+    for bit in BFLY_BITS:
+        if (1 << bit) >= count:
+            continue
+        pairs = [(source, source ^ (1 << bit)) for source in range(count)]
+        value = value + lax.ppermute(value, axes, pairs)
+    return value
+
+
+def halving_scatter(value, axis):
+    count = lax.axis_size(axis)
+    me = lax.axis_index(axis)
+    levels = count.bit_length() - 1
+    share = value.shape[0] // count
+    buf = value.reshape((2,) * levels + (share,) + value.shape[1:])
+    for bit in range(levels):
+        dim = levels - 1 - bit
+        mine = (me >> bit) & 1
+        keep = lax.dynamic_index_in_dim(buf, mine, dim, keepdims=False)
+        send = lax.dynamic_index_in_dim(buf, 1 - mine, dim, keepdims=False)
+        pairs = [(source, source ^ (1 << bit)) for source in range(count)]
+        buf = keep + lax.ppermute(send, axis, pairs)
+    return buf
 
 
 def gelu_tanh(values):
@@ -36,6 +63,7 @@
     step_count = tile_block.shape[1]
     replicas = lax.axis_size("rep")
     replica = lax.axis_index("rep")
+    devices = lax.axis_size("rows") * replicas
     inv_deg = lax.rsqrt(degree.astype(jnp.float32))
     scaled = (features.astype(jnp.float32) * inv_deg[:, None]).astype(jnp.bfloat16)
 
@@ -55,7 +83,7 @@
         return (current, running + local_sums(current, step_index))
 
     buffer, partial_total = lax.fori_loop(1, step_count, advance, (buffer, partial_total))
-    edge_sums = lax.psum_scatter(partial_total, "rep", scatter_dimension=0, tiled=True)
+    edge_sums = halving_scatter(partial_total, "rep")
     share_rows = edge_sums.shape[0]
     share_start = replica * share_rows
     own_rows = lax.dynamic_slice_in_dim(scaled, share_start, share_rows, 0).astype(jnp.float32)
@@ -68,7 +96,13 @@
         aggregate, delta_bf, (((0,), (0,)), ((), ())), preferred_element_type=jnp.float32
     )
     local_bias = jnp.sum(delta_bf.astype(jnp.float32), axis=0)
-    grad_weight, grad_bias = lax.psum((local_weight, local_bias), ("rows", "rep"))
+    feat_rows = local_weight.shape[0]
+    packed = jnp.concatenate(
+        [local_weight, jnp.broadcast_to(local_bias[None, :], (8, local_bias.shape[0]))], axis=0
+    )
+    packed = butterfly_sum(packed, ("rows", "rep"), devices)
+    grad_weight = packed[:feat_rows]
+    grad_bias = packed[feat_rows]
     return (activated.astype(jnp.bfloat16), grad_weight, grad_bias)
 
 

time: 562 us -> 332 us (0.59)
  waiting for transfers between devices: 225 us -> 81.7 us
  blocking collectives: 98 us -> 0 us
  starting transfers between devices: 83.1 us -> 113 us
  between operations: 14.2 us -> 1 us
    psum x1 -> x0, waiting for transfers between devices: 168 us -> none  [local(): lax.psum((local_weight, local_bias), ('rows', 'rep'))]
    psum x1 -> x0, blocking collectives: 98 us -> none  [local(): lax.psum((local_weight, local_bias), ('rows', 'rep'))]
    ppermute x0 -> x12, waiting for transfers between devices: none -> 63.1 us  [the longest x9 52.2 us: butterfly_sum(): value = value + lax.ppermute(value, axes, pairs)]
    reduce_scatter x1 -> x0, waiting for transfers between devices: 38 us -> none  [local(): lax.psum_scatter(partial_total, 'rep', scatter_dimension=0, tiled=True)]
    ppermute x0 -> x12, starting transfers between devices: none -> 30.1 us  [the longest x9 20.8 us: butterfly_sum(): value = value + lax.ppermute(value, axes, pairs)]
  transfers between devices with their start and end apart: 12 -> 22, of which waited for: 12 -> 22; matrix products, arithmetic and copies ran while one was open for 2% -> 3% of each run, Pallas kernels for 0% -> 0%
where the time goes in v1:
time: 332 us; the launch traced here: 330 us
  starting transfers between devices  113 us (34%)
  local copies, waits for them, and re-layouts  104 us (31%)
  waiting for transfers between devices  81.7 us (25%)
  other arithmetic  24.6 us (7%)
  matrix products  4.71 us (1%)
    gather x8, local copies, waits for them, and re-layouts, tile_sums(): jnp.take(buffer, far_node.reshape(-1), axis=0)  97 us
    ppermute x10, starting transfers between devices, from_behind(): return lax.ppermute(value, axis, pairs)  82.9 us
    ppermute x9, waiting for transfers between devices, butterfly_sum(): value = value + lax.ppermute(value, axes, pairs)  52.2 us
    ppermute x9, starting transfers between devices, butterfly_sum(): value = value + lax.ppermute(value, axes, pairs)  20.8 us
    ppermute x10, waiting for transfers between devices, from_behind(): return lax.ppermute(value, axis, pairs)  18.6 us
    select_n x8, other arithmetic, tile_sums(): jnp.take(buffer, far_node.reshape(-1), axis=0)  17.2 us
    ppermute x3, waiting for transfers between devices, halving_scatter(): buf = keep + lax.ppermute(send, axis, pairs)  10.9 us
    ppermute x3, starting transfers between devices, halving_scatter(): buf = keep + lax.ppermute(send, axis, pairs)  9.28 us
  transfers between devices with their start and end apart: 22, of which 22 were waited for; matrix products, arithmetic and copies ran while one was open for 3% of the time, Pallas kernels for 0%

profile of v1, /device:TPU:6, one launch (start us, length us, event | category | flops | bytes accessed | tf_op | source)
XLA Modules:
  0.0 329.9 jit_solution(367456133677186763)
XLA Ops:
  2.4 5.4 %collective-permute-start.1 = (bf16[512,128]{1,0:T(8,128)(2,1)S(1)}, bf16[512,128]{1,0:T(8,128)(2,1)S(1)}, u32[]{:S(2)}, u32[]{:S(2)}) collective-permute-start(bf16[512,128]{1,0:T(8,128)(2,1)S(1)} %multiply_convert_fusion), channel_id=1, source_target_pairs={{0,448},{8,456},{16,464},{24,472},{32,480},{40,488},{48,496},{56,5... | collective-permute-start | bytes 393224 | tf_op jit(solution)/shard_map/ppermute | solution.py:12
  11.6 5.2 %collective-permute-start.2 = (bf16[512,128]{1,0:T(8,128)(2,1)S(1)}, bf16[512,128]{1,0:T(8,128)(2,1)S(1)}, u32[]{:S(2)}, u32[]{:S(2)}) collective-permute-start(bf16[512,128]{1,0:T(8,128)(2,1)S(1)} %broadcast_select_fusion.2), channel_id=1, source_target_pairs={{0,384},{8,392},{16,400},{24,408},{32,416},{40,424},{48,432},{56,4... | collective-permute-start | bytes 393224 | tf_op jit(solution)/shard_map/ppermute | solution.py:12
  17.6 3.2 collective-permute-done.2
  20.8 7.6 %collective-permute-start.3 = (bf16[512,128]{1,0:T(8,128)(2,1)S(1)}, bf16[512,128]{1,0:T(8,128)(2,1)S(1)}, u32[]{:S(2)}, u32[]{:S(2)}) collective-permute-start(bf16[512,128]{1,0:T(8,128)(2,1)S(1)} %broadcast_select_fusion.3), channel_id=1, source_target_pairs={{0,256},{8,264},{16,272},{24,280},{32,288},{40,296},{48,304},{56,3... | collective-permute-start | bytes 393224 | tf_op jit(solution)/shard_map/ppermute | solution.py:12
  28.5 4.4 %collective-permute-done.3 = bf16[512,128]{1,0:T(8,128)(2,1)S(1)} collective-permute-done((bf16[512,128]{1,0:T(8,128)(2,1)S(1)}, bf16[512,128]{1,0:T(8,128)(2,1)S(1)}, u32[]{:S(2)}, u32[]{:S(2)}) %collective-permute-start.3) | collective-permute-done | bytes 131104 | tf_op jit(solution)/shard_map/ppermute | solution.py:12
  32.9 12.1 %gather_fusion.1 = bf16[4096,128]{1,0:T(8,128)(2,1)S(1)} fusion(bf16[512,128]{1,0:T(8,128)(2,1)S(1)} %broadcast_select_fusion.4, s32[4096]{0:T(1024)S(1)} %broadcast_clamp_fusion.1), kind=kCustom, calls=%fused_computation.1.clone | custom fusion | bytes 2113536 | tf_op jit(solution)/shard_map/jit(_take)/gather | solution.py:51
  45.1 2.1 broadcast_select_fusion.1
  47.7 186.2 %while.19 = (s32[]{:T(128)}, bf16[512,128]{1,0:T(8,128)(2,1)S(1)}, f32[512,128]{1,0:T(8,128)S(1)}, s32[4,8,8]{2,1,0:T(8,128)}, s32[4,8,8,128]{3,2,1,0:T(8,128)S(...) while((s32[]{:T(128)}, bf16[512,128]{1,0:T(8,128)(2,1)S(1)}, f32[512,128]{1,0:T(8,128)S(1)}, ...), condition=%wide.region_1.3_spmd, body=%wide.region_0.2_spmd.sunk | while | flops 135540768 | bytes 7202111 | solution.py:85
  47.7 13.9 %collective-permute-start = (bf16[512,128]{1,0:T(8,128)(2,1)S(1)}, bf16[512,128]{1,0:T(8,128)(2,1)S(1)}, u32[]{:S(2)}, u32[]{:S(2)}) collective-permute-start(bf16[512,128]{1,0:T(8,128)(2,1)S(1)} %get-tuple-element.293), channel_id=1, source_target_pairs={{0,504},{8,0},{16,8},{24,16},{32,24},{40,32},{48,40},{56,48},{64,5... | collective-permute-start | bytes 393224 | tf_op jit(solution)/shard_map/while/body/eval_jaxpr/ppermute | solution.py:12
  64.1 12.1 %gather_fusion = bf16[4096,128]{1,0:T(8,128)(2,1)S(1)} fusion(bf16[512,128]{1,0:T(8,128)(2,1)S(1)} %collective-permute-done, s32[4096]{0:T(1024)S(1)} %broadcast_clamp_fusion.3), kind=kCustom, calls=%fused_computation.clone.clone.1 | custom fusion | bytes 2113536 | tf_op jit(solution)/shard_map/while/body/eval_jaxpr/jit(_take)/gather | solution.py:51
  76.2 2.1 broadcast_select_fusion.6
  78.9 8.5 %collective-permute-start = (bf16[512,128]{1,0:T(8,128)(2,1)S(1)}, bf16[512,128]{1,0:T(8,128)(2,1)S(1)}, u32[]{:S(2)}, u32[]{:S(2)}) collective-permute-start(bf16[512,128]{1,0:T(8,128)(2,1)S(1)} %get-tuple-element.293), channel_id=1, source_target_pairs={{0,504},{8,0},{16,8},{24,16},{32,24},{40,32},{48,40},{56,48},{64,5... | collective-permute-start | bytes 393224 | tf_op jit(solution)/shard_map/while/body/eval_jaxpr/ppermute | solution.py:12
  89.9 12.1 %gather_fusion = bf16[4096,128]{1,0:T(8,128)(2,1)S(1)} fusion(bf16[512,128]{1,0:T(8,128)(2,1)S(1)} %collective-permute-done, s32[4096]{0:T(1024)S(1)} %broadcast_clamp_fusion.3), kind=kCustom, calls=%fused_computation.clone.clone.1 | custom fusion | bytes 2113536 | tf_op jit(solution)/shard_map/while/body/eval_jaxpr/jit(_take)/gather | solution.py:51
  102.1 2.1 broadcast_select_fusion.6
  104.8 8.5 %collective-permute-start = (bf16[512,128]{1,0:T(8,128)(2,1)S(1)}, bf16[512,128]{1,0:T(8,128)(2,1)S(1)}, u32[]{:S(2)}, u32[]{:S(2)}) collective-permute-start(bf16[512,128]{1,0:T(8,128)(2,1)S(1)} %get-tuple-element.293), channel_id=1, source_target_pairs={{0,504},{8,0},{16,8},{24,16},{32,24},{40,32},{48,40},{56,48},{64,5... | collective-permute-start | bytes 393224 | tf_op jit(solution)/shard_map/while/body/eval_jaxpr/ppermute | solution.py:12
  115.8 12.1 %gather_fusion = bf16[4096,128]{1,0:T(8,128)(2,1)S(1)} fusion(bf16[512,128]{1,0:T(8,128)(2,1)S(1)} %collective-permute-done, s32[4096]{0:T(1024)S(1)} %broadcast_clamp_fusion.3), kind=kCustom, calls=%fused_computation.clone.clone.1 | custom fusion | bytes 2113536 | tf_op jit(solution)/shard_map/while/body/eval_jaxpr/jit(_take)/gather | solution.py:51
  127.9 2.1 broadcast_select_fusion.6
  130.6 8.5 %collective-permute-start = (bf16[512,128]{1,0:T(8,128)(2,1)S(1)}, bf16[512,128]{1,0:T(8,128)(2,1)S(1)}, u32[]{:S(2)}, u32[]{:S(2)}) collective-permute-start(bf16[512,128]{1,0:T(8,128)(2,1)S(1)} %get-tuple-element.293), channel_id=1, source_target_pairs={{0,504},{8,0},{16,8},{24,16},{32,24},{40,32},{48,40},{56,48},{64,5... | collective-permute-start | bytes 393224 | tf_op jit(solution)/shard_map/while/body/eval_jaxpr/ppermute | solution.py:12
  141.6 12.1 %gather_fusion = bf16[4096,128]{1,0:T(8,128)(2,1)S(1)} fusion(bf16[512,128]{1,0:T(8,128)(2,1)S(1)} %collective-permute-done, s32[4096]{0:T(1024)S(1)} %broadcast_clamp_fusion.3), kind=kCustom, calls=%fused_computation.clone.clone.1 | custom fusion | bytes 2113536 | tf_op jit(solution)/shard_map/while/body/eval_jaxpr/jit(_take)/gather | solution.py:51
  153.7 2.1 broadcast_select_fusion.6
  156.4 8.5 %collective-permute-start = (bf16[512,128]{1,0:T(8,128)(2,1)S(1)}, bf16[512,128]{1,0:T(8,128)(2,1)S(1)}, u32[]{:S(2)}, u32[]{:S(2)}) collective-permute-start(bf16[512,128]{1,0:T(8,128)(2,1)S(1)} %get-tuple-element.293), channel_id=1, source_target_pairs={{0,504},{8,0},{16,8},{24,16},{32,24},{40,32},{48,40},{56,48},{64,5... | collective-permute-start | bytes 393224 | tf_op jit(solution)/shard_map/while/body/eval_jaxpr/ppermute | solution.py:12
  167.4 12.1 %gather_fusion = bf16[4096,128]{1,0:T(8,128)(2,1)S(1)} fusion(bf16[512,128]{1,0:T(8,128)(2,1)S(1)} %collective-permute-done, s32[4096]{0:T(1024)S(1)} %broadcast_clamp_fusion.3), kind=kCustom, calls=%fused_computation.clone.clone.1 | custom fusion | bytes 2113536 | tf_op jit(solution)/shard_map/while/body/eval_jaxpr/jit(_take)/gather | solution.py:51
  179.5 2.1 broadcast_select_fusion.6
  182.3 8.5 %collective-permute-start = (bf16[512,128]{1,0:T(8,128)(2,1)S(1)}, bf16[512,128]{1,0:T(8,128)(2,1)S(1)}, u32[]{:S(2)}, u32[]{:S(2)}) collective-permute-start(bf16[512,128]{1,0:T(8,128)(2,1)S(1)} %get-tuple-element.293), channel_id=1, source_target_pairs={{0,504},{8,0},{16,8},{24,16},{32,24},{40,32},{48,40},{56,48},{64,5... | collective-permute-start | bytes 393224 | tf_op jit(solution)/shard_map/while/body/eval_jaxpr/ppermute | solution.py:12
  193.2 12.1 %gather_fusion = bf16[4096,128]{1,0:T(8,128)(2,1)S(1)} fusion(bf16[512,128]{1,0:T(8,128)(2,1)S(1)} %collective-permute-done, s32[4096]{0:T(1024)S(1)} %broadcast_clamp_fusion.3), kind=kCustom, calls=%fused_computation.clone.clone.1 | custom fusion | bytes 2113536 | tf_op jit(solution)/shard_map/while/body/eval_jaxpr/jit(_take)/gather | solution.py:51
  205.4 2.1 broadcast_select_fusion.6
  208.1 8.5 %collective-permute-start = (bf16[512,128]{1,0:T(8,128)(2,1)S(1)}, bf16[512,128]{1,0:T(8,128)(2,1)S(1)}, u32[]{:S(2)}, u32[]{:S(2)}) collective-permute-start(bf16[512,128]{1,0:T(8,128)(2,1)S(1)} %get-tuple-element.293), channel_id=1, source_target_pairs={{0,504},{8,0},{16,8},{24,16},{32,24},{40,32},{48,40},{56,48},{64,5... | collective-permute-start | bytes 393224 | tf_op jit(solution)/shard_map/while/body/eval_jaxpr/ppermute | solution.py:12
  219.0 12.1 %gather_fusion = bf16[4096,128]{1,0:T(8,128)(2,1)S(1)} fusion(bf16[512,128]{1,0:T(8,128)(2,1)S(1)} %collective-permute-done, s32[4096]{0:T(1024)S(1)} %broadcast_clamp_fusion.3), kind=kCustom, calls=%fused_computation.clone.clone.1 | custom fusion | bytes 2113536 | tf_op jit(solution)/shard_map/while/body/eval_jaxpr/jit(_take)/gather | solution.py:51
  231.2 2.1 broadcast_select_fusion.6
  233.9 3.4 %collective-permute-start.4 = (f32[2,2,64,128]{3,2,1,0:T(8,128)S(1)}, f32[2,2,64,128]{3,2,1,0:T(8,128)S(1)}, u32[]{:S(2)}, u32[]{:S(2)}) collective-permute-start(f32[2,2,64,128]{3,2,1,0:T(8,128)S(1)} %dynamic-slice_bitcast_fusion), channel_id=1, source_target_pairs={{0,1},{1,0},{2,3},{3,2},{4,5},{5,4},{6,7},{7,6},{8,9},{9,8},{10,11... | collective-permute-start | bytes 393224 | tf_op jit(solution)/shard_map/ppermute | solution.py:36
  237.3 3.4 %collective-permute-done.4 = f32[2,2,64,128]{3,2,1,0:T(8,128)S(1)} collective-permute-done((f32[2,2,64,128]{3,2,1,0:T(8,128)S(1)}, f32[2,2,64,128]{3,2,1,0:T(8,128)S(1)}, u32[]{:S(2)}, u32[]{:S(2)}) %collective-permute-start.4) | collective-permute-done | bytes 131104 | tf_op jit(solution)/shard_map/ppermute | solution.py:36
  240.8 2.6 collective-permute-start.5
  243.5 3.5 %collective-permute-done.5 = f32[2,64,128]{2,1,0:T(8,128)S(1)} collective-permute-done((f32[2,64,128]{2,1,0:T(8,128)S(1)}, f32[2,64,128]{2,1,0:T(8,128)S(1)}, u32[]{:S(2)}, u32[]{:S(2)}) %collective-permute-start.5) | collective-permute-done | bytes 65568 | tf_op jit(solution)/shard_map/ppermute | solution.py:36
  247.0 3.2 collective-permute-start.6
  250.3 4.0 %collective-permute-done.6 = f32[64,128]{1,0:T(8,128)S(1)} collective-permute-done((f32[64,128]{1,0:T(8,128)S(1)}, f32[64,128]{1,0:T(8,128)S(1)}, u32[]{:S(2)}, u32[]{:S(2)}) %collective-permute-start.6) | collective-permute-done | bytes 32800 | tf_op jit(solution)/shard_map/ppermute | solution.py:36
  255.5 1.9 collective-permute-start.7
  258.7 3.4 %collective-permute-start.8 = (f32[136,256]{1,0:T(8,128)S(1)}, f32[136,256]{1,0:T(8,128)S(1)}, u32[]{:S(2)}, u32[]{:S(2)}) collective-permute-start(f32[136,256]{1,0:T(8,128)S(1)} %fusion.29), channel_id=1, source_target_pairs={{0,1},{1,0},{2,3},{3,2},{4,5},{5,4},{6,7},{7,6},{8,9},{9,8},{10,11... | collective-permute-start | bytes 417800 | tf_op jit(solution)/shard_map/ppermute | solution.py:20
  262.2 4.2 %collective-permute-done.8 = f32[136,256]{1,0:T(8,128)S(1)} collective-permute-done((f32[136,256]{1,0:T(8,128)S(1)}, f32[136,256]{1,0:T(8,128)S(1)}, u32[]{:S(2)}, u32[]{:S(2)}) %collective-permute-start.8) | collective-permute-done | bytes 139296 | tf_op jit(solution)/shard_map/ppermute | solution.py:20
  266.4 2.6 collective-permute-start.9
  269.0 4.3 %collective-permute-done.9 = f32[136,256]{1,0:T(8,128)S(1)} collective-permute-done((f32[136,256]{1,0:T(8,128)S(1)}, f32[136,256]{1,0:T(8,128)S(1)}, u32[]{:S(2)}, u32[]{:S(2)}) %collective-permute-start.9) | collective-permute-done | bytes 139296 | tf_op jit(solution)/shard_map/ppermute | solution.py:20
  275.3 5.0 %collective-permute-done.10 = f32[136,256]{1,0:T(8,128)S(1)} collective-permute-done((f32[136,256]{1,0:T(8,128)S(1)}, f32[136,256]{1,0:T(8,128)S(1)}, u32[]{:S(2)}, u32[]{:S(2)}) %collective-permute-start.10) | collective-permute-done | bytes 139296 | tf_op jit(solution)/shard_map/ppermute | solution.py:20
  280.3 1.9 collective-permute-start.11
  282.2 7.4 %collective-permute-done.11 = f32[136,256]{1,0:T(8,128)S(1)} collective-permute-done((f32[136,256]{1,0:T(8,128)S(1)}, f32[136,256]{1,0:T(8,128)S(1)}, u32[]{:S(2)}, u32[]{:S(2)}) %collective-permute-start.11) | collective-permute-done | bytes 139296 | tf_op jit(solution)/shard_map/ppermute | solution.py:20
  289.7 3.2 collective-permute-start.12
  292.9 5.2 %collective-permute-done.12 = f32[136,256]{1,0:T(8,128)S(1)} collective-permute-done((f32[136,256]{1,0:T(8,128)S(1)}, f32[136,256]{1,0:T(8,128)S(1)}, u32[]{:S(2)}, u32[]{:S(2)}) %collective-permute-start.12) | collective-permute-done | bytes 139296 | tf_op jit(solution)/shard_map/ppermute | solution.py:20
  300.1 6.9 %collective-permute-done.13 = f32[136,256]{1,0:T(8,128)S(1)} collective-permute-done((f32[136,256]{1,0:T(8,128)S(1)}, f32[136,256]{1,0:T(8,128)S(1)}, u32[]{:S(2)}, u32[]{:S(2)}) %collective-permute-start.13) | collective-permute-done | bytes 139296 | tf_op jit(solution)/shard_map/ppermute | solution.py:20
  308.9 8.9 %collective-permute-done.14 = f32[136,256]{1,0:T(8,128)S(1)} collective-permute-done((f32[136,256]{1,0:T(8,128)S(1)}, f32[136,256]{1,0:T(8,128)S(1)}, u32[]{:S(2)}, u32[]{:S(2)}) %collective-permute-start.14) | collective-permute-done | bytes 139296 | tf_op jit(solution)/shard_map/ppermute | solution.py:20
  319.8 8.9 %collective-permute-done.15 = f32[136,256]{1,0:T(8,128)S(1)} collective-permute-done((f32[136,256]{1,0:T(8,128)S(1)}, f32[136,256]{1,0:T(8,128)S(1)}, u32[]{:S(2)}, u32[]{:S(2)}) %collective-permute-start.15) | collective-permute-done | bytes 139296 | tf_op jit(solution)/shard_map/ppermute | solution.py:20
  (110 shorter events, 39.6 us)
Async XLA Ops:
  0.6 253.8 %copy-start = (bf16[128,256]{1,0:T(8,128)(2,1)S(1)}, bf16[128,256]{1,0:T(8,128)(2,1)}, u32[]{:S(2)}) copy-start(bf16[128,256]{1,0:T(8,128)(2,1)} %param.17) | copy-start | bytes 196612
  0.6 27.8 %copy-start.1 = (s32[4,8,8,128]{3,2,1,0:T(8,128)S(1)}, s32[4,8,8,128]{3,2,1,0:T(8,128)}, u32[]{:S(2)}) copy-start(s32[4,8,8,128]{3,2,1,0:T(8,128)} %param.16) | copy-start | bytes 393220
  2.4 8.1 %collective-permute-start.1 = (bf16[512,128]{1,0:T(8,128)(2,1)S(1)}, bf16[512,128]{1,0:T(8,128)(2,1)S(1)}, u32[]{:S(2)}, u32[]{:S(2)}) collective-permute-start(bf16[512,128]{1,0:T(8,128)(2,1)S(1)} %multiply_convert_fusion), channel_id=1, source_target_pairs={{0,448},{8,456},{16,464},{24,472},{32,480},{40,488},{48,496},{56,5... | collective-permute-start | bytes 393224 | tf_op jit(solution)/shard_map/ppermute | solution.py:12
  11.6 9.2 %collective-permute-start.2 = (bf16[512,128]{1,0:T(8,128)(2,1)S(1)}, bf16[512,128]{1,0:T(8,128)(2,1)S(1)}, u32[]{:S(2)}, u32[]{:S(2)}) collective-permute-start(bf16[512,128]{1,0:T(8,128)(2,1)S(1)} %broadcast_select_fusion.2), channel_id=1, source_target_pairs={{0,384},{8,392},{16,400},{24,408},{32,416},{40,424},{48,432},{56,4... | collective-permute-start | bytes 393224 | tf_op jit(solution)/shard_map/ppermute | solution.py:12
  20.8 12.1 %collective-permute-start.3 = (bf16[512,128]{1,0:T(8,128)(2,1)S(1)}, bf16[512,128]{1,0:T(8,128)(2,1)S(1)}, u32[]{:S(2)}, u32[]{:S(2)}) collective-permute-start(bf16[512,128]{1,0:T(8,128)(2,1)S(1)} %broadcast_select_fusion.3), channel_id=1, source_target_pairs={{0,256},{8,264},{16,272},{24,280},{32,288},{40,296},{48,304},{56,3... | collective-permute-start | bytes 393224 | tf_op jit(solution)/shard_map/ppermute | solution.py:12
  47.7 16.4 %collective-permute-start = (bf16[512,128]{1,0:T(8,128)(2,1)S(1)}, bf16[512,128]{1,0:T(8,128)(2,1)S(1)}, u32[]{:S(2)}, u32[]{:S(2)}) collective-permute-start(bf16[512,128]{1,0:T(8,128)(2,1)S(1)} %get-tuple-element.293), channel_id=1, source_target_pairs={{0,504},{8,0},{16,8},{24,16},{32,24},{40,32},{48,40},{56,48},{64,5... | collective-permute-start | bytes 393224 | tf_op jit(solution)/shard_map/while/body/eval_jaxpr/ppermute | solution.py:12
  78.9 11.0 %collective-permute-start = (bf16[512,128]{1,0:T(8,128)(2,1)S(1)}, bf16[512,128]{1,0:T(8,128)(2,1)S(1)}, u32[]{:S(2)}, u32[]{:S(2)}) collective-permute-start(bf16[512,128]{1,0:T(8,128)(2,1)S(1)} %get-tuple-element.293), channel_id=1, source_target_pairs={{0,504},{8,0},{16,8},{24,16},{32,24},{40,32},{48,40},{56,48},{64,5... | collective-permute-start | bytes 393224 | tf_op jit(solution)/shard_map/while/body/eval_jaxpr/ppermute | solution.py:12
  104.8 11.0 %collective-permute-start = (bf16[512,128]{1,0:T(8,128)(2,1)S(1)}, bf16[512,128]{1,0:T(8,128)(2,1)S(1)}, u32[]{:S(2)}, u32[]{:S(2)}) collective-permute-start(bf16[512,128]{1,0:T(8,128)(2,1)S(1)} %get-tuple-element.293), channel_id=1, source_target_pairs={{0,504},{8,0},{16,8},{24,16},{32,24},{40,32},{48,40},{56,48},{64,5... | collective-permute-start | bytes 393224 | tf_op jit(solution)/shard_map/while/body/eval_jaxpr/ppermute | solution.py:12
  130.6 11.0 %collective-permute-start = (bf16[512,128]{1,0:T(8,128)(2,1)S(1)}, bf16[512,128]{1,0:T(8,128)(2,1)S(1)}, u32[]{:S(2)}, u32[]{:S(2)}) collective-permute-start(bf16[512,128]{1,0:T(8,128)(2,1)S(1)} %get-tuple-element.293), channel_id=1, source_target_pairs={{0,504},{8,0},{16,8},{24,16},{32,24},{40,32},{48,40},{56,48},{64,5... | collective-permute-start | bytes 393224 | tf_op jit(solution)/shard_map/while/body/eval_jaxpr/ppermute | solution.py:12
  156.4 11.0 %collective-permute-start = (bf16[512,128]{1,0:T(8,128)(2,1)S(1)}, bf16[512,128]{1,0:T(8,128)(2,1)S(1)}, u32[]{:S(2)}, u32[]{:S(2)}) collective-permute-start(bf16[512,128]{1,0:T(8,128)(2,1)S(1)} %get-tuple-element.293), channel_id=1, source_target_pairs={{0,504},{8,0},{16,8},{24,16},{32,24},{40,32},{48,40},{56,48},{64,5... | collective-permute-start | bytes 393224 | tf_op jit(solution)/shard_map/while/body/eval_jaxpr/ppermute | solution.py:12
  182.3 11.0 %collective-permute-start = (bf16[512,128]{1,0:T(8,128)(2,1)S(1)}, bf16[512,128]{1,0:T(8,128)(2,1)S(1)}, u32[]{:S(2)}, u32[]{:S(2)}) collective-permute-start(bf16[512,128]{1,0:T(8,128)(2,1)S(1)} %get-tuple-element.293), channel_id=1, source_target_pairs={{0,504},{8,0},{16,8},{24,16},{32,24},{40,32},{48,40},{56,48},{64,5... | collective-permute-start | bytes 393224 | tf_op jit(solution)/shard_map/while/body/eval_jaxpr/ppermute | solution.py:12
  208.1 11.0 %collective-permute-start = (bf16[512,128]{1,0:T(8,128)(2,1)S(1)}, bf16[512,128]{1,0:T(8,128)(2,1)S(1)}, u32[]{:S(2)}, u32[]{:S(2)}) collective-permute-start(bf16[512,128]{1,0:T(8,128)(2,1)S(1)} %get-tuple-element.293), channel_id=1, source_target_pairs={{0,504},{8,0},{16,8},{24,16},{32,24},{40,32},{48,40},{56,48},{64,5... | collective-permute-start | bytes 393224 | tf_op jit(solution)/shard_map/while/body/eval_jaxpr/ppermute | solution.py:12
  233.9 20.5 %copy-start.2 = (bf16[64,256]{1,0:T(8,128)(2,1)S(1)}, bf16[64,256]{1,0:T(8,128)(2,1)}, u32[]{:S(2)}) copy-start(bf16[64,256]{1,0:T(8,128)(2,1)} %param.19) | copy-start | bytes 98308
  233.9 20.5 %copy-start.3 = (f32[256]{0:T(256)S(1)}, f32[256]{0:T(256)}, u32[]{:S(2)}) copy-start(f32[256]{0:T(256)} %param.18) | copy-start | bytes 3076
  233.9 6.9 %collective-permute-start.4 = (f32[2,2,64,128]{3,2,1,0:T(8,128)S(1)}, f32[2,2,64,128]{3,2,1,0:T(8,128)S(1)}, u32[]{:S(2)}, u32[]{:S(2)}) collective-permute-start(f32[2,2,64,128]{3,2,1,0:T(8,128)S(1)} %dynamic-slice_bitcast_fusion), channel_id=1, source_target_pairs={{0,1},{1,0},{2,3},{3,2},{4,5},{5,4},{6,7},{7,6},{8,9},{9,8},{10,11... | collective-permute-start | bytes 393224 | tf_op jit(solution)/shard_map/ppermute | solution.py:36
  240.8 6.2 %collective-permute-start.5 = (f32[2,64,128]{2,1,0:T(8,128)S(1)}, f32[2,64,128]{2,1,0:T(8,128)S(1)}, u32[]{:S(2)}, u32[]{:S(2)}) collective-permute-start(f32[2,64,128]{2,1,0:T(8,128)S(1)} %dynamic-slice_bitcast_fusion.1), channel_id=1, source_target_pairs={{0,2},{1,3},{2,0},{3,1},{4,6},{5,7},{6,4},{7,5},{8,10},{9,11},{10,... | collective-permute-start | bytes 196616 | tf_op jit(solution)/shard_map/ppermute | solution.py:36
  247.0 7.3 %collective-permute-start.6 = (f32[64,128]{1,0:T(8,128)S(1)}, f32[64,128]{1,0:T(8,128)S(1)}, u32[]{:S(2)}, u32[]{:S(2)}) collective-permute-start(f32[64,128]{1,0:T(8,128)S(1)} %dynamic-slice_bitcast_fusion.2), channel_id=1, source_target_pairs={{0,4},{1,5},{2,6},{3,7},{4,0},{5,1},{6,2},{7,3},{8,12},{9,13},{10,... | collective-permute-start | bytes 98312 | tf_op jit(solution)/shard_map/ppermute | solution.py:36
  255.5 3.3 collective-permute-start.7
  258.7 7.6 %collective-permute-start.8 = (f32[136,256]{1,0:T(8,128)S(1)}, f32[136,256]{1,0:T(8,128)S(1)}, u32[]{:S(2)}, u32[]{:S(2)}) collective-permute-start(f32[136,256]{1,0:T(8,128)S(1)} %fusion.29), channel_id=1, source_target_pairs={{0,1},{1,0},{2,3},{3,2},{4,5},{5,4},{6,7},{7,6},{8,9},{9,8},{10,11... | collective-permute-start | bytes 417800 | tf_op jit(solution)/shard_map/ppermute | solution.py:20
  266.4 6.9 %collective-permute-start.9 = (f32[136,256]{1,0:T(8,128)S(1)}, f32[136,256]{1,0:T(8,128)S(1)}, u32[]{:S(2)}, u32[]{:S(2)}) collective-permute-start(f32[136,256]{1,0:T(8,128)S(1)} %add.267), channel_id=1, source_target_pairs={{0,2},{1,3},{2,0},{3,1},{4,6},{5,7},{6,4},{7,5},{8,10},{9,11},{10,... | collective-permute-start | bytes 417800 | tf_op jit(solution)/shard_map/ppermute | solution.py:20
  273.3 6.9 %collective-permute-start.10 = (f32[136,256]{1,0:T(8,128)S(1)}, f32[136,256]{1,0:T(8,128)S(1)}, u32[]{:S(2)}, u32[]{:S(2)}) collective-permute-start(f32[136,256]{1,0:T(8,128)S(1)} %add.268), channel_id=1, source_target_pairs={{0,64},{1,65},{2,66},{3,67},{4,68},{5,69},{6,70},{7,71},{8,72},{9,... | collective-permute-start | bytes 417800 | tf_op jit(solution)/shard_map/ppermute | solution.py:20
  280.3 9.3 %collective-permute-start.11 = (f32[136,256]{1,0:T(8,128)S(1)}, f32[136,256]{1,0:T(8,128)S(1)}, u32[]{:S(2)}, u32[]{:S(2)}) collective-permute-start(f32[136,256]{1,0:T(8,128)S(1)} %add.269), channel_id=1, source_target_pairs={{0,16},{1,17},{2,18},{3,19},{4,20},{5,21},{6,22},{7,23},{8,24},{9,... | collective-permute-start | bytes 417800 | tf_op jit(solution)/shard_map/ppermute | solution.py:20
  289.7 8.5 %collective-permute-start.12 = (f32[136,256]{1,0:T(8,128)S(1)}, f32[136,256]{1,0:T(8,128)S(1)}, u32[]{:S(2)}, u32[]{:S(2)}) collective-permute-start(f32[136,256]{1,0:T(8,128)S(1)} %add.270), channel_id=1, source_target_pairs={{0,4},{1,5},{2,6},{3,7},{4,0},{5,1},{6,2},{7,3},{8,12},{9,13},{10,... | collective-permute-start | bytes 417800 | tf_op jit(solution)/shard_map/ppermute | solution.py:20
  298.1 8.8 %collective-permute-start.13 = (f32[136,256]{1,0:T(8,128)S(1)}, f32[136,256]{1,0:T(8,128)S(1)}, u32[]{:S(2)}, u32[]{:S(2)}) collective-permute-start(f32[136,256]{1,0:T(8,128)S(1)} %add.271), channel_id=1, source_target_pairs={{0,128},{1,129},{2,130},{3,131},{4,132},{5,133},{6,134},{7,135},{8... | collective-permute-start | bytes 417800 | tf_op jit(solution)/shard_map/ppermute | solution.py:20
  307.0 10.9 %collective-permute-start.14 = (f32[136,256]{1,0:T(8,128)S(1)}, f32[136,256]{1,0:T(8,128)S(1)}, u32[]{:S(2)}, u32[]{:S(2)}) collective-permute-start(f32[136,256]{1,0:T(8,128)S(1)} %add.272), channel_id=1, source_target_pairs={{0,32},{1,33},{2,34},{3,35},{4,36},{5,37},{6,38},{7,39},{8,40},{9,... | collective-permute-start | bytes 417800 | tf_op jit(solution)/shard_map/ppermute | solution.py:20
  317.8 10.9 %collective-permute-start.15 = (f32[136,256]{1,0:T(8,128)S(1)}, f32[136,256]{1,0:T(8,128)S(1)}, u32[]{:S(2)}, u32[]{:S(2)}) collective-permute-start(f32[136,256]{1,0:T(8,128)S(1)} %add.273), channel_id=1, source_target_pairs={{0,256},{1,257},{2,258},{3,259},{4,260},{5,261},{6,262},{7,263},{8... | collective-permute-start | bytes 417800 | tf_op jit(solution)/shard_map/ppermute | solution.py:20

commit v2 on v1

--- a/solution.py
+++ b/solution.py
@@ -48,9 +48,11 @@
     block_total, slot_count, edge_cap = codes.shape
     feat_width = buffer.shape[1]
     far_node = block_ids[:, :, None] * 128 + codes % 128
-    picked = jnp.take(buffer, far_node.reshape(-1), axis=0).reshape(
-        block_total, slot_count, edge_cap, feat_width
-    )
+    col_iota = lax.broadcasted_iota(jnp.int32, (1, 1, 1, buffer.shape[0]), 3)
+    onehot_col = (far_node[..., None] == col_iota).astype(jnp.bfloat16)
+    picked = jnp.einsum(
+        "bkec,cf->bkef", onehot_col, buffer, preferred_element_type=jnp.float32
+    ).astype(jnp.bfloat16)
     is_live = lax.broadcasted_iota(jnp.int32, codes.shape, 2) < live_count[:, :, None]
     target = jnp.where(is_live, codes // 128, -1)
     row_iota = lax.broadcasted_iota(jnp.int32, (1, 1, 128, 1), 2)
@@ -70,19 +72,21 @@
     def local_sums(buffer, offset):
         return tile_sums(buffer, offset, tile_block, edge_count, edge_code)
 
-    buffer = scaled
-    for bit_index in range(replicas.bit_length() - 1):
-        shifted = from_behind(buffer, "rows", -(step_count << bit_index))
-        select = replica // (1 << bit_index) % 2 == 1
-        buffer = jnp.where(select, shifted, buffer)
-    partial_total = local_sums(buffer, 0)
-
-    def advance(step_index, loop_state):
-        current, running = loop_state
-        current = from_behind(current, "rows", -1)
-        return (current, running + local_sums(current, step_index))
-
-    buffer, partial_total = lax.fori_loop(1, step_count, advance, (buffer, partial_total))
+    row_count = lax.axis_size("rows")
+    pairs = []
+    for rep_index in range(replicas):
+        for source in range(row_count):
+            target = (source - step_count * rep_index) % row_count
+            pairs.append((source * replicas + rep_index, target * replicas + rep_index))
+    current = lax.ppermute(scaled, ("rows", "rep"), pairs)
+    partial_total = None
+    for step_index in range(step_count):
+        if step_index + 1 < step_count:
+            following = from_behind(current, "rows", -1)
+        sums = local_sums(current, step_index)
+        partial_total = sums if partial_total is None else partial_total + sums
+        if step_index + 1 < step_count:
+            current = following
     edge_sums = halving_scatter(partial_total, "rep")
     share_rows = edge_sums.shape[0]
     share_start = replica * share_rows

time: 332 us -> 199 us (0.60)
  local copies, waits for them, and re-layouts: 104 us -> 1.4 us
  other arithmetic: 24.6 us -> 2.38 us
  matrix products: 4.71 us -> 17.2 us
  starting transfers between devices: 113 us -> 102 us
  waiting for transfers between devices: 81.7 us -> 73.3 us
    gather x8 -> x0, local copies, waits for them, and re-layouts: 97 us -> none  [tile_sums(): jnp.take(buffer, far_node.reshape(-1), axis=0)]
    ppermute x10 -> x7, starting transfers between devices: 82.9 us -> 62 us  [from_behind(): return lax.ppermute(value, axis, pairs)]
    select_n x11 -> x0, other arithmetic: 18.2 us -> none  [the longest x8 17.2 us: tile_sums(): jnp.take(buffer, far_node.reshape(-1), axis=0)]
    ppermute x10 -> x7, waiting for transfers between devices: 18.6 us -> 3.13 us  [from_behind(): return lax.ppermute(value, axis, pairs)]
    dot_general x8, matrix products: 3.71 us -> 16.2 us  [tile_sums(): jnp.einsum('bkre,bkef->brf', onehot, picked, preferred_element_type=jnp.f...]
    ppermute x0 -> x1, waiting for transfers between devices: none -> 5.7 us  [local(): current = lax.ppermute(scaled, ('rows', 'rep'), pairs)]
    ppermute x3, starting transfers between devices: 9.28 us -> 14.5 us  [halving_scatter(): buf = keep + lax.ppermute(send, axis, pairs)]
    dynamic_slice x7 -> x0, local copies, waits for them, and re-layouts: 5.23 us -> none  [tile_sums(): block_ids = lax.dynamic_index_in_dim(tile_block, offset, 1, keepdims=False)]
  transfers between devices with their start and end apart: 22 -> 20, of which waited for: 22 -> 20; matrix products, arithmetic and copies ran while one was open for 3% -> 7% of each run, Pallas kernels for 0% -> 0%
where the time goes in v2:
time: 199 us; the launch traced here: 197 us
  starting transfers between devices  102 us (51%)
  waiting for transfers between devices  73.3 us (37%)
  matrix products  17.2 us (9%)
  other arithmetic  2.38 us (1%)
    ppermute x7, starting transfers between devices, from_behind(): return lax.ppermute(value, axis, pairs)  62 us
    ppermute x9, waiting for transfers between devices, butterfly_sum(): value = value + lax.ppermute(value, axes, pairs)  52 us
    ppermute x9, starting transfers between devices, butterfly_sum(): value = value + lax.ppermute(value, axes, pairs)  21.1 us
    dot_general x8, matrix products, tile_sums(): jnp.einsum('bkre,bkef->brf', onehot, picked, preferred_element_type=jnp.f...  16.2 us
    ppermute x3, starting transfers between devices, halving_scatter(): buf = keep + lax.ppermute(send, axis, pairs)  14.5 us
    ppermute x3, waiting for transfers between devices, halving_scatter(): buf = keep + lax.ppermute(send, axis, pairs)  12.5 us
    ppermute x1, waiting for transfers between devices, local(): current = lax.ppermute(scaled, ('rows', 'rep'), pairs)  5.7 us
    ppermute x1, starting transfers between devices, local(): current = lax.ppermute(scaled, ('rows', 'rep'), pairs)  4.5 us
  transfers between devices with their start and end apart: 20, of which 20 were waited for; matrix products, arithmetic and copies ran while one was open for 7% of the time, Pallas kernels for 0%

profile of v2, /device:TPU:6, one launch (start us, length us, event | category | flops | bytes accessed | tf_op | source)
XLA Modules:
  0.0 197.4 jit_solution(3684873351466948058)
XLA Ops:
  0.7 0.7 convert_rsqrt_fusion
  1.4 1.0 multiply_convert_fusion
  2.5 4.5 %collective-permute-start = (bf16[512,128]{1,0:T(8,128)(2,1)S(1)}, bf16[512,128]{1,0:T(8,128)(2,1)S(1)}, u32[]{:S(2)}, u32[]{:S(2)}) collective-permute-start(bf16[512,128]{1,0:T(8,128)(2,1)S(1)} %multiply_convert_fusion), channel_id=1, source_target_pairs={{0,0},{8,8},{16,16},{24,24},{32,32},{40,40},{48,48},{56,56},{64,64... | collective-permute-start | bytes 393224 | tf_op jit(solution)/shard_map/ppermute | solution.py:81
  7.4 5.7 %collective-permute-done = bf16[512,128]{1,0:T(8,128)(2,1)S(1)} collective-permute-done((bf16[512,128]{1,0:T(8,128)(2,1)S(1)}, bf16[512,128]{1,0:T(8,128)(2,1)S(1)}, u32[]{:S(2)}, u32[]{:S(2)}) %collective-permute-start) | collective-permute-done | bytes 131104 | tf_op jit(solution)/shard_map/ppermute | solution.py:81
  13.1 12.2 %collective-permute-start.1 = (bf16[512,128]{1,0:T(8,128)(2,1)S(1)}, bf16[512,128]{1,0:T(8,128)(2,1)S(1)}, u32[]{:S(2)}, u32[]{:S(2)}) collective-permute-start(bf16[512,128]{1,0:T(8,128)(2,1)S(1)} %collective-permute-done), channel_id=1, source_target_pairs={{0,504},{8,0},{16,8},{24,16},{32,24},{40,32},{48,40},{56,48},{64,5... | collective-permute-start | bytes 393224 | tf_op jit(solution)/shard_map/ppermute | solution.py:12
  25.2 2.0 %fusion.39 = f32[4,128,128]{2,1,0:T(8,128)S(1)} fusion(s32[4,8,128]{2,1,0:T(8,128)S(1)} %get-tuple-element.28, s32[4,8,128]{2,1,0:T(8,128)S(1)} %get-tuple-element.39, bf16[512,128]{1,0:T(8,128)(2,1)S(1)} %collective-permute-done), kind=kOutput, calls=%fused_computation.55 | convolution fusion | flops 674234368 | bytes 425984 | tf_op jit(solution)/shard_map/bkre,bkef->brf/dot_general | solution.py:60
  27.2 0.5 collective-permute-done.1
  27.7 8.1 %collective-permute-start.2 = (bf16[512,128]{1,0:T(8,128)(2,1)S(1)}, bf16[512,128]{1,0:T(8,128)(2,1)S(1)}, u32[]{:S(2)}, u32[]{:S(2)}) collective-permute-start(bf16[512,128]{1,0:T(8,128)(2,1)S(1)} %collective-permute-done.1), channel_id=1, source_target_pairs={{0,504},{8,0},{16,8},{24,16},{32,24},{40,32},{48,40},{56,48},{64,5... | collective-permute-start | bytes 393224 | tf_op jit(solution)/shard_map/ppermute | solution.py:12
  35.8 2.0 %fusion.40 = f32[4,128,128]{2,1,0:T(8,128)S(1)} fusion(f32[4,128,128]{2,1,0:T(8,128)S(1)} %fusion.39, s32[4,8,128]{2,1,0:T(8,128)S(1)} %get-tuple-element.25, s32[4,8,128]{2,1,0:T(8,128)S(1)} %get-tuple-element.35, bf16[512,128]{1,0:T(8,128)(2,1)S(1)} %collective-permute-done.1), kind=kOutput, calls=%fused_computation.56 | convolution fusion | flops 674299904 | bytes 688128 | tf_op jit(solution)/shard_map/bkre,bkef->brf/dot_general | solution.py:60
  38.3 8.0 %collective-permute-start.3 = (bf16[512,128]{1,0:T(8,128)(2,1)S(1)}, bf16[512,128]{1,0:T(8,128)(2,1)S(1)}, u32[]{:S(2)}, u32[]{:S(2)}) collective-permute-start(bf16[512,128]{1,0:T(8,128)(2,1)S(1)} %collective-permute-done.2), channel_id=1, source_target_pairs={{0,504},{8,0},{16,8},{24,16},{32,24},{40,32},{48,40},{56,48},{64,5... | collective-permute-start | bytes 393224 | tf_op jit(solution)/shard_map/ppermute | solution.py:12
  46.3 2.0 %fusion.41 = f32[4,128,128]{2,1,0:T(8,128)S(1)} fusion(f32[4,128,128]{2,1,0:T(8,128)S(1)} %fusion.40, s32[4,8,128]{2,1,0:T(8,128)S(1)} %get-tuple-element.27, s32[4,8,128]{2,1,0:T(8,128)S(1)} %get-tuple-element.15, bf16[512,128]{1,0:T(8,128)(2,1)S(1)} %collective-permute-done.2), kind=kOutput, calls=%fused_computation.57 | convolution fusion | flops 674299904 | bytes 688128 | tf_op jit(solution)/shard_map/bkre,bkef->brf/dot_general | solution.py:60
  48.8 8.1 %collective-permute-start.4 = (bf16[512,128]{1,0:T(8,128)(2,1)S(1)}, bf16[512,128]{1,0:T(8,128)(2,1)S(1)}, u32[]{:S(2)}, u32[]{:S(2)}) collective-permute-start(bf16[512,128]{1,0:T(8,128)(2,1)S(1)} %collective-permute-done.3), channel_id=1, source_target_pairs={{0,504},{8,0},{16,8},{24,16},{32,24},{40,32},{48,40},{56,48},{64,5... | collective-permute-start | bytes 393224 | tf_op jit(solution)/shard_map/ppermute | solution.py:12
  56.9 2.0 %fusion.42 = f32[4,128,128]{2,1,0:T(8,128)S(1)} fusion(f32[4,128,128]{2,1,0:T(8,128)S(1)} %fusion.41, s32[4,8,128]{2,1,0:T(8,128)S(1)} %get-tuple-element.23, s32[4,8,128]{2,1,0:T(8,128)S(1)} %get-tuple-element.33, bf16[512,128]{1,0:T(8,128)(2,1)S(1)} %collective-permute-done.3), kind=kOutput, calls=%fused_computation.58 | convolution fusion | flops 674299904 | bytes 688128 | tf_op jit(solution)/shard_map/bkre,bkef->brf/dot_general | solution.py:60
  58.9 0.5 collective-permute-done.4
  59.4 8.7 %collective-permute-start.5 = (bf16[512,128]{1,0:T(8,128)(2,1)S(1)}, bf16[512,128]{1,0:T(8,128)(2,1)S(1)}, u32[]{:S(2)}, u32[]{:S(2)}) collective-permute-start(bf16[512,128]{1,0:T(8,128)(2,1)S(1)} %collective-permute-done.4), channel_id=1, source_target_pairs={{0,504},{8,0},{16,8},{24,16},{32,24},{40,32},{48,40},{56,48},{64,5... | collective-permute-start | bytes 393224 | tf_op jit(solution)/shard_map/ppermute | solution.py:12
  68.1 2.0 %fusion.43 = f32[4,128,128]{2,1,0:T(8,128)S(1)} fusion(f32[4,128,128]{2,1,0:T(8,128)S(1)} %fusion.42, s32[4,8,128]{2,1,0:T(8,128)S(1)} %get-tuple-element.22, s32[4,8,128]{2,1,0:T(8,128)S(1)} %get-tuple-element.31, bf16[512,128]{1,0:T(8,128)(2,1)S(1)} %collective-permute-done.4), kind=kOutput, calls=%fused_computation.59 | convolution fusion | flops 674299904 | bytes 688128 | tf_op jit(solution)/shard_map/bkre,bkef->brf/dot_general | solution.py:60
  70.6 8.6 %collective-permute-start.6 = (bf16[512,128]{1,0:T(8,128)(2,1)S(1)}, bf16[512,128]{1,0:T(8,128)(2,1)S(1)}, u32[]{:S(2)}, u32[]{:S(2)}) collective-permute-start(bf16[512,128]{1,0:T(8,128)(2,1)S(1)} %collective-permute-done.5), channel_id=1, source_target_pairs={{0,504},{8,0},{16,8},{24,16},{32,24},{40,32},{48,40},{56,48},{64,5... | collective-permute-start | bytes 393224 | tf_op jit(solution)/shard_map/ppermute | solution.py:12
  79.2 2.0 %fusion.44 = f32[4,128,128]{2,1,0:T(8,128)S(1)} fusion(f32[4,128,128]{2,1,0:T(8,128)S(1)} %fusion.43, s32[4,8,128]{2,1,0:T(8,128)S(1)} %get-tuple-element.24, s32[4,8,128]{2,1,0:T(8,128)S(1)} %get-tuple-element.37, bf16[512,128]{1,0:T(8,128)(2,1)S(1)} %collective-permute-done.5), kind=kOutput, calls=%fused_computation.60 | convolution fusion | flops 674299904 | bytes 688128 | tf_op jit(solution)/shard_map/bkre,bkef->brf/dot_general | solution.py:60
  81.5 8.4 %collective-permute-start.7 = (bf16[512,128]{1,0:T(8,128)(2,1)S(1)}, bf16[512,128]{1,0:T(8,128)(2,1)S(1)}, u32[]{:S(2)}, u32[]{:S(2)}) collective-permute-start(bf16[512,128]{1,0:T(8,128)(2,1)S(1)} %collective-permute-done.6), channel_id=1, source_target_pairs={{0,504},{8,0},{16,8},{24,16},{32,24},{40,32},{48,40},{56,48},{64,5... | collective-permute-start | bytes 393224 | tf_op jit(solution)/shard_map/ppermute | solution.py:12
  89.9 2.0 %fusion.45 = f32[4,128,128]{2,1,0:T(8,128)S(1)} fusion(f32[4,128,128]{2,1,0:T(8,128)S(1)} %fusion.44, s32[4,8,128]{2,1,0:T(8,128)S(1)} %get-tuple-element.26, s32[4,8,128]{2,1,0:T(8,128)S(1)} %get-tuple-element.29, bf16[512,128]{1,0:T(8,128)(2,1)S(1)} %collective-permute-done.6), kind=kOutput, calls=%fused_computation.61 | convolution fusion | flops 674299904 | bytes 688128 | tf_op jit(solution)/shard_map/bkre,bkef->brf/dot_general | solution.py:60
  92.4 2.0 %fusion.46 = f32[4,128,128]{2,1,0:T(8,128)S(1)} fusion(f32[4,128,128]{2,1,0:T(8,128)S(1)} %fusion.45, s32[4,8,128]{2,1,0:T(8,128)S(1)} %get-tuple-element.21, s32[4,8,128]{2,1,0:T(8,128)S(1)} %get-tuple-element.5, bf16[512,128]{1,0:T(8,128)(2,1)S(1)} %collective-permute-done.7), kind=kOutput, calls=%fused_computation.62 | convolution fusion | flops 674299904 | bytes 688128 | tf_op jit(solution)/shard_map/bkre,bkef->brf/dot_general | solution.py:60
  94.5 1.9 collective-permute-start.8
  96.4 4.9 %collective-permute-done.8 = f32[2,2,64,128]{3,2,1,0:T(8,128)S(1)} collective-permute-done((f32[2,2,64,128]{3,2,1,0:T(8,128)S(1)}, f32[2,2,64,128]{3,2,1,0:T(8,128)S(1)}, u32[]{:S(2)}, u32[]{:S(2)}) %collective-permute-start.8) | collective-permute-done | bytes 131104 | tf_op jit(solution)/shard_map/ppermute | solution.py:36
  101.4 10.7 %collective-permute-start.9 = (f32[2,64,128]{2,1,0:T(8,128)S(1)}, f32[2,64,128]{2,1,0:T(8,128)S(1)}, u32[]{:S(2)}, u32[]{:S(2)}) collective-permute-start(f32[2,64,128]{2,1,0:T(8,128)S(1)} %dynamic-slice_bitcast_fusion.1), channel_id=1, source_target_pairs={{0,2},{1,3},{2,0},{3,1},{4,6},{5,7},{6,4},{7,5},{8,10},{9,11},{10,... | collective-permute-start | bytes 196616 | tf_op jit(solution)/shard_map/ppermute | solution.py:36
  112.1 2.2 %collective-permute-done.9 = f32[2,64,128]{2,1,0:T(8,128)S(1)} collective-permute-done((f32[2,64,128]{2,1,0:T(8,128)S(1)}, f32[2,64,128]{2,1,0:T(8,128)S(1)}, u32[]{:S(2)}, u32[]{:S(2)}) %collective-permute-start.9) | collective-permute-done | bytes 65568 | tf_op jit(solution)/shard_map/ppermute | solution.py:36
  114.4 1.9 collective-permute-start.10
  116.4 5.3 %collective-permute-done.10 = f32[64,128]{1,0:T(8,128)S(1)} collective-permute-done((f32[64,128]{1,0:T(8,128)S(1)}, f32[64,128]{1,0:T(8,128)S(1)}, u32[]{:S(2)}, u32[]{:S(2)}) %collective-permute-start.10) | collective-permute-done | bytes 32800 | tf_op jit(solution)/shard_map/ppermute | solution.py:36
  121.8 0.8 convert_reduce_fusion
  122.8 1.9 collective-permute-start.11
  124.7 1.3 collective-permute-done.11
  126.1 3.1 %collective-permute-start.12 = (f32[136,256]{1,0:T(8,128)S(1)}, f32[136,256]{1,0:T(8,128)S(1)}, u32[]{:S(2)}, u32[]{:S(2)}) collective-permute-start(f32[136,256]{1,0:T(8,128)S(1)} %fusion.124), channel_id=1, source_target_pairs={{0,1},{1,0},{2,3},{3,2},{4,5},{5,4},{6,7},{7,6},{8,9},{9,8},{10,11... | collective-permute-start | bytes 417800 | tf_op jit(solution)/shard_map/ppermute | solution.py:20
  129.2 4.5 %collective-permute-done.12 = f32[136,256]{1,0:T(8,128)S(1)} collective-permute-done((f32[136,256]{1,0:T(8,128)S(1)}, f32[136,256]{1,0:T(8,128)S(1)}, u32[]{:S(2)}, u32[]{:S(2)}) %collective-permute-start.12) | collective-permute-done | bytes 139296 | tf_op jit(solution)/shard_map/ppermute | solution.py:20
  133.7 3.9 %collective-permute-start.13 = (f32[136,256]{1,0:T(8,128)S(1)}, f32[136,256]{1,0:T(8,128)S(1)}, u32[]{:S(2)}, u32[]{:S(2)}) collective-permute-start(f32[136,256]{1,0:T(8,128)S(1)} %add.392), channel_id=1, source_target_pairs={{0,2},{1,3},{2,0},{3,1},{4,6},{5,7},{6,4},{7,5},{8,10},{9,11},{10,... | collective-permute-start | bytes 417800 | tf_op jit(solution)/shard_map/ppermute | solution.py:20
  137.7 3.1 %collective-permute-done.13 = f32[136,256]{1,0:T(8,128)S(1)} collective-permute-done((f32[136,256]{1,0:T(8,128)S(1)}, f32[136,256]{1,0:T(8,128)S(1)}, u32[]{:S(2)}, u32[]{:S(2)}) %collective-permute-start.13) | collective-permute-done | bytes 139296 | tf_op jit(solution)/shard_map/ppermute | solution.py:20
  140.8 1.9 collective-permute-start.14
  142.7 5.0 %collective-permute-done.14 = f32[136,256]{1,0:T(8,128)S(1)} collective-permute-done((f32[136,256]{1,0:T(8,128)S(1)}, f32[136,256]{1,0:T(8,128)S(1)}, u32[]{:S(2)}, u32[]{:S(2)}) %collective-permute-start.14) | collective-permute-done | bytes 139296 | tf_op jit(solution)/shard_map/ppermute | solution.py:20
  147.8 1.9 collective-permute-start.15
  149.7 7.4 %collective-permute-done.15 = f32[136,256]{1,0:T(8,128)S(1)} collective-permute-done((f32[136,256]{1,0:T(8,128)S(1)}, f32[136,256]{1,0:T(8,128)S(1)}, u32[]{:S(2)}, u32[]{:S(2)}) %collective-permute-start.15) | collective-permute-done | bytes 139296 | tf_op jit(solution)/shard_map/ppermute | solution.py:20
  157.1 2.5 %collective-permute-start.16 = (f32[136,256]{1,0:T(8,128)S(1)}, f32[136,256]{1,0:T(8,128)S(1)}, u32[]{:S(2)}, u32[]{:S(2)}) collective-permute-start(f32[136,256]{1,0:T(8,128)S(1)} %add.395), channel_id=1, source_target_pairs={{0,4},{1,5},{2,6},{3,7},{4,0},{5,1},{6,2},{7,3},{8,12},{9,13},{10,... | collective-permute-start | bytes 417800 | tf_op jit(solution)/shard_map/ppermute | solution.py:20
  159.7 5.9 %collective-permute-done.16 = f32[136,256]{1,0:T(8,128)S(1)} collective-permute-done((f32[136,256]{1,0:T(8,128)S(1)}, f32[136,256]{1,0:T(8,128)S(1)}, u32[]{:S(2)}, u32[]{:S(2)}) %collective-permute-start.16) | collective-permute-done | bytes 139296 | tf_op jit(solution)/shard_map/ppermute | solution.py:20
  165.6 1.9 collective-permute-start.17
  167.5 6.9 %collective-permute-done.17 = f32[136,256]{1,0:T(8,128)S(1)} collective-permute-done((f32[136,256]{1,0:T(8,128)S(1)}, f32[136,256]{1,0:T(8,128)S(1)}, u32[]{:S(2)}, u32[]{:S(2)}) %collective-permute-start.17) | collective-permute-done | bytes 139296 | tf_op jit(solution)/shard_map/ppermute | solution.py:20
  174.4 1.9 collective-permute-start.18
  176.3 8.9 %collective-permute-done.18 = f32[136,256]{1,0:T(8,128)S(1)} collective-permute-done((f32[136,256]{1,0:T(8,128)S(1)}, f32[136,256]{1,0:T(8,128)S(1)}, u32[]{:S(2)}, u32[]{:S(2)}) %collective-permute-start.18) | collective-permute-done | bytes 139296 | tf_op jit(solution)/shard_map/ppermute | solution.py:20
  185.3 1.9 collective-permute-start.19
  187.2 8.9 %collective-permute-done.19 = f32[136,256]{1,0:T(8,128)S(1)} collective-permute-done((f32[136,256]{1,0:T(8,128)S(1)}, f32[136,256]{1,0:T(8,128)S(1)}, u32[]{:S(2)}, u32[]{:S(2)}) %collective-permute-start.19) | collective-permute-done | bytes 139296 | tf_op jit(solution)/shard_map/ppermute | solution.py:20
  196.2 0.7 slice.32
  196.8 0.6 slice.33
  (41 shorter events, 3.1 us)
Async XLA Ops:
  0.6 121.1 %copy-start = (bf16[128,256]{1,0:T(8,128)(2,1)S(1)}, bf16[128,256]{1,0:T(8,128)(2,1)}, u32[]{:S(2)}) copy-start(bf16[128,256]{1,0:T(8,128)(2,1)} %param.13) | copy-start | bytes 196612
  0.6 6.3 %copy-start.2 = (s32[4,8,8]{2,1,0:T(8,128)S(1)}, s32[4,8,8]{2,1,0:T(8,128)}, u32[]{:S(2)}) copy-start(s32[4,8,8]{2,1,0:T(8,128)} %param.11) | copy-start | bytes 3076
  0.7 6.4 %copy-start.3 = (s32[4,8,8]{2,1,0:T(8,128)S(1)}, s32[4,8,8]{2,1,0:T(8,128)}, u32[]{:S(2)}) copy-start(s32[4,8,8]{2,1,0:T(8,128)} %param.10) | copy-start | bytes 3076
  0.7 6.4 %copy-start.1 = (s32[4,8,8,128]{3,2,1,0:T(8,128)S(1)}, s32[4,8,8,128]{3,2,1,0:T(8,128)}, u32[]{:S(2)}) copy-start(s32[4,8,8,128]{3,2,1,0:T(8,128)} %param.12) | copy-start | bytes 393220
  2.5 10.6 %collective-permute-start = (bf16[512,128]{1,0:T(8,128)(2,1)S(1)}, bf16[512,128]{1,0:T(8,128)(2,1)S(1)}, u32[]{:S(2)}, u32[]{:S(2)}) collective-permute-start(bf16[512,128]{1,0:T(8,128)(2,1)S(1)} %multiply_convert_fusion), channel_id=1, source_target_pairs={{0,0},{8,8},{16,16},{24,24},{32,32},{40,40},{48,48},{56,56},{64,64... | collective-permute-start | bytes 393224 | tf_op jit(solution)/shard_map/ppermute | solution.py:81
  13.1 14.7 %collective-permute-start.1 = (bf16[512,128]{1,0:T(8,128)(2,1)S(1)}, bf16[512,128]{1,0:T(8,128)(2,1)S(1)}, u32[]{:S(2)}, u32[]{:S(2)}) collective-permute-start(bf16[512,128]{1,0:T(8,128)(2,1)S(1)} %collective-permute-done), channel_id=1, source_target_pairs={{0,504},{8,0},{16,8},{24,16},{32,24},{40,32},{48,40},{56,48},{64,5... | collective-permute-start | bytes 393224 | tf_op jit(solution)/shard_map/ppermute | solution.py:12
  27.7 10.6 %collective-permute-start.2 = (bf16[512,128]{1,0:T(8,128)(2,1)S(1)}, bf16[512,128]{1,0:T(8,128)(2,1)S(1)}, u32[]{:S(2)}, u32[]{:S(2)}) collective-permute-start(bf16[512,128]{1,0:T(8,128)(2,1)S(1)} %collective-permute-done.1), channel_id=1, source_target_pairs={{0,504},{8,0},{16,8},{24,16},{32,24},{40,32},{48,40},{56,48},{64,5... | collective-permute-start | bytes 393224 | tf_op jit(solution)/shard_map/ppermute | solution.py:12
  38.3 10.5 %collective-permute-start.3 = (bf16[512,128]{1,0:T(8,128)(2,1)S(1)}, bf16[512,128]{1,0:T(8,128)(2,1)S(1)}, u32[]{:S(2)}, u32[]{:S(2)}) collective-permute-start(bf16[512,128]{1,0:T(8,128)(2,1)S(1)} %collective-permute-done.2), channel_id=1, source_target_pairs={{0,504},{8,0},{16,8},{24,16},{32,24},{40,32},{48,40},{56,48},{64,5... | collective-permute-start | bytes 393224 | tf_op jit(solution)/shard_map/ppermute | solution.py:12
  48.8 10.6 %collective-permute-start.4 = (bf16[512,128]{1,0:T(8,128)(2,1)S(1)}, bf16[512,128]{1,0:T(8,128)(2,1)S(1)}, u32[]{:S(2)}, u32[]{:S(2)}) collective-permute-start(bf16[512,128]{1,0:T(8,128)(2,1)S(1)} %collective-permute-done.3), channel_id=1, source_target_pairs={{0,504},{8,0},{16,8},{24,16},{32,24},{40,32},{48,40},{56,48},{64,5... | collective-permute-start | bytes 393224 | tf_op jit(solution)/shard_map/ppermute | solution.py:12
  59.4 11.2 %collective-permute-start.5 = (bf16[512,128]{1,0:T(8,128)(2,1)S(1)}, bf16[512,128]{1,0:T(8,128)(2,1)S(1)}, u32[]{:S(2)}, u32[]{:S(2)}) collective-permute-start(bf16[512,128]{1,0:T(8,128)(2,1)S(1)} %collective-permute-done.4), channel_id=1, source_target_pairs={{0,504},{8,0},{16,8},{24,16},{32,24},{40,32},{48,40},{56,48},{64,5... | collective-permute-start | bytes 393224 | tf_op jit(solution)/shard_map/ppermute | solution.py:12
  70.6 10.9 %collective-permute-start.6 = (bf16[512,128]{1,0:T(8,128)(2,1)S(1)}, bf16[512,128]{1,0:T(8,128)(2,1)S(1)}, u32[]{:S(2)}, u32[]{:S(2)}) collective-permute-start(bf16[512,128]{1,0:T(8,128)(2,1)S(1)} %collective-permute-done.5), channel_id=1, source_target_pairs={{0,504},{8,0},{16,8},{24,16},{32,24},{40,32},{48,40},{56,48},{64,5... | collective-permute-start | bytes 393224 | tf_op jit(solution)/shard_map/ppermute | solution.py:12
  81.5 10.9 %collective-permute-start.7 = (bf16[512,128]{1,0:T(8,128)(2,1)S(1)}, bf16[512,128]{1,0:T(8,128)(2,1)S(1)}, u32[]{:S(2)}, u32[]{:S(2)}) collective-permute-start(bf16[512,128]{1,0:T(8,128)(2,1)S(1)} %collective-permute-done.6), channel_id=1, source_target_pairs={{0,504},{8,0},{16,8},{24,16},{32,24},{40,32},{48,40},{56,48},{64,5... | collective-permute-start | bytes 393224 | tf_op jit(solution)/shard_map/ppermute | solution.py:12
  94.5 6.9 %collective-permute-start.8 = (f32[2,2,64,128]{3,2,1,0:T(8,128)S(1)}, f32[2,2,64,128]{3,2,1,0:T(8,128)S(1)}, u32[]{:S(2)}, u32[]{:S(2)}) collective-permute-start(f32[2,2,64,128]{3,2,1,0:T(8,128)S(1)} %dynamic-slice_bitcast_fusion), channel_id=1, source_target_pairs={{0,1},{1,0},{2,3},{3,2},{4,5},{5,4},{6,7},{7,6},{8,9},{9,8},{10,11... | collective-permute-start | bytes 393224 | tf_op jit(solution)/shard_map/ppermute | solution.py:36
  101.4 20.4 %copy-start.4 = (bf16[64,256]{1,0:T(8,128)(2,1)S(1)}, bf16[64,256]{1,0:T(8,128)(2,1)}, u32[]{:S(2)}) copy-start(bf16[64,256]{1,0:T(8,128)(2,1)} %param.15) | copy-start | bytes 98308
  101.4 20.4 %copy-start.5 = (f32[256]{0:T(256)S(1)}, f32[256]{0:T(256)}, u32[]{:S(2)}) copy-start(f32[256]{0:T(256)} %param.14) | copy-start | bytes 3076
  101.4 12.9 %collective-permute-start.9 = (f32[2,64,128]{2,1,0:T(8,128)S(1)}, f32[2,64,128]{2,1,0:T(8,128)S(1)}, u32[]{:S(2)}, u32[]{:S(2)}) collective-permute-start(f32[2,64,128]{2,1,0:T(8,128)S(1)} %dynamic-slice_bitcast_fusion.1), channel_id=1, source_target_pairs={{0,2},{1,3},{2,0},{3,1},{4,6},{5,7},{6,4},{7,5},{8,10},{9,11},{10,... | collective-permute-start | bytes 196616 | tf_op jit(solution)/shard_map/ppermute | solution.py:36
  114.4 7.3 %collective-permute-start.10 = (f32[64,128]{1,0:T(8,128)S(1)}, f32[64,128]{1,0:T(8,128)S(1)}, u32[]{:S(2)}, u32[]{:S(2)}) collective-permute-start(f32[64,128]{1,0:T(8,128)S(1)} %dynamic-slice_bitcast_fusion.2), channel_id=1, source_target_pairs={{0,4},{1,5},{2,6},{3,7},{4,0},{5,1},{6,2},{7,3},{8,12},{9,13},{10,... | collective-permute-start | bytes 98312 | tf_op jit(solution)/shard_map/ppermute | solution.py:36
  122.8 3.3 %collective-permute-start.11 = (f32[136,256]{1,0:T(8,128)S(1)}, f32[136,256]{1,0:T(8,128)S(1)}, u32[]{:S(2)}, u32[]{:S(2)}) collective-permute-start(f32[136,256]{1,0:T(8,128)S(1)} %pad_maximum_fusion), channel_id=1, source_target_pairs={{0,8},{1,9},{2,10},{3,11},{4,12},{5,13},{6,14},{7,15},{8,0},{9,1},... | collective-permute-start | bytes 417800 | tf_op jit(solution)/shard_map/ppermute | solution.py:20
  126.1 7.6 %collective-permute-start.12 = (f32[136,256]{1,0:T(8,128)S(1)}, f32[136,256]{1,0:T(8,128)S(1)}, u32[]{:S(2)}, u32[]{:S(2)}) collective-permute-start(f32[136,256]{1,0:T(8,128)S(1)} %fusion.124), channel_id=1, source_target_pairs={{0,1},{1,0},{2,3},{3,2},{4,5},{5,4},{6,7},{7,6},{8,9},{9,8},{10,11... | collective-permute-start | bytes 417800 | tf_op jit(solution)/shard_map/ppermute | solution.py:20
  133.7 7.0 %collective-permute-start.13 = (f32[136,256]{1,0:T(8,128)S(1)}, f32[136,256]{1,0:T(8,128)S(1)}, u32[]{:S(2)}, u32[]{:S(2)}) collective-permute-start(f32[136,256]{1,0:T(8,128)S(1)} %add.392), channel_id=1, source_target_pairs={{0,2},{1,3},{2,0},{3,1},{4,6},{5,7},{6,4},{7,5},{8,10},{9,11},{10,... | collective-permute-start | bytes 417800 | tf_op jit(solution)/shard_map/ppermute | solution.py:20
  140.8 6.9 %collective-permute-start.14 = (f32[136,256]{1,0:T(8,128)S(1)}, f32[136,256]{1,0:T(8,128)S(1)}, u32[]{:S(2)}, u32[]{:S(2)}) collective-permute-start(f32[136,256]{1,0:T(8,128)S(1)} %add.393), channel_id=1, source_target_pairs={{0,64},{1,65},{2,66},{3,67},{4,68},{5,69},{6,70},{7,71},{8,72},{9,... | collective-permute-start | bytes 417800 | tf_op jit(solution)/shard_map/ppermute | solution.py:20
  147.8 9.3 %collective-permute-start.15 = (f32[136,256]{1,0:T(8,128)S(1)}, f32[136,256]{1,0:T(8,128)S(1)}, u32[]{:S(2)}, u32[]{:S(2)}) collective-permute-start(f32[136,256]{1,0:T(8,128)S(1)} %add.394), channel_id=1, source_target_pairs={{0,16},{1,17},{2,18},{3,19},{4,20},{5,21},{6,22},{7,23},{8,24},{9,... | collective-permute-start | bytes 417800 | tf_op jit(solution)/shard_map/ppermute | solution.py:20
  157.1 8.5 %collective-permute-start.16 = (f32[136,256]{1,0:T(8,128)S(1)}, f32[136,256]{1,0:T(8,128)S(1)}, u32[]{:S(2)}, u32[]{:S(2)}) collective-permute-start(f32[136,256]{1,0:T(8,128)S(1)} %add.395), channel_id=1, source_target_pairs={{0,4},{1,5},{2,6},{3,7},{4,0},{5,1},{6,2},{7,3},{8,12},{9,13},{10,... | collective-permute-start | bytes 417800 | tf_op jit(solution)/shard_map/ppermute | solution.py:20
  165.6 8.8 %collective-permute-start.17 = (f32[136,256]{1,0:T(8,128)S(1)}, f32[136,256]{1,0:T(8,128)S(1)}, u32[]{:S(2)}, u32[]{:S(2)}) collective-permute-start(f32[136,256]{1,0:T(8,128)S(1)} %add.396), channel_id=1, source_target_pairs={{0,128},{1,129},{2,130},{3,131},{4,132},{5,133},{6,134},{7,135},{8... | collective-permute-start | bytes 417800 | tf_op jit(solution)/shard_map/ppermute | solution.py:20
  174.4 10.9 %collective-permute-start.18 = (f32[136,256]{1,0:T(8,128)S(1)}, f32[136,256]{1,0:T(8,128)S(1)}, u32[]{:S(2)}, u32[]{:S(2)}) collective-permute-start(f32[136,256]{1,0:T(8,128)S(1)} %add.397), channel_id=1, source_target_pairs={{0,32},{1,33},{2,34},{3,35},{4,36},{5,37},{6,38},{7,39},{8,40},{9,... | collective-permute-start | bytes 417800 | tf_op jit(solution)/shard_map/ppermute | solution.py:20
  185.3 10.9 %collective-permute-start.19 = (f32[136,256]{1,0:T(8,128)S(1)}, f32[136,256]{1,0:T(8,128)S(1)}, u32[]{:S(2)}, u32[]{:S(2)}) collective-permute-start(f32[136,256]{1,0:T(8,128)S(1)} %add.398), channel_id=1, source_target_pairs={{0,256},{1,257},{2,258},{3,259},{4,260},{5,261},{6,262},{7,263},{8... | collective-permute-start | bytes 417800 | tf_op jit(solution)/shard_map/ppermute | solution.py:20

commit v3 on v2

--- a/solution.py
+++ b/solution.py
@@ -3,7 +3,8 @@
 from jax import lax
 from jax.sharding import PartitionSpec as P
 
-BFLY_BITS = (3, 0, 1, 6, 4, 2, 7, 5, 8)
+ROWS_BITS = (0, 3, 1, 4, 2, 5)
+REP_BITS = (0, 1, 2)
 
 
 def from_behind(value, axis, steps):
@@ -12,12 +13,13 @@
     return lax.ppermute(value, axis, pairs)
 
 
-def butterfly_sum(value, axes, count):
-    for bit in BFLY_BITS:
+def butterfly_sum(value, axis, order):
+    count = lax.axis_size(axis)
+    for bit in order:
         if (1 << bit) >= count:
             continue
         pairs = [(source, source ^ (1 << bit)) for source in range(count)]
-        value = value + lax.ppermute(value, axes, pairs)
+        value = value + lax.ppermute(value, axis, pairs)
     return value
 
 
@@ -65,7 +67,6 @@
     step_count = tile_block.shape[1]
     replicas = lax.axis_size("rep")
     replica = lax.axis_index("rep")
-    devices = lax.axis_size("rows") * replicas
     inv_deg = lax.rsqrt(degree.astype(jnp.float32))
     scaled = (features.astype(jnp.float32) * inv_deg[:, None]).astype(jnp.bfloat16)
 
@@ -78,24 +79,20 @@
         for source in range(row_count):
             target = (source - step_count * rep_index) % row_count
             pairs.append((source * replicas + rep_index, target * replicas + rep_index))
-    current = lax.ppermute(scaled, ("rows", "rep"), pairs)
-    partial_total = None
-    for step_index in range(step_count):
-        if step_index + 1 < step_count:
-            following = from_behind(current, "rows", -1)
-        sums = local_sums(current, step_index)
-        partial_total = sums if partial_total is None else partial_total + sums
-        if step_index + 1 < step_count:
-            current = following
-    edge_sums = halving_scatter(partial_total, "rep")
-    share_rows = edge_sums.shape[0]
-    share_start = replica * share_rows
-    own_rows = lax.dynamic_slice_in_dim(scaled, share_start, share_rows, 0).astype(jnp.float32)
-    own_inv = lax.dynamic_slice_in_dim(inv_deg, share_start, share_rows, 0)
-    aggregate = (own_inv[:, None] * (edge_sums + own_rows)).astype(jnp.bfloat16)
+    held = lax.ppermute(scaled, ("rows", "rep"), pairs)[None]
+    cot_group = lax.all_gather(cotangent, "rep", axis=0, tiled=True)
+    partial_total = local_sums(held[0], 0)
+    while held.shape[0] < step_count:
+        have = held.shape[0]
+        arrived = from_behind(held, "rows", -have)
+        for extra in range(arrived.shape[0]):
+            partial_total = partial_total + local_sums(arrived[extra], have + extra)
+        held = jnp.concatenate([held, arrived], axis=0)
+    edge_sums = butterfly_sum(partial_total, "rep", REP_BITS)
+    aggregate = (inv_deg[:, None] * (edge_sums + scaled.astype(jnp.float32))).astype(jnp.bfloat16)
     pre_act = jnp.dot(aggregate, weight, preferred_element_type=jnp.float32) + bias
     activated, pull_back = jax.vjp(gelu_tanh, pre_act)
-    delta_bf = pull_back(cotangent.astype(jnp.float32))[0].astype(jnp.bfloat16)
+    delta_bf = pull_back(cot_group.astype(jnp.float32))[0].astype(jnp.bfloat16)
     local_weight = lax.dot_general(
         aggregate, delta_bf, (((0,), (0,)), ((), ())), preferred_element_type=jnp.float32
     )
@@ -104,10 +101,12 @@
     packed = jnp.concatenate(
         [local_weight, jnp.broadcast_to(local_bias[None, :], (8, local_bias.shape[0]))], axis=0
     )
-    packed = butterfly_sum(packed, ("rows", "rep"), devices)
+    packed = butterfly_sum(packed, "rows", ROWS_BITS)
     grad_weight = packed[:feat_rows]
     grad_bias = packed[feat_rows]
-    return (activated.astype(jnp.bfloat16), grad_weight, grad_bias)
+    share_rows = cotangent.shape[0]
+    own_act = lax.dynamic_slice_in_dim(activated, replica * share_rows, share_rows, 0)
+    return (own_act.astype(jnp.bfloat16), grad_weight, grad_bias)
 
 
 def solution(mesh):

time: 199 us -> 200 us (level)
  starting transfers between devices: 102 us -> 64.5 us
  blocking collectives: 0 us -> 26.9 us
  waiting for transfers between devices: 73.3 us -> 81.4 us
  other arithmetic: 2.38 us -> 4.88 us
    ppermute x7 -> x3, starting transfers between devices: 62 us -> 19.3 us  [from_behind(): return lax.ppermute(value, axis, pairs)]
    ppermute x7 -> x3, waiting for transfers between devices: 3.13 us -> 33.2 us  [from_behind(): return lax.ppermute(value, axis, pairs)]
    all_gather x0 -> x1, blocking collectives: none -> 26.9 us  [local(): cot_group = lax.all_gather(cotangent, 'rep', axis=0, tiled=True)]
    ppermute x13 -> x10, waiting for transfers between devices: 70.1 us -> 48.2 us  [the longest x9 44 us: butterfly_sum(): value = value + lax.ppermute(value, axis, pairs)]
    ppermute x13 -> x10, starting transfers between devices: 40.1 us -> 45.3 us  [the longest x9 40.8 us: butterfly_sum(): value = value + lax.ppermute(value, axis, pairs)]
  transfers between devices with their start and end apart: 20 -> 13, of which waited for: 20 -> 12; matrix products, arithmetic and copies ran while one was open for 7% -> 5% of each run, Pallas kernels for 0% -> 0%
where the time goes in v3:
time: 200 us; the launch traced here: 198 us
  waiting for transfers between devices  81.4 us (41%)
  starting transfers between devices  64.5 us (32%)
  blocking collectives  26.9 us (13%)
  matrix products  17.2 us (9%)
  other arithmetic  4.88 us (2%)
  local copies, waits for them, and re-layouts  2.29 us (1%)
    ppermute x9, waiting for transfers between devices, butterfly_sum(): value = value + lax.ppermute(value, axis, pairs)  44 us
    ppermute x9, starting transfers between devices, butterfly_sum(): value = value + lax.ppermute(value, axis, pairs)  40.8 us
    ppermute x3, waiting for transfers between devices, from_behind(): return lax.ppermute(value, axis, pairs)  33.2 us
    all_gather x1, blocking collectives, local(): cot_group = lax.all_gather(cotangent, 'rep', axis=0, tiled=True)  26.9 us
    ppermute x3, starting transfers between devices, from_behind(): return lax.ppermute(value, axis, pairs)  19.3 us
    dot_general x8, matrix products, tile_sums(): jnp.einsum('bkre,bkef->brf', onehot, picked, preferred_element_type=jnp.f...  16.4 us
    ppermute x1, starting transfers between devices, local(): held = lax.ppermute(scaled, ('rows', 'rep'), pairs)[None]  4.5 us
    ppermute x1, waiting for transfers between devices, local(): held = lax.ppermute(scaled, ('rows', 'rep'), pairs)[None]  4.24 us
  transfers between devices with their start and end apart: 13, of which 12 were waited for; matrix products, arithmetic and copies ran while one was open for 5% of the time, Pallas kernels for 0%

profile of v3, /device:TPU:6, one launch (start us, length us, event | category | flops | bytes accessed | tf_op | source)
XLA Modules:
  0.0 198.1 jit_solution(17865963059281801463)
XLA Ops:
  0.7 0.7 convert_rsqrt_fusion
  1.4 1.0 multiply_convert_fusion.1
  2.4 4.5 %collective-permute-start = (bf16[512,128]{1,0:T(8,128)(2,1)S(1)}, bf16[512,128]{1,0:T(8,128)(2,1)S(1)}, u32[]{:S(2)}, u32[]{:S(2)}) collective-permute-start(bf16[512,128]{1,0:T(8,128)(2,1)S(1)} %multiply_convert_fusion.1), channel_id=1, source_target_pairs={{0,0},{8,8},{16,16},{24,24},{32,32},{40,40},{48,48},{56,56},{64,64... | collective-permute-start | bytes 393224 | tf_op jit(solution)/shard_map/ppermute | solution.py:82
  6.9 1.0 fusion.112
  8.0 0.8 fusion.76
  8.8 4.2 %collective-permute-done = bf16[512,128]{1,0:T(8,128)(2,1)S(1)} collective-permute-done((bf16[512,128]{1,0:T(8,128)(2,1)S(1)}, bf16[512,128]{1,0:T(8,128)(2,1)S(1)}, u32[]{:S(2)}, u32[]{:S(2)}) %collective-permute-start) | collective-permute-done | bytes 131104 | tf_op jit(solution)/shard_map/ppermute | solution.py:82
  13.0 12.2 %collective-permute-start.1 = (bf16[1,512,128]{2,1,0:T(8,128)(2,1)S(1)}, bf16[1,512,128]{2,1,0:T(8,128)(2,1)S(1)}, u32[]{:S(2)}, u32[]{:S(2)}) collective-permute-start(bf16[1,512,128]{2,1,0:T(8,128)(2,1)S(1)} %bitcast.322), channel_id=1, source_target_pairs={{0,504},{8,0},{16,8},{24,16},{32,24},{40,32},{48,40},{56,48},{64,5... | collective-permute-start | bytes 393224 | tf_op jit(solution)/shard_map/ppermute | solution.py:13
  25.2 1.0 slice_multiply_fusion.7
  26.2 1.5 collective-permute-done.1
  27.7 3.8 %collective-permute-start.2 = (bf16[2,512,128]{2,1,0:T(8,128)(2,1)S(1)}, bf16[2,512,128]{2,1,0:T(8,128)(2,1)S(1)}, u32[]{:S(2)}, u32[]{:S(2)}) collective-permute-start(bf16[2,512,128]{2,1,0:T(8,128)(2,1)S(1)} %pad_maximum_fusion.1), channel_id=1, source_target_pairs={{0,496},{8,504},{16,0},{24,8},{32,16},{40,24},{48,32},{56,40},{64,... | collective-permute-start | bytes 786440 | tf_op jit(solution)/shard_map/ppermute | solution.py:13
  31.6 0.1 fusion.70
  31.7 0.1 fusion.71
  31.8 12.0 %collective-permute-done.2 = bf16[2,512,128]{2,1,0:T(8,128)(2,1)S(1)} collective-permute-done((bf16[2,512,128]{2,1,0:T(8,128)(2,1)S(1)}, bf16[2,512,128]{2,1,0:T(8,128)(2,1)S(1)}, u32[]{:S(2)}, u32[]{:S(2)}) %collective-permute-start.2) | collective-permute-done | bytes 262176 | tf_op jit(solution)/shard_map/ppermute | solution.py:13
  43.8 0.1 pad_maximum_fusion
  43.9 3.2 %collective-permute-start.3 = (bf16[4,512,128]{2,1,0:T(8,128)(2,1)S(1)}, bf16[4,512,128]{2,1,0:T(8,128)(2,1)S(1)}, u32[]{:S(2)}, u32[]{:S(2)}) collective-permute-start(bf16[4,512,128]{2,1,0:T(8,128)(2,1)S(1)} %pad_maximum_fusion), channel_id=1, source_target_pairs={{0,480},{8,488},{16,496},{24,504},{32,0},{40,8},{48,16},{56,24},{6... | collective-permute-start | bytes 1572872 | tf_op jit(solution)/shard_map/ppermute | solution.py:13
  47.2 2.0 %fusion.38 = f32[4,128,128]{2,1,0:T(8,128)S(1)} fusion(s32[4,8,128]{2,1,0:T(8,128)S(1)} %get-tuple-element.26, s32[4,8,128]{2,1,0:T(8,128)S(1)} %get-tuple-element.36, bf16[1,512,128]{2,1,0:T(8,128)(2,1)S(1)} %collective-permute-done.1), kind=kOutput, calls=%fused_computation.55 | convolution fusion | flops 674234368 | bytes 425984 | tf_op jit(solution)/shard_map/bkre,bkef->brf/dot_general | solution.py:62
  49.2 2.0 %fusion.36 = f32[4,128,128]{2,1,0:T(8,128)S(1)} fusion(s32[4,8,128]{2,1,0:T(8,128)S(1)} %get-tuple-element.28, s32[4,8,128]{2,1,0:T(8,128)S(1)} %get-tuple-element.11, bf16[2,512,128]{2,1,0:T(8,128)(2,1)S(1)} %collective-permute-done.2), kind=kOutput, calls=%fused_computation.53 | convolution fusion | flops 674234368 | bytes 425984 | tf_op jit(solution)/shard_map/bkre,bkef->brf/dot_general | solution.py:62
  51.2 2.0 %fusion.37 = f32[4,128,128]{2,1,0:T(8,128)S(1)} fusion(s32[4,8,128]{2,1,0:T(8,128)S(1)} %get-tuple-element.24, s32[4,8,128]{2,1,0:T(8,128)S(1)} %get-tuple-element.34, bf16[2,512,128]{2,1,0:T(8,128)(2,1)S(1)} %collective-permute-done.2), kind=kOutput, calls=%fused_computation.54 | convolution fusion | flops 674234368 | bytes 425984 | tf_op jit(solution)/shard_map/bkre,bkef->brf/dot_general | solution.py:62
  53.2 19.7 %collective-permute-done.3 = bf16[4,512,128]{2,1,0:T(8,128)(2,1)S(1)} collective-permute-done((bf16[4,512,128]{2,1,0:T(8,128)(2,1)S(1)}, bf16[4,512,128]{2,1,0:T(8,128)(2,1)S(1)}, u32[]{:S(2)}, u32[]{:S(2)}) %collective-permute-start.3) | collective-permute-done | bytes 524320 | tf_op jit(solution)/shard_map/ppermute | solution.py:13
  73.0 2.0 %fusion.32 = f32[4,128,128]{2,1,0:T(8,128)S(1)} fusion(s32[4,8,128]{2,1,0:T(8,128)S(1)} %get-tuple-element.29, s32[4,8,128]{2,1,0:T(8,128)S(1)} %get-tuple-element.40, bf16[4,512,128]{2,1,0:T(8,128)(2,1)S(1)} %collective-permute-done.3), kind=kOutput, calls=%fused_computation.49 | convolution fusion | flops 674234368 | bytes 425984 | tf_op jit(solution)/shard_map/bkre,bkef->brf/dot_general | solution.py:62
  75.0 2.0 %fusion.33 = f32[4,128,128]{2,1,0:T(8,128)S(1)} fusion(s32[4,8,128]{2,1,0:T(8,128)S(1)} %get-tuple-element.27, s32[4,8,128]{2,1,0:T(8,128)S(1)} %get-tuple-element.30, bf16[4,512,128]{2,1,0:T(8,128)(2,1)S(1)} %collective-permute-done.3), kind=kOutput, calls=%fused_computation.50 | convolution fusion | flops 674234368 | bytes 425984 | tf_op jit(solution)/shard_map/bkre,bkef->brf/dot_general | solution.py:62
  77.0 2.2 %fusion.34 = f32[4,128,128]{2,1,0:T(8,128)S(1)} fusion(s32[4,8,128]{2,1,0:T(8,128)S(1)} %get-tuple-element.25, s32[4,8,128]{2,1,0:T(8,128)S(1)} %get-tuple-element.38, bf16[4,512,128]{2,1,0:T(8,128)(2,1)S(1)} %collective-permute-done.3), kind=kOutput, calls=%fused_computation.51 | convolution fusion | flops 674234368 | bytes 425984 | tf_op jit(solution)/shard_map/bkre,bkef->brf/dot_general | solution.py:62
  79.2 2.0 %fusion.35 = f32[4,128,128]{2,1,0:T(8,128)S(1)} fusion(s32[4,8,128]{2,1,0:T(8,128)S(1)} %get-tuple-element.23, s32[4,8,128]{2,1,0:T(8,128)S(1)} %get-tuple-element.32, bf16[4,512,128]{2,1,0:T(8,128)(2,1)S(1)} %collective-permute-done.3), kind=kOutput, calls=%fused_computation.52 | convolution fusion | flops 674234368 | bytes 425984 | tf_op jit(solution)/shard_map/bkre,bkef->brf/dot_general | solution.py:62
  81.2 2.1 %fusion.46 = f32[4,128,128]{2,1,0:T(8,128)S(1)} fusion(f32[4,128,128]{2,1,0:T(8,128)S(1)} %fusion.32, f32[4,128,128]{2,1,0:T(8,128)S(1)} %fusion.33, f32[4,128,128]{2,1,0:T(8,128)S(1)} %fusion.34, f32[4,128,128]{2,1,0:T(8,128)S(1)} %fusion.35, f32[4,128,128]{2,1,0:T(8,128)S(1)} %fusion.36, f32[4,128,128]{2,1,0:T(8,128)S(1)} %fusion.37, ...), kind=kOutput, calls=%fused_computation.63 | convolution fusion | flops 674693120 | bytes 2260992 | tf_op jit(solution)/shard_map/bkre,bkef->brf/dot_general | solution.py:62
  83.3 1.9 collective-permute-start.4
  85.2 6.3 %collective-permute-done.4 = f32[512,128]{1,0:T(8,128)S(1)} collective-permute-done((f32[512,128]{1,0:T(8,128)S(1)}, f32[512,128]{1,0:T(8,128)S(1)}, u32[]{:S(2)}, u32[]{:S(2)}) %collective-permute-start.4) | collective-permute-done | bytes 262176 | tf_op jit(solution)/shard_map/ppermute | solution.py:22
  91.6 6.2 %collective-permute-start.5 = (f32[512,128]{1,0:T(8,128)S(1)}, f32[512,128]{1,0:T(8,128)S(1)}, u32[]{:S(2)}, u32[]{:S(2)}) collective-permute-start(f32[512,128]{1,0:T(8,128)S(1)} %bitcast_add_fusion), channel_id=1, source_target_pairs={{0,2},{1,3},{2,0},{3,1},{4,6},{5,7},{6,4},{7,5},{8,10},{9,11},{10,... | collective-permute-start | bytes 786440 | tf_op jit(solution)/shard_map/ppermute | solution.py:22
  97.8 5.8 %collective-permute-done.5 = f32[512,128]{1,0:T(8,128)S(1)} collective-permute-done((f32[512,128]{1,0:T(8,128)S(1)}, f32[512,128]{1,0:T(8,128)S(1)}, u32[]{:S(2)}, u32[]{:S(2)}) %collective-permute-start.5) | collective-permute-done | bytes 262176 | tf_op jit(solution)/shard_map/ppermute | solution.py:22
  103.7 5.7 %collective-permute-start.6 = (f32[512,128]{1,0:T(8,128)S(1)}, f32[512,128]{1,0:T(8,128)S(1)}, u32[]{:S(2)}, u32[]{:S(2)}) collective-permute-start(f32[512,128]{1,0:T(8,128)S(1)} %add.336), channel_id=1, source_target_pairs={{0,4},{1,5},{2,6},{3,7},{4,0},{5,1},{6,2},{7,3},{8,12},{9,13},{10,... | collective-permute-start | bytes 786440 | tf_op jit(solution)/shard_map/ppermute | solution.py:22
  109.3 26.9 %all_gather.3 = bf16[512,256]{1,0:T(8,128)(2,1)S(1)} all-gather(bf16[64,256]{1,0:T(8,128)(2,1)S(1)} %copy-done.3), channel_id=1, replica_groups=mesh['rows'=64,'rep'=8] {'rep'}, dimensions={0}, use_global_device_ids=true | all-gather | bytes 294912 | tf_op jit(solution)/shard_map/all_gather | solution.py:83
  136.2 0.1 multiply_convert_fusion
  136.4 0.6 convert_reduce_fusion
  137.0 0.2 fusion.113
  137.2 1.9 collective-permute-start.7
  139.2 1.3 collective-permute-done.7
  140.5 1.9 collective-permute-start.8
  142.4 5.7 %collective-permute-done.8 = f32[136,256]{1,0:T(8,128)S(1)} collective-permute-done((f32[136,256]{1,0:T(8,128)S(1)}, f32[136,256]{1,0:T(8,128)S(1)}, u32[]{:S(2)}, u32[]{:S(2)}) %collective-permute-start.8) | collective-permute-done | bytes 139296 | tf_op jit(solution)/shard_map/ppermute | solution.py:22
  148.2 4.3 %collective-permute-start.9 = (f32[136,256]{1,0:T(8,128)S(1)}, f32[136,256]{1,0:T(8,128)S(1)}, u32[]{:S(2)}, u32[]{:S(2)}) collective-permute-start(f32[136,256]{1,0:T(8,128)S(1)} %add.345), channel_id=1, source_target_pairs={{0,16},{8,24},{16,0},{24,8},{32,48},{40,56},{48,32},{56,40},{64,80... | collective-permute-start | bytes 417800 | tf_op jit(solution)/shard_map/ppermute | solution.py:22
  152.4 6.6 %collective-permute-done.9 = f32[136,256]{1,0:T(8,128)S(1)} collective-permute-done((f32[136,256]{1,0:T(8,128)S(1)}, f32[136,256]{1,0:T(8,128)S(1)}, u32[]{:S(2)}, u32[]{:S(2)}) %collective-permute-start.9) | collective-permute-done | bytes 139296 | tf_op jit(solution)/shard_map/ppermute | solution.py:22
  159.0 4.4 %collective-permute-start.10 = (f32[136,256]{1,0:T(8,128)S(1)}, f32[136,256]{1,0:T(8,128)S(1)}, u32[]{:S(2)}, u32[]{:S(2)}) collective-permute-start(f32[136,256]{1,0:T(8,128)S(1)} %add.346), channel_id=1, source_target_pairs={{0,128},{8,136},{16,144},{24,152},{32,160},{40,168},{48,176},{56,1... | collective-permute-start | bytes 417800 | tf_op jit(solution)/shard_map/ppermute | solution.py:22
  163.4 5.8 %collective-permute-done.10 = f32[136,256]{1,0:T(8,128)S(1)} collective-permute-done((f32[136,256]{1,0:T(8,128)S(1)}, f32[136,256]{1,0:T(8,128)S(1)}, u32[]{:S(2)}, u32[]{:S(2)}) %collective-permute-start.10) | collective-permute-done | bytes 139296 | tf_op jit(solution)/shard_map/ppermute | solution.py:22
  169.2 5.3 %collective-permute-start.11 = (f32[136,256]{1,0:T(8,128)S(1)}, f32[136,256]{1,0:T(8,128)S(1)}, u32[]{:S(2)}, u32[]{:S(2)}) collective-permute-start(f32[136,256]{1,0:T(8,128)S(1)} %add.347), channel_id=1, source_target_pairs={{0,32},{8,40},{16,48},{24,56},{32,0},{40,8},{48,16},{56,24},{64,96... | collective-permute-start | bytes 417800 | tf_op jit(solution)/shard_map/ppermute | solution.py:22
  174.5 7.1 %collective-permute-done.11 = f32[136,256]{1,0:T(8,128)S(1)} collective-permute-done((f32[136,256]{1,0:T(8,128)S(1)}, f32[136,256]{1,0:T(8,128)S(1)}, u32[]{:S(2)}, u32[]{:S(2)}) %collective-permute-start.11) | collective-permute-done | bytes 139296 | tf_op jit(solution)/shard_map/ppermute | solution.py:22
  181.6 9.3 %collective-permute-start.12 = (f32[136,256]{1,0:T(8,128)S(1)}, f32[136,256]{1,0:T(8,128)S(1)}, u32[]{:S(2)}, u32[]{:S(2)}) collective-permute-start(f32[136,256]{1,0:T(8,128)S(1)} %add.348), channel_id=1, source_target_pairs={{0,256},{8,264},{16,272},{24,280},{32,288},{40,296},{48,304},{56,3... | collective-permute-start | bytes 417800 | tf_op jit(solution)/shard_map/ppermute | solution.py:22
  190.9 0.6 fusion.69
  191.5 5.4 %collective-permute-done.12 = f32[136,256]{1,0:T(8,128)S(1)} collective-permute-done((f32[136,256]{1,0:T(8,128)S(1)}, f32[136,256]{1,0:T(8,128)S(1)}, u32[]{:S(2)}, u32[]{:S(2)}) %collective-permute-start.12) | collective-permute-done | bytes 139296 | tf_op jit(solution)/shard_map/ppermute | solution.py:22
  196.9 0.7 slice.62
  197.6 0.6 slice.63
  (22 shorter events, 0.3 us)
Async XLA Ops:
  0.6 135.7 %copy-start = (bf16[128,256]{1,0:T(8,128)(2,1)S(1)}, bf16[128,256]{1,0:T(8,128)(2,1)}, u32[]{:S(2)}) copy-start(bf16[128,256]{1,0:T(8,128)(2,1)} %param.13) | copy-start | bytes 196612
  0.6 30.9 %copy-start.1 = (s32[4,8,8,128]{3,2,1,0:T(8,128)S(1)}, s32[4,8,8,128]{3,2,1,0:T(8,128)}, u32[]{:S(2)}) copy-start(s32[4,8,8,128]{3,2,1,0:T(8,128)} %param.12) | copy-start | bytes 393220
  2.4 10.6 %collective-permute-start = (bf16[512,128]{1,0:T(8,128)(2,1)S(1)}, bf16[512,128]{1,0:T(8,128)(2,1)S(1)}, u32[]{:S(2)}, u32[]{:S(2)}) collective-permute-start(bf16[512,128]{1,0:T(8,128)(2,1)S(1)} %multiply_convert_fusion.1), channel_id=1, source_target_pairs={{0,0},{8,8},{16,16},{24,24},{32,32},{40,40},{48,48},{56,56},{64,64... | collective-permute-start | bytes 393224 | tf_op jit(solution)/shard_map/ppermute | solution.py:82
  13.0 14.7 %collective-permute-start.1 = (bf16[1,512,128]{2,1,0:T(8,128)(2,1)S(1)}, bf16[1,512,128]{2,1,0:T(8,128)(2,1)S(1)}, u32[]{:S(2)}, u32[]{:S(2)}) collective-permute-start(bf16[1,512,128]{2,1,0:T(8,128)(2,1)S(1)} %bitcast.322), channel_id=1, source_target_pairs={{0,504},{8,0},{16,8},{24,16},{32,24},{40,32},{48,40},{56,48},{64,5... | collective-permute-start | bytes 393224 | tf_op jit(solution)/shard_map/ppermute | solution.py:13
  27.7 16.1 %collective-permute-start.2 = (bf16[2,512,128]{2,1,0:T(8,128)(2,1)S(1)}, bf16[2,512,128]{2,1,0:T(8,128)(2,1)S(1)}, u32[]{:S(2)}, u32[]{:S(2)}) collective-permute-start(bf16[2,512,128]{2,1,0:T(8,128)(2,1)S(1)} %pad_maximum_fusion.1), channel_id=1, source_target_pairs={{0,496},{8,504},{16,0},{24,8},{32,16},{40,24},{48,32},{56,40},{64,... | collective-permute-start | bytes 786440 | tf_op jit(solution)/shard_map/ppermute | solution.py:13
  43.9 29.1 %collective-permute-start.3 = (bf16[4,512,128]{2,1,0:T(8,128)(2,1)S(1)}, bf16[4,512,128]{2,1,0:T(8,128)(2,1)S(1)}, u32[]{:S(2)}, u32[]{:S(2)}) collective-permute-start(bf16[4,512,128]{2,1,0:T(8,128)(2,1)S(1)} %pad_maximum_fusion), channel_id=1, source_target_pairs={{0,480},{8,488},{16,496},{24,504},{32,0},{40,8},{48,16},{56,24},{6... | collective-permute-start | bytes 1572872 | tf_op jit(solution)/shard_map/ppermute | solution.py:13
  83.3 8.3 %collective-permute-start.4 = (f32[512,128]{1,0:T(8,128)S(1)}, f32[512,128]{1,0:T(8,128)S(1)}, u32[]{:S(2)}, u32[]{:S(2)}) collective-permute-start(f32[512,128]{1,0:T(8,128)S(1)} %bitcast.325), channel_id=1, source_target_pairs={{0,1},{1,0},{2,3},{3,2},{4,5},{5,4},{6,7},{7,6},{8,9},{9,8},{10,11... | collective-permute-start | bytes 786440 | tf_op jit(solution)/shard_map/ppermute | solution.py:22
  91.6 17.7 %copy-start.3 = (bf16[64,256]{1,0:T(8,128)(2,1)S(1)}, bf16[64,256]{1,0:T(8,128)(2,1)}, u32[]{:S(2)}) copy-start(bf16[64,256]{1,0:T(8,128)(2,1)} %param.15) | copy-start | bytes 98308
  91.6 44.6 %copy-start.2 = (bf16[512,128]{1,0:T(8,128)(2,1)S(1)}, bf16[512,128]{1,0:T(8,128)(2,1)}, u32[]{:S(2)}) copy-start(bf16[512,128]{1,0:T(8,128)(2,1)} %param.8) | copy-start | bytes 393220
  91.6 12.0 %collective-permute-start.5 = (f32[512,128]{1,0:T(8,128)S(1)}, f32[512,128]{1,0:T(8,128)S(1)}, u32[]{:S(2)}, u32[]{:S(2)}) collective-permute-start(f32[512,128]{1,0:T(8,128)S(1)} %bitcast_add_fusion), channel_id=1, source_target_pairs={{0,2},{1,3},{2,0},{3,1},{4,6},{5,7},{6,4},{7,5},{8,10},{9,11},{10,... | collective-permute-start | bytes 786440 | tf_op jit(solution)/shard_map/ppermute | solution.py:22
  103.6 32.7 %copy-start.4 = (f32[256]{0:T(256)S(1)}, f32[256]{0:T(256)}, u32[]{:S(2)}) copy-start(f32[256]{0:T(256)} %param.14) | copy-start | bytes 3076
  103.7 32.6 %collective-permute-start.6 = (f32[512,128]{1,0:T(8,128)S(1)}, f32[512,128]{1,0:T(8,128)S(1)}, u32[]{:S(2)}, u32[]{:S(2)}) collective-permute-start(f32[512,128]{1,0:T(8,128)S(1)} %add.336), channel_id=1, source_target_pairs={{0,4},{1,5},{2,6},{3,7},{4,0},{5,1},{6,2},{7,3},{8,12},{9,13},{10,... | collective-permute-start | bytes 786440 | tf_op jit(solution)/shard_map/ppermute | solution.py:22
  137.2 3.3 %collective-permute-start.7 = (f32[136,256]{1,0:T(8,128)S(1)}, f32[136,256]{1,0:T(8,128)S(1)}, u32[]{:S(2)}, u32[]{:S(2)}) collective-permute-start(f32[136,256]{1,0:T(8,128)S(1)} %pad_maximum_fusion.2), channel_id=1, source_target_pairs={{0,8},{8,0},{16,24},{24,16},{32,40},{40,32},{48,56},{56,48},{64,72... | collective-permute-start | bytes 417800 | tf_op jit(solution)/shard_map/ppermute | solution.py:22
  140.5 7.6 %collective-permute-start.8 = (f32[136,256]{1,0:T(8,128)S(1)}, f32[136,256]{1,0:T(8,128)S(1)}, u32[]{:S(2)}, u32[]{:S(2)}) collective-permute-start(f32[136,256]{1,0:T(8,128)S(1)} %fusion.110), channel_id=1, source_target_pairs={{0,64},{8,72},{16,80},{24,88},{32,96},{40,104},{48,112},{56,120},{... | collective-permute-start | bytes 417800 | tf_op jit(solution)/shard_map/ppermute | solution.py:22
  148.2 10.8 %collective-permute-start.9 = (f32[136,256]{1,0:T(8,128)S(1)}, f32[136,256]{1,0:T(8,128)S(1)}, u32[]{:S(2)}, u32[]{:S(2)}) collective-permute-start(f32[136,256]{1,0:T(8,128)S(1)} %add.345), channel_id=1, source_target_pairs={{0,16},{8,24},{16,0},{24,8},{32,48},{40,56},{48,32},{56,40},{64,80... | collective-permute-start | bytes 417800 | tf_op jit(solution)/shard_map/ppermute | solution.py:22
  159.0 10.2 %collective-permute-start.10 = (f32[136,256]{1,0:T(8,128)S(1)}, f32[136,256]{1,0:T(8,128)S(1)}, u32[]{:S(2)}, u32[]{:S(2)}) collective-permute-start(f32[136,256]{1,0:T(8,128)S(1)} %add.346), channel_id=1, source_target_pairs={{0,128},{8,136},{16,144},{24,152},{32,160},{40,168},{48,176},{56,1... | collective-permute-start | bytes 417800 | tf_op jit(solution)/shard_map/ppermute | solution.py:22
  169.2 12.3 %collective-permute-start.11 = (f32[136,256]{1,0:T(8,128)S(1)}, f32[136,256]{1,0:T(8,128)S(1)}, u32[]{:S(2)}, u32[]{:S(2)}) collective-permute-start(f32[136,256]{1,0:T(8,128)S(1)} %add.347), channel_id=1, source_target_pairs={{0,32},{8,40},{16,48},{24,56},{32,0},{40,8},{48,16},{56,24},{64,96... | collective-permute-start | bytes 417800 | tf_op jit(solution)/shard_map/ppermute | solution.py:22
  181.6 15.3 %collective-permute-start.12 = (f32[136,256]{1,0:T(8,128)S(1)}, f32[136,256]{1,0:T(8,128)S(1)}, u32[]{:S(2)}, u32[]{:S(2)}) collective-permute-start(f32[136,256]{1,0:T(8,128)S(1)} %add.348), channel_id=1, source_target_pairs={{0,256},{8,264},{16,272},{24,280},{32,288},{40,296},{48,304},{56,3... | collective-permute-start | bytes 417800 | tf_op jit(solution)/shard_map/ppermute | solution.py:22

commit v4 on v3

--- a/solution.py
+++ b/solution.py
@@ -80,7 +80,6 @@
             target = (source - step_count * rep_index) % row_count
             pairs.append((source * replicas + rep_index, target * replicas + rep_index))
     held = lax.ppermute(scaled, ("rows", "rep"), pairs)[None]
-    cot_group = lax.all_gather(cotangent, "rep", axis=0, tiled=True)
     partial_total = local_sums(held[0], 0)
     while held.shape[0] < step_count:
         have = held.shape[0]
@@ -88,11 +87,17 @@
         for extra in range(arrived.shape[0]):
             partial_total = partial_total + local_sums(arrived[extra], have + extra)
         held = jnp.concatenate([held, arrived], axis=0)
-    edge_sums = butterfly_sum(partial_total, "rep", REP_BITS)
-    aggregate = (inv_deg[:, None] * (edge_sums + scaled.astype(jnp.float32))).astype(jnp.bfloat16)
+    pieces = partial_total.reshape((replicas, -1) + partial_total.shape[1:])
+    pieces = lax.all_to_all(pieces, "rep", 0, 0)
+    edge_sums = jnp.sum(pieces, axis=0)
+    share_rows = edge_sums.shape[0]
+    share_start = replica * share_rows
+    own_rows = lax.dynamic_slice_in_dim(scaled, share_start, share_rows, 0).astype(jnp.float32)
+    own_inv = lax.dynamic_slice_in_dim(inv_deg, share_start, share_rows, 0)
+    aggregate = (own_inv[:, None] * (edge_sums + own_rows)).astype(jnp.bfloat16)
     pre_act = jnp.dot(aggregate, weight, preferred_element_type=jnp.float32) + bias
     activated, pull_back = jax.vjp(gelu_tanh, pre_act)
-    delta_bf = pull_back(cot_group.astype(jnp.float32))[0].astype(jnp.bfloat16)
+    delta_bf = pull_back(cotangent.astype(jnp.float32))[0].astype(jnp.bfloat16)
     local_weight = lax.dot_general(
         aggregate, delta_bf, (((0,), (0,)), ((), ())), preferred_element_type=jnp.float32
     )
@@ -101,12 +106,11 @@
     packed = jnp.concatenate(
         [local_weight, jnp.broadcast_to(local_bias[None, :], (8, local_bias.shape[0]))], axis=0
     )
+    packed = butterfly_sum(packed, "rep", REP_BITS)
     packed = butterfly_sum(packed, "rows", ROWS_BITS)
     grad_weight = packed[:feat_rows]
     grad_bias = packed[feat_rows]
-    share_rows = cotangent.shape[0]
-    own_act = lax.dynamic_slice_in_dim(activated, replica * share_rows, share_rows, 0)
-    return (own_act.astype(jnp.bfloat16), grad_weight, grad_bias)
+    return (activated.astype(jnp.bfloat16), grad_weight, grad_bias)
 
 
 def solution(mesh):

time: 200 us -> 185 us (0.925)
  the two profiles are of different devices: /device:TPU:6 before, /device:TPU:57 now
where the time goes in v4:
time: 185 us; the launch traced here: 184 us
  starting transfers between devices  83.7 us (45%)
  waiting for transfers between devices  75 us (41%)
  matrix products  18 us (10%)
  other arithmetic  4.21 us (2%)
  local copies, waits for them, and re-layouts  2.35 us (1%)
    ppermute x9, waiting for transfers between devices, butterfly_sum(): value = value + lax.ppermute(value, axis, pairs)  46.9 us
    ppermute x9, starting transfers between devices, butterfly_sum(): value = value + lax.ppermute(value, axis, pairs)  38.6 us
    all_to_all x1, starting transfers between devices, local(): pieces = lax.all_to_all(pieces, 'rep', 0, 0)  24.8 us
    ppermute x3, waiting for transfers between devices, from_behind(): return lax.ppermute(value, axis, pairs)  22 us
    ppermute x3, starting transfers between devices, from_behind(): return lax.ppermute(value, axis, pairs)  19.6 us
    dot_general x8, matrix products, tile_sums(): jnp.einsum('bkre,bkef->brf', onehot, picked, preferred_element_type=jnp.f...  17 us
    all_to_all x1, waiting for transfers between devices, local(): pieces = lax.all_to_all(pieces, 'rep', 0, 0)  6.1 us
  transfers between devices with their start and end apart: 14, of which 13 were waited for; matrix products, arithmetic and copies ran while one was open for 5% of the time, Pallas kernels for 0%

profile of v4, /device:TPU:57, one launch (start us, length us, event | category | flops | bytes accessed | tf_op | source)
XLA Modules:
  0.0 184.2 jit_solution(5072344351870279245)
XLA Ops:
  0.7 0.7 convert_rsqrt_fusion
  1.4 1.0 multiply_convert_fusion
  2.4 0.7 collective-permute-start
  3.1 1.0 fusion.111
  4.1 0.8 fusion.75
  5.0 2.6 %collective-permute-start.1 = (bf16[1,512,128]{2,1,0:T(8,128)(2,1)S(1)}, bf16[1,512,128]{2,1,0:T(8,128)(2,1)S(1)}, u32[]{:S(2)}, u32[]{:S(2)}) collective-permute-start(bf16[1,512,128]{2,1,0:T(8,128)(2,1)S(1)} %bitcast.321), channel_id=1, source_target_pairs={{0,504},{8,0},{16,8},{24,16},{32,24},{40,32},{48,40},{56,48},{64,5... | collective-permute-start | bytes 393224 | tf_op jit(solution)/shard_map/ppermute | solution.py:13
  7.6 1.0 slice_multiply_fusion.7
  8.6 5.4 %collective-permute-done.1 = bf16[1,512,128]{2,1,0:T(8,128)(2,1)S(1)} collective-permute-done((bf16[1,512,128]{2,1,0:T(8,128)(2,1)S(1)}, bf16[1,512,128]{2,1,0:T(8,128)(2,1)S(1)}, u32[]{:S(2)}, u32[]{:S(2)}) %collective-permute-start.1) | collective-permute-done | bytes 131104 | tf_op jit(solution)/shard_map/ppermute | solution.py:13
  14.0 11.7 %collective-permute-start.2 = (bf16[2,512,128]{2,1,0:T(8,128)(2,1)S(1)}, bf16[2,512,128]{2,1,0:T(8,128)(2,1)S(1)}, u32[]{:S(2)}, u32[]{:S(2)}) collective-permute-start(bf16[2,512,128]{2,1,0:T(8,128)(2,1)S(1)} %pad_maximum_fusion.1), channel_id=1, source_target_pairs={{0,496},{8,504},{16,0},{24,8},{32,16},{40,24},{48,32},{56,40},{64,... | collective-permute-start | bytes 786440 | tf_op jit(solution)/shard_map/ppermute | solution.py:13
  25.8 0.1 fusion.69
  25.9 0.1 fusion.70
  26.0 3.5 %collective-permute-done.2 = bf16[2,512,128]{2,1,0:T(8,128)(2,1)S(1)} collective-permute-done((bf16[2,512,128]{2,1,0:T(8,128)(2,1)S(1)}, bf16[2,512,128]{2,1,0:T(8,128)(2,1)S(1)}, u32[]{:S(2)}, u32[]{:S(2)}) %collective-permute-start.2) | collective-permute-done | bytes 262176 | tf_op jit(solution)/shard_map/ppermute | solution.py:13
  29.5 5.3 %collective-permute-start.3 = (bf16[4,512,128]{2,1,0:T(8,128)(2,1)S(1)}, bf16[4,512,128]{2,1,0:T(8,128)(2,1)S(1)}, u32[]{:S(2)}, u32[]{:S(2)}) collective-permute-start(bf16[4,512,128]{2,1,0:T(8,128)(2,1)S(1)} %pad_maximum_fusion), channel_id=1, source_target_pairs={{0,480},{8,488},{16,496},{24,504},{32,0},{40,8},{48,16},{56,24},{6... | collective-permute-start | bytes 1572872 | tf_op jit(solution)/shard_map/ppermute | solution.py:13
  34.8 2.0 %fusion.38 = f32[4,128,128]{2,1,0:T(8,128)S(1)} fusion(s32[4,8,128]{2,1,0:T(8,128)S(1)} %get-tuple-element.25, s32[4,8,128]{2,1,0:T(8,128)S(1)} %get-tuple-element.35, bf16[1,512,128]{2,1,0:T(8,128)(2,1)S(1)} %collective-permute-done.1), kind=kOutput, calls=%fused_computation.54 | convolution fusion | flops 674234368 | bytes 425984 | tf_op jit(solution)/shard_map/bkre,bkef->brf/dot_general | solution.py:62
  36.9 2.0 %fusion.36 = f32[4,128,128]{2,1,0:T(8,128)S(1)} fusion(s32[4,8,128]{2,1,0:T(8,128)S(1)} %get-tuple-element.27, s32[4,8,128]{2,1,0:T(8,128)S(1)} %get-tuple-element.11, bf16[2,512,128]{2,1,0:T(8,128)(2,1)S(1)} %collective-permute-done.2), kind=kOutput, calls=%fused_computation.52 | convolution fusion | flops 674234368 | bytes 425984 | tf_op jit(solution)/shard_map/bkre,bkef->brf/dot_general | solution.py:62
  38.9 2.0 %fusion.37 = f32[4,128,128]{2,1,0:T(8,128)S(1)} fusion(s32[4,8,128]{2,1,0:T(8,128)S(1)} %get-tuple-element.23, s32[4,8,128]{2,1,0:T(8,128)S(1)} %get-tuple-element.33, bf16[2,512,128]{2,1,0:T(8,128)(2,1)S(1)} %collective-permute-done.2), kind=kOutput, calls=%fused_computation.53 | convolution fusion | flops 674234368 | bytes 425984 | tf_op jit(solution)/shard_map/bkre,bkef->brf/dot_general | solution.py:62
  40.9 13.2 %collective-permute-done.3 = bf16[4,512,128]{2,1,0:T(8,128)(2,1)S(1)} collective-permute-done((bf16[4,512,128]{2,1,0:T(8,128)(2,1)S(1)}, bf16[4,512,128]{2,1,0:T(8,128)(2,1)S(1)}, u32[]{:S(2)}, u32[]{:S(2)}) %collective-permute-start.3) | collective-permute-done | bytes 524320 | tf_op jit(solution)/shard_map/ppermute | solution.py:13
  54.1 2.0 %fusion.32 = f32[4,128,128]{2,1,0:T(8,128)S(1)} fusion(s32[4,8,128]{2,1,0:T(8,128)S(1)} %get-tuple-element.28, s32[4,8,128]{2,1,0:T(8,128)S(1)} %get-tuple-element.39, bf16[4,512,128]{2,1,0:T(8,128)(2,1)S(1)} %collective-permute-done.3), kind=kOutput, calls=%fused_computation.48 | convolution fusion | flops 674234368 | bytes 425984 | tf_op jit(solution)/shard_map/bkre,bkef->brf/dot_general | solution.py:62
  56.1 2.0 %fusion.33 = f32[4,128,128]{2,1,0:T(8,128)S(1)} fusion(s32[4,8,128]{2,1,0:T(8,128)S(1)} %get-tuple-element.26, s32[4,8,128]{2,1,0:T(8,128)S(1)} %get-tuple-element.29, bf16[4,512,128]{2,1,0:T(8,128)(2,1)S(1)} %collective-permute-done.3), kind=kOutput, calls=%fused_computation.49 | convolution fusion | flops 674234368 | bytes 425984 | tf_op jit(solution)/shard_map/bkre,bkef->brf/dot_general | solution.py:62
  58.1 2.2 %fusion.34 = f32[4,128,128]{2,1,0:T(8,128)S(1)} fusion(s32[4,8,128]{2,1,0:T(8,128)S(1)} %get-tuple-element.24, s32[4,8,128]{2,1,0:T(8,128)S(1)} %get-tuple-element.37, bf16[4,512,128]{2,1,0:T(8,128)(2,1)S(1)} %collective-permute-done.3), kind=kOutput, calls=%fused_computation.50 | convolution fusion | flops 674234368 | bytes 425984 | tf_op jit(solution)/shard_map/bkre,bkef->brf/dot_general | solution.py:62
  60.3 2.0 %fusion.35 = f32[4,128,128]{2,1,0:T(8,128)S(1)} fusion(s32[4,8,128]{2,1,0:T(8,128)S(1)} %get-tuple-element.22, s32[4,8,128]{2,1,0:T(8,128)S(1)} %get-tuple-element.31, bf16[4,512,128]{2,1,0:T(8,128)(2,1)S(1)} %collective-permute-done.3), kind=kOutput, calls=%fused_computation.51 | convolution fusion | flops 674234368 | bytes 425984 | tf_op jit(solution)/shard_map/bkre,bkef->brf/dot_general | solution.py:62
  62.3 2.7 %fusion.46 = f32[4,128,128]{2,1,0:T(8,128)} fusion(f32[4,128,128]{2,1,0:T(8,128)S(1)} %fusion.32, f32[4,128,128]{2,1,0:T(8,128)S(1)} %fusion.33, f32[4,128,128]{2,1,0:T(8,128)S(1)} %fusion.34, f32[4,128,128]{2,1,0:T(8,128)S(1)} %fusion.35, f32[4,128,128]{2,1,0:T(8,128)S(1)} %fusion.36, f32[4,128,128]{2,1,0:T(8,128)S(1)} %fusion.37, ...), kind=kOutput, calls=%fused_computation.62 | convolution fusion | flops 674693120 | bytes 2260992 | tf_op jit(solution)/shard_map/bkre,bkef->brf/dot_general | solution.py:62
  65.1 24.8 %all-to-all-start = ((f32[8,64,128]{2,1,0:T(8,128)}), f32[8,64,128]{2,1,0:T(8,128)S(1)}, u32[]{:S(2)}, u32[]{:S(2)}) async-start(f32[8,64,128]{2,1,0:T(8,128)} %bitcast.64), calls=%async_computation | async-start | bytes 524288 | tf_op jit(solution)/shard_map/all_to_all | solution.py:91
  89.8 0.1 dynamic_slice.80
  89.9 6.1 %all-to-all-done = f32[8,64,128]{2,1,0:T(8,128)S(1)} async-done(((f32[8,64,128]{2,1,0:T(8,128)}), f32[8,64,128]{2,1,0:T(8,128)S(1)}, u32[]{:S(2)}, u32[]{:S(2)}) %all-to-all-start) | async-done | bytes 262176 | tf_op jit(solution)/shard_map/all_to_all | solution.py:91
  96.0 0.1 multiply_convert_fusion.2
  96.1 0.8 convert_reduce_fusion
  96.9 0.2 fusion.112
  97.2 2.4 %collective-permute-start.4 = (f32[136,256]{1,0:T(8,128)S(1)}, f32[136,256]{1,0:T(8,128)S(1)}, u32[]{:S(2)}, u32[]{:S(2)}) collective-permute-start(f32[136,256]{1,0:T(8,128)S(1)} %pad_maximum_fusion.2), channel_id=1, source_target_pairs={{0,1},{1,0},{2,3},{3,2},{4,5},{5,4},{6,7},{7,6},{8,9},{9,8},{10,11... | collective-permute-start | bytes 417800 | tf_op jit(solution)/shard_map/ppermute | solution.py:22
  99.6 3.3 %collective-permute-done.4 = f32[136,256]{1,0:T(8,128)S(1)} collective-permute-done((f32[136,256]{1,0:T(8,128)S(1)}, f32[136,256]{1,0:T(8,128)S(1)}, u32[]{:S(2)}, u32[]{:S(2)}) %collective-permute-start.4) | collective-permute-done | bytes 139296 | tf_op jit(solution)/shard_map/ppermute | solution.py:22
  103.0 1.9 %collective-permute-start.5 = (f32[136,256]{1,0:T(8,128)S(1)}, f32[136,256]{1,0:T(8,128)S(1)}, u32[]{:S(2)}, u32[]{:S(2)}) collective-permute-start(f32[136,256]{1,0:T(8,128)S(1)} %fusion.109), channel_id=1, source_target_pairs={{0,2},{1,3},{2,0},{3,1},{4,6},{5,7},{6,4},{7,5},{8,10},{9,11},{10,... | collective-permute-start | bytes 417800 | tf_op jit(solution)/shard_map/ppermute | solution.py:22
  104.9 3.9 %collective-permute-done.5 = f32[136,256]{1,0:T(8,128)S(1)} collective-permute-done((f32[136,256]{1,0:T(8,128)S(1)}, f32[136,256]{1,0:T(8,128)S(1)}, u32[]{:S(2)}, u32[]{:S(2)}) %collective-permute-start.5) | collective-permute-done | bytes 139296 | tf_op jit(solution)/shard_map/ppermute | solution.py:22
  108.8 3.0 %collective-permute-start.6 = (f32[136,256]{1,0:T(8,128)S(1)}, f32[136,256]{1,0:T(8,128)S(1)}, u32[]{:S(2)}, u32[]{:S(2)}) collective-permute-start(f32[136,256]{1,0:T(8,128)S(1)} %add.350), channel_id=1, source_target_pairs={{0,4},{1,5},{2,6},{3,7},{4,0},{5,1},{6,2},{7,3},{8,12},{9,13},{10,... | collective-permute-start | bytes 417800 | tf_op jit(solution)/shard_map/ppermute | solution.py:22
  111.8 4.3 %collective-permute-done.6 = f32[136,256]{1,0:T(8,128)S(1)} collective-permute-done((f32[136,256]{1,0:T(8,128)S(1)}, f32[136,256]{1,0:T(8,128)S(1)}, u32[]{:S(2)}, u32[]{:S(2)}) %collective-permute-start.6) | collective-permute-done | bytes 139296 | tf_op jit(solution)/shard_map/ppermute | solution.py:22
  116.1 7.8 %collective-permute-start.7 = (f32[136,256]{1,0:T(8,128)S(1)}, f32[136,256]{1,0:T(8,128)S(1)}, u32[]{:S(2)}, u32[]{:S(2)}) collective-permute-start(f32[136,256]{1,0:T(8,128)S(1)} %add.351), channel_id=1, source_target_pairs={{0,8},{8,0},{16,24},{24,16},{32,40},{40,32},{48,56},{56,48},{64,72... | collective-permute-start | bytes 417800 | tf_op jit(solution)/shard_map/ppermute | solution.py:22
  123.9 1.0 collective-permute-done.7
  124.9 4.4 %collective-permute-start.8 = (f32[136,256]{1,0:T(8,128)S(1)}, f32[136,256]{1,0:T(8,128)S(1)}, u32[]{:S(2)}, u32[]{:S(2)}) collective-permute-start(f32[136,256]{1,0:T(8,128)S(1)} %add.352), channel_id=1, source_target_pairs={{0,64},{8,72},{16,80},{24,88},{32,96},{40,104},{48,112},{56,120},{... | collective-permute-start | bytes 417800 | tf_op jit(solution)/shard_map/ppermute | solution.py:22
  129.3 3.7 %collective-permute-done.8 = f32[136,256]{1,0:T(8,128)S(1)} collective-permute-done((f32[136,256]{1,0:T(8,128)S(1)}, f32[136,256]{1,0:T(8,128)S(1)}, u32[]{:S(2)}, u32[]{:S(2)}) %collective-permute-start.8) | collective-permute-done | bytes 139296 | tf_op jit(solution)/shard_map/ppermute | solution.py:22
  133.0 2.8 %collective-permute-start.9 = (f32[136,256]{1,0:T(8,128)S(1)}, f32[136,256]{1,0:T(8,128)S(1)}, u32[]{:S(2)}, u32[]{:S(2)}) collective-permute-start(f32[136,256]{1,0:T(8,128)S(1)} %add.353), channel_id=1, source_target_pairs={{0,16},{8,24},{16,0},{24,8},{32,48},{40,56},{48,32},{56,40},{64,80... | collective-permute-start | bytes 417800 | tf_op jit(solution)/shard_map/ppermute | solution.py:22
  135.8 8.3 %collective-permute-done.9 = f32[136,256]{1,0:T(8,128)S(1)} collective-permute-done((f32[136,256]{1,0:T(8,128)S(1)}, f32[136,256]{1,0:T(8,128)S(1)}, u32[]{:S(2)}, u32[]{:S(2)}) %collective-permute-start.9) | collective-permute-done | bytes 139296 | tf_op jit(solution)/shard_map/ppermute | solution.py:22
  144.1 4.7 %collective-permute-start.10 = (f32[136,256]{1,0:T(8,128)S(1)}, f32[136,256]{1,0:T(8,128)S(1)}, u32[]{:S(2)}, u32[]{:S(2)}) collective-permute-start(f32[136,256]{1,0:T(8,128)S(1)} %add.354), channel_id=1, source_target_pairs={{0,128},{8,136},{16,144},{24,152},{32,160},{40,168},{48,176},{56,1... | collective-permute-start | bytes 417800 | tf_op jit(solution)/shard_map/ppermute | solution.py:22
  148.8 6.7 %collective-permute-done.10 = f32[136,256]{1,0:T(8,128)S(1)} collective-permute-done((f32[136,256]{1,0:T(8,128)S(1)}, f32[136,256]{1,0:T(8,128)S(1)}, u32[]{:S(2)}, u32[]{:S(2)}) %collective-permute-start.10) | collective-permute-done | bytes 139296 | tf_op jit(solution)/shard_map/ppermute | solution.py:22
  155.5 6.5 %collective-permute-start.11 = (f32[136,256]{1,0:T(8,128)S(1)}, f32[136,256]{1,0:T(8,128)S(1)}, u32[]{:S(2)}, u32[]{:S(2)}) collective-permute-start(f32[136,256]{1,0:T(8,128)S(1)} %add.355), channel_id=1, source_target_pairs={{0,32},{8,40},{16,48},{24,56},{32,0},{40,8},{48,16},{56,24},{64,96... | collective-permute-start | bytes 417800 | tf_op jit(solution)/shard_map/ppermute | solution.py:22
  162.0 6.6 %collective-permute-done.11 = f32[136,256]{1,0:T(8,128)S(1)} collective-permute-done((f32[136,256]{1,0:T(8,128)S(1)}, f32[136,256]{1,0:T(8,128)S(1)}, u32[]{:S(2)}, u32[]{:S(2)}) %collective-permute-start.11) | collective-permute-done | bytes 139296 | tf_op jit(solution)/shard_map/ppermute | solution.py:22
  168.6 5.1 %collective-permute-start.12 = (f32[136,256]{1,0:T(8,128)S(1)}, f32[136,256]{1,0:T(8,128)S(1)}, u32[]{:S(2)}, u32[]{:S(2)}) collective-permute-start(f32[136,256]{1,0:T(8,128)S(1)} %add.356), channel_id=1, source_target_pairs={{0,256},{8,264},{16,272},{24,280},{32,288},{40,296},{48,304},{56,3... | collective-permute-start | bytes 417800 | tf_op jit(solution)/shard_map/ppermute | solution.py:22
  173.7 9.2 %collective-permute-done.12 = f32[136,256]{1,0:T(8,128)S(1)} collective-permute-done((f32[136,256]{1,0:T(8,128)S(1)}, f32[136,256]{1,0:T(8,128)S(1)}, u32[]{:S(2)}, u32[]{:S(2)}) %collective-permute-start.12) | collective-permute-done | bytes 139296 | tf_op jit(solution)/shard_map/ppermute | solution.py:22
  182.9 0.7 slice.62
  183.6 0.6 slice.63
  (23 shorter events, 0.3 us)
Async XLA Ops:
  0.6 95.5 %copy-start = (bf16[128,256]{1,0:T(8,128)(2,1)S(1)}, bf16[128,256]{1,0:T(8,128)(2,1)}, u32[]{:S(2)}) copy-start(bf16[128,256]{1,0:T(8,128)(2,1)} %param.13) | copy-start | bytes 196612
  0.6 25.1 %copy-start.1 = (s32[4,8,8,128]{3,2,1,0:T(8,128)S(1)}, s32[4,8,8,128]{3,2,1,0:T(8,128)}, u32[]{:S(2)}) copy-start(s32[4,8,8,128]{3,2,1,0:T(8,128)} %param.12) | copy-start | bytes 393220
  2.4 2.5 %collective-permute-start = (bf16[512,128]{1,0:T(8,128)(2,1)S(1)}, bf16[512,128]{1,0:T(8,128)(2,1)S(1)}, u32[]{:S(2)}, u32[]{:S(2)}) collective-permute-start(bf16[512,128]{1,0:T(8,128)(2,1)S(1)} %multiply_convert_fusion), channel_id=1, source_target_pairs={{0,0},{8,8},{16,16},{24,24},{32,32},{40,40},{48,48},{56,56},{64,64... | collective-permute-start | bytes 393224 | tf_op jit(solution)/shard_map/ppermute | solution.py:82
  5.0 9.0 %collective-permute-start.1 = (bf16[1,512,128]{2,1,0:T(8,128)(2,1)S(1)}, bf16[1,512,128]{2,1,0:T(8,128)(2,1)S(1)}, u32[]{:S(2)}, u32[]{:S(2)}) collective-permute-start(bf16[1,512,128]{2,1,0:T(8,128)(2,1)S(1)} %bitcast.321), channel_id=1, source_target_pairs={{0,504},{8,0},{16,8},{24,16},{32,24},{40,32},{48,40},{56,48},{64,5... | collective-permute-start | bytes 393224 | tf_op jit(solution)/shard_map/ppermute | solution.py:13
  14.0 15.5 %collective-permute-start.2 = (bf16[2,512,128]{2,1,0:T(8,128)(2,1)S(1)}, bf16[2,512,128]{2,1,0:T(8,128)(2,1)S(1)}, u32[]{:S(2)}, u32[]{:S(2)}) collective-permute-start(bf16[2,512,128]{2,1,0:T(8,128)(2,1)S(1)} %pad_maximum_fusion.1), channel_id=1, source_target_pairs={{0,496},{8,504},{16,0},{24,8},{32,16},{40,24},{48,32},{56,40},{64,... | collective-permute-start | bytes 786440 | tf_op jit(solution)/shard_map/ppermute | solution.py:13
  29.5 24.5 %collective-permute-start.3 = (bf16[4,512,128]{2,1,0:T(8,128)(2,1)S(1)}, bf16[4,512,128]{2,1,0:T(8,128)(2,1)S(1)}, u32[]{:S(2)}, u32[]{:S(2)}) collective-permute-start(bf16[4,512,128]{2,1,0:T(8,128)(2,1)S(1)} %pad_maximum_fusion), channel_id=1, source_target_pairs={{0,480},{8,488},{16,496},{24,504},{32,0},{40,8},{48,16},{56,24},{6... | collective-permute-start | bytes 1572872 | tf_op jit(solution)/shard_map/ppermute | solution.py:13
  65.1 31.0 %copy-start.2 = (bf16[64,256]{1,0:T(8,128)(2,1)S(1)}, bf16[64,256]{1,0:T(8,128)(2,1)}, u32[]{:S(2)}) copy-start(bf16[64,256]{1,0:T(8,128)(2,1)} %param.15) | copy-start | bytes 98308
  65.1 31.0 %copy-start.3 = (f32[256]{0:T(256)S(1)}, f32[256]{0:T(256)}, u32[]{:S(2)}) copy-start(f32[256]{0:T(256)} %param.14) | copy-start | bytes 3076
  65.1 30.9 %all-to-all-start = ((f32[8,64,128]{2,1,0:T(8,128)}), f32[8,64,128]{2,1,0:T(8,128)S(1)}, u32[]{:S(2)}, u32[]{:S(2)}) async-start(f32[8,64,128]{2,1,0:T(8,128)} %bitcast.64), calls=%async_computation | async-start | bytes 524288 | tf_op jit(solution)/shard_map/all_to_all | solution.py:91
  97.2 5.8 %collective-permute-start.4 = (f32[136,256]{1,0:T(8,128)S(1)}, f32[136,256]{1,0:T(8,128)S(1)}, u32[]{:S(2)}, u32[]{:S(2)}) collective-permute-start(f32[136,256]{1,0:T(8,128)S(1)} %pad_maximum_fusion.2), channel_id=1, source_target_pairs={{0,1},{1,0},{2,3},{3,2},{4,5},{5,4},{6,7},{7,6},{8,9},{9,8},{10,11... | collective-permute-start | bytes 417800 | tf_op jit(solution)/shard_map/ppermute | solution.py:22
  103.0 5.8 %collective-permute-start.5 = (f32[136,256]{1,0:T(8,128)S(1)}, f32[136,256]{1,0:T(8,128)S(1)}, u32[]{:S(2)}, u32[]{:S(2)}) collective-permute-start(f32[136,256]{1,0:T(8,128)S(1)} %fusion.109), channel_id=1, source_target_pairs={{0,2},{1,3},{2,0},{3,1},{4,6},{5,7},{6,4},{7,5},{8,10},{9,11},{10,... | collective-permute-start | bytes 417800 | tf_op jit(solution)/shard_map/ppermute | solution.py:22
  108.8 7.3 %collective-permute-start.6 = (f32[136,256]{1,0:T(8,128)S(1)}, f32[136,256]{1,0:T(8,128)S(1)}, u32[]{:S(2)}, u32[]{:S(2)}) collective-permute-start(f32[136,256]{1,0:T(8,128)S(1)} %add.350), channel_id=1, source_target_pairs={{0,4},{1,5},{2,6},{3,7},{4,0},{5,1},{6,2},{7,3},{8,12},{9,13},{10,... | collective-permute-start | bytes 417800 | tf_op jit(solution)/shard_map/ppermute | solution.py:22
  116.1 8.8 %collective-permute-start.7 = (f32[136,256]{1,0:T(8,128)S(1)}, f32[136,256]{1,0:T(8,128)S(1)}, u32[]{:S(2)}, u32[]{:S(2)}) collective-permute-start(f32[136,256]{1,0:T(8,128)S(1)} %add.351), channel_id=1, source_target_pairs={{0,8},{8,0},{16,24},{24,16},{32,40},{40,32},{48,56},{56,48},{64,72... | collective-permute-start | bytes 417800 | tf_op jit(solution)/shard_map/ppermute | solution.py:22
  124.9 8.0 %collective-permute-start.8 = (f32[136,256]{1,0:T(8,128)S(1)}, f32[136,256]{1,0:T(8,128)S(1)}, u32[]{:S(2)}, u32[]{:S(2)}) collective-permute-start(f32[136,256]{1,0:T(8,128)S(1)} %add.352), channel_id=1, source_target_pairs={{0,64},{8,72},{16,80},{24,88},{32,96},{40,104},{48,112},{56,120},{... | collective-permute-start | bytes 417800 | tf_op jit(solution)/shard_map/ppermute | solution.py:22
  133.0 11.1 %collective-permute-start.9 = (f32[136,256]{1,0:T(8,128)S(1)}, f32[136,256]{1,0:T(8,128)S(1)}, u32[]{:S(2)}, u32[]{:S(2)}) collective-permute-start(f32[136,256]{1,0:T(8,128)S(1)} %add.353), channel_id=1, source_target_pairs={{0,16},{8,24},{16,0},{24,8},{32,48},{40,56},{48,32},{56,40},{64,80... | collective-permute-start | bytes 417800 | tf_op jit(solution)/shard_map/ppermute | solution.py:22
  144.1 11.4 %collective-permute-start.10 = (f32[136,256]{1,0:T(8,128)S(1)}, f32[136,256]{1,0:T(8,128)S(1)}, u32[]{:S(2)}, u32[]{:S(2)}) collective-permute-start(f32[136,256]{1,0:T(8,128)S(1)} %add.354), channel_id=1, source_target_pairs={{0,128},{8,136},{16,144},{24,152},{32,160},{40,168},{48,176},{56,1... | collective-permute-start | bytes 417800 | tf_op jit(solution)/shard_map/ppermute | solution.py:22
  155.5 13.1 %collective-permute-start.11 = (f32[136,256]{1,0:T(8,128)S(1)}, f32[136,256]{1,0:T(8,128)S(1)}, u32[]{:S(2)}, u32[]{:S(2)}) collective-permute-start(f32[136,256]{1,0:T(8,128)S(1)} %add.355), channel_id=1, source_target_pairs={{0,32},{8,40},{16,48},{24,56},{32,0},{40,8},{48,16},{56,24},{64,96... | collective-permute-start | bytes 417800 | tf_op jit(solution)/shard_map/ppermute | solution.py:22
  168.6 14.3 %collective-permute-start.12 = (f32[136,256]{1,0:T(8,128)S(1)}, f32[136,256]{1,0:T(8,128)S(1)}, u32[]{:S(2)}, u32[]{:S(2)}) collective-permute-start(f32[136,256]{1,0:T(8,128)S(1)} %add.356), channel_id=1, source_target_pairs={{0,256},{8,264},{16,272},{24,280},{32,288},{40,296},{48,304},{56,3... | collective-permute-start | bytes 417800 | tf_op jit(solution)/shard_map/ppermute | solution.py:22

commit v5 on v4

--- a/solution.py
+++ b/solution.py
@@ -1,6 +1,8 @@
 import jax
 import jax.numpy as jnp
 from jax import lax
+from jax.experimental import pallas as pl
+from jax.experimental.pallas import tpu as pltpu
 from jax.sharding import PartitionSpec as P
 
 ROWS_BITS = (0, 3, 1, 4, 2, 5)
@@ -43,6 +45,44 @@
     return jax.nn.gelu(values, approximate=True)
 
 
+def _edge_kernel(bufT_ref, far_ref, tgt_ref, out_ref):
+    groups, feat, cols = bufT_ref.shape
+    blocks, _, slots, edges = far_ref.shape
+    col_iota = lax.broadcasted_iota(jnp.int32, (cols, edges), 0)
+    row_iota = lax.broadcasted_iota(jnp.int32, (out_ref.shape[1], edges), 0)
+    for b in range(blocks):
+        acc = jnp.zeros((out_ref.shape[1], feat), jnp.float32)
+        for g in range(groups):
+            tableT = bufT_ref[g]
+            for k in range(slots):
+                far = far_ref[b, g, pl.ds(k, 1), :]
+                tgt = tgt_ref[b, g, pl.ds(k, 1), :]
+                pick = (col_iota == far).astype(jnp.bfloat16)
+                pickedT = jnp.dot(tableT, pick, preferred_element_type=jnp.float32).astype(jnp.bfloat16)
+                scatter = (row_iota == tgt).astype(jnp.bfloat16)
+                acc = acc + lax.dot_general(
+                    scatter, pickedT, (((1,), (1,)), ((), ())), preferred_element_type=jnp.float32
+                )
+        out_ref[b] = acc
+
+
+def edge_sums_kernel(bufT, far, tgt):
+    groups, feat, cols = bufT.shape
+    blocks = far.shape[0]
+    rows = 128
+    flops = 2 * blocks * groups * far.shape[2] * (feat * cols * 128 + rows * 128 * feat)
+    return pl.pallas_call(
+        _edge_kernel,
+        out_shape=jax.ShapeDtypeStruct((blocks, rows, feat), jnp.float32),
+        in_specs=[pl.BlockSpec(memory_space=pltpu.VMEM)] * 3,
+        out_specs=pl.BlockSpec(memory_space=pltpu.VMEM),
+        cost_estimate=pl.CostEstimate(
+            flops=flops, transcendentals=0,
+            bytes_accessed=bufT.size * 2 + far.size * 8 + blocks * rows * feat * 4,
+        ),
+    )(bufT, far, tgt)
+
+
 def tile_sums(buffer, offset, tile_block, edge_count, edge_code):
     block_ids = lax.dynamic_index_in_dim(tile_block, offset, 1, keepdims=False)
     live_count = lax.dynamic_index_in_dim(edge_count, offset, 1, keepdims=False)
@@ -70,8 +110,13 @@
     inv_deg = lax.rsqrt(degree.astype(jnp.float32))
     scaled = (features.astype(jnp.float32) * inv_deg[:, None]).astype(jnp.bfloat16)
 
-    def local_sums(buffer, offset):
-        return tile_sums(buffer, offset, tile_block, edge_count, edge_code)
+    far = tile_block[..., None] * 128 + edge_code % 128
+    is_live = lax.broadcasted_iota(jnp.int32, edge_code.shape, 3) < edge_count[..., None]
+    tgt = jnp.where(is_live, edge_code // 128, -1)
+
+    def local_sums(held_t, first):
+        count = held_t.shape[0]
+        return edge_sums_kernel(held_t, far[:, first:first + count], tgt[:, first:first + count])
 
     row_count = lax.axis_size("rows")
     pairs = []
@@ -79,14 +124,14 @@
         for source in range(row_count):
             target = (source - step_count * rep_index) % row_count
             pairs.append((source * replicas + rep_index, target * replicas + rep_index))
-    held = lax.ppermute(scaled, ("rows", "rep"), pairs)[None]
-    partial_total = local_sums(held[0], 0)
+    held = lax.ppermute(scaled.T, ("rows", "rep"), pairs)[None]
+    partial_total = local_sums(held, 0)
     while held.shape[0] < step_count:
         have = held.shape[0]
         arrived = from_behind(held, "rows", -have)
-        for extra in range(arrived.shape[0]):
-            partial_total = partial_total + local_sums(arrived[extra], have + extra)
+        partial_total = partial_total + local_sums(arrived, have)
         held = jnp.concatenate([held, arrived], axis=0)
+    partial_total = partial_total.reshape(-1, partial_total.shape[-1])
     pieces = partial_total.reshape((replicas, -1) + partial_total.shape[1:])
     pieces = lax.all_to_all(pieces, "rep", 0, 0)
     edge_sums = jnp.sum(pieces, axis=0)

time: 185 us -> 197 us (1.065)
  the two profiles are of different devices: /device:TPU:57 before, /device:TPU:6 now
where the time goes in v5:
time: 197 us; the launch traced here: 194 us
  waiting for transfers between devices  75.1 us (38%)
  starting transfers between devices  66.5 us (34%)
  Pallas kernels  40.1 us (20%)
  local copies, waits for them, and re-layouts  7.62 us (4%)
  other arithmetic  2.99 us (2%)
    ppermute x9, waiting for transfers between devices, butterfly_sum(): value = value + lax.ppermute(value, axis, pairs)  48.6 us
    pallas_call x4, Pallas kernels, edge_sums_kernel(): pl.pallas_call(_edge_kernel, out_shape=jax.ShapeDtypeStruct((blocks, rows...  40.1 us
    ppermute x9, starting transfers between devices, butterfly_sum(): value = value + lax.ppermute(value, axis, pairs)  34 us
    ppermute x3, starting transfers between devices, from_behind(): return lax.ppermute(value, axis, pairs)  20 us
    ppermute x3, waiting for transfers between devices, from_behind(): return lax.ppermute(value, axis, pairs)  14.5 us
    all_to_all x1, starting transfers between devices, local(): pieces = lax.all_to_all(pieces, 'rep', 0, 0)  8.05 us
    ppermute x1, waiting for transfers between devices, local(): held = lax.ppermute(scaled.T, ('rows', 'rep'), pairs)[None]  6.08 us
    all_to_all x1, waiting for transfers between devices, local(): pieces = lax.all_to_all(pieces, 'rep', 0, 0)  5.96 us
  transfers between devices with their start and end apart: 14, of which 14 were waited for; matrix products, arithmetic and copies ran while one was open for 2% of the time, Pallas kernels for 11%

profile of v5, /device:TPU:6, one launch (start us, length us, event | category | flops | bytes accessed | tf_op | source)
XLA Modules:
  0.0 194.2 jit_solution(10335031599602382901)
XLA Ops:
  0.6 0.7 convert_rsqrt_fusion
  1.4 1.0 copy.12
  2.4 4.5 %collective-permute-start = (bf16[128,512]{1,0:T(8,128)(2,1)S(1)}, bf16[128,512]{1,0:T(8,128)(2,1)S(1)}, u32[]{:S(2)}, u32[]{:S(2)}) collective-permute-start(bf16[128,512]{1,0:T(8,128)(2,1)S(1)} %fusion.23), channel_id=1, source_target_pairs={{0,0},{8,8},{16,16},{24,24},{32,32},{40,40},{48,48},{56,56},{64,64... | collective-permute-start | bytes 393224 | tf_op jit(solution)/shard_map/ppermute | solution.py:127
  6.9 6.1 %collective-permute-done = bf16[128,512]{1,0:T(8,128)(2,1)S(1)} collective-permute-done((bf16[128,512]{1,0:T(8,128)(2,1)S(1)}, bf16[128,512]{1,0:T(8,128)(2,1)S(1)}, u32[]{:S(2)}, u32[]{:S(2)}) %collective-permute-start) | collective-permute-done | bytes 131104 | tf_op jit(solution)/shard_map/ppermute | solution.py:127
  13.0 12.3 %collective-permute-start.1 = (bf16[1,128,512]{2,1,0:T(8,128)(2,1)S(1)}, bf16[1,128,512]{2,1,0:T(8,128)(2,1)S(1)}, u32[]{:S(2)}, u32[]{:S(2)}) collective-permute-start(bf16[1,128,512]{2,1,0:T(8,128)(2,1)S(1)} %bitcast.9), channel_id=1, source_target_pairs={{0,504},{8,0},{16,8},{24,16},{32,24},{40,32},{48,40},{56,48},{64,5... | collective-permute-start | bytes 393224 | tf_op jit(solution)/shard_map/ppermute | solution.py:15
  25.3 2.5 %collective-permute-done.1.bufT_ref = bf16[1,128,512]{2,1,0:T(8,128)(2,1)S(1)} collective-permute-done((bf16[1,128,512]{2,1,0:T(8,128)(2,1)S(1)}, bf16[1,128,512]{2,1,0:T(8,128)(2,1)S(1)}, u32[]{:S(2)}, u32[]{:S(2)}) %collective-permute-start.1) | collective-permute-done | bytes 131104 | tf_op jit(solution)/shard_map/ppermute | solution.py:15
  27.8 3.8 %collective-permute-start.2 = (bf16[2,128,512]{2,1,0:T(8,128)(2,1)S(1)}, bf16[2,128,512]{2,1,0:T(8,128)(2,1)S(1)}, u32[]{:S(2)}, u32[]{:S(2)}) collective-permute-start(bf16[2,128,512]{2,1,0:T(8,128)(2,1)S(1)} %pad_maximum_fusion.1), channel_id=1, source_target_pairs={{0,496},{8,504},{16,0},{24,8},{32,16},{40,24},{48,32},{56,40},{64,... | collective-permute-start | bytes 786440 | tf_op jit(solution)/shard_map/ppermute | solution.py:15
  31.7 11.6 %collective-permute-done.2.bufT_ref = bf16[2,128,512]{2,1,0:T(8,128)(2,1)S(1)} collective-permute-done((bf16[2,128,512]{2,1,0:T(8,128)(2,1)S(1)}, bf16[2,128,512]{2,1,0:T(8,128)(2,1)S(1)}, u32[]{:S(2)}, u32[]{:S(2)}) %collective-permute-start.2) | collective-permute-done | bytes 262176 | tf_op jit(solution)/shard_map/ppermute | solution.py:15
  43.4 0.6 copy-done.6
  44.0 3.9 %collective-permute-start.3 = (bf16[4,128,512]{2,1,0:T(8,128)(2,1)S(1)}, bf16[4,128,512]{2,1,0:T(8,128)(2,1)S(1)}, u32[]{:S(2)}, u32[]{:S(2)}) collective-permute-start(bf16[4,128,512]{2,1,0:T(8,128)(2,1)S(1)} %pad_maximum_fusion), channel_id=1, source_target_pairs={{0,480},{8,488},{16,496},{24,504},{32,0},{40,8},{48,16},{56,24},{6... | collective-permute-start | bytes 1572872 | tf_op jit(solution)/shard_map/ppermute | solution.py:15
  47.9 0.1 fusion.1
  48.1 0.6 slice.46.far_ref
  48.7 0.6 slice.44.far_ref
  49.3 0.6 slice.47.tgt_ref
  49.9 0.6 slice.45.tgt_ref
  50.5 0.6 fusion.16
  51.2 5.8 %shard_map.103 = f32[4,128,128]{2,1,0:T(8,128)} custom-call(bf16[1,128,512]{2,1,0:T(8,128)(2,1)} %bitcast.12, s32[4,1,8,128]{3,2,1,0:T(8,128)} %get-tuple-element.12.far_ref, s32[4,1,8,128]{3,2,1,0:T(8,128)} %get-tuple-element.6.tgt_ref), custom_call_target="tpu_custom_call" | custom-call | flops 671088640 | bytes 425984 | tf_op jit(solution)/shard_map/pallas_call | solution.py:74
  57.0 5.8 %shard_map.104 = f32[4,128,128]{2,1,0:T(8,128)} custom-call(bf16[1,128,512]{2,1,0:T(8,128)(2,1)} %copy-done.2, s32[4,1,8,128]{3,2,1,0:T(8,128)} %get-tuple-element.13.far_ref, s32[4,1,8,128]{3,2,1,0:T(8,128)} %get-tuple-element.5.tgt_ref), custom_call_target="tpu_custom_call" | custom-call | flops 671088640 | bytes 425984 | tf_op jit(solution)/shard_map/pallas_call | solution.py:74
  62.8 9.8 %shard_map.105 = f32[4,128,128]{2,1,0:T(8,128)} custom-call(bf16[2,128,512]{2,1,0:T(8,128)(2,1)} %copy-done.6, s32[4,2,8,128]{3,2,1,0:T(8,128)} %slice.44.far_ref, s32[4,2,8,128]{3,2,1,0:T(8,128)} %slice.45.tgt_ref), custom_call_target="tpu_custom_call" | custom-call | flops 1342177280 | bytes 589824 | tf_op jit(solution)/shard_map/pallas_call | solution.py:74
  72.7 0.4 collective-permute-done.3.bufT_ref
  73.1 0.8 copy-done.10
  73.9 18.6 %shard_map.106 = f32[4,128,128]{2,1,0:T(8,128)} custom-call(bf16[4,128,512]{2,1,0:T(8,128)(2,1)} %copy-done.10, s32[4,4,8,128]{3,2,1,0:T(8,128)} %slice.46.far_ref, s32[4,4,8,128]{3,2,1,0:T(8,128)} %slice.47.tgt_ref), custom_call_target="tpu_custom_call" | custom-call | flops 2684354560 | bytes 917504 | tf_op jit(solution)/shard_map/pallas_call | solution.py:74
  92.5 1.7 add_add_fusion
  94.2 8.0 %all-to-all-start = ((f32[8,64,128]{2,1,0:T(8,128)}), f32[8,64,128]{2,1,0:T(8,128)S(1)}, u32[]{:S(2)}, u32[]{:S(2)}) async-start(f32[8,64,128]{2,1,0:T(8,128)} %bitcast.2), calls=%async_computation | async-start | bytes 524288 | tf_op jit(solution)/shard_map/all_to_all | solution.py:136
  102.3 6.0 %all-to-all-done = f32[8,64,128]{2,1,0:T(8,128)S(1)} async-done(((f32[8,64,128]{2,1,0:T(8,128)}), f32[8,64,128]{2,1,0:T(8,128)S(1)}, u32[]{:S(2)}, u32[]{:S(2)}) %all-to-all-start) | async-done | bytes 262176 | tf_op jit(solution)/shard_map/all_to_all | solution.py:136
  108.5 0.6 copy-done.11
  109.2 0.8 convert_reduce_fusion
  110.0 0.1 fusion.18
  110.2 3.3 %collective-permute-start.4 = (f32[136,256]{1,0:T(8,128)S(1)}, f32[136,256]{1,0:T(8,128)S(1)}, u32[]{:S(2)}, u32[]{:S(2)}) collective-permute-start(f32[136,256]{1,0:T(8,128)S(1)} %pad_maximum_fusion.2), channel_id=1, source_target_pairs={{0,1},{1,0},{2,3},{3,2},{4,5},{5,4},{6,7},{7,6},{8,9},{9,8},{10,11... | collective-permute-start | bytes 417800 | tf_op jit(solution)/shard_map/ppermute | solution.py:24
  113.5 4.3 %collective-permute-done.4 = f32[136,256]{1,0:T(8,128)S(1)} collective-permute-done((f32[136,256]{1,0:T(8,128)S(1)}, f32[136,256]{1,0:T(8,128)S(1)}, u32[]{:S(2)}, u32[]{:S(2)}) %collective-permute-start.4) | collective-permute-done | bytes 139296 | tf_op jit(solution)/shard_map/ppermute | solution.py:24
  117.8 2.6 %collective-permute-start.5 = (f32[136,256]{1,0:T(8,128)S(1)}, f32[136,256]{1,0:T(8,128)S(1)}, u32[]{:S(2)}, u32[]{:S(2)}) collective-permute-start(f32[136,256]{1,0:T(8,128)S(1)} %fusion.14), channel_id=1, source_target_pairs={{0,2},{1,3},{2,0},{3,1},{4,6},{5,7},{6,4},{7,5},{8,10},{9,11},{10,... | collective-permute-start | bytes 417800 | tf_op jit(solution)/shard_map/ppermute | solution.py:24
  120.4 4.4 %collective-permute-done.5 = f32[136,256]{1,0:T(8,128)S(1)} collective-permute-done((f32[136,256]{1,0:T(8,128)S(1)}, f32[136,256]{1,0:T(8,128)S(1)}, u32[]{:S(2)}, u32[]{:S(2)}) %collective-permute-start.5) | collective-permute-done | bytes 139296 | tf_op jit(solution)/shard_map/ppermute | solution.py:24
  124.8 3.8 %collective-permute-start.6 = (f32[136,256]{1,0:T(8,128)S(1)}, f32[136,256]{1,0:T(8,128)S(1)}, u32[]{:S(2)}, u32[]{:S(2)}) collective-permute-start(f32[136,256]{1,0:T(8,128)S(1)} %add.86), channel_id=1, source_target_pairs={{0,4},{1,5},{2,6},{3,7},{4,0},{5,1},{6,2},{7,3},{8,12},{9,13},{10,... | collective-permute-start | bytes 417800 | tf_op jit(solution)/shard_map/ppermute | solution.py:24
  128.6 4.6 %collective-permute-done.6 = f32[136,256]{1,0:T(8,128)S(1)} collective-permute-done((f32[136,256]{1,0:T(8,128)S(1)}, f32[136,256]{1,0:T(8,128)S(1)}, u32[]{:S(2)}, u32[]{:S(2)}) %collective-permute-start.6) | collective-permute-done | bytes 139296 | tf_op jit(solution)/shard_map/ppermute | solution.py:24
  133.2 1.9 collective-permute-start.7
  135.2 1.3 collective-permute-done.7
  136.5 1.9 collective-permute-start.8
  138.4 5.7 %collective-permute-done.8 = f32[136,256]{1,0:T(8,128)S(1)} collective-permute-done((f32[136,256]{1,0:T(8,128)S(1)}, f32[136,256]{1,0:T(8,128)S(1)}, u32[]{:S(2)}, u32[]{:S(2)}) %collective-permute-start.8) | collective-permute-done | bytes 139296 | tf_op jit(solution)/shard_map/ppermute | solution.py:24
  144.1 2.6 %collective-permute-start.9 = (f32[136,256]{1,0:T(8,128)S(1)}, f32[136,256]{1,0:T(8,128)S(1)}, u32[]{:S(2)}, u32[]{:S(2)}) collective-permute-start(f32[136,256]{1,0:T(8,128)S(1)} %add.89), channel_id=1, source_target_pairs={{0,16},{8,24},{16,0},{24,8},{32,48},{40,56},{48,32},{56,40},{64,80... | collective-permute-start | bytes 417800 | tf_op jit(solution)/shard_map/ppermute | solution.py:24
  146.7 8.1 %collective-permute-done.9 = f32[136,256]{1,0:T(8,128)S(1)} collective-permute-done((f32[136,256]{1,0:T(8,128)S(1)}, f32[136,256]{1,0:T(8,128)S(1)}, u32[]{:S(2)}, u32[]{:S(2)}) %collective-permute-start.9) | collective-permute-done | bytes 139296 | tf_op jit(solution)/shard_map/ppermute | solution.py:24
  154.8 4.1 %collective-permute-start.10 = (f32[136,256]{1,0:T(8,128)S(1)}, f32[136,256]{1,0:T(8,128)S(1)}, u32[]{:S(2)}, u32[]{:S(2)}) collective-permute-start(f32[136,256]{1,0:T(8,128)S(1)} %add.90), channel_id=1, source_target_pairs={{0,128},{8,136},{16,144},{24,152},{32,160},{40,168},{48,176},{56,1... | collective-permute-start | bytes 417800 | tf_op jit(solution)/shard_map/ppermute | solution.py:24
  159.0 6.4 %collective-permute-done.10 = f32[136,256]{1,0:T(8,128)S(1)} collective-permute-done((f32[136,256]{1,0:T(8,128)S(1)}, f32[136,256]{1,0:T(8,128)S(1)}, u32[]{:S(2)}, u32[]{:S(2)}) %collective-permute-start.10) | collective-permute-done | bytes 139296 | tf_op jit(solution)/shard_map/ppermute | solution.py:24
  165.4 6.1 %collective-permute-start.11 = (f32[136,256]{1,0:T(8,128)S(1)}, f32[136,256]{1,0:T(8,128)S(1)}, u32[]{:S(2)}, u32[]{:S(2)}) collective-permute-start(f32[136,256]{1,0:T(8,128)S(1)} %add.91), channel_id=1, source_target_pairs={{0,32},{8,40},{16,48},{24,56},{32,0},{40,8},{48,16},{56,24},{64,96... | collective-permute-start | bytes 417800 | tf_op jit(solution)/shard_map/ppermute | solution.py:24
  171.5 7.5 %collective-permute-done.11 = f32[136,256]{1,0:T(8,128)S(1)} collective-permute-done((f32[136,256]{1,0:T(8,128)S(1)}, f32[136,256]{1,0:T(8,128)S(1)}, u32[]{:S(2)}, u32[]{:S(2)}) %collective-permute-start.11) | collective-permute-done | bytes 139296 | tf_op jit(solution)/shard_map/ppermute | solution.py:24
  179.0 7.6 %collective-permute-start.12 = (f32[136,256]{1,0:T(8,128)S(1)}, f32[136,256]{1,0:T(8,128)S(1)}, u32[]{:S(2)}, u32[]{:S(2)}) collective-permute-start(f32[136,256]{1,0:T(8,128)S(1)} %add.92), channel_id=1, source_target_pairs={{0,256},{8,264},{16,272},{24,280},{32,288},{40,296},{48,304},{56,3... | collective-permute-start | bytes 417800 | tf_op jit(solution)/shard_map/ppermute | solution.py:24
  186.7 6.3 %collective-permute-done.12 = f32[136,256]{1,0:T(8,128)S(1)} collective-permute-done((f32[136,256]{1,0:T(8,128)S(1)}, f32[136,256]{1,0:T(8,128)S(1)}, u32[]{:S(2)}, u32[]{:S(2)}) %collective-permute-start.12) | collective-permute-done | bytes 139296 | tf_op jit(solution)/shard_map/ppermute | solution.py:24
  193.0 0.7 slice.48
  193.6 0.6 slice.49
  (43 shorter events, 0.7 us)
Async XLA Ops:
  0.6 107.9 %copy-start = (bf16[128,256]{1,0:T(8,128)(2,1)S(1)}, bf16[128,256]{1,0:T(8,128)(2,1)}, u32[]{:S(2)}) copy-start(bf16[128,256]{1,0:T(8,128)(2,1)} %param.13) | copy-start | bytes 196612
  2.4 10.6 %collective-permute-start = (bf16[128,512]{1,0:T(8,128)(2,1)S(1)}, bf16[128,512]{1,0:T(8,128)(2,1)S(1)}, u32[]{:S(2)}, u32[]{:S(2)}) collective-permute-start(bf16[128,512]{1,0:T(8,128)(2,1)S(1)} %fusion.23), channel_id=1, source_target_pairs={{0,0},{8,8},{16,16},{24,24},{32,32},{40,40},{48,48},{56,56},{64,64... | collective-permute-start | bytes 393224 | tf_op jit(solution)/shard_map/ppermute | solution.py:127
  13.0 30.3 %copy-start.1 = (bf16[128,512]{1,0:T(8,128)(2,1)}, bf16[128,512]{1,0:T(8,128)(2,1)S(1)}, u32[]{:S(2)}) copy-start(bf16[128,512]{1,0:T(8,128)(2,1)S(1)} %collective-permute-done) | copy-start | bytes 393220
  13.0 18.7 %copy-start.8 = (s32[4,8,8]{2,1,0:T(8,128)S(1)}, s32[4,8,8]{2,1,0:T(8,128)}, u32[]{:S(2)}) copy-start(s32[4,8,8]{2,1,0:T(8,128)} %param.10) | copy-start | bytes 3076
  13.0 14.8 %collective-permute-start.1 = (bf16[1,128,512]{2,1,0:T(8,128)(2,1)S(1)}, bf16[1,128,512]{2,1,0:T(8,128)(2,1)S(1)}, u32[]{:S(2)}, u32[]{:S(2)}) collective-permute-start(bf16[1,128,512]{2,1,0:T(8,128)(2,1)S(1)} %bitcast.9), channel_id=1, source_target_pairs={{0,504},{8,0},{16,8},{24,16},{32,24},{40,32},{48,40},{56,48},{64,5... | collective-permute-start | bytes 393224 | tf_op jit(solution)/shard_map/ppermute | solution.py:15
  27.8 15.5 %copy-start.2 = (bf16[1,128,512]{2,1,0:T(8,128)(2,1)}, bf16[1,128,512]{2,1,0:T(8,128)(2,1)S(1)}, u32[]{:S(2)}) copy-start(bf16[1,128,512]{2,1,0:T(8,128)(2,1)S(1)} %collective-permute-done.1.bufT_ref) | copy-start | bytes 393220
  27.8 15.5 %collective-permute-start.2 = (bf16[2,128,512]{2,1,0:T(8,128)(2,1)S(1)}, bf16[2,128,512]{2,1,0:T(8,128)(2,1)S(1)}, u32[]{:S(2)}, u32[]{:S(2)}) collective-permute-start(bf16[2,128,512]{2,1,0:T(8,128)(2,1)S(1)} %pad_maximum_fusion.1), channel_id=1, source_target_pairs={{0,496},{8,504},{16,0},{24,8},{32,16},{40,24},{48,32},{56,40},{64,... | collective-permute-start | bytes 786440 | tf_op jit(solution)/shard_map/ppermute | solution.py:15
  31.7 16.2 %copy-start.7 = (s32[4,8,8,128]{3,2,1,0:T(8,128)S(1)}, s32[4,8,8,128]{3,2,1,0:T(8,128)}, u32[]{:S(2)}) copy-start(s32[4,8,8,128]{3,2,1,0:T(8,128)} %param.12) | copy-start | bytes 393220
  31.7 16.2 %copy-start.9 = (s32[4,8,8]{2,1,0:T(8,128)S(1)}, s32[4,8,8]{2,1,0:T(8,128)}, u32[]{:S(2)}) copy-start(s32[4,8,8]{2,1,0:T(8,128)} %param.11) | copy-start | bytes 3076
  43.3 0.7 copy-start.6
  44.0 29.1 %collective-permute-start.3 = (bf16[4,128,512]{2,1,0:T(8,128)(2,1)S(1)}, bf16[4,128,512]{2,1,0:T(8,128)(2,1)S(1)}, u32[]{:S(2)}, u32[]{:S(2)}) collective-permute-start(bf16[4,128,512]{2,1,0:T(8,128)(2,1)S(1)} %pad_maximum_fusion), channel_id=1, source_target_pairs={{0,480},{8,488},{16,496},{24,504},{32,0},{40,8},{48,16},{56,24},{6... | collective-permute-start | bytes 1572872 | tf_op jit(solution)/shard_map/ppermute | solution.py:15
  72.7 19.8 %copy-start.3 = (f32[4,128,128]{2,1,0:T(8,128)S(1)}, f32[4,128,128]{2,1,0:T(8,128)}, u32[]{:S(2)}) copy-start(f32[4,128,128]{2,1,0:T(8,128)} %shard_map.103) | copy-start | bytes 786436
  72.7 19.8 %copy-start.4 = (f32[4,128,128]{2,1,0:T(8,128)S(1)}, f32[4,128,128]{2,1,0:T(8,128)}, u32[]{:S(2)}) copy-start(f32[4,128,128]{2,1,0:T(8,128)} %shard_map.104) | copy-start | bytes 786436
  72.7 19.8 %copy-start.5 = (f32[4,128,128]{2,1,0:T(8,128)S(1)}, f32[4,128,128]{2,1,0:T(8,128)}, u32[]{:S(2)}) copy-start(f32[4,128,128]{2,1,0:T(8,128)} %shard_map.105) | copy-start | bytes 786436
  73.1 0.8 copy-start.10
  94.2 14.1 %all-to-all-start = ((f32[8,64,128]{2,1,0:T(8,128)}), f32[8,64,128]{2,1,0:T(8,128)S(1)}, u32[]{:S(2)}, u32[]{:S(2)}) async-start(f32[8,64,128]{2,1,0:T(8,128)} %bitcast.2), calls=%async_computation | async-start | bytes 524288 | tf_op jit(solution)/shard_map/all_to_all | solution.py:136
  108.4 0.8 copy-start.11
  108.4 0.8 copy-start.12
  110.2 7.6 %collective-permute-start.4 = (f32[136,256]{1,0:T(8,128)S(1)}, f32[136,256]{1,0:T(8,128)S(1)}, u32[]{:S(2)}, u32[]{:S(2)}) collective-permute-start(f32[136,256]{1,0:T(8,128)S(1)} %pad_maximum_fusion.2), channel_id=1, source_target_pairs={{0,1},{1,0},{2,3},{3,2},{4,5},{5,4},{6,7},{7,6},{8,9},{9,8},{10,11... | collective-permute-start | bytes 417800 | tf_op jit(solution)/shard_map/ppermute | solution.py:24
  117.8 6.9 %collective-permute-start.5 = (f32[136,256]{1,0:T(8,128)S(1)}, f32[136,256]{1,0:T(8,128)S(1)}, u32[]{:S(2)}, u32[]{:S(2)}) collective-permute-start(f32[136,256]{1,0:T(8,128)S(1)} %fusion.14), channel_id=1, source_target_pairs={{0,2},{1,3},{2,0},{3,1},{4,6},{5,7},{6,4},{7,5},{8,10},{9,11},{10,... | collective-permute-start | bytes 417800 | tf_op jit(solution)/shard_map/ppermute | solution.py:24
  124.8 8.5 %collective-permute-start.6 = (f32[136,256]{1,0:T(8,128)S(1)}, f32[136,256]{1,0:T(8,128)S(1)}, u32[]{:S(2)}, u32[]{:S(2)}) collective-permute-start(f32[136,256]{1,0:T(8,128)S(1)} %add.86), channel_id=1, source_target_pairs={{0,4},{1,5},{2,6},{3,7},{4,0},{5,1},{6,2},{7,3},{8,12},{9,13},{10,... | collective-permute-start | bytes 417800 | tf_op jit(solution)/shard_map/ppermute | solution.py:24
  133.2 3.3 %collective-permute-start.7 = (f32[136,256]{1,0:T(8,128)S(1)}, f32[136,256]{1,0:T(8,128)S(1)}, u32[]{:S(2)}, u32[]{:S(2)}) collective-permute-start(f32[136,256]{1,0:T(8,128)S(1)} %add.87), channel_id=1, source_target_pairs={{0,8},{8,0},{16,24},{24,16},{32,40},{40,32},{48,56},{56,48},{64,72... | collective-permute-start | bytes 417800 | tf_op jit(solution)/shard_map/ppermute | solution.py:24
  136.5 7.6 %collective-permute-start.8 = (f32[136,256]{1,0:T(8,128)S(1)}, f32[136,256]{1,0:T(8,128)S(1)}, u32[]{:S(2)}, u32[]{:S(2)}) collective-permute-start(f32[136,256]{1,0:T(8,128)S(1)} %add.88), channel_id=1, source_target_pairs={{0,64},{8,72},{16,80},{24,88},{32,96},{40,104},{48,112},{56,120},{... | collective-permute-start | bytes 417800 | tf_op jit(solution)/shard_map/ppermute | solution.py:24
  144.1 10.6 %collective-permute-start.9 = (f32[136,256]{1,0:T(8,128)S(1)}, f32[136,256]{1,0:T(8,128)S(1)}, u32[]{:S(2)}, u32[]{:S(2)}) collective-permute-start(f32[136,256]{1,0:T(8,128)S(1)} %add.89), channel_id=1, source_target_pairs={{0,16},{8,24},{16,0},{24,8},{32,48},{40,56},{48,32},{56,40},{64,80... | collective-permute-start | bytes 417800 | tf_op jit(solution)/shard_map/ppermute | solution.py:24
  154.8 10.5 %collective-permute-start.10 = (f32[136,256]{1,0:T(8,128)S(1)}, f32[136,256]{1,0:T(8,128)S(1)}, u32[]{:S(2)}, u32[]{:S(2)}) collective-permute-start(f32[136,256]{1,0:T(8,128)S(1)} %add.90), channel_id=1, source_target_pairs={{0,128},{8,136},{16,144},{24,152},{32,160},{40,168},{48,176},{56,1... | collective-permute-start | bytes 417800 | tf_op jit(solution)/shard_map/ppermute | solution.py:24
  165.4 13.6 %collective-permute-start.11 = (f32[136,256]{1,0:T(8,128)S(1)}, f32[136,256]{1,0:T(8,128)S(1)}, u32[]{:S(2)}, u32[]{:S(2)}) collective-permute-start(f32[136,256]{1,0:T(8,128)S(1)} %add.91), channel_id=1, source_target_pairs={{0,32},{8,40},{16,48},{24,56},{32,0},{40,8},{48,16},{56,24},{64,96... | collective-permute-start | bytes 417800 | tf_op jit(solution)/shard_map/ppermute | solution.py:24
  179.0 13.9 %collective-permute-start.12 = (f32[136,256]{1,0:T(8,128)S(1)}, f32[136,256]{1,0:T(8,128)S(1)}, u32[]{:S(2)}, u32[]{:S(2)}) collective-permute-start(f32[136,256]{1,0:T(8,128)S(1)} %add.92), channel_id=1, source_target_pairs={{0,256},{8,264},{16,272},{24,280},{32,288},{40,296},{48,304},{56,3... | collective-permute-start | bytes 417800 | tf_op jit(solution)/shard_map/ppermute | solution.py:24

commit v6 on v5

--- a/solution.py
+++ b/solution.py
@@ -53,16 +53,19 @@
     for b in range(blocks):
         acc = jnp.zeros((out_ref.shape[1], feat), jnp.float32)
         for g in range(groups):
-            tableT = bufT_ref[g]
-            for k in range(slots):
-                far = far_ref[b, g, pl.ds(k, 1), :]
-                tgt = tgt_ref[b, g, pl.ds(k, 1), :]
-                pick = (col_iota == far).astype(jnp.bfloat16)
-                pickedT = jnp.dot(tableT, pick, preferred_element_type=jnp.float32).astype(jnp.bfloat16)
-                scatter = (row_iota == tgt).astype(jnp.bfloat16)
-                acc = acc + lax.dot_general(
-                    scatter, pickedT, (((1,), (1,)), ((), ())), preferred_element_type=jnp.float32
-                )
+            far = far_ref[b, g]
+            tgt = tgt_ref[b, g]
+            pick = jnp.concatenate(
+                [(col_iota == far[k:k + 1, :]).astype(jnp.bfloat16) for k in range(slots)], axis=1
+            )
+            scatter = jnp.concatenate(
+                [(row_iota == tgt[k:k + 1, :]).astype(jnp.bfloat16) for k in range(slots)], axis=1
+            )
+            pickedT = jnp.dot(bufT_ref[g], pick, preferred_element_type=jnp.float32)
+            acc = acc + lax.dot_general(
+                scatter, pickedT.astype(jnp.bfloat16), (((1,), (1,)), ((), ())),
+                preferred_element_type=jnp.float32,
+            )
         out_ref[b] = acc
 
 

time: 197 us -> 184 us (0.934)
  the two profiles are of different devices: /device:TPU:6 before, /device:TPU:57 now
where the time goes in v6:
time: 184 us; the launch traced here: 183 us
  starting transfers between devices  85.2 us (46%)
  waiting for transfers between devices  69.5 us (38%)
  Pallas kernels  15.9 us (9%)
  local copies, waits for them, and re-layouts  7.63 us (4%)
  other arithmetic  2.99 us (2%)
    ppermute x9, waiting for transfers between devices, butterfly_sum(): value = value + lax.ppermute(value, axis, pairs)  47.2 us
    ppermute x9, starting transfers between devices, butterfly_sum(): value = value + lax.ppermute(value, axis, pairs)  38.5 us
    all_to_all x1, starting transfers between devices, local(): pieces = lax.all_to_all(pieces, 'rep', 0, 0)  26.8 us
    ppermute x3, starting transfers between devices, from_behind(): return lax.ppermute(value, axis, pairs)  19.2 us
    ppermute x3, waiting for transfers between devices, from_behind(): return lax.ppermute(value, axis, pairs)  16.3 us
    pallas_call x4, Pallas kernels, edge_sums_kernel(): pl.pallas_call(_edge_kernel, out_shape=jax.ShapeDtypeStruct((blocks, rows...  15.9 us
    all_to_all x1, waiting for transfers between devices, local(): pieces = lax.all_to_all(pieces, 'rep', 0, 0)  6.07 us
  transfers between devices with their start and end apart: 14, of which 13 were waited for; matrix products, arithmetic and copies ran while one was open for 2% of the time, Pallas kernels for 5%

profile of v6, /device:TPU:57, one launch (start us, length us, event | category | flops | bytes accessed | tf_op | source)
XLA Modules:
  0.0 183.2 jit_solution(4094609853507780655)
XLA Ops:
  0.6 0.7 convert_rsqrt_fusion
  1.4 1.0 copy.12
  2.4 0.7 collective-permute-start
  3.1 2.7 %collective-permute-start.1 = (bf16[1,128,512]{2,1,0:T(8,128)(2,1)S(1)}, bf16[1,128,512]{2,1,0:T(8,128)(2,1)S(1)}, u32[]{:S(2)}, u32[]{:S(2)}) collective-permute-start(bf16[1,128,512]{2,1,0:T(8,128)(2,1)S(1)} %bitcast.9), channel_id=1, source_target_pairs={{0,504},{8,0},{16,8},{24,16},{32,24},{40,32},{48,40},{56,48},{64,5... | collective-permute-start | bytes 393224 | tf_op jit(solution)/shard_map/ppermute | solution.py:15
  5.8 6.4 %collective-permute-done.1.bufT_ref = bf16[1,128,512]{2,1,0:T(8,128)(2,1)S(1)} collective-permute-done((bf16[1,128,512]{2,1,0:T(8,128)(2,1)S(1)}, bf16[1,128,512]{2,1,0:T(8,128)(2,1)S(1)}, u32[]{:S(2)}, u32[]{:S(2)}) %collective-permute-start.1) | collective-permute-done | bytes 131104 | tf_op jit(solution)/shard_map/ppermute | solution.py:15
  12.3 11.7 %collective-permute-start.2 = (bf16[2,128,512]{2,1,0:T(8,128)(2,1)S(1)}, bf16[2,128,512]{2,1,0:T(8,128)(2,1)S(1)}, u32[]{:S(2)}, u32[]{:S(2)}) collective-permute-start(bf16[2,128,512]{2,1,0:T(8,128)(2,1)S(1)} %pad_maximum_fusion.1), channel_id=1, source_target_pairs={{0,496},{8,504},{16,0},{24,8},{32,16},{40,24},{48,32},{56,40},{64,... | collective-permute-start | bytes 786440 | tf_op jit(solution)/shard_map/ppermute | solution.py:15
  24.1 3.7 %collective-permute-done.2.bufT_ref = bf16[2,128,512]{2,1,0:T(8,128)(2,1)S(1)} collective-permute-done((bf16[2,128,512]{2,1,0:T(8,128)(2,1)S(1)}, bf16[2,128,512]{2,1,0:T(8,128)(2,1)S(1)}, u32[]{:S(2)}, u32[]{:S(2)}) %collective-permute-start.2) | collective-permute-done | bytes 262176 | tf_op jit(solution)/shard_map/ppermute | solution.py:15
  27.8 0.6 copy-done.6
  28.5 4.8 %collective-permute-start.3 = (bf16[4,128,512]{2,1,0:T(8,128)(2,1)S(1)}, bf16[4,128,512]{2,1,0:T(8,128)(2,1)S(1)}, u32[]{:S(2)}, u32[]{:S(2)}) collective-permute-start(bf16[4,128,512]{2,1,0:T(8,128)(2,1)S(1)} %pad_maximum_fusion), channel_id=1, source_target_pairs={{0,480},{8,488},{16,496},{24,504},{32,0},{40,8},{48,16},{56,24},{6... | collective-permute-start | bytes 1572872 | tf_op jit(solution)/shard_map/ppermute | solution.py:15
  33.3 0.1 fusion.1
  33.4 0.6 slice.46.far_ref
  34.0 0.6 slice.44.far_ref
  34.7 0.6 slice.47.tgt_ref
  35.3 0.6 slice.45.tgt_ref
  35.9 0.6 fusion.16
  36.5 3.0 %shard_map.103 = f32[4,128,128]{2,1,0:T(8,128)} custom-call(bf16[1,128,512]{2,1,0:T(8,128)(2,1)} %bitcast.12, s32[4,1,8,128]{3,2,1,0:T(8,128)} %get-tuple-element.12.far_ref, s32[4,1,8,128]{3,2,1,0:T(8,128)} %get-tuple-element.6.tgt_ref), custom_call_target="tpu_custom_call" | custom-call | flops 671088640 | bytes 425984 | tf_op jit(solution)/shard_map/pallas_call | solution.py:77
  39.5 3.0 %shard_map.104 = f32[4,128,128]{2,1,0:T(8,128)} custom-call(bf16[1,128,512]{2,1,0:T(8,128)(2,1)} %copy-done.2, s32[4,1,8,128]{3,2,1,0:T(8,128)} %get-tuple-element.13.far_ref, s32[4,1,8,128]{3,2,1,0:T(8,128)} %get-tuple-element.5.tgt_ref), custom_call_target="tpu_custom_call" | custom-call | flops 671088640 | bytes 425984 | tf_op jit(solution)/shard_map/pallas_call | solution.py:77
  42.4 4.0 %shard_map.105 = f32[4,128,128]{2,1,0:T(8,128)} custom-call(bf16[2,128,512]{2,1,0:T(8,128)(2,1)} %copy-done.6, s32[4,2,8,128]{3,2,1,0:T(8,128)} %slice.44.far_ref, s32[4,2,8,128]{3,2,1,0:T(8,128)} %slice.45.tgt_ref), custom_call_target="tpu_custom_call" | custom-call | flops 1342177280 | bytes 589824 | tf_op jit(solution)/shard_map/pallas_call | solution.py:77
  46.5 6.2 %collective-permute-done.3.bufT_ref = bf16[4,128,512]{2,1,0:T(8,128)(2,1)S(1)} collective-permute-done((bf16[4,128,512]{2,1,0:T(8,128)(2,1)S(1)}, bf16[4,128,512]{2,1,0:T(8,128)(2,1)S(1)}, u32[]{:S(2)}, u32[]{:S(2)}) %collective-permute-start.3) | collective-permute-done | bytes 524320 | tf_op jit(solution)/shard_map/ppermute | solution.py:15
  52.7 0.8 copy-done.10
  53.5 6.0 %shard_map.106 = f32[4,128,128]{2,1,0:T(8,128)} custom-call(bf16[4,128,512]{2,1,0:T(8,128)(2,1)} %copy-done.10, s32[4,4,8,128]{3,2,1,0:T(8,128)} %slice.46.far_ref, s32[4,4,8,128]{3,2,1,0:T(8,128)} %slice.47.tgt_ref), custom_call_target="tpu_custom_call" | custom-call | flops 2684354560 | bytes 917504 | tf_op jit(solution)/shard_map/pallas_call | solution.py:77
  59.5 1.7 add_add_fusion
  61.1 26.8 %all-to-all-start = ((f32[8,64,128]{2,1,0:T(8,128)}), f32[8,64,128]{2,1,0:T(8,128)S(1)}, u32[]{:S(2)}, u32[]{:S(2)}) async-start(f32[8,64,128]{2,1,0:T(8,128)} %bitcast.2), calls=%async_computation | async-start | bytes 524288 | tf_op jit(solution)/shard_map/all_to_all | solution.py:139
  88.0 6.1 %all-to-all-done = f32[8,64,128]{2,1,0:T(8,128)S(1)} async-done(((f32[8,64,128]{2,1,0:T(8,128)}), f32[8,64,128]{2,1,0:T(8,128)S(1)}, u32[]{:S(2)}, u32[]{:S(2)}) %all-to-all-start) | async-done | bytes 262176 | tf_op jit(solution)/shard_map/all_to_all | solution.py:139
  94.1 0.1 copy.13
  94.4 0.6 copy-done.11
  95.0 0.8 convert_reduce_fusion
  95.8 0.1 fusion.18
  96.0 2.4 %collective-permute-start.4 = (f32[136,256]{1,0:T(8,128)S(1)}, f32[136,256]{1,0:T(8,128)S(1)}, u32[]{:S(2)}, u32[]{:S(2)}) collective-permute-start(f32[136,256]{1,0:T(8,128)S(1)} %pad_maximum_fusion.2), channel_id=1, source_target_pairs={{0,1},{1,0},{2,3},{3,2},{4,5},{5,4},{6,7},{7,6},{8,9},{9,8},{10,11... | collective-permute-start | bytes 417800 | tf_op jit(solution)/shard_map/ppermute | solution.py:24
  98.5 3.3 %collective-permute-done.4 = f32[136,256]{1,0:T(8,128)S(1)} collective-permute-done((f32[136,256]{1,0:T(8,128)S(1)}, f32[136,256]{1,0:T(8,128)S(1)}, u32[]{:S(2)}, u32[]{:S(2)}) %collective-permute-start.4) | collective-permute-done | bytes 139296 | tf_op jit(solution)/shard_map/ppermute | solution.py:24
  101.8 1.9 %collective-permute-start.5 = (f32[136,256]{1,0:T(8,128)S(1)}, f32[136,256]{1,0:T(8,128)S(1)}, u32[]{:S(2)}, u32[]{:S(2)}) collective-permute-start(f32[136,256]{1,0:T(8,128)S(1)} %fusion.14), channel_id=1, source_target_pairs={{0,2},{1,3},{2,0},{3,1},{4,6},{5,7},{6,4},{7,5},{8,10},{9,11},{10,... | collective-permute-start | bytes 417800 | tf_op jit(solution)/shard_map/ppermute | solution.py:24
  103.8 3.9 %collective-permute-done.5 = f32[136,256]{1,0:T(8,128)S(1)} collective-permute-done((f32[136,256]{1,0:T(8,128)S(1)}, f32[136,256]{1,0:T(8,128)S(1)}, u32[]{:S(2)}, u32[]{:S(2)}) %collective-permute-start.5) | collective-permute-done | bytes 139296 | tf_op jit(solution)/shard_map/ppermute | solution.py:24
  107.6 3.0 %collective-permute-start.6 = (f32[136,256]{1,0:T(8,128)S(1)}, f32[136,256]{1,0:T(8,128)S(1)}, u32[]{:S(2)}, u32[]{:S(2)}) collective-permute-start(f32[136,256]{1,0:T(8,128)S(1)} %add.86), channel_id=1, source_target_pairs={{0,4},{1,5},{2,6},{3,7},{4,0},{5,1},{6,2},{7,3},{8,12},{9,13},{10,... | collective-permute-start | bytes 417800 | tf_op jit(solution)/shard_map/ppermute | solution.py:24
  110.6 4.3 %collective-permute-done.6 = f32[136,256]{1,0:T(8,128)S(1)} collective-permute-done((f32[136,256]{1,0:T(8,128)S(1)}, f32[136,256]{1,0:T(8,128)S(1)}, u32[]{:S(2)}, u32[]{:S(2)}) %collective-permute-start.6) | collective-permute-done | bytes 139296 | tf_op jit(solution)/shard_map/ppermute | solution.py:24
  115.0 7.8 %collective-permute-start.7 = (f32[136,256]{1,0:T(8,128)S(1)}, f32[136,256]{1,0:T(8,128)S(1)}, u32[]{:S(2)}, u32[]{:S(2)}) collective-permute-start(f32[136,256]{1,0:T(8,128)S(1)} %add.87), channel_id=1, source_target_pairs={{0,8},{8,0},{16,24},{24,16},{32,40},{40,32},{48,56},{56,48},{64,72... | collective-permute-start | bytes 417800 | tf_op jit(solution)/shard_map/ppermute | solution.py:24
  122.8 1.0 collective-permute-done.7
  123.8 4.4 %collective-permute-start.8 = (f32[136,256]{1,0:T(8,128)S(1)}, f32[136,256]{1,0:T(8,128)S(1)}, u32[]{:S(2)}, u32[]{:S(2)}) collective-permute-start(f32[136,256]{1,0:T(8,128)S(1)} %add.88), channel_id=1, source_target_pairs={{0,64},{8,72},{16,80},{24,88},{32,96},{40,104},{48,112},{56,120},{... | collective-permute-start | bytes 417800 | tf_op jit(solution)/shard_map/ppermute | solution.py:24
  128.2 3.7 %collective-permute-done.8 = f32[136,256]{1,0:T(8,128)S(1)} collective-permute-done((f32[136,256]{1,0:T(8,128)S(1)}, f32[136,256]{1,0:T(8,128)S(1)}, u32[]{:S(2)}, u32[]{:S(2)}) %collective-permute-start.8) | collective-permute-done | bytes 139296 | tf_op jit(solution)/shard_map/ppermute | solution.py:24
  131.9 2.8 %collective-permute-start.9 = (f32[136,256]{1,0:T(8,128)S(1)}, f32[136,256]{1,0:T(8,128)S(1)}, u32[]{:S(2)}, u32[]{:S(2)}) collective-permute-start(f32[136,256]{1,0:T(8,128)S(1)} %add.89), channel_id=1, source_target_pairs={{0,16},{8,24},{16,0},{24,8},{32,48},{40,56},{48,32},{56,40},{64,80... | collective-permute-start | bytes 417800 | tf_op jit(solution)/shard_map/ppermute | solution.py:24
  134.6 8.3 %collective-permute-done.9 = f32[136,256]{1,0:T(8,128)S(1)} collective-permute-done((f32[136,256]{1,0:T(8,128)S(1)}, f32[136,256]{1,0:T(8,128)S(1)}, u32[]{:S(2)}, u32[]{:S(2)}) %collective-permute-start.9) | collective-permute-done | bytes 139296 | tf_op jit(solution)/shard_map/ppermute | solution.py:24
  142.9 4.8 %collective-permute-start.10 = (f32[136,256]{1,0:T(8,128)S(1)}, f32[136,256]{1,0:T(8,128)S(1)}, u32[]{:S(2)}, u32[]{:S(2)}) collective-permute-start(f32[136,256]{1,0:T(8,128)S(1)} %add.90), channel_id=1, source_target_pairs={{0,128},{8,136},{16,144},{24,152},{32,160},{40,168},{48,176},{56,1... | collective-permute-start | bytes 417800 | tf_op jit(solution)/shard_map/ppermute | solution.py:24
  147.7 6.7 %collective-permute-done.10 = f32[136,256]{1,0:T(8,128)S(1)} collective-permute-done((f32[136,256]{1,0:T(8,128)S(1)}, f32[136,256]{1,0:T(8,128)S(1)}, u32[]{:S(2)}, u32[]{:S(2)}) %collective-permute-start.10) | collective-permute-done | bytes 139296 | tf_op jit(solution)/shard_map/ppermute | solution.py:24
  154.4 6.5 %collective-permute-start.11 = (f32[136,256]{1,0:T(8,128)S(1)}, f32[136,256]{1,0:T(8,128)S(1)}, u32[]{:S(2)}, u32[]{:S(2)}) collective-permute-start(f32[136,256]{1,0:T(8,128)S(1)} %add.91), channel_id=1, source_target_pairs={{0,32},{8,40},{16,48},{24,56},{32,0},{40,8},{48,16},{56,24},{64,96... | collective-permute-start | bytes 417800 | tf_op jit(solution)/shard_map/ppermute | solution.py:24
  160.9 6.6 %collective-permute-done.11 = f32[136,256]{1,0:T(8,128)S(1)} collective-permute-done((f32[136,256]{1,0:T(8,128)S(1)}, f32[136,256]{1,0:T(8,128)S(1)}, u32[]{:S(2)}, u32[]{:S(2)}) %collective-permute-start.11) | collective-permute-done | bytes 139296 | tf_op jit(solution)/shard_map/ppermute | solution.py:24
  167.6 5.0 %collective-permute-start.12 = (f32[136,256]{1,0:T(8,128)S(1)}, f32[136,256]{1,0:T(8,128)S(1)}, u32[]{:S(2)}, u32[]{:S(2)}) collective-permute-start(f32[136,256]{1,0:T(8,128)S(1)} %add.92), channel_id=1, source_target_pairs={{0,256},{8,264},{16,272},{24,280},{32,288},{40,296},{48,304},{56,3... | collective-permute-start | bytes 417800 | tf_op jit(solution)/shard_map/ppermute | solution.py:24
  172.6 9.4 %collective-permute-done.12 = f32[136,256]{1,0:T(8,128)S(1)} collective-permute-done((f32[136,256]{1,0:T(8,128)S(1)}, f32[136,256]{1,0:T(8,128)S(1)}, u32[]{:S(2)}, u32[]{:S(2)}) %collective-permute-start.12) | collective-permute-done | bytes 139296 | tf_op jit(solution)/shard_map/ppermute | solution.py:24
  181.9 0.7 slice.48
  182.6 0.6 slice.49
  (43 shorter events, 0.6 us)
Async XLA Ops:
  0.6 93.7 %copy-start = (bf16[128,256]{1,0:T(8,128)(2,1)S(1)}, bf16[128,256]{1,0:T(8,128)(2,1)}, u32[]{:S(2)}) copy-start(bf16[128,256]{1,0:T(8,128)(2,1)} %param.13) | copy-start | bytes 196612
  2.4 0.7 collective-permute-start
  3.1 24.7 %copy-start.1 = (bf16[128,512]{1,0:T(8,128)(2,1)}, bf16[128,512]{1,0:T(8,128)(2,1)S(1)}, u32[]{:S(2)}) copy-start(bf16[128,512]{1,0:T(8,128)(2,1)S(1)} %collective-permute-done) | copy-start | bytes 393220
  3.1 20.9 %copy-start.8 = (s32[4,8,8]{2,1,0:T(8,128)S(1)}, s32[4,8,8]{2,1,0:T(8,128)}, u32[]{:S(2)}) copy-start(s32[4,8,8]{2,1,0:T(8,128)} %param.10) | copy-start | bytes 3076
  3.1 9.1 %collective-permute-start.1 = (bf16[1,128,512]{2,1,0:T(8,128)(2,1)S(1)}, bf16[1,128,512]{2,1,0:T(8,128)(2,1)S(1)}, u32[]{:S(2)}, u32[]{:S(2)}) collective-permute-start(bf16[1,128,512]{2,1,0:T(8,128)(2,1)S(1)} %bitcast.9), channel_id=1, source_target_pairs={{0,504},{8,0},{16,8},{24,16},{32,24},{40,32},{48,40},{56,48},{64,5... | collective-permute-start | bytes 393224 | tf_op jit(solution)/shard_map/ppermute | solution.py:15
  12.3 15.5 %copy-start.2 = (bf16[1,128,512]{2,1,0:T(8,128)(2,1)}, bf16[1,128,512]{2,1,0:T(8,128)(2,1)S(1)}, u32[]{:S(2)}) copy-start(bf16[1,128,512]{2,1,0:T(8,128)(2,1)S(1)} %collective-permute-done.1.bufT_ref) | copy-start | bytes 393220
  12.3 15.5 %collective-permute-start.2 = (bf16[2,128,512]{2,1,0:T(8,128)(2,1)S(1)}, bf16[2,128,512]{2,1,0:T(8,128)(2,1)S(1)}, u32[]{:S(2)}, u32[]{:S(2)}) collective-permute-start(bf16[2,128,512]{2,1,0:T(8,128)(2,1)S(1)} %pad_maximum_fusion.1), channel_id=1, source_target_pairs={{0,496},{8,504},{16,0},{24,8},{32,16},{40,24},{48,32},{56,40},{64,... | collective-permute-start | bytes 786440 | tf_op jit(solution)/shard_map/ppermute | solution.py:15
  24.1 9.2 %copy-start.7 = (s32[4,8,8,128]{3,2,1,0:T(8,128)S(1)}, s32[4,8,8,128]{3,2,1,0:T(8,128)}, u32[]{:S(2)}) copy-start(s32[4,8,8,128]{3,2,1,0:T(8,128)} %param.12) | copy-start | bytes 393220
  24.1 9.2 %copy-start.9 = (s32[4,8,8]{2,1,0:T(8,128)S(1)}, s32[4,8,8]{2,1,0:T(8,128)}, u32[]{:S(2)}) copy-start(s32[4,8,8]{2,1,0:T(8,128)} %param.11) | copy-start | bytes 3076
  27.8 0.7 copy-start.6
  28.5 24.2 %collective-permute-start.3 = (bf16[4,128,512]{2,1,0:T(8,128)(2,1)S(1)}, bf16[4,128,512]{2,1,0:T(8,128)(2,1)S(1)}, u32[]{:S(2)}, u32[]{:S(2)}) collective-permute-start(bf16[4,128,512]{2,1,0:T(8,128)(2,1)S(1)} %pad_maximum_fusion), channel_id=1, source_target_pairs={{0,480},{8,488},{16,496},{24,504},{32,0},{40,8},{48,16},{56,24},{6... | collective-permute-start | bytes 1572872 | tf_op jit(solution)/shard_map/ppermute | solution.py:15
  46.5 13.0 %copy-start.3 = (f32[4,128,128]{2,1,0:T(8,128)S(1)}, f32[4,128,128]{2,1,0:T(8,128)}, u32[]{:S(2)}) copy-start(f32[4,128,128]{2,1,0:T(8,128)} %shard_map.103) | copy-start | bytes 786436
  46.5 13.0 %copy-start.4 = (f32[4,128,128]{2,1,0:T(8,128)S(1)}, f32[4,128,128]{2,1,0:T(8,128)}, u32[]{:S(2)}) copy-start(f32[4,128,128]{2,1,0:T(8,128)} %shard_map.104) | copy-start | bytes 786436
  46.5 13.0 %copy-start.5 = (f32[4,128,128]{2,1,0:T(8,128)S(1)}, f32[4,128,128]{2,1,0:T(8,128)}, u32[]{:S(2)}) copy-start(f32[4,128,128]{2,1,0:T(8,128)} %shard_map.105) | copy-start | bytes 786436
  52.7 0.8 copy-start.10
  61.1 33.0 %all-to-all-start = ((f32[8,64,128]{2,1,0:T(8,128)}), f32[8,64,128]{2,1,0:T(8,128)S(1)}, u32[]{:S(2)}, u32[]{:S(2)}) async-start(f32[8,64,128]{2,1,0:T(8,128)} %bitcast.2), calls=%async_computation | async-start | bytes 524288 | tf_op jit(solution)/shard_map/all_to_all | solution.py:139
  94.2 0.8 copy-start.11
  94.2 0.8 copy-start.12
  96.0 5.8 %collective-permute-start.4 = (f32[136,256]{1,0:T(8,128)S(1)}, f32[136,256]{1,0:T(8,128)S(1)}, u32[]{:S(2)}, u32[]{:S(2)}) collective-permute-start(f32[136,256]{1,0:T(8,128)S(1)} %pad_maximum_fusion.2), channel_id=1, source_target_pairs={{0,1},{1,0},{2,3},{3,2},{4,5},{5,4},{6,7},{7,6},{8,9},{9,8},{10,11... | collective-permute-start | bytes 417800 | tf_op jit(solution)/shard_map/ppermute | solution.py:24
  101.8 5.8 %collective-permute-start.5 = (f32[136,256]{1,0:T(8,128)S(1)}, f32[136,256]{1,0:T(8,128)S(1)}, u32[]{:S(2)}, u32[]{:S(2)}) collective-permute-start(f32[136,256]{1,0:T(8,128)S(1)} %fusion.14), channel_id=1, source_target_pairs={{0,2},{1,3},{2,0},{3,1},{4,6},{5,7},{6,4},{7,5},{8,10},{9,11},{10,... | collective-permute-start | bytes 417800 | tf_op jit(solution)/shard_map/ppermute | solution.py:24
  107.6 7.3 %collective-permute-start.6 = (f32[136,256]{1,0:T(8,128)S(1)}, f32[136,256]{1,0:T(8,128)S(1)}, u32[]{:S(2)}, u32[]{:S(2)}) collective-permute-start(f32[136,256]{1,0:T(8,128)S(1)} %add.86), channel_id=1, source_target_pairs={{0,4},{1,5},{2,6},{3,7},{4,0},{5,1},{6,2},{7,3},{8,12},{9,13},{10,... | collective-permute-start | bytes 417800 | tf_op jit(solution)/shard_map/ppermute | solution.py:24
  115.0 8.8 %collective-permute-start.7 = (f32[136,256]{1,0:T(8,128)S(1)}, f32[136,256]{1,0:T(8,128)S(1)}, u32[]{:S(2)}, u32[]{:S(2)}) collective-permute-start(f32[136,256]{1,0:T(8,128)S(1)} %add.87), channel_id=1, source_target_pairs={{0,8},{8,0},{16,24},{24,16},{32,40},{40,32},{48,56},{56,48},{64,72... | collective-permute-start | bytes 417800 | tf_op jit(solution)/shard_map/ppermute | solution.py:24
  123.8 8.0 %collective-permute-start.8 = (f32[136,256]{1,0:T(8,128)S(1)}, f32[136,256]{1,0:T(8,128)S(1)}, u32[]{:S(2)}, u32[]{:S(2)}) collective-permute-start(f32[136,256]{1,0:T(8,128)S(1)} %add.88), channel_id=1, source_target_pairs={{0,64},{8,72},{16,80},{24,88},{32,96},{40,104},{48,112},{56,120},{... | collective-permute-start | bytes 417800 | tf_op jit(solution)/shard_map/ppermute | solution.py:24
  131.9 11.1 %collective-permute-start.9 = (f32[136,256]{1,0:T(8,128)S(1)}, f32[136,256]{1,0:T(8,128)S(1)}, u32[]{:S(2)}, u32[]{:S(2)}) collective-permute-start(f32[136,256]{1,0:T(8,128)S(1)} %add.89), channel_id=1, source_target_pairs={{0,16},{8,24},{16,0},{24,8},{32,48},{40,56},{48,32},{56,40},{64,80... | collective-permute-start | bytes 417800 | tf_op jit(solution)/shard_map/ppermute | solution.py:24
  142.9 11.5 %collective-permute-start.10 = (f32[136,256]{1,0:T(8,128)S(1)}, f32[136,256]{1,0:T(8,128)S(1)}, u32[]{:S(2)}, u32[]{:S(2)}) collective-permute-start(f32[136,256]{1,0:T(8,128)S(1)} %add.90), channel_id=1, source_target_pairs={{0,128},{8,136},{16,144},{24,152},{32,160},{40,168},{48,176},{56,1... | collective-permute-start | bytes 417800 | tf_op jit(solution)/shard_map/ppermute | solution.py:24
  154.4 13.1 %collective-permute-start.11 = (f32[136,256]{1,0:T(8,128)S(1)}, f32[136,256]{1,0:T(8,128)S(1)}, u32[]{:S(2)}, u32[]{:S(2)}) collective-permute-start(f32[136,256]{1,0:T(8,128)S(1)} %add.91), channel_id=1, source_target_pairs={{0,32},{8,40},{16,48},{24,56},{32,0},{40,8},{48,16},{56,24},{64,96... | collective-permute-start | bytes 417800 | tf_op jit(solution)/shard_map/ppermute | solution.py:24
  167.6 14.3 %collective-permute-start.12 = (f32[136,256]{1,0:T(8,128)S(1)}, f32[136,256]{1,0:T(8,128)S(1)}, u32[]{:S(2)}, u32[]{:S(2)}) collective-permute-start(f32[136,256]{1,0:T(8,128)S(1)} %add.92), channel_id=1, source_target_pairs={{0,256},{8,264},{16,272},{24,280},{32,288},{40,296},{48,304},{56,3... | collective-permute-start | bytes 417800 | tf_op jit(solution)/shard_map/ppermute | solution.py:24

commit v7 on v6

--- a/solution.py
+++ b/solution.py
@@ -117,9 +117,9 @@
     is_live = lax.broadcasted_iota(jnp.int32, edge_code.shape, 3) < edge_count[..., None]
     tgt = jnp.where(is_live, edge_code // 128, -1)
 
-    def local_sums(held_t, first):
-        count = held_t.shape[0]
-        return edge_sums_kernel(held_t, far[:, first:first + count], tgt[:, first:first + count])
+    def local_sums(held_t, chosen):
+        index = jnp.array(chosen, jnp.int32)
+        return edge_sums_kernel(held_t, far[:, index], tgt[:, index])
 
     row_count = lax.axis_size("rows")
     pairs = []
@@ -128,12 +128,16 @@
             target = (source - step_count * rep_index) % row_count
             pairs.append((source * replicas + rep_index, target * replicas + rep_index))
     held = lax.ppermute(scaled.T, ("rows", "rep"), pairs)[None]
-    partial_total = local_sums(held, 0)
-    while held.shape[0] < step_count:
-        have = held.shape[0]
-        arrived = from_behind(held, "rows", -have)
-        partial_total = partial_total + local_sums(arrived, have)
+    offsets = [0]
+    partial_total = local_sums(held, offsets)
+    stride = step_count
+    while stride > 1:
+        stride //= 2
+        arrived = from_behind(held, "rows", -stride)
+        arrived_offsets = [offset + stride for offset in offsets]
+        partial_total = partial_total + local_sums(arrived, arrived_offsets)
         held = jnp.concatenate([held, arrived], axis=0)
+        offsets = offsets + arrived_offsets
     partial_total = partial_total.reshape(-1, partial_total.shape[-1])
     pieces = partial_total.reshape((replicas, -1) + partial_total.shape[1:])
     pieces = lax.all_to_all(pieces, "rep", 0, 0)

time: 184 us -> 178 us (0.967)
  the two profiles are of different devices: /device:TPU:57 before, /device:TPU:1 now
where the time goes in v7:
time: 178 us; the launch traced here: 177 us
  starting transfers between devices  86 us (48%)
  waiting for transfers between devices  61.6 us (35%)
  Pallas kernels  16.1 us (9%)
  local copies, waits for them, and re-layouts  8.7 us (5%)
  other arithmetic  3.01 us (2%)
    ppermute x9, waiting for transfers between devices, butterfly_sum(): value = value + lax.ppermute(value, axis, pairs)  49.9 us
    ppermute x9, starting transfers between devices, butterfly_sum(): value = value + lax.ppermute(value, axis, pairs)  35 us
    ppermute x3, starting transfers between devices, from_behind(): return lax.ppermute(value, axis, pairs)  29.4 us
    all_to_all x1, starting transfers between devices, local(): pieces = lax.all_to_all(pieces, 'rep', 0, 0)  20.9 us
    pallas_call x4, Pallas kernels, edge_sums_kernel(): pl.pallas_call(_edge_kernel, out_shape=jax.ShapeDtypeStruct((blocks, rows...  16.1 us
    all_to_all x1, waiting for transfers between devices, local(): pieces = lax.all_to_all(pieces, 'rep', 0, 0)  6.85 us
    ppermute x3, waiting for transfers between devices, from_behind(): return lax.ppermute(value, axis, pairs)  4.87 us
    gather x7, local copies, waits for them, and re-layouts, local_sums(): return edge_sums_kernel(held_t, far[:, index], tgt[:, index])  4.12 us
  transfers between devices with their start and end apart: 14, of which 12 were waited for; matrix products, arithmetic and copies ran while one was open for 2% of the time, Pallas kernels for 6%

profile of v7, /device:TPU:1, one launch (start us, length us, event | category | flops | bytes accessed | tf_op | source)
XLA Modules:
  0.0 177.4 jit_solution(8677649336271236189)
XLA Ops:
  0.6 0.7 convert_rsqrt_fusion
  1.4 1.0 copy.21
  2.4 0.8 collective-permute-start
  3.3 0.1 fusion.1
  3.5 14.4 %collective-permute-start.1 = (bf16[1,128,512]{2,1,0:T(8,128)(2,1)S(1)}, bf16[1,128,512]{2,1,0:T(8,128)(2,1)S(1)}, u32[]{:S(2)}, u32[]{:S(2)}) collective-permute-start(bf16[1,128,512]{2,1,0:T(8,128)(2,1)S(1)} %bitcast.17), channel_id=1, source_target_pairs={{0,480},{8,488},{16,496},{24,504},{32,0},{40,8},{48,16},{56,24},{6... | collective-permute-start | bytes 393224 | tf_op jit(solution)/shard_map/ppermute | solution.py:15
  17.8 0.6 fusion.16
  18.5 1.5 collective-permute-done.1.bufT_ref
  20.0 11.1 %collective-permute-start.2 = (bf16[2,128,512]{2,1,0:T(8,128)(2,1)S(1)}, bf16[2,128,512]{2,1,0:T(8,128)(2,1)S(1)}, u32[]{:S(2)}, u32[]{:S(2)}) collective-permute-start(bf16[2,128,512]{2,1,0:T(8,128)(2,1)S(1)} %pad_maximum_fusion.1), channel_id=1, source_target_pairs={{0,496},{8,504},{16,0},{24,8},{32,16},{40,24},{48,32},{56,40},{64,... | collective-permute-start | bytes 786440 | tf_op jit(solution)/shard_map/ppermute | solution.py:15
  31.2 0.6 gather_fusion
  31.7 0.6 gather_fusion.1
  32.3 0.6 copy_bitcast_fusion.2
  32.9 3.3 %collective-permute-done.2.bufT_ref = bf16[2,128,512]{2,1,0:T(8,128)(2,1)S(1)} collective-permute-done((bf16[2,128,512]{2,1,0:T(8,128)(2,1)S(1)}, bf16[2,128,512]{2,1,0:T(8,128)(2,1)S(1)}, u32[]{:S(2)}, u32[]{:S(2)}) %collective-permute-start.2) | collective-permute-done | bytes 262176 | tf_op jit(solution)/shard_map/ppermute | solution.py:15
  36.3 0.6 copy-done.6
  37.0 3.9 %collective-permute-start.3 = (bf16[4,128,512]{2,1,0:T(8,128)(2,1)S(1)}, bf16[4,128,512]{2,1,0:T(8,128)(2,1)S(1)}, u32[]{:S(2)}, u32[]{:S(2)}) collective-permute-start(bf16[4,128,512]{2,1,0:T(8,128)(2,1)S(1)} %pad_maximum_fusion), channel_id=1, source_target_pairs={{0,504},{8,0},{16,8},{24,16},{32,24},{40,32},{48,40},{56,48},{64,5... | collective-permute-start | bytes 1572872 | tf_op jit(solution)/shard_map/ppermute | solution.py:15
  40.9 0.6 gather_fusion.2
  41.5 0.6 gather_fusion.3
  42.0 0.7 copy_bitcast_fusion
  42.7 3.0 %shard_map.139 = f32[4,128,128]{2,1,0:T(8,128)} custom-call(bf16[1,128,512]{2,1,0:T(8,128)(2,1)} %bitcast.20, s32[4,1,8,128]{3,2,1,0:T(8,128)} %get-tuple-element.56.far_ref, s32[4,1,8,128]{3,2,1,0:T(8,128)} %get-tuple-element.50.tgt_ref), custom_call_target="tpu_custom_call" | custom-call | flops 671088640 | bytes 425984 | tf_op jit(solution)/shard_map/pallas_call | solution.py:77
  45.7 3.0 %shard_map.140 = f32[4,128,128]{2,1,0:T(8,128)} custom-call(bf16[1,128,512]{2,1,0:T(8,128)(2,1)} %copy-done.2, s32[4,1,8,128]{3,2,1,0:T(8,128)} %get-tuple-element.57.far_ref, s32[4,1,8,128]{3,2,1,0:T(8,128)} %get-tuple-element.49.tgt_ref), custom_call_target="tpu_custom_call" | custom-call | flops 671088640 | bytes 425984 | tf_op jit(solution)/shard_map/pallas_call | solution.py:77
  48.6 4.0 %shard_map.141 = f32[4,128,128]{2,1,0:T(8,128)} custom-call(bf16[2,128,512]{2,1,0:T(8,128)(2,1)} %copy-done.6, s32[4,2,8,128]{3,2,1,0:T(8,128)} %get-tuple-element.61.far_ref, s32[4,2,8,128]{3,2,1,0:T(8,128)} %get-tuple-element.60.tgt_ref), custom_call_target="tpu_custom_call" | custom-call | flops 1342177280 | bytes 589824 | tf_op jit(solution)/shard_map/pallas_call | solution.py:77
  52.7 0.8 copy-done.12
  53.5 6.1 %shard_map.142 = f32[4,128,128]{2,1,0:T(8,128)} custom-call(bf16[4,128,512]{2,1,0:T(8,128)(2,1)} %copy-done.12, s32[4,4,8,128]{3,2,1,0:T(8,128)} %get-tuple-element.59.far_ref, s32[4,4,8,128]{3,2,1,0:T(8,128)} %get-tuple-element.58.tgt_ref), custom_call_target="tpu_custom_call" | custom-call | flops 2684354560 | bytes 917504 | tf_op jit(solution)/shard_map/pallas_call | solution.py:77
  59.6 1.7 add_add_fusion
  61.3 20.9 %all-to-all-start = ((f32[8,64,128]{2,1,0:T(8,128)}), f32[8,64,128]{2,1,0:T(8,128)S(1)}, u32[]{:S(2)}, u32[]{:S(2)}) async-start(f32[8,64,128]{2,1,0:T(8,128)} %bitcast.6), calls=%async_computation | async-start | bytes 524288 | tf_op jit(solution)/shard_map/all_to_all | solution.py:143
  82.3 6.9 %all-to-all-done = f32[8,64,128]{2,1,0:T(8,128)S(1)} async-done(((f32[8,64,128]{2,1,0:T(8,128)}), f32[8,64,128]{2,1,0:T(8,128)S(1)}, u32[]{:S(2)}, u32[]{:S(2)}) %all-to-all-start) | async-done | bytes 262176 | tf_op jit(solution)/shard_map/all_to_all | solution.py:143
  89.4 0.6 copy-done.13
  90.0 0.8 convert_reduce_fusion
  90.8 0.1 fusion.18
  91.0 2.3 %collective-permute-start.4 = (f32[136,256]{1,0:T(8,128)S(1)}, f32[136,256]{1,0:T(8,128)S(1)}, u32[]{:S(2)}, u32[]{:S(2)}) collective-permute-start(f32[136,256]{1,0:T(8,128)S(1)} %pad_maximum_fusion.2), channel_id=1, source_target_pairs={{0,1},{1,0},{2,3},{3,2},{4,5},{5,4},{6,7},{7,6},{8,9},{9,8},{10,11... | collective-permute-start | bytes 417800 | tf_op jit(solution)/shard_map/ppermute | solution.py:24
  93.3 3.5 %collective-permute-done.4 = f32[136,256]{1,0:T(8,128)S(1)} collective-permute-done((f32[136,256]{1,0:T(8,128)S(1)}, f32[136,256]{1,0:T(8,128)S(1)}, u32[]{:S(2)}, u32[]{:S(2)}) %collective-permute-start.4) | collective-permute-done | bytes 139296 | tf_op jit(solution)/shard_map/ppermute | solution.py:24
  96.8 1.9 %collective-permute-start.5 = (f32[136,256]{1,0:T(8,128)S(1)}, f32[136,256]{1,0:T(8,128)S(1)}, u32[]{:S(2)}, u32[]{:S(2)}) collective-permute-start(f32[136,256]{1,0:T(8,128)S(1)} %fusion.14), channel_id=1, source_target_pairs={{0,2},{1,3},{2,0},{3,1},{4,6},{5,7},{6,4},{7,5},{8,10},{9,11},{10,... | collective-permute-start | bytes 417800 | tf_op jit(solution)/shard_map/ppermute | solution.py:24
  98.8 3.9 %collective-permute-done.5 = f32[136,256]{1,0:T(8,128)S(1)} collective-permute-done((f32[136,256]{1,0:T(8,128)S(1)}, f32[136,256]{1,0:T(8,128)S(1)}, u32[]{:S(2)}, u32[]{:S(2)}) %collective-permute-start.5) | collective-permute-done | bytes 139296 | tf_op jit(solution)/shard_map/ppermute | solution.py:24
  102.7 2.5 %collective-permute-start.6 = (f32[136,256]{1,0:T(8,128)S(1)}, f32[136,256]{1,0:T(8,128)S(1)}, u32[]{:S(2)}, u32[]{:S(2)}) collective-permute-start(f32[136,256]{1,0:T(8,128)S(1)} %add.106), channel_id=1, source_target_pairs={{0,4},{1,5},{2,6},{3,7},{4,0},{5,1},{6,2},{7,3},{8,12},{9,13},{10,... | collective-permute-start | bytes 417800 | tf_op jit(solution)/shard_map/ppermute | solution.py:24
  105.1 4.8 %collective-permute-done.6 = f32[136,256]{1,0:T(8,128)S(1)} collective-permute-done((f32[136,256]{1,0:T(8,128)S(1)}, f32[136,256]{1,0:T(8,128)S(1)}, u32[]{:S(2)}, u32[]{:S(2)}) %collective-permute-start.6) | collective-permute-done | bytes 139296 | tf_op jit(solution)/shard_map/ppermute | solution.py:24
  110.0 6.6 %collective-permute-start.7 = (f32[136,256]{1,0:T(8,128)S(1)}, f32[136,256]{1,0:T(8,128)S(1)}, u32[]{:S(2)}, u32[]{:S(2)}) collective-permute-start(f32[136,256]{1,0:T(8,128)S(1)} %add.107), channel_id=1, source_target_pairs={{0,8},{8,0},{16,24},{24,16},{32,40},{40,32},{48,56},{56,48},{64,72... | collective-permute-start | bytes 417800 | tf_op jit(solution)/shard_map/ppermute | solution.py:24
  116.6 1.0 collective-permute-done.7
  117.6 2.3 %collective-permute-start.8 = (f32[136,256]{1,0:T(8,128)S(1)}, f32[136,256]{1,0:T(8,128)S(1)}, u32[]{:S(2)}, u32[]{:S(2)}) collective-permute-start(f32[136,256]{1,0:T(8,128)S(1)} %add.108), channel_id=1, source_target_pairs={{0,64},{8,72},{16,80},{24,88},{32,96},{40,104},{48,112},{56,120},{... | collective-permute-start | bytes 417800 | tf_op jit(solution)/shard_map/ppermute | solution.py:24
  119.9 4.5 %collective-permute-done.8 = f32[136,256]{1,0:T(8,128)S(1)} collective-permute-done((f32[136,256]{1,0:T(8,128)S(1)}, f32[136,256]{1,0:T(8,128)S(1)}, u32[]{:S(2)}, u32[]{:S(2)}) %collective-permute-start.8) | collective-permute-done | bytes 139296 | tf_op jit(solution)/shard_map/ppermute | solution.py:24
  124.4 3.9 %collective-permute-start.9 = (f32[136,256]{1,0:T(8,128)S(1)}, f32[136,256]{1,0:T(8,128)S(1)}, u32[]{:S(2)}, u32[]{:S(2)}) collective-permute-start(f32[136,256]{1,0:T(8,128)S(1)} %add.109), channel_id=1, source_target_pairs={{0,16},{8,24},{16,0},{24,8},{32,48},{40,56},{48,32},{56,40},{64,80... | collective-permute-start | bytes 417800 | tf_op jit(solution)/shard_map/ppermute | solution.py:24
  128.3 7.1 %collective-permute-done.9 = f32[136,256]{1,0:T(8,128)S(1)} collective-permute-done((f32[136,256]{1,0:T(8,128)S(1)}, f32[136,256]{1,0:T(8,128)S(1)}, u32[]{:S(2)}, u32[]{:S(2)}) %collective-permute-start.9) | collective-permute-done | bytes 139296 | tf_op jit(solution)/shard_map/ppermute | solution.py:24
  135.5 6.0 %collective-permute-start.10 = (f32[136,256]{1,0:T(8,128)S(1)}, f32[136,256]{1,0:T(8,128)S(1)}, u32[]{:S(2)}, u32[]{:S(2)}) collective-permute-start(f32[136,256]{1,0:T(8,128)S(1)} %add.110), channel_id=1, source_target_pairs={{0,128},{8,136},{16,144},{24,152},{32,160},{40,168},{48,176},{56,1... | collective-permute-start | bytes 417800 | tf_op jit(solution)/shard_map/ppermute | solution.py:24
  141.5 6.7 %collective-permute-done.10 = f32[136,256]{1,0:T(8,128)S(1)} collective-permute-done((f32[136,256]{1,0:T(8,128)S(1)}, f32[136,256]{1,0:T(8,128)S(1)}, u32[]{:S(2)}, u32[]{:S(2)}) %collective-permute-start.10) | collective-permute-done | bytes 139296 | tf_op jit(solution)/shard_map/ppermute | solution.py:24
  148.2 4.3 %collective-permute-start.11 = (f32[136,256]{1,0:T(8,128)S(1)}, f32[136,256]{1,0:T(8,128)S(1)}, u32[]{:S(2)}, u32[]{:S(2)}) collective-permute-start(f32[136,256]{1,0:T(8,128)S(1)} %add.111), channel_id=1, source_target_pairs={{0,32},{8,40},{16,48},{24,56},{32,0},{40,8},{48,16},{56,24},{64,96... | collective-permute-start | bytes 417800 | tf_op jit(solution)/shard_map/ppermute | solution.py:24
  152.5 9.4 %collective-permute-done.11 = f32[136,256]{1,0:T(8,128)S(1)} collective-permute-done((f32[136,256]{1,0:T(8,128)S(1)}, f32[136,256]{1,0:T(8,128)S(1)}, u32[]{:S(2)}, u32[]{:S(2)}) %collective-permute-start.11) | collective-permute-done | bytes 139296 | tf_op jit(solution)/shard_map/ppermute | solution.py:24
  161.9 5.2 %collective-permute-start.12 = (f32[136,256]{1,0:T(8,128)S(1)}, f32[136,256]{1,0:T(8,128)S(1)}, u32[]{:S(2)}, u32[]{:S(2)}) collective-permute-start(f32[136,256]{1,0:T(8,128)S(1)} %add.112), channel_id=1, source_target_pairs={{0,256},{8,264},{16,272},{24,280},{32,288},{40,296},{48,304},{56,3... | collective-permute-start | bytes 417800 | tf_op jit(solution)/shard_map/ppermute | solution.py:24
  167.1 9.0 %collective-permute-done.12 = f32[136,256]{1,0:T(8,128)S(1)} collective-permute-done((f32[136,256]{1,0:T(8,128)S(1)}, f32[136,256]{1,0:T(8,128)S(1)}, u32[]{:S(2)}, u32[]{:S(2)}) %collective-permute-start.12) | collective-permute-done | bytes 139296 | tf_op jit(solution)/shard_map/ppermute | solution.py:24
  176.1 0.7 slice.68
  176.8 0.6 slice.69
  (51 shorter events, 0.7 us)
Async XLA Ops:
  0.6 88.7 %copy-start = (bf16[128,256]{1,0:T(8,128)(2,1)S(1)}, bf16[128,256]{1,0:T(8,128)(2,1)}, u32[]{:S(2)}) copy-start(bf16[128,256]{1,0:T(8,128)(2,1)} %param.17) | copy-start | bytes 196612
  2.4 0.9 copy-start.8
  2.4 0.9 copy-start.7
  2.4 0.9 copy-start.9
  2.4 1.0 collective-permute-start
  3.5 32.8 %copy-start.1 = (bf16[128,512]{1,0:T(8,128)(2,1)}, bf16[128,512]{1,0:T(8,128)(2,1)S(1)}, u32[]{:S(2)}) copy-start(bf16[128,512]{1,0:T(8,128)(2,1)S(1)} %collective-permute-done) | copy-start | bytes 393220
  3.5 16.5 %collective-permute-start.1 = (bf16[1,128,512]{2,1,0:T(8,128)(2,1)S(1)}, bf16[1,128,512]{2,1,0:T(8,128)(2,1)S(1)}, u32[]{:S(2)}, u32[]{:S(2)}) collective-permute-start(bf16[1,128,512]{2,1,0:T(8,128)(2,1)S(1)} %bitcast.17), channel_id=1, source_target_pairs={{0,480},{8,488},{16,496},{24,504},{32,0},{40,8},{48,16},{56,24},{6... | collective-permute-start | bytes 393224 | tf_op jit(solution)/shard_map/ppermute | solution.py:15
  18.5 12.7 %copy-start.11 = (s32[2]{0:T(128)S(1)}, s32[2]{0:T(128)}, u32[]{:S(2)}) copy-start(s32[2]{0:T(128)} %constant.168) | copy-start | bytes 28
  20.0 16.3 %copy-start.2 = (bf16[1,128,512]{2,1,0:T(8,128)(2,1)}, bf16[1,128,512]{2,1,0:T(8,128)(2,1)S(1)}, u32[]{:S(2)}) copy-start(bf16[1,128,512]{2,1,0:T(8,128)(2,1)S(1)} %collective-permute-done.1.bufT_ref) | copy-start | bytes 393220
  20.0 16.2 %collective-permute-start.2 = (bf16[2,128,512]{2,1,0:T(8,128)(2,1)S(1)}, bf16[2,128,512]{2,1,0:T(8,128)(2,1)S(1)}, u32[]{:S(2)}, u32[]{:S(2)}) collective-permute-start(bf16[2,128,512]{2,1,0:T(8,128)(2,1)S(1)} %pad_maximum_fusion.1), channel_id=1, source_target_pairs={{0,496},{8,504},{16,0},{24,8},{32,16},{40,24},{48,32},{56,40},{64,... | collective-permute-start | bytes 786440 | tf_op jit(solution)/shard_map/ppermute | solution.py:15
  32.9 7.9 %copy-start.10 = (s32[4]{0:T(128)S(1)}, s32[4]{0:T(128)}, u32[]{:S(2)}) copy-start(s32[4]{0:T(128)} %constant.170) | copy-start | bytes 52
  36.3 0.7 copy-start.6
  37.0 15.7 %collective-permute-start.3 = (bf16[4,128,512]{2,1,0:T(8,128)(2,1)S(1)}, bf16[4,128,512]{2,1,0:T(8,128)(2,1)S(1)}, u32[]{:S(2)}, u32[]{:S(2)}) collective-permute-start(bf16[4,128,512]{2,1,0:T(8,128)(2,1)S(1)} %pad_maximum_fusion), channel_id=1, source_target_pairs={{0,504},{8,0},{16,8},{24,16},{32,24},{40,32},{48,40},{56,48},{64,5... | collective-permute-start | bytes 1572872 | tf_op jit(solution)/shard_map/ppermute | solution.py:15
  52.7 0.8 copy-start.12
  53.5 6.1 %copy-start.3 = (f32[4,128,128]{2,1,0:T(8,128)S(1)}, f32[4,128,128]{2,1,0:T(8,128)}, u32[]{:S(2)}) copy-start(f32[4,128,128]{2,1,0:T(8,128)} %shard_map.139) | copy-start | bytes 786436
  53.5 6.1 %copy-start.4 = (f32[4,128,128]{2,1,0:T(8,128)S(1)}, f32[4,128,128]{2,1,0:T(8,128)}, u32[]{:S(2)}) copy-start(f32[4,128,128]{2,1,0:T(8,128)} %shard_map.140) | copy-start | bytes 786436
  53.5 6.1 %copy-start.5 = (f32[4,128,128]{2,1,0:T(8,128)S(1)}, f32[4,128,128]{2,1,0:T(8,128)}, u32[]{:S(2)}) copy-start(f32[4,128,128]{2,1,0:T(8,128)} %shard_map.141) | copy-start | bytes 786436
  61.3 27.8 %all-to-all-start = ((f32[8,64,128]{2,1,0:T(8,128)}), f32[8,64,128]{2,1,0:T(8,128)S(1)}, u32[]{:S(2)}, u32[]{:S(2)}) async-start(f32[8,64,128]{2,1,0:T(8,128)} %bitcast.6), calls=%async_computation | async-start | bytes 524288 | tf_op jit(solution)/shard_map/all_to_all | solution.py:143
  89.2 0.8 copy-start.13
  89.2 0.8 copy-start.14
  91.0 5.8 %collective-permute-start.4 = (f32[136,256]{1,0:T(8,128)S(1)}, f32[136,256]{1,0:T(8,128)S(1)}, u32[]{:S(2)}, u32[]{:S(2)}) collective-permute-start(f32[136,256]{1,0:T(8,128)S(1)} %pad_maximum_fusion.2), channel_id=1, source_target_pairs={{0,1},{1,0},{2,3},{3,2},{4,5},{5,4},{6,7},{7,6},{8,9},{9,8},{10,11... | collective-permute-start | bytes 417800 | tf_op jit(solution)/shard_map/ppermute | solution.py:24
  96.8 5.8 %collective-permute-start.5 = (f32[136,256]{1,0:T(8,128)S(1)}, f32[136,256]{1,0:T(8,128)S(1)}, u32[]{:S(2)}, u32[]{:S(2)}) collective-permute-start(f32[136,256]{1,0:T(8,128)S(1)} %fusion.14), channel_id=1, source_target_pairs={{0,2},{1,3},{2,0},{3,1},{4,6},{5,7},{6,4},{7,5},{8,10},{9,11},{10,... | collective-permute-start | bytes 417800 | tf_op jit(solution)/shard_map/ppermute | solution.py:24
  102.7 7.3 %collective-permute-start.6 = (f32[136,256]{1,0:T(8,128)S(1)}, f32[136,256]{1,0:T(8,128)S(1)}, u32[]{:S(2)}, u32[]{:S(2)}) collective-permute-start(f32[136,256]{1,0:T(8,128)S(1)} %add.106), channel_id=1, source_target_pairs={{0,4},{1,5},{2,6},{3,7},{4,0},{5,1},{6,2},{7,3},{8,12},{9,13},{10,... | collective-permute-start | bytes 417800 | tf_op jit(solution)/shard_map/ppermute | solution.py:24
  110.0 7.6 %collective-permute-start.7 = (f32[136,256]{1,0:T(8,128)S(1)}, f32[136,256]{1,0:T(8,128)S(1)}, u32[]{:S(2)}, u32[]{:S(2)}) collective-permute-start(f32[136,256]{1,0:T(8,128)S(1)} %add.107), channel_id=1, source_target_pairs={{0,8},{8,0},{16,24},{24,16},{32,40},{40,32},{48,56},{56,48},{64,72... | collective-permute-start | bytes 417800 | tf_op jit(solution)/shard_map/ppermute | solution.py:24
  117.6 6.8 %collective-permute-start.8 = (f32[136,256]{1,0:T(8,128)S(1)}, f32[136,256]{1,0:T(8,128)S(1)}, u32[]{:S(2)}, u32[]{:S(2)}) collective-permute-start(f32[136,256]{1,0:T(8,128)S(1)} %add.108), channel_id=1, source_target_pairs={{0,64},{8,72},{16,80},{24,88},{32,96},{40,104},{48,112},{56,120},{... | collective-permute-start | bytes 417800 | tf_op jit(solution)/shard_map/ppermute | solution.py:24
  124.4 11.1 %collective-permute-start.9 = (f32[136,256]{1,0:T(8,128)S(1)}, f32[136,256]{1,0:T(8,128)S(1)}, u32[]{:S(2)}, u32[]{:S(2)}) collective-permute-start(f32[136,256]{1,0:T(8,128)S(1)} %add.109), channel_id=1, source_target_pairs={{0,16},{8,24},{16,0},{24,8},{32,48},{40,56},{48,32},{56,40},{64,80... | collective-permute-start | bytes 417800 | tf_op jit(solution)/shard_map/ppermute | solution.py:24
  135.5 12.7 %collective-permute-start.10 = (f32[136,256]{1,0:T(8,128)S(1)}, f32[136,256]{1,0:T(8,128)S(1)}, u32[]{:S(2)}, u32[]{:S(2)}) collective-permute-start(f32[136,256]{1,0:T(8,128)S(1)} %add.110), channel_id=1, source_target_pairs={{0,128},{8,136},{16,144},{24,152},{32,160},{40,168},{48,176},{56,1... | collective-permute-start | bytes 417800 | tf_op jit(solution)/shard_map/ppermute | solution.py:24
  148.2 13.6 %collective-permute-start.11 = (f32[136,256]{1,0:T(8,128)S(1)}, f32[136,256]{1,0:T(8,128)S(1)}, u32[]{:S(2)}, u32[]{:S(2)}) collective-permute-start(f32[136,256]{1,0:T(8,128)S(1)} %add.111), channel_id=1, source_target_pairs={{0,32},{8,40},{16,48},{24,56},{32,0},{40,8},{48,16},{56,24},{64,96... | collective-permute-start | bytes 417800 | tf_op jit(solution)/shard_map/ppermute | solution.py:24
  161.9 14.2 %collective-permute-start.12 = (f32[136,256]{1,0:T(8,128)S(1)}, f32[136,256]{1,0:T(8,128)S(1)}, u32[]{:S(2)}, u32[]{:S(2)}) collective-permute-start(f32[136,256]{1,0:T(8,128)S(1)} %add.112), channel_id=1, source_target_pairs={{0,256},{8,264},{16,272},{24,280},{32,288},{40,296},{48,304},{56,3... | collective-permute-start | bytes 417800 | tf_op jit(solution)/shard_map/ppermute | solution.py:24

commit v8 on v7

--- a/solution.py
+++ b/solution.py
@@ -5,8 +5,8 @@
 from jax.experimental.pallas import tpu as pltpu
 from jax.sharding import PartitionSpec as P
 
+
 ROWS_BITS = (0, 3, 1, 4, 2, 5)
-REP_BITS = (0, 1, 2)
 
 
 def from_behind(value, axis, steps):
@@ -23,22 +23,6 @@
         pairs = [(source, source ^ (1 << bit)) for source in range(count)]
         value = value + lax.ppermute(value, axis, pairs)
     return value
-
-
-def halving_scatter(value, axis):
-    count = lax.axis_size(axis)
-    me = lax.axis_index(axis)
-    levels = count.bit_length() - 1
-    share = value.shape[0] // count
-    buf = value.reshape((2,) * levels + (share,) + value.shape[1:])
-    for bit in range(levels):
-        dim = levels - 1 - bit
-        mine = (me >> bit) & 1
-        keep = lax.dynamic_index_in_dim(buf, mine, dim, keepdims=False)
-        send = lax.dynamic_index_in_dim(buf, 1 - mine, dim, keepdims=False)
-        pairs = [(source, source ^ (1 << bit)) for source in range(count)]
-        buf = keep + lax.ppermute(send, axis, pairs)
-    return buf
 
 
 def gelu_tanh(values):
@@ -86,27 +70,7 @@
     )(bufT, far, tgt)
 
 
-def tile_sums(buffer, offset, tile_block, edge_count, edge_code):
-    block_ids = lax.dynamic_index_in_dim(tile_block, offset, 1, keepdims=False)
-    live_count = lax.dynamic_index_in_dim(edge_count, offset, 1, keepdims=False)
-    codes = lax.dynamic_index_in_dim(edge_code, offset, 1, keepdims=False)
-    block_total, slot_count, edge_cap = codes.shape
-    feat_width = buffer.shape[1]
-    far_node = block_ids[:, :, None] * 128 + codes % 128
-    col_iota = lax.broadcasted_iota(jnp.int32, (1, 1, 1, buffer.shape[0]), 3)
-    onehot_col = (far_node[..., None] == col_iota).astype(jnp.bfloat16)
-    picked = jnp.einsum(
-        "bkec,cf->bkef", onehot_col, buffer, preferred_element_type=jnp.float32
-    ).astype(jnp.bfloat16)
-    is_live = lax.broadcasted_iota(jnp.int32, codes.shape, 2) < live_count[:, :, None]
-    target = jnp.where(is_live, codes // 128, -1)
-    row_iota = lax.broadcasted_iota(jnp.int32, (1, 1, 128, 1), 2)
-    onehot = (target[:, :, None, :] == row_iota).astype(jnp.bfloat16)
-    summed = jnp.einsum("bkre,bkef->brf", onehot, picked, preferred_element_type=jnp.float32)
-    return summed.reshape(block_total * 128, feat_width)
-
-
-def local(features, degree, tile_block, edge_count, edge_code, weight, bias, cotangent):
+def layer(features, degree, tile_block, edge_count, edge_code, weight, bias, cotangent):
     step_count = tile_block.shape[1]
     replicas = lax.axis_size("rep")
     replica = lax.axis_index("rep")
@@ -128,6 +92,8 @@
             target = (source - step_count * rep_index) % row_count
             pairs.append((source * replicas + rep_index, target * replicas + rep_index))
     held = lax.ppermute(scaled.T, ("rows", "rep"), pairs)[None]
+    cot_copies = jnp.broadcast_to(cotangent[None], (replicas,) + cotangent.shape)
+    cot_group = lax.all_to_all(cot_copies, "rep", 0, 0).reshape(-1, cotangent.shape[1])
     offsets = [0]
     partial_total = local_sums(held, offsets)
     stride = step_count
@@ -141,15 +107,13 @@
     partial_total = partial_total.reshape(-1, partial_total.shape[-1])
     pieces = partial_total.reshape((replicas, -1) + partial_total.shape[1:])
     pieces = lax.all_to_all(pieces, "rep", 0, 0)
-    edge_sums = jnp.sum(pieces, axis=0)
-    share_rows = edge_sums.shape[0]
-    share_start = replica * share_rows
-    own_rows = lax.dynamic_slice_in_dim(scaled, share_start, share_rows, 0).astype(jnp.float32)
-    own_inv = lax.dynamic_slice_in_dim(inv_deg, share_start, share_rows, 0)
-    aggregate = (own_inv[:, None] * (edge_sums + own_rows)).astype(jnp.bfloat16)
+    share = jnp.sum(pieces, axis=0)
+    copies = jnp.broadcast_to(share[None], (replicas,) + share.shape)
+    edge_sums = lax.all_to_all(copies, "rep", 0, 0).reshape(partial_total.shape)
+    aggregate = (inv_deg[:, None] * (edge_sums + scaled.astype(jnp.float32))).astype(jnp.bfloat16)
     pre_act = jnp.dot(aggregate, weight, preferred_element_type=jnp.float32) + bias
     activated, pull_back = jax.vjp(gelu_tanh, pre_act)
-    delta_bf = pull_back(cotangent.astype(jnp.float32))[0].astype(jnp.bfloat16)
+    delta_bf = pull_back(cot_group.astype(jnp.float32))[0].astype(jnp.bfloat16)
     local_weight = lax.dot_general(
         aggregate, delta_bf, (((0,), (0,)), ((), ())), preferred_element_type=jnp.float32
     )
@@ -158,11 +122,12 @@
     packed = jnp.concatenate(
         [local_weight, jnp.broadcast_to(local_bias[None, :], (8, local_bias.shape[0]))], axis=0
     )
-    packed = butterfly_sum(packed, "rep", REP_BITS)
     packed = butterfly_sum(packed, "rows", ROWS_BITS)
     grad_weight = packed[:feat_rows]
     grad_bias = packed[feat_rows]
-    return (activated.astype(jnp.bfloat16), grad_weight, grad_bias)
+    share_rows = cotangent.shape[0]
+    own_act = lax.dynamic_slice_in_dim(activated, replica * share_rows, share_rows, 0)
+    return (own_act.astype(jnp.bfloat16), grad_weight, grad_bias)
 
 
 def solution(mesh):
@@ -177,4 +142,4 @@
         P(("rows", "rep"), None),
     )
     out_specs = (P(("rows", "rep"), None), P(), P())
-    return jax.shard_map(local, mesh=mesh, in_specs=in_specs, out_specs=out_specs, check_vma=False)
+    return jax.shard_map(layer, mesh=mesh, in_specs=in_specs, out_specs=out_specs, check_vma=False)

time: 178 us -> 174 us (0.978)
  blocking collectives: 0 us -> 36.2 us
  starting transfers between devices: 86 us -> 59.6 us
  waiting for transfers between devices: 61.6 us -> 48.7 us
    all_to_all x0 -> x2, blocking collectives: none -> 36.2 us  [the longest x1 27.7 us: layer(): pieces = lax.all_to_all(pieces, 'rep', 0, 0)]
    all_to_all x1, starting transfers between devices: 20.9 us -> 3.41 us  [layer(): lax.all_to_all(cot_copies, 'rep', 0, 0).reshape(-1, cotangent.shape[1])]
    ppermute x9 -> x6, waiting for transfers between devices: 49.9 us -> 37.9 us  [butterfly_sum(): value = value + lax.ppermute(value, axis, pairs)]
    ppermute x9 -> x6, starting transfers between devices: 35 us -> 26 us  [butterfly_sum(): value = value + lax.ppermute(value, axis, pairs)]
  transfers between devices with their start and end apart: 14 -> 11, of which waited for: 12 -> 9; matrix products, arithmetic and copies ran while one was open for 2% -> 3% of each run, Pallas kernels for 6% -> 6%
where the time goes in v8:
time: 174 us; the launch traced here: 173 us
  starting transfers between devices  59.6 us (34%)
  waiting for transfers between devices  48.7 us (28%)
  blocking collectives  36.2 us (21%)
  Pallas kernels  16 us (9%)
  local copies, waits for them, and re-layouts  8.79 us (5%)
  other arithmetic  2.1 us (1%)
    ppermute x6, waiting for transfers between devices, butterfly_sum(): value = value + lax.ppermute(value, axis, pairs)  37.9 us
    ppermute x3, starting transfers between devices, from_behind(): return lax.ppermute(value, axis, pairs)  29.4 us
    all_to_all x1, blocking collectives, layer(): pieces = lax.all_to_all(pieces, 'rep', 0, 0)  27.7 us
    ppermute x6, starting transfers between devices, butterfly_sum(): value = value + lax.ppermute(value, axis, pairs)  26 us
    pallas_call x4, Pallas kernels, edge_sums_kernel(): pl.pallas_call(_edge_kernel, out_shape=jax.ShapeDtypeStruct((blocks, rows...  16 us
    all_to_all x1, blocking collectives, layer(): edge_sums = lax.all_to_all(copies, 'rep', 0, 0).reshape(partial_total.shape)  8.59 us
    all_to_all x1, waiting for transfers between devices, layer(): lax.all_to_all(cot_copies, 'rep', 0, 0).reshape(-1, cotangent.shape[1])  5.87 us
    ppermute x3, waiting for transfers between devices, from_behind(): return lax.ppermute(value, axis, pairs)  4.88 us
  transfers between devices with their start and end apart: 11, of which 9 were waited for; matrix products, arithmetic and copies ran while one was open for 3% of the time, Pallas kernels for 6%

profile of v8, /device:TPU:1, one launch (start us, length us, event | category | flops | bytes accessed | tf_op | source)
XLA Modules:
  0.0 173.3 jit_solution(5698303104729517720)
XLA Ops:
  0.6 0.0 copy-start
  0.7 1.0 copy.16
  1.8 0.8 collective-permute-start
  2.6 0.0 copy-done.7
  2.7 0.1 fusion.11
  2.8 14.4 %collective-permute-start.1 = (bf16[1,128,512]{2,1,0:T(8,128)(2,1)S(1)}, bf16[1,128,512]{2,1,0:T(8,128)(2,1)S(1)}, u32[]{:S(2)}, u32[]{:S(2)}) collective-permute-start(bf16[1,128,512]{2,1,0:T(8,128)(2,1)S(1)} %bitcast.24), channel_id=1, source_target_pairs={{0,480},{8,488},{16,496},{24,504},{32,0},{40,8},{48,16},{56,24},{6... | collective-permute-start | bytes 393224 | tf_op jit(solution)/shard_map/ppermute | solution.py:15
  17.2 0.6 fusion.18
  17.8 1.5 collective-permute-done.1.bufT_ref
  19.4 11.1 %collective-permute-start.2 = (bf16[2,128,512]{2,1,0:T(8,128)(2,1)S(1)}, bf16[2,128,512]{2,1,0:T(8,128)(2,1)S(1)}, u32[]{:S(2)}, u32[]{:S(2)}) collective-permute-start(bf16[2,128,512]{2,1,0:T(8,128)(2,1)S(1)} %pad_maximum_fusion.1), channel_id=1, source_target_pairs={{0,496},{8,504},{16,0},{24,8},{32,16},{40,24},{48,32},{56,40},{64,... | collective-permute-start | bytes 786440 | tf_op jit(solution)/shard_map/ppermute | solution.py:15
  30.5 0.6 gather_fusion
  31.1 0.6 gather_fusion.1
  31.7 0.6 copy_bitcast_fusion.2
  32.3 3.3 %collective-permute-done.2.bufT_ref = bf16[2,128,512]{2,1,0:T(8,128)(2,1)S(1)} collective-permute-done((bf16[2,128,512]{2,1,0:T(8,128)(2,1)S(1)}, bf16[2,128,512]{2,1,0:T(8,128)(2,1)S(1)}, u32[]{:S(2)}, u32[]{:S(2)}) %collective-permute-start.2) | collective-permute-done | bytes 262176 | tf_op jit(solution)/shard_map/ppermute | solution.py:15
  35.6 0.1 pad_maximum_fusion
  35.7 0.6 copy-done.6
  36.3 3.9 %collective-permute-start.3 = (bf16[4,128,512]{2,1,0:T(8,128)(2,1)S(1)}, bf16[4,128,512]{2,1,0:T(8,128)(2,1)S(1)}, u32[]{:S(2)}, u32[]{:S(2)}) collective-permute-start(bf16[4,128,512]{2,1,0:T(8,128)(2,1)S(1)} %pad_maximum_fusion), channel_id=1, source_target_pairs={{0,504},{8,0},{16,8},{24,16},{32,24},{40,32},{48,40},{56,48},{64,5... | collective-permute-start | bytes 1572872 | tf_op jit(solution)/shard_map/ppermute | solution.py:15
  40.2 0.6 gather_fusion.2
  40.8 0.6 gather_fusion.3
  41.4 0.7 copy_bitcast_fusion
  42.0 3.0 %shard_map.139 = f32[4,128,128]{2,1,0:T(8,128)} custom-call(bf16[1,128,512]{2,1,0:T(8,128)(2,1)} %bitcast.27, s32[4,1,8,128]{3,2,1,0:T(8,128)} %get-tuple-element.57.far_ref, s32[4,1,8,128]{3,2,1,0:T(8,128)} %get-tuple-element.51.tgt_ref), custom_call_target="tpu_custom_call" | custom-call | flops 671088640 | bytes 425984 | tf_op jit(solution)/shard_map/pallas_call | solution.py:61
  45.0 3.0 %shard_map.140 = f32[4,128,128]{2,1,0:T(8,128)} custom-call(bf16[1,128,512]{2,1,0:T(8,128)(2,1)} %copy-done.2, s32[4,1,8,128]{3,2,1,0:T(8,128)} %get-tuple-element.58.far_ref, s32[4,1,8,128]{3,2,1,0:T(8,128)} %get-tuple-element.50.tgt_ref), custom_call_target="tpu_custom_call" | custom-call | flops 671088640 | bytes 425984 | tf_op jit(solution)/shard_map/pallas_call | solution.py:61
  47.9 4.0 %shard_map.141 = f32[4,128,128]{2,1,0:T(8,128)} custom-call(bf16[2,128,512]{2,1,0:T(8,128)(2,1)} %copy-done.6, s32[4,2,8,128]{3,2,1,0:T(8,128)} %get-tuple-element.62.far_ref, s32[4,2,8,128]{3,2,1,0:T(8,128)} %get-tuple-element.61.tgt_ref), custom_call_target="tpu_custom_call" | custom-call | flops 1342177280 | bytes 589824 | tf_op jit(solution)/shard_map/pallas_call | solution.py:61
  52.0 0.8 copy-done.14
  52.8 6.1 %shard_map.142 = f32[4,128,128]{2,1,0:T(8,128)} custom-call(bf16[4,128,512]{2,1,0:T(8,128)(2,1)} %copy-done.14, s32[4,4,8,128]{3,2,1,0:T(8,128)} %get-tuple-element.60.far_ref, s32[4,4,8,128]{3,2,1,0:T(8,128)} %get-tuple-element.59.tgt_ref), custom_call_target="tpu_custom_call" | custom-call | flops 2684354560 | bytes 917504 | tf_op jit(solution)/shard_map/pallas_call | solution.py:61
  58.9 1.0 add_add_fusion
  59.9 27.7 %all_to_all.15 = f32[8,64,128]{2,1,0:T(8,128)S(1)} all-to-all(f32[8,64,128]{2,1,0:T(8,128)S(1)} %bitcast.22), channel_id=1, replica_groups=mesh['rows'=64,'rep'=8] {'rep'}, dimensions={0} | all-to-all | bytes 524288 | tf_op jit(solution)/shard_map/all_to_all | solution.py:109
  87.6 8.6 %all_to_all.16 = f32[8,64,128]{2,1,0:T(8,128)S(1)} all-to-all(f32[8,64,128]{2,1,0:T(8,128)S(1)} %broadcast_in_dim.23), channel_id=1, replica_groups=mesh['rows'=64,'rep'=8] {'rep'}, dimensions={0} | all-to-all | bytes 524288 | tf_op jit(solution)/shard_map/all_to_all | solution.py:112
  96.2 0.7 broadcast_in_dim.24
  96.9 3.4 %all-to-all-start.2 = ((bf16[8,64,256]{2,1,0:T(8,128)(2,1)}), bf16[8,64,256]{2,1,0:T(8,128)(2,1)S(1)}, u32[]{:S(2)}, u32[]{:S(2)}) async-start(bf16[8,64,256]{2,1,0:T(8,128)(2,1)} %broadcast_in_dim.24), calls=%async_computation.2 | async-start | bytes 524288 | tf_op jit(solution)/shard_map/all_to_all | solution.py:96
  100.3 0.1 copy.21
  100.5 5.9 %all-to-all-done.2 = bf16[8,64,256]{2,1,0:T(8,128)(2,1)S(1)} async-done(((bf16[8,64,256]{2,1,0:T(8,128)(2,1)}), bf16[8,64,256]{2,1,0:T(8,128)(2,1)S(1)}, u32[]{:S(2)}, u32[]{:S(2)}) %all-to-all-start.2) | async-done | bytes 262176 | tf_op jit(solution)/shard_map/all_to_all | solution.py:96
  106.4 0.6 convert_reduce_fusion
  107.0 0.2 fusion.20
  107.2 5.5 %collective-permute-start.4 = (f32[136,256]{1,0:T(8,128)S(1)}, f32[136,256]{1,0:T(8,128)S(1)}, u32[]{:S(2)}, u32[]{:S(2)}) collective-permute-start(f32[136,256]{1,0:T(8,128)S(1)} %pad_maximum_fusion.2), channel_id=1, source_target_pairs={{0,8},{8,0},{16,24},{24,16},{32,40},{40,32},{48,56},{56,48},{64,72... | collective-permute-start | bytes 417800 | tf_op jit(solution)/shard_map/ppermute | solution.py:24
  112.8 1.0 collective-permute-done.4
  113.8 2.2 %collective-permute-start.5 = (f32[136,256]{1,0:T(8,128)S(1)}, f32[136,256]{1,0:T(8,128)S(1)}, u32[]{:S(2)}, u32[]{:S(2)}) collective-permute-start(f32[136,256]{1,0:T(8,128)S(1)} %fusion.16), channel_id=1, source_target_pairs={{0,64},{8,72},{16,80},{24,88},{32,96},{40,104},{48,112},{56,120},{... | collective-permute-start | bytes 417800 | tf_op jit(solution)/shard_map/ppermute | solution.py:24
  116.0 4.6 %collective-permute-done.5 = f32[136,256]{1,0:T(8,128)S(1)} collective-permute-done((f32[136,256]{1,0:T(8,128)S(1)}, f32[136,256]{1,0:T(8,128)S(1)}, u32[]{:S(2)}, u32[]{:S(2)}) %collective-permute-start.5) | collective-permute-done | bytes 139296 | tf_op jit(solution)/shard_map/ppermute | solution.py:24
  120.6 2.7 %collective-permute-start.6 = (f32[136,256]{1,0:T(8,128)S(1)}, f32[136,256]{1,0:T(8,128)S(1)}, u32[]{:S(2)}, u32[]{:S(2)}) collective-permute-start(f32[136,256]{1,0:T(8,128)S(1)} %add.96), channel_id=1, source_target_pairs={{0,16},{8,24},{16,0},{24,8},{32,48},{40,56},{48,32},{56,40},{64,80... | collective-permute-start | bytes 417800 | tf_op jit(solution)/shard_map/ppermute | solution.py:24
  123.3 8.4 %collective-permute-done.6 = f32[136,256]{1,0:T(8,128)S(1)} collective-permute-done((f32[136,256]{1,0:T(8,128)S(1)}, f32[136,256]{1,0:T(8,128)S(1)}, u32[]{:S(2)}, u32[]{:S(2)}) %collective-permute-start.6) | collective-permute-done | bytes 139296 | tf_op jit(solution)/shard_map/ppermute | solution.py:24
  131.7 5.5 %collective-permute-start.7 = (f32[136,256]{1,0:T(8,128)S(1)}, f32[136,256]{1,0:T(8,128)S(1)}, u32[]{:S(2)}, u32[]{:S(2)}) collective-permute-start(f32[136,256]{1,0:T(8,128)S(1)} %add.97), channel_id=1, source_target_pairs={{0,128},{8,136},{16,144},{24,152},{32,160},{40,168},{48,176},{56,1... | collective-permute-start | bytes 417800 | tf_op jit(solution)/shard_map/ppermute | solution.py:24
  137.2 6.7 %collective-permute-done.7 = f32[136,256]{1,0:T(8,128)S(1)} collective-permute-done((f32[136,256]{1,0:T(8,128)S(1)}, f32[136,256]{1,0:T(8,128)S(1)}, u32[]{:S(2)}, u32[]{:S(2)}) %collective-permute-start.7) | collective-permute-done | bytes 139296 | tf_op jit(solution)/shard_map/ppermute | solution.py:24
  143.9 4.7 %collective-permute-start.8 = (f32[136,256]{1,0:T(8,128)S(1)}, f32[136,256]{1,0:T(8,128)S(1)}, u32[]{:S(2)}, u32[]{:S(2)}) collective-permute-start(f32[136,256]{1,0:T(8,128)S(1)} %add.98), channel_id=1, source_target_pairs={{0,32},{8,40},{16,48},{24,56},{32,0},{40,8},{48,16},{56,24},{64,96... | collective-permute-start | bytes 417800 | tf_op jit(solution)/shard_map/ppermute | solution.py:24
  148.6 9.4 %collective-permute-done.8 = f32[136,256]{1,0:T(8,128)S(1)} collective-permute-done((f32[136,256]{1,0:T(8,128)S(1)}, f32[136,256]{1,0:T(8,128)S(1)}, u32[]{:S(2)}, u32[]{:S(2)}) %collective-permute-start.8) | collective-permute-done | bytes 139296 | tf_op jit(solution)/shard_map/ppermute | solution.py:24
  158.0 5.4 %collective-permute-start.9 = (f32[136,256]{1,0:T(8,128)S(1)}, f32[136,256]{1,0:T(8,128)S(1)}, u32[]{:S(2)}, u32[]{:S(2)}) collective-permute-start(f32[136,256]{1,0:T(8,128)S(1)} %add.99), channel_id=1, source_target_pairs={{0,256},{8,264},{16,272},{24,280},{32,288},{40,296},{48,304},{56,3... | collective-permute-start | bytes 417800 | tf_op jit(solution)/shard_map/ppermute | solution.py:24
  163.4 0.6 fusion.15
  164.1 7.9 %collective-permute-done.9 = f32[136,256]{1,0:T(8,128)S(1)} collective-permute-done((f32[136,256]{1,0:T(8,128)S(1)}, f32[136,256]{1,0:T(8,128)S(1)}, u32[]{:S(2)}, u32[]{:S(2)}) %collective-permute-start.9) | collective-permute-done | bytes 139296 | tf_op jit(solution)/shard_map/ppermute | solution.py:24
  172.0 0.7 slice.68
  172.7 0.6 slice.69
  (47 shorter events, 0.4 us)
Async XLA Ops:
  0.6 105.8 %copy-start = (bf16[128,256]{1,0:T(8,128)(2,1)S(1)}, bf16[128,256]{1,0:T(8,128)(2,1)}, u32[]{:S(2)}) copy-start(bf16[128,256]{1,0:T(8,128)(2,1)} %param.17) | copy-start | bytes 196612
  0.6 1.1 copy-start.11
  1.7 0.9 copy-start.9
  1.7 0.9 copy-start.7
  1.8 0.9 copy-start.10
  1.8 1.0 collective-permute-start
  2.8 32.8 %copy-start.1 = (bf16[128,512]{1,0:T(8,128)(2,1)}, bf16[128,512]{1,0:T(8,128)(2,1)S(1)}, u32[]{:S(2)}) copy-start(bf16[128,512]{1,0:T(8,128)(2,1)S(1)} %collective-permute-done) | copy-start | bytes 393220
  2.8 16.5 %collective-permute-start.1 = (bf16[1,128,512]{2,1,0:T(8,128)(2,1)S(1)}, bf16[1,128,512]{2,1,0:T(8,128)(2,1)S(1)}, u32[]{:S(2)}, u32[]{:S(2)}) collective-permute-start(bf16[1,128,512]{2,1,0:T(8,128)(2,1)S(1)} %bitcast.24), channel_id=1, source_target_pairs={{0,480},{8,488},{16,496},{24,504},{32,0},{40,8},{48,16},{56,24},{6... | collective-permute-start | bytes 393224 | tf_op jit(solution)/shard_map/ppermute | solution.py:15
  17.8 12.7 %copy-start.13 = (s32[2]{0:T(128)S(1)}, s32[2]{0:T(128)}, u32[]{:S(2)}) copy-start(s32[2]{0:T(128)} %constant.168) | copy-start | bytes 28
  19.3 16.3 %copy-start.2 = (bf16[1,128,512]{2,1,0:T(8,128)(2,1)}, bf16[1,128,512]{2,1,0:T(8,128)(2,1)S(1)}, u32[]{:S(2)}) copy-start(bf16[1,128,512]{2,1,0:T(8,128)(2,1)S(1)} %collective-permute-done.1.bufT_ref) | copy-start | bytes 393220
  19.4 16.2 %collective-permute-start.2 = (bf16[2,128,512]{2,1,0:T(8,128)(2,1)S(1)}, bf16[2,128,512]{2,1,0:T(8,128)(2,1)S(1)}, u32[]{:S(2)}, u32[]{:S(2)}) collective-permute-start(bf16[2,128,512]{2,1,0:T(8,128)(2,1)S(1)} %pad_maximum_fusion.1), channel_id=1, source_target_pairs={{0,496},{8,504},{16,0},{24,8},{32,16},{40,24},{48,32},{56,40},{64,... | collective-permute-start | bytes 786440 | tf_op jit(solution)/shard_map/ppermute | solution.py:15
  32.3 7.9 %copy-start.12 = (s32[4]{0:T(128)S(1)}, s32[4]{0:T(128)}, u32[]{:S(2)}) copy-start(s32[4]{0:T(128)} %constant.170) | copy-start | bytes 52
  35.6 0.7 copy-start.6
  36.3 15.7 %collective-permute-start.3 = (bf16[4,128,512]{2,1,0:T(8,128)(2,1)S(1)}, bf16[4,128,512]{2,1,0:T(8,128)(2,1)S(1)}, u32[]{:S(2)}, u32[]{:S(2)}) collective-permute-start(bf16[4,128,512]{2,1,0:T(8,128)(2,1)S(1)} %pad_maximum_fusion), channel_id=1, source_target_pairs={{0,504},{8,0},{16,8},{24,16},{32,24},{40,32},{48,40},{56,48},{64,5... | collective-permute-start | bytes 1572872 | tf_op jit(solution)/shard_map/ppermute | solution.py:15
  52.0 0.8 copy-start.14
  52.8 6.1 %copy-start.3 = (f32[4,128,128]{2,1,0:T(8,128)S(1)}, f32[4,128,128]{2,1,0:T(8,128)}, u32[]{:S(2)}) copy-start(f32[4,128,128]{2,1,0:T(8,128)} %shard_map.139) | copy-start | bytes 786436
  52.8 6.1 %copy-start.4 = (f32[4,128,128]{2,1,0:T(8,128)S(1)}, f32[4,128,128]{2,1,0:T(8,128)}, u32[]{:S(2)}) copy-start(f32[4,128,128]{2,1,0:T(8,128)} %shard_map.140) | copy-start | bytes 786436
  52.8 6.1 %copy-start.5 = (f32[4,128,128]{2,1,0:T(8,128)S(1)}, f32[4,128,128]{2,1,0:T(8,128)}, u32[]{:S(2)}) copy-start(f32[4,128,128]{2,1,0:T(8,128)} %shard_map.141) | copy-start | bytes 786436
  87.6 8.6 %copy-start.8 = (bf16[64,256]{1,0:T(8,128)(2,1)S(1)}, bf16[64,256]{1,0:T(8,128)(2,1)}, u32[]{:S(2)}) copy-start(bf16[64,256]{1,0:T(8,128)(2,1)} %param.19) | copy-start | bytes 98308
  96.9 9.5 %all-to-all-start.2 = ((bf16[8,64,256]{2,1,0:T(8,128)(2,1)}), bf16[8,64,256]{2,1,0:T(8,128)(2,1)S(1)}, u32[]{:S(2)}, u32[]{:S(2)}) async-start(bf16[8,64,256]{2,1,0:T(8,128)(2,1)} %broadcast_in_dim.24), calls=%async_computation.2 | async-start | bytes 524288 | tf_op jit(solution)/shard_map/all_to_all | solution.py:96
  100.5 5.9 %copy-start.15 = (f32[256]{0:T(256)S(1)}, f32[256]{0:T(256)}, u32[]{:S(2)}) copy-start(f32[256]{0:T(256)} %param.18) | copy-start | bytes 3076
  107.2 6.5 %collective-permute-start.4 = (f32[136,256]{1,0:T(8,128)S(1)}, f32[136,256]{1,0:T(8,128)S(1)}, u32[]{:S(2)}, u32[]{:S(2)}) collective-permute-start(f32[136,256]{1,0:T(8,128)S(1)} %pad_maximum_fusion.2), channel_id=1, source_target_pairs={{0,8},{8,0},{16,24},{24,16},{32,40},{40,32},{48,56},{56,48},{64,72... | collective-permute-start | bytes 417800 | tf_op jit(solution)/shard_map/ppermute | solution.py:24
  113.8 6.8 %collective-permute-start.5 = (f32[136,256]{1,0:T(8,128)S(1)}, f32[136,256]{1,0:T(8,128)S(1)}, u32[]{:S(2)}, u32[]{:S(2)}) collective-permute-start(f32[136,256]{1,0:T(8,128)S(1)} %fusion.16), channel_id=1, source_target_pairs={{0,64},{8,72},{16,80},{24,88},{32,96},{40,104},{48,112},{56,120},{... | collective-permute-start | bytes 417800 | tf_op jit(solution)/shard_map/ppermute | solution.py:24
  120.6 11.1 %collective-permute-start.6 = (f32[136,256]{1,0:T(8,128)S(1)}, f32[136,256]{1,0:T(8,128)S(1)}, u32[]{:S(2)}, u32[]{:S(2)}) collective-permute-start(f32[136,256]{1,0:T(8,128)S(1)} %add.96), channel_id=1, source_target_pairs={{0,16},{8,24},{16,0},{24,8},{32,48},{40,56},{48,32},{56,40},{64,80... | collective-permute-start | bytes 417800 | tf_op jit(solution)/shard_map/ppermute | solution.py:24
  131.7 12.2 %collective-permute-start.7 = (f32[136,256]{1,0:T(8,128)S(1)}, f32[136,256]{1,0:T(8,128)S(1)}, u32[]{:S(2)}, u32[]{:S(2)}) collective-permute-start(f32[136,256]{1,0:T(8,128)S(1)} %add.97), channel_id=1, source_target_pairs={{0,128},{8,136},{16,144},{24,152},{32,160},{40,168},{48,176},{56,1... | collective-permute-start | bytes 417800 | tf_op jit(solution)/shard_map/ppermute | solution.py:24
  143.9 14.1 %collective-permute-start.8 = (f32[136,256]{1,0:T(8,128)S(1)}, f32[136,256]{1,0:T(8,128)S(1)}, u32[]{:S(2)}, u32[]{:S(2)}) collective-permute-start(f32[136,256]{1,0:T(8,128)S(1)} %add.98), channel_id=1, source_target_pairs={{0,32},{8,40},{16,48},{24,56},{32,0},{40,8},{48,16},{56,24},{64,96... | collective-permute-start | bytes 417800 | tf_op jit(solution)/shard_map/ppermute | solution.py:24
  158.0 14.0 %collective-permute-start.9 = (f32[136,256]{1,0:T(8,128)S(1)}, f32[136,256]{1,0:T(8,128)S(1)}, u32[]{:S(2)}, u32[]{:S(2)}) collective-permute-start(f32[136,256]{1,0:T(8,128)S(1)} %add.99), channel_id=1, source_target_pairs={{0,256},{8,264},{16,272},{24,280},{32,288},{40,296},{48,304},{56,3... | collective-permute-start | bytes 417800 | tf_op jit(solution)/shard_map/ppermute | solution.py:24

commit v9 on v8

--- a/solution.py
+++ b/solution.py
@@ -6,22 +6,37 @@
 from jax.sharding import PartitionSpec as P
 
 
-ROWS_BITS = (0, 3, 1, 4, 2, 5)
-
-
 def from_behind(value, axis, steps):
     count = lax.axis_size(axis)
     pairs = [(source, (source + steps) % count) for source in range(count)]
     return lax.ppermute(value, axis, pairs)
 
 
-def butterfly_sum(value, axis, order):
+def quad_sum(value, axis, bit_pairs):
     count = lax.axis_size(axis)
-    for bit in order:
-        if (1 << bit) >= count:
-            continue
-        pairs = [(source, source ^ (1 << bit)) for source in range(count)]
-        value = value + lax.ppermute(value, axis, pairs)
+    me = lax.axis_index(axis)
+    for low, high in bit_pairs:
+        masks = (1 << low, 1 << high, (1 << low) | (1 << high))
+        got = {0: value}
+        for mask in masks:
+            pairs = [(source, source ^ mask) for source in range(count)]
+            got[mask] = lax.ppermute(value, axis, pairs)
+        lo_bit = (me >> low) & 1
+        hi_bit = (me >> high) & 1
+        terms = {}
+        for mask, term in got.items():
+            slot_lo = lo_bit ^ ((mask >> low) & 1)
+            slot_hi = hi_bit ^ ((mask >> high) & 1)
+            terms[mask] = (slot_lo, slot_hi, term)
+        ordered = [None] * 4
+        for position in range(4):
+            want_lo, want_hi = position & 1, position >> 1
+            pick = None
+            for slot_lo, slot_hi, term in terms.values():
+                hit = (slot_lo == want_lo) & (slot_hi == want_hi)
+                pick = term if pick is None else jnp.where(hit, term, pick)
+            ordered[position] = pick
+        value = (ordered[0] + ordered[1]) + (ordered[2] + ordered[3])
     return value
 
 
@@ -122,7 +137,7 @@
     packed = jnp.concatenate(
         [local_weight, jnp.broadcast_to(local_bias[None, :], (8, local_bias.shape[0]))], axis=0
     )
-    packed = butterfly_sum(packed, "rows", ROWS_BITS)
+    packed = quad_sum(packed, "rows", ((0, 3), (1, 4), (2, 5)))
     grad_weight = packed[:feat_rows]
     grad_bias = packed[feat_rows]
     share_rows = cotangent.shape[0]

time: 174 us -> 172 us (0.989)
  the two profiles are of different devices: /device:TPU:1 before, /device:TPU:25 now
where the time goes in v9:
time: 172 us; the launch traced here: 171 us
  starting transfers between devices  64.1 us (37%)
  waiting for transfers between devices  41.8 us (24%)
  blocking collectives  36.5 us (21%)
  Pallas kernels  16.1 us (9%)
  local copies, waits for them, and re-layouts  8.87 us (5%)
  other arithmetic  2.21 us (1%)
    ppermute x9, starting transfers between devices, quad_sum(): got[mask] = lax.ppermute(value, axis, pairs)  37.4 us
    all_to_all x1, blocking collectives, layer(): pieces = lax.all_to_all(pieces, 'rep', 0, 0)  27.9 us
    ppermute x9, waiting for transfers between devices, quad_sum(): got[mask] = lax.ppermute(value, axis, pairs)  24.9 us
    ppermute x3, starting transfers between devices, from_behind(): return lax.ppermute(value, axis, pairs)  22.4 us
    pallas_call x4, Pallas kernels, edge_sums_kernel(): pl.pallas_call(_edge_kernel, out_shape=jax.ShapeDtypeStruct((blocks, rows...  16.1 us
    ppermute x3, waiting for transfers between devices, from_behind(): return lax.ppermute(value, axis, pairs)  11.1 us
    all_to_all x1, blocking collectives, layer(): edge_sums = lax.all_to_all(copies, 'rep', 0, 0).reshape(partial_total.shape)  8.56 us
    all_to_all x1, waiting for transfers between devices, layer(): lax.all_to_all(cot_copies, 'rep', 0, 0).reshape(-1, cotangent.shape[1])  5.87 us
  transfers between devices with their start and end apart: 14, of which 9 were waited for; matrix products, arithmetic and copies ran while one was open for 3% of the time, Pallas kernels for 6%

profile of v9, /device:TPU:25, one launch (start us, length us, event | category | flops | bytes accessed | tf_op | source)
XLA Modules:
  0.0 171.5 jit_solution(7920391414382560937)
XLA Ops:
  0.7 1.0 copy.16
  1.8 0.8 collective-permute-start
  2.7 0.1 fusion.11
  2.8 10.5 %collective-permute-start.1 = (bf16[1,128,512]{2,1,0:T(8,128)(2,1)S(1)}, bf16[1,128,512]{2,1,0:T(8,128)(2,1)S(1)}, u32[]{:S(2)}, u32[]{:S(2)}) collective-permute-start(bf16[1,128,512]{2,1,0:T(8,128)(2,1)S(1)} %bitcast.24), channel_id=1, source_target_pairs={{0,480},{8,488},{16,496},{24,504},{32,0},{40,8},{48,16},{56,24},{6... | collective-permute-start | bytes 393224 | tf_op jit(solution)/shard_map/ppermute | solution.py:12
  13.3 0.6 fusion.17
  14.0 2.7 %collective-permute-done.1.bufT_ref = bf16[1,128,512]{2,1,0:T(8,128)(2,1)S(1)} collective-permute-done((bf16[1,128,512]{2,1,0:T(8,128)(2,1)S(1)}, bf16[1,128,512]{2,1,0:T(8,128)(2,1)S(1)}, u32[]{:S(2)}, u32[]{:S(2)}) %collective-permute-start.1) | collective-permute-done | bytes 131104 | tf_op jit(solution)/shard_map/ppermute | solution.py:12
  16.7 9.5 %collective-permute-start.2 = (bf16[2,128,512]{2,1,0:T(8,128)(2,1)S(1)}, bf16[2,128,512]{2,1,0:T(8,128)(2,1)S(1)}, u32[]{:S(2)}, u32[]{:S(2)}) collective-permute-start(bf16[2,128,512]{2,1,0:T(8,128)(2,1)S(1)} %pad_maximum_fusion.1), channel_id=1, source_target_pairs={{0,496},{8,504},{16,0},{24,8},{32,16},{40,24},{48,32},{56,40},{64,... | collective-permute-start | bytes 786440 | tf_op jit(solution)/shard_map/ppermute | solution.py:12
  26.2 0.6 gather_fusion
  26.8 0.6 gather_fusion.1
  27.4 0.6 copy_bitcast_fusion.2
  28.0 8.4 %collective-permute-done.2.bufT_ref = bf16[2,128,512]{2,1,0:T(8,128)(2,1)S(1)} collective-permute-done((bf16[2,128,512]{2,1,0:T(8,128)(2,1)S(1)}, bf16[2,128,512]{2,1,0:T(8,128)(2,1)S(1)}, u32[]{:S(2)}, u32[]{:S(2)}) %collective-permute-start.2) | collective-permute-done | bytes 262176 | tf_op jit(solution)/shard_map/ppermute | solution.py:12
  36.5 0.6 copy-done.6
  37.1 2.4 %collective-permute-start.3 = (bf16[4,128,512]{2,1,0:T(8,128)(2,1)S(1)}, bf16[4,128,512]{2,1,0:T(8,128)(2,1)S(1)}, u32[]{:S(2)}, u32[]{:S(2)}) collective-permute-start(bf16[4,128,512]{2,1,0:T(8,128)(2,1)S(1)} %pad_maximum_fusion), channel_id=1, source_target_pairs={{0,504},{8,0},{16,8},{24,16},{32,24},{40,32},{48,40},{56,48},{64,5... | collective-permute-start | bytes 1572872 | tf_op jit(solution)/shard_map/ppermute | solution.py:12
  39.5 0.6 gather_fusion.2
  40.1 0.6 gather_fusion.3
  40.7 0.7 copy_bitcast_fusion
  41.3 3.0 %shard_map.139 = f32[4,128,128]{2,1,0:T(8,128)} custom-call(bf16[1,128,512]{2,1,0:T(8,128)(2,1)} %bitcast.27, s32[4,1,8,128]{3,2,1,0:T(8,128)} %get-tuple-element.57.far_ref, s32[4,1,8,128]{3,2,1,0:T(8,128)} %get-tuple-element.51.tgt_ref), custom_call_target="tpu_custom_call" | custom-call | flops 671088640 | bytes 425984 | tf_op jit(solution)/shard_map/pallas_call | solution.py:76
  44.3 3.0 %shard_map.140 = f32[4,128,128]{2,1,0:T(8,128)} custom-call(bf16[1,128,512]{2,1,0:T(8,128)(2,1)} %copy-done.2, s32[4,1,8,128]{3,2,1,0:T(8,128)} %get-tuple-element.58.far_ref, s32[4,1,8,128]{3,2,1,0:T(8,128)} %get-tuple-element.50.tgt_ref), custom_call_target="tpu_custom_call" | custom-call | flops 671088640 | bytes 425984 | tf_op jit(solution)/shard_map/pallas_call | solution.py:76
  47.3 4.1 %shard_map.141 = f32[4,128,128]{2,1,0:T(8,128)} custom-call(bf16[2,128,512]{2,1,0:T(8,128)(2,1)} %copy-done.6, s32[4,2,8,128]{3,2,1,0:T(8,128)} %get-tuple-element.62.far_ref, s32[4,2,8,128]{3,2,1,0:T(8,128)} %get-tuple-element.61.tgt_ref), custom_call_target="tpu_custom_call" | custom-call | flops 1342177280 | bytes 589824 | tf_op jit(solution)/shard_map/pallas_call | solution.py:76
  51.4 0.8 copy-done.14
  52.2 6.1 %shard_map.142 = f32[4,128,128]{2,1,0:T(8,128)} custom-call(bf16[4,128,512]{2,1,0:T(8,128)(2,1)} %copy-done.14, s32[4,4,8,128]{3,2,1,0:T(8,128)} %get-tuple-element.60.far_ref, s32[4,4,8,128]{3,2,1,0:T(8,128)} %get-tuple-element.59.tgt_ref), custom_call_target="tpu_custom_call" | custom-call | flops 2684354560 | bytes 917504 | tf_op jit(solution)/shard_map/pallas_call | solution.py:76
  58.3 1.0 add_add_fusion
  59.3 27.9 %all_to_all.15 = f32[8,64,128]{2,1,0:T(8,128)S(1)} all-to-all(f32[8,64,128]{2,1,0:T(8,128)S(1)} %bitcast.22), channel_id=1, replica_groups=mesh['rows'=64,'rep'=8] {'rep'}, dimensions={0} | all-to-all | bytes 524288 | tf_op jit(solution)/shard_map/all_to_all | solution.py:124
  87.3 8.6 %all_to_all.16 = f32[8,64,128]{2,1,0:T(8,128)S(1)} all-to-all(f32[8,64,128]{2,1,0:T(8,128)S(1)} %broadcast_in_dim.23), channel_id=1, replica_groups=mesh['rows'=64,'rep'=8] {'rep'}, dimensions={0} | all-to-all | bytes 524288 | tf_op jit(solution)/shard_map/all_to_all | solution.py:127
  95.8 0.7 broadcast_in_dim.24
  96.5 3.4 %all-to-all-start.2 = ((bf16[8,64,256]{2,1,0:T(8,128)(2,1)}), bf16[8,64,256]{2,1,0:T(8,128)(2,1)S(1)}, u32[]{:S(2)}, u32[]{:S(2)}) async-start(bf16[8,64,256]{2,1,0:T(8,128)(2,1)} %broadcast_in_dim.24), calls=%async_computation.2 | async-start | bytes 524288 | tf_op jit(solution)/shard_map/all_to_all | solution.py:111
  100.0 0.1 copy.21
  100.2 5.9 %all-to-all-done.2 = bf16[8,64,256]{2,1,0:T(8,128)(2,1)S(1)} async-done(((bf16[8,64,256]{2,1,0:T(8,128)(2,1)}), bf16[8,64,256]{2,1,0:T(8,128)(2,1)S(1)}, u32[]{:S(2)}, u32[]{:S(2)}) %all-to-all-start.2) | async-done | bytes 262176 | tf_op jit(solution)/shard_map/all_to_all | solution.py:111
  106.0 0.6 convert_reduce_fusion
  106.7 0.2 fusion.19
  106.9 6.5 %collective-permute-start.4 = (f32[136,256]{1,0:T(8,128)S(1)}, f32[136,256]{1,0:T(8,128)S(1)}, u32[]{:S(2)}, u32[]{:S(2)}) collective-permute-start(f32[136,256]{1,0:T(8,128)S(1)} %pad_maximum_fusion.2), channel_id=1, source_target_pairs={{0,72},{8,64},{16,88},{24,80},{32,104},{40,96},{48,120},{56,112},{... | collective-permute-start | bytes 417800 | tf_op jit(solution)/shard_map/ppermute | solution.py:23
  113.4 2.6 %collective-permute-start.5 = (f32[136,256]{1,0:T(8,128)S(1)}, f32[136,256]{1,0:T(8,128)S(1)}, u32[]{:S(2)}, u32[]{:S(2)}) collective-permute-start(f32[136,256]{1,0:T(8,128)S(1)} %pad_maximum_fusion.2), channel_id=1, source_target_pairs={{0,64},{8,72},{16,80},{24,88},{32,96},{40,104},{48,112},{56,120},{... | collective-permute-start | bytes 417800 | tf_op jit(solution)/shard_map/ppermute | solution.py:23
  116.0 1.9 %collective-permute-start.6 = (f32[136,256]{1,0:T(8,128)S(1)}, f32[136,256]{1,0:T(8,128)S(1)}, u32[]{:S(2)}, u32[]{:S(2)}) collective-permute-start(f32[136,256]{1,0:T(8,128)S(1)} %pad_maximum_fusion.2), channel_id=1, source_target_pairs={{0,8},{8,0},{16,24},{24,16},{32,40},{40,32},{48,56},{56,48},{64,72... | collective-permute-start | bytes 417800 | tf_op jit(solution)/shard_map/ppermute | solution.py:23
  118.0 2.8 %collective-permute-done.5 = f32[136,256]{1,0:T(8,128)S(1)} collective-permute-done((f32[136,256]{1,0:T(8,128)S(1)}, f32[136,256]{1,0:T(8,128)S(1)}, u32[]{:S(2)}, u32[]{:S(2)}) %collective-permute-start.5) | collective-permute-done | bytes 139296 | tf_op jit(solution)/shard_map/ppermute | solution.py:23
  120.9 1.9 %collective-permute-start.7 = (f32[136,256]{1,0:T(8,128)S(1)}, f32[136,256]{1,0:T(8,128)S(1)}, u32[]{:S(2)}, u32[]{:S(2)}) collective-permute-start(f32[136,256]{1,0:T(8,128)S(1)} %add_add_fusion.3), channel_id=1, source_target_pairs={{0,144},{8,152},{16,128},{24,136},{32,176},{40,184},{48,160},{56,1... | collective-permute-start | bytes 417800 | tf_op jit(solution)/shard_map/ppermute | solution.py:23
  122.8 3.9 %collective-permute-start.8 = (f32[136,256]{1,0:T(8,128)S(1)}, f32[136,256]{1,0:T(8,128)S(1)}, u32[]{:S(2)}, u32[]{:S(2)}) collective-permute-start(f32[136,256]{1,0:T(8,128)S(1)} %add_add_fusion.3), channel_id=1, source_target_pairs={{0,128},{8,136},{16,144},{24,152},{32,160},{40,168},{48,176},{56,1... | collective-permute-start | bytes 417800 | tf_op jit(solution)/shard_map/ppermute | solution.py:23
  126.8 4.3 %collective-permute-start.9 = (f32[136,256]{1,0:T(8,128)S(1)}, f32[136,256]{1,0:T(8,128)S(1)}, u32[]{:S(2)}, u32[]{:S(2)}) collective-permute-start(f32[136,256]{1,0:T(8,128)S(1)} %add_add_fusion.3), channel_id=1, source_target_pairs={{0,16},{8,24},{16,0},{24,8},{32,48},{40,56},{48,32},{56,40},{64,80... | collective-permute-start | bytes 417800 | tf_op jit(solution)/shard_map/ppermute | solution.py:23
  131.1 6.4 %collective-permute-done.7 = f32[136,256]{1,0:T(8,128)S(1)} collective-permute-done((f32[136,256]{1,0:T(8,128)S(1)}, f32[136,256]{1,0:T(8,128)S(1)}, u32[]{:S(2)}, u32[]{:S(2)}) %collective-permute-start.7) | collective-permute-done | bytes 139296 | tf_op jit(solution)/shard_map/ppermute | solution.py:23
  137.6 0.7 collective-permute-done.8
  138.2 3.6 %collective-permute-done.9 = f32[136,256]{1,0:T(8,128)S(1)} collective-permute-done((f32[136,256]{1,0:T(8,128)S(1)}, f32[136,256]{1,0:T(8,128)S(1)}, u32[]{:S(2)}, u32[]{:S(2)}) %collective-permute-start.9) | collective-permute-done | bytes 139296 | tf_op jit(solution)/shard_map/ppermute | solution.py:23
  141.9 6.1 %collective-permute-start.10 = (f32[136,256]{1,0:T(8,128)S(1)}, f32[136,256]{1,0:T(8,128)S(1)}, u32[]{:S(2)}, u32[]{:S(2)}) collective-permute-start(f32[136,256]{1,0:T(8,128)S(1)} %add_add_fusion.2), channel_id=1, source_target_pairs={{0,288},{8,296},{16,304},{24,312},{32,256},{40,264},{48,272},{56,2... | collective-permute-start | bytes 417800 | tf_op jit(solution)/shard_map/ppermute | solution.py:23
  148.1 5.7 %collective-permute-start.11 = (f32[136,256]{1,0:T(8,128)S(1)}, f32[136,256]{1,0:T(8,128)S(1)}, u32[]{:S(2)}, u32[]{:S(2)}) collective-permute-start(f32[136,256]{1,0:T(8,128)S(1)} %add_add_fusion.2), channel_id=1, source_target_pairs={{0,256},{8,264},{16,272},{24,280},{32,288},{40,296},{48,304},{56,3... | collective-permute-start | bytes 417800 | tf_op jit(solution)/shard_map/ppermute | solution.py:23
  153.7 4.4 %collective-permute-start.12 = (f32[136,256]{1,0:T(8,128)S(1)}, f32[136,256]{1,0:T(8,128)S(1)}, u32[]{:S(2)}, u32[]{:S(2)}) collective-permute-start(f32[136,256]{1,0:T(8,128)S(1)} %add_add_fusion.2), channel_id=1, source_target_pairs={{0,32},{8,40},{16,48},{24,56},{32,0},{40,8},{48,16},{56,24},{64,96... | collective-permute-start | bytes 417800 | tf_op jit(solution)/shard_map/ppermute | solution.py:23
  158.2 0.6 fusion.15
  158.8 7.1 %collective-permute-done.10 = f32[136,256]{1,0:T(8,128)S(1)} collective-permute-done((f32[136,256]{1,0:T(8,128)S(1)}, f32[136,256]{1,0:T(8,128)S(1)}, u32[]{:S(2)}, u32[]{:S(2)}) %collective-permute-start.10) | collective-permute-done | bytes 139296 | tf_op jit(solution)/shard_map/ppermute | solution.py:23
  166.0 4.2 %collective-permute-done.12 = f32[136,256]{1,0:T(8,128)S(1)} collective-permute-done((f32[136,256]{1,0:T(8,128)S(1)}, f32[136,256]{1,0:T(8,128)S(1)}, u32[]{:S(2)}, u32[]{:S(2)}) %collective-permute-start.12) | collective-permute-done | bytes 139296 | tf_op jit(solution)/shard_map/ppermute | solution.py:23
  170.2 0.7 slice.68
  170.9 0.6 slice.69
  (50 shorter events, 0.6 us)
Async XLA Ops:
  0.6 105.4 %copy-start = (bf16[128,256]{1,0:T(8,128)(2,1)S(1)}, bf16[128,256]{1,0:T(8,128)(2,1)}, u32[]{:S(2)}) copy-start(bf16[128,256]{1,0:T(8,128)(2,1)} %param.17) | copy-start | bytes 196612
  0.6 1.1 copy-start.11
  1.7 0.9 copy-start.9
  1.7 0.9 copy-start.7
  1.8 0.9 copy-start.10
  1.8 1.0 collective-permute-start
  2.8 33.6 %copy-start.1 = (bf16[128,512]{1,0:T(8,128)(2,1)}, bf16[128,512]{1,0:T(8,128)(2,1)S(1)}, u32[]{:S(2)}) copy-start(bf16[128,512]{1,0:T(8,128)(2,1)S(1)} %collective-permute-done) | copy-start | bytes 393220
  2.8 13.8 %collective-permute-start.1 = (bf16[1,128,512]{2,1,0:T(8,128)(2,1)S(1)}, bf16[1,128,512]{2,1,0:T(8,128)(2,1)S(1)}, u32[]{:S(2)}, u32[]{:S(2)}) collective-permute-start(bf16[1,128,512]{2,1,0:T(8,128)(2,1)S(1)} %bitcast.24), channel_id=1, source_target_pairs={{0,480},{8,488},{16,496},{24,504},{32,0},{40,8},{48,16},{56,24},{6... | collective-permute-start | bytes 393224 | tf_op jit(solution)/shard_map/ppermute | solution.py:12
  14.0 12.2 %copy-start.13 = (s32[2]{0:T(128)S(1)}, s32[2]{0:T(128)}, u32[]{:S(2)}) copy-start(s32[2]{0:T(128)} %constant.182) | copy-start | bytes 28
  16.6 19.8 %copy-start.2 = (bf16[1,128,512]{2,1,0:T(8,128)(2,1)}, bf16[1,128,512]{2,1,0:T(8,128)(2,1)S(1)}, u32[]{:S(2)}) copy-start(bf16[1,128,512]{2,1,0:T(8,128)(2,1)S(1)} %collective-permute-done.1.bufT_ref) | copy-start | bytes 393220
  16.7 19.7 %collective-permute-start.2 = (bf16[2,128,512]{2,1,0:T(8,128)(2,1)S(1)}, bf16[2,128,512]{2,1,0:T(8,128)(2,1)S(1)}, u32[]{:S(2)}, u32[]{:S(2)}) collective-permute-start(bf16[2,128,512]{2,1,0:T(8,128)(2,1)S(1)} %pad_maximum_fusion.1), channel_id=1, source_target_pairs={{0,496},{8,504},{16,0},{24,8},{32,16},{40,24},{48,32},{56,40},{64,... | collective-permute-start | bytes 786440 | tf_op jit(solution)/shard_map/ppermute | solution.py:12
  28.0 11.5 %copy-start.12 = (s32[4]{0:T(128)S(1)}, s32[4]{0:T(128)}, u32[]{:S(2)}) copy-start(s32[4]{0:T(128)} %constant.184) | copy-start | bytes 52
  36.4 0.7 copy-start.6
  37.1 14.2 %collective-permute-start.3 = (bf16[4,128,512]{2,1,0:T(8,128)(2,1)S(1)}, bf16[4,128,512]{2,1,0:T(8,128)(2,1)S(1)}, u32[]{:S(2)}, u32[]{:S(2)}) collective-permute-start(bf16[4,128,512]{2,1,0:T(8,128)(2,1)S(1)} %pad_maximum_fusion), channel_id=1, source_target_pairs={{0,504},{8,0},{16,8},{24,16},{32,24},{40,32},{48,40},{56,48},{64,5... | collective-permute-start | bytes 1572872 | tf_op jit(solution)/shard_map/ppermute | solution.py:12
  51.4 0.8 copy-start.14
  52.2 6.1 %copy-start.3 = (f32[4,128,128]{2,1,0:T(8,128)S(1)}, f32[4,128,128]{2,1,0:T(8,128)}, u32[]{:S(2)}) copy-start(f32[4,128,128]{2,1,0:T(8,128)} %shard_map.139) | copy-start | bytes 786436
  52.2 6.1 %copy-start.4 = (f32[4,128,128]{2,1,0:T(8,128)S(1)}, f32[4,128,128]{2,1,0:T(8,128)}, u32[]{:S(2)}) copy-start(f32[4,128,128]{2,1,0:T(8,128)} %shard_map.140) | copy-start | bytes 786436
  52.2 6.1 %copy-start.5 = (f32[4,128,128]{2,1,0:T(8,128)S(1)}, f32[4,128,128]{2,1,0:T(8,128)}, u32[]{:S(2)}) copy-start(f32[4,128,128]{2,1,0:T(8,128)} %shard_map.141) | copy-start | bytes 786436
  87.2 8.6 %copy-start.8 = (bf16[64,256]{1,0:T(8,128)(2,1)S(1)}, bf16[64,256]{1,0:T(8,128)(2,1)}, u32[]{:S(2)}) copy-start(bf16[64,256]{1,0:T(8,128)(2,1)} %param.19) | copy-start | bytes 98308
  96.5 9.5 %all-to-all-start.2 = ((bf16[8,64,256]{2,1,0:T(8,128)(2,1)}), bf16[8,64,256]{2,1,0:T(8,128)(2,1)S(1)}, u32[]{:S(2)}, u32[]{:S(2)}) async-start(bf16[8,64,256]{2,1,0:T(8,128)(2,1)} %broadcast_in_dim.24), calls=%async_computation.2 | async-start | bytes 524288 | tf_op jit(solution)/shard_map/all_to_all | solution.py:111
  100.1 5.9 %copy-start.15 = (f32[256]{0:T(256)S(1)}, f32[256]{0:T(256)}, u32[]{:S(2)}) copy-start(f32[256]{0:T(256)} %param.18) | copy-start | bytes 3076
  106.9 11.1 %collective-permute-start.4 = (f32[136,256]{1,0:T(8,128)S(1)}, f32[136,256]{1,0:T(8,128)S(1)}, u32[]{:S(2)}, u32[]{:S(2)}) collective-permute-start(f32[136,256]{1,0:T(8,128)S(1)} %pad_maximum_fusion.2), channel_id=1, source_target_pairs={{0,72},{8,64},{16,88},{24,80},{32,104},{40,96},{48,120},{56,112},{... | collective-permute-start | bytes 417800 | tf_op jit(solution)/shard_map/ppermute | solution.py:23
  113.4 7.4 %collective-permute-start.5 = (f32[136,256]{1,0:T(8,128)S(1)}, f32[136,256]{1,0:T(8,128)S(1)}, u32[]{:S(2)}, u32[]{:S(2)}) collective-permute-start(f32[136,256]{1,0:T(8,128)S(1)} %pad_maximum_fusion.2), channel_id=1, source_target_pairs={{0,64},{8,72},{16,80},{24,88},{32,96},{40,104},{48,112},{56,120},{... | collective-permute-start | bytes 417800 | tf_op jit(solution)/shard_map/ppermute | solution.py:23
  116.0 4.8 %collective-permute-start.6 = (f32[136,256]{1,0:T(8,128)S(1)}, f32[136,256]{1,0:T(8,128)S(1)}, u32[]{:S(2)}, u32[]{:S(2)}) collective-permute-start(f32[136,256]{1,0:T(8,128)S(1)} %pad_maximum_fusion.2), channel_id=1, source_target_pairs={{0,8},{8,0},{16,24},{24,16},{32,40},{40,32},{48,56},{56,48},{64,72... | collective-permute-start | bytes 417800 | tf_op jit(solution)/shard_map/ppermute | solution.py:23
  120.9 16.7 %collective-permute-start.7 = (f32[136,256]{1,0:T(8,128)S(1)}, f32[136,256]{1,0:T(8,128)S(1)}, u32[]{:S(2)}, u32[]{:S(2)}) collective-permute-start(f32[136,256]{1,0:T(8,128)S(1)} %add_add_fusion.3), channel_id=1, source_target_pairs={{0,144},{8,152},{16,128},{24,136},{32,176},{40,184},{48,160},{56,1... | collective-permute-start | bytes 417800 | tf_op jit(solution)/shard_map/ppermute | solution.py:23
  122.8 15.4 %collective-permute-start.8 = (f32[136,256]{1,0:T(8,128)S(1)}, f32[136,256]{1,0:T(8,128)S(1)}, u32[]{:S(2)}, u32[]{:S(2)}) collective-permute-start(f32[136,256]{1,0:T(8,128)S(1)} %add_add_fusion.3), channel_id=1, source_target_pairs={{0,128},{8,136},{16,144},{24,152},{32,160},{40,168},{48,176},{56,1... | collective-permute-start | bytes 417800 | tf_op jit(solution)/shard_map/ppermute | solution.py:23
  126.8 15.1 %collective-permute-start.9 = (f32[136,256]{1,0:T(8,128)S(1)}, f32[136,256]{1,0:T(8,128)S(1)}, u32[]{:S(2)}, u32[]{:S(2)}) collective-permute-start(f32[136,256]{1,0:T(8,128)S(1)} %add_add_fusion.3), channel_id=1, source_target_pairs={{0,16},{8,24},{16,0},{24,8},{32,48},{40,56},{48,32},{56,40},{64,80... | collective-permute-start | bytes 417800 | tf_op jit(solution)/shard_map/ppermute | solution.py:23
  141.9 24.0 %collective-permute-start.10 = (f32[136,256]{1,0:T(8,128)S(1)}, f32[136,256]{1,0:T(8,128)S(1)}, u32[]{:S(2)}, u32[]{:S(2)}) collective-permute-start(f32[136,256]{1,0:T(8,128)S(1)} %add_add_fusion.2), channel_id=1, source_target_pairs={{0,288},{8,296},{16,304},{24,312},{32,256},{40,264},{48,272},{56,2... | collective-permute-start | bytes 417800 | tf_op jit(solution)/shard_map/ppermute | solution.py:23
  148.1 17.9 %collective-permute-start.11 = (f32[136,256]{1,0:T(8,128)S(1)}, f32[136,256]{1,0:T(8,128)S(1)}, u32[]{:S(2)}, u32[]{:S(2)}) collective-permute-start(f32[136,256]{1,0:T(8,128)S(1)} %add_add_fusion.2), channel_id=1, source_target_pairs={{0,256},{8,264},{16,272},{24,280},{32,288},{40,296},{48,304},{56,3... | collective-permute-start | bytes 417800 | tf_op jit(solution)/shard_map/ppermute | solution.py:23
  153.7 16.4 %collective-permute-start.12 = (f32[136,256]{1,0:T(8,128)S(1)}, f32[136,256]{1,0:T(8,128)S(1)}, u32[]{:S(2)}, u32[]{:S(2)}) collective-permute-start(f32[136,256]{1,0:T(8,128)S(1)} %add_add_fusion.2), channel_id=1, source_target_pairs={{0,32},{8,40},{16,48},{24,56},{32,0},{40,8},{48,16},{56,24},{64,96... | collective-permute-start | bytes 417800 | tf_op jit(solution)/shard_map/ppermute | solution.py:23

commit v10 on v8

--- a/solution.py
+++ b/solution.py
@@ -92,8 +92,6 @@
             target = (source - step_count * rep_index) % row_count
             pairs.append((source * replicas + rep_index, target * replicas + rep_index))
     held = lax.ppermute(scaled.T, ("rows", "rep"), pairs)[None]
-    cot_copies = jnp.broadcast_to(cotangent[None], (replicas,) + cotangent.shape)
-    cot_group = lax.all_to_all(cot_copies, "rep", 0, 0).reshape(-1, cotangent.shape[1])
     offsets = [0]
     partial_total = local_sums(held, offsets)
     stride = step_count
@@ -106,14 +104,19 @@
         offsets = offsets + arrived_offsets
     partial_total = partial_total.reshape(-1, partial_total.shape[-1])
     pieces = partial_total.reshape((replicas, -1) + partial_total.shape[1:])
-    pieces = lax.all_to_all(pieces, "rep", 0, 0)
-    share = jnp.sum(pieces, axis=0)
+    cot_copies = jnp.broadcast_to(
+        cotangent.astype(jnp.float32)[None], (replicas,) + cotangent.shape
+    )
+    feat_width = pieces.shape[-1]
+    pieces = lax.all_to_all(jnp.concatenate([pieces, cot_copies], axis=-1), "rep", 0, 0)
+    share = jnp.sum(pieces[..., :feat_width], axis=0)
+    cot_group = pieces[..., feat_width:].reshape(-1, cotangent.shape[1])
     copies = jnp.broadcast_to(share[None], (replicas,) + share.shape)
     edge_sums = lax.all_to_all(copies, "rep", 0, 0).reshape(partial_total.shape)
     aggregate = (inv_deg[:, None] * (edge_sums + scaled.astype(jnp.float32))).astype(jnp.bfloat16)
     pre_act = jnp.dot(aggregate, weight, preferred_element_type=jnp.float32) + bias
     activated, pull_back = jax.vjp(gelu_tanh, pre_act)
-    delta_bf = pull_back(cot_group.astype(jnp.float32))[0].astype(jnp.bfloat16)
+    delta_bf = pull_back(cot_group)[0].astype(jnp.bfloat16)
     local_weight = lax.dot_general(
         aggregate, delta_bf, (((0,), (0,)), ((), ())), preferred_element_type=jnp.float32
     )

time: 174 us -> 171 us (0.983)
  blocking collectives: 36.2 us -> 33.3 us
  starting transfers between devices: 59.6 us -> 57.4 us
    all_to_all x2 -> x1, blocking collectives: 36.2 us -> 33.3 us  [layer(): lax.all_to_all(jnp.concatenate([pieces, cot_copies], axis=-1), 'rep', 0, 0)]
    ppermute x6, starting transfers between devices: 26 us -> 23.8 us  [butterfly_sum(): value = value + lax.ppermute(value, axis, pairs)]
where the time goes in v10:
time: 171 us; the launch traced here: 170 us
  starting transfers between devices  57.4 us (34%)
  waiting for transfers between devices  49.9 us (29%)
  blocking collectives  33.3 us (19%)
  Pallas kernels  16.1 us (9%)
  local copies, waits for them, and re-layouts  9.78 us (6%)
  other arithmetic  2.16 us (1%)
    ppermute x6, waiting for transfers between devices, butterfly_sum(): value = value + lax.ppermute(value, axis, pairs)  39 us
    all_to_all x1, blocking collectives, layer(): lax.all_to_all(jnp.concatenate([pieces, cot_copies], axis=-1), 'rep', 0, 0)  33.3 us
    ppermute x3, starting transfers between devices, from_behind(): return lax.ppermute(value, axis, pairs)  29.4 us
    ppermute x6, starting transfers between devices, butterfly_sum(): value = value + lax.ppermute(value, axis, pairs)  23.8 us
    pallas_call x4, Pallas kernels, edge_sums_kernel(): pl.pallas_call(_edge_kernel, out_shape=jax.ShapeDtypeStruct((blocks, rows...  16.1 us
    all_to_all x1, waiting for transfers between devices, layer(): edge_sums = lax.all_to_all(copies, 'rep', 0, 0).reshape(partial_total.shape)  6.09 us
    ppermute x3, waiting for transfers between devices, from_behind(): return lax.ppermute(value, axis, pairs)  4.86 us
    gather x7, local copies, waits for them, and re-layouts, local_sums(): return edge_sums_kernel(held_t, far[:, index], tgt[:, index])  4.16 us
  transfers between devices with their start and end apart: 11, of which 9 were waited for; matrix products, arithmetic and copies ran while one was open for 3% of the time, Pallas kernels for 6%

profile of v10, /device:TPU:1, one launch (start us, length us, event | category | flops | bytes accessed | tf_op | source)
XLA Modules:
  0.0 170.4 jit_solution(8979349884308215513)
XLA Ops:
  0.7 1.0 copy.16
  1.8 0.8 collective-permute-start
  2.6 0.0 copy-done.8
  2.7 0.1 fusion.11
  2.8 14.4 %collective-permute-start.1 = (bf16[1,128,512]{2,1,0:T(8,128)(2,1)S(1)}, bf16[1,128,512]{2,1,0:T(8,128)(2,1)S(1)}, u32[]{:S(2)}, u32[]{:S(2)}) collective-permute-start(bf16[1,128,512]{2,1,0:T(8,128)(2,1)S(1)} %bitcast.34), channel_id=1, source_target_pairs={{0,480},{8,488},{16,496},{24,504},{32,0},{40,8},{48,16},{56,24},{6... | collective-permute-start | bytes 393224 | tf_op jit(solution)/shard_map/ppermute | solution.py:15
  17.2 0.6 fusion.18
  17.8 1.5 collective-permute-done.1.bufT_ref
  19.4 11.1 %collective-permute-start.2 = (bf16[2,128,512]{2,1,0:T(8,128)(2,1)S(1)}, bf16[2,128,512]{2,1,0:T(8,128)(2,1)S(1)}, u32[]{:S(2)}, u32[]{:S(2)}) collective-permute-start(bf16[2,128,512]{2,1,0:T(8,128)(2,1)S(1)} %pad_maximum_fusion.2), channel_id=1, source_target_pairs={{0,496},{8,504},{16,0},{24,8},{32,16},{40,24},{48,32},{56,40},{64,... | collective-permute-start | bytes 786440 | tf_op jit(solution)/shard_map/ppermute | solution.py:15
  30.5 0.6 gather_fusion
  31.1 0.6 gather_fusion.1
  31.7 0.6 copy_bitcast_fusion.2
  32.3 3.3 %collective-permute-done.2.bufT_ref = bf16[2,128,512]{2,1,0:T(8,128)(2,1)S(1)} collective-permute-done((bf16[2,128,512]{2,1,0:T(8,128)(2,1)S(1)}, bf16[2,128,512]{2,1,0:T(8,128)(2,1)S(1)}, u32[]{:S(2)}, u32[]{:S(2)}) %collective-permute-start.2) | collective-permute-done | bytes 262176 | tf_op jit(solution)/shard_map/ppermute | solution.py:15
  35.6 0.1 pad_maximum_fusion.1
  35.7 0.6 copy-done.7
  36.3 3.9 %collective-permute-start.3 = (bf16[4,128,512]{2,1,0:T(8,128)(2,1)S(1)}, bf16[4,128,512]{2,1,0:T(8,128)(2,1)S(1)}, u32[]{:S(2)}, u32[]{:S(2)}) collective-permute-start(bf16[4,128,512]{2,1,0:T(8,128)(2,1)S(1)} %pad_maximum_fusion.1), channel_id=1, source_target_pairs={{0,504},{8,0},{16,8},{24,16},{32,24},{40,32},{48,40},{56,48},{64,5... | collective-permute-start | bytes 1572872 | tf_op jit(solution)/shard_map/ppermute | solution.py:15
  40.2 0.6 gather_fusion.2
  40.8 0.6 gather_fusion.3
  41.4 0.7 copy_bitcast_fusion
  42.0 3.0 %shard_map.139 = f32[4,128,128]{2,1,0:T(8,128)} custom-call(bf16[1,128,512]{2,1,0:T(8,128)(2,1)} %bitcast.37, s32[4,1,8,128]{3,2,1,0:T(8,128)} %get-tuple-element.57.far_ref, s32[4,1,8,128]{3,2,1,0:T(8,128)} %get-tuple-element.51.tgt_ref), custom_call_target="tpu_custom_call" | custom-call | flops 671088640 | bytes 425984 | tf_op jit(solution)/shard_map/pallas_call | solution.py:61
  45.0 3.0 %shard_map.140 = f32[4,128,128]{2,1,0:T(8,128)} custom-call(bf16[1,128,512]{2,1,0:T(8,128)(2,1)} %copy-done.3, s32[4,1,8,128]{3,2,1,0:T(8,128)} %get-tuple-element.58.far_ref, s32[4,1,8,128]{3,2,1,0:T(8,128)} %get-tuple-element.50.tgt_ref), custom_call_target="tpu_custom_call" | custom-call | flops 671088640 | bytes 425984 | tf_op jit(solution)/shard_map/pallas_call | solution.py:61
  48.0 4.1 %shard_map.141 = f32[4,128,128]{2,1,0:T(8,128)} custom-call(bf16[2,128,512]{2,1,0:T(8,128)(2,1)} %copy-done.7, s32[4,2,8,128]{3,2,1,0:T(8,128)} %get-tuple-element.62.far_ref, s32[4,2,8,128]{3,2,1,0:T(8,128)} %get-tuple-element.61.tgt_ref), custom_call_target="tpu_custom_call" | custom-call | flops 1342177280 | bytes 589824 | tf_op jit(solution)/shard_map/pallas_call | solution.py:61
  52.1 0.8 copy-done.15
  52.9 6.1 %shard_map.142 = f32[4,128,128]{2,1,0:T(8,128)} custom-call(bf16[4,128,512]{2,1,0:T(8,128)(2,1)} %copy-done.15, s32[4,4,8,128]{3,2,1,0:T(8,128)} %get-tuple-element.60.far_ref, s32[4,4,8,128]{3,2,1,0:T(8,128)} %get-tuple-element.59.tgt_ref), custom_call_target="tpu_custom_call" | custom-call | flops 2684354560 | bytes 917504 | tf_op jit(solution)/shard_map/pallas_call | solution.py:61
  59.0 1.0 add_add_fusion
  60.1 0.1 pad_maximum_fusion
  60.1 33.3 %all_to_all.10 = f32[8,64,384]{2,1,0:T(8,128)S(1)} all-to-all(f32[8,64,384]{2,1,0:T(8,128)S(1)} %pad_maximum_fusion), channel_id=1, replica_groups=mesh['rows'=64,'rep'=8] {'rep'}, dimensions={0} | all-to-all | bytes 1572864 | tf_op jit(solution)/shard_map/all_to_all | solution.py:111
  93.4 0.8 broadcast_in_dim.24
  94.2 3.4 %all-to-all-start.1 = ((f32[8,64,128]{2,1,0:T(8,128)}), f32[8,64,128]{2,1,0:T(8,128)S(1)}, u32[]{:S(2)}, u32[]{:S(2)}) async-start(f32[8,64,128]{2,1,0:T(8,128)} %broadcast_in_dim.24), calls=%async_computation.1 | async-start | bytes 524288 | tf_op jit(solution)/shard_map/all_to_all | solution.py:115
  97.6 6.1 %all-to-all-done.1 = f32[8,64,128]{2,1,0:T(8,128)S(1)} async-done(((f32[8,64,128]{2,1,0:T(8,128)}), f32[8,64,128]{2,1,0:T(8,128)S(1)}, u32[]{:S(2)}, u32[]{:S(2)}) %all-to-all-start.1) | async-done | bytes 262176 | tf_op jit(solution)/shard_map/all_to_all | solution.py:115
  103.7 0.1 copy.21
  103.9 0.8 slice-done
  104.8 0.6 convert_reduce_fusion
  105.3 0.2 fusion.20
  105.6 4.3 %collective-permute-start.4 = (f32[136,256]{1,0:T(8,128)S(1)}, f32[136,256]{1,0:T(8,128)S(1)}, u32[]{:S(2)}, u32[]{:S(2)}) collective-permute-start(f32[136,256]{1,0:T(8,128)S(1)} %pad_maximum_fusion.3), channel_id=1, source_target_pairs={{0,8},{8,0},{16,24},{24,16},{32,40},{40,32},{48,56},{56,48},{64,72... | collective-permute-start | bytes 417800 | tf_op jit(solution)/shard_map/ppermute | solution.py:24
  109.9 1.0 collective-permute-done.4
  110.9 2.2 %collective-permute-start.5 = (f32[136,256]{1,0:T(8,128)S(1)}, f32[136,256]{1,0:T(8,128)S(1)}, u32[]{:S(2)}, u32[]{:S(2)}) collective-permute-start(f32[136,256]{1,0:T(8,128)S(1)} %fusion.16), channel_id=1, source_target_pairs={{0,64},{8,72},{16,80},{24,88},{32,96},{40,104},{48,112},{56,120},{... | collective-permute-start | bytes 417800 | tf_op jit(solution)/shard_map/ppermute | solution.py:24
  113.1 4.6 %collective-permute-done.5 = f32[136,256]{1,0:T(8,128)S(1)} collective-permute-done((f32[136,256]{1,0:T(8,128)S(1)}, f32[136,256]{1,0:T(8,128)S(1)}, u32[]{:S(2)}, u32[]{:S(2)}) %collective-permute-start.5) | collective-permute-done | bytes 139296 | tf_op jit(solution)/shard_map/ppermute | solution.py:24
  117.7 1.9 %collective-permute-start.6 = (f32[136,256]{1,0:T(8,128)S(1)}, f32[136,256]{1,0:T(8,128)S(1)}, u32[]{:S(2)}, u32[]{:S(2)}) collective-permute-start(f32[136,256]{1,0:T(8,128)S(1)} %add.96), channel_id=1, source_target_pairs={{0,16},{8,24},{16,0},{24,8},{32,48},{40,56},{48,32},{56,40},{64,80... | collective-permute-start | bytes 417800 | tf_op jit(solution)/shard_map/ppermute | solution.py:24
  119.6 9.2 %collective-permute-done.6 = f32[136,256]{1,0:T(8,128)S(1)} collective-permute-done((f32[136,256]{1,0:T(8,128)S(1)}, f32[136,256]{1,0:T(8,128)S(1)}, u32[]{:S(2)}, u32[]{:S(2)}) %collective-permute-start.6) | collective-permute-done | bytes 139296 | tf_op jit(solution)/shard_map/ppermute | solution.py:24
  128.8 5.6 %collective-permute-start.7 = (f32[136,256]{1,0:T(8,128)S(1)}, f32[136,256]{1,0:T(8,128)S(1)}, u32[]{:S(2)}, u32[]{:S(2)}) collective-permute-start(f32[136,256]{1,0:T(8,128)S(1)} %add.97), channel_id=1, source_target_pairs={{0,128},{8,136},{16,144},{24,152},{32,160},{40,168},{48,176},{56,1... | collective-permute-start | bytes 417800 | tf_op jit(solution)/shard_map/ppermute | solution.py:24
  134.4 6.8 %collective-permute-done.7 = f32[136,256]{1,0:T(8,128)S(1)} collective-permute-done((f32[136,256]{1,0:T(8,128)S(1)}, f32[136,256]{1,0:T(8,128)S(1)}, u32[]{:S(2)}, u32[]{:S(2)}) %collective-permute-start.7) | collective-permute-done | bytes 139296 | tf_op jit(solution)/shard_map/ppermute | solution.py:24
  141.2 4.5 %collective-permute-start.8 = (f32[136,256]{1,0:T(8,128)S(1)}, f32[136,256]{1,0:T(8,128)S(1)}, u32[]{:S(2)}, u32[]{:S(2)}) collective-permute-start(f32[136,256]{1,0:T(8,128)S(1)} %add.98), channel_id=1, source_target_pairs={{0,32},{8,40},{16,48},{24,56},{32,0},{40,8},{48,16},{56,24},{64,96... | collective-permute-start | bytes 417800 | tf_op jit(solution)/shard_map/ppermute | solution.py:24
  145.7 9.4 %collective-permute-done.8 = f32[136,256]{1,0:T(8,128)S(1)} collective-permute-done((f32[136,256]{1,0:T(8,128)S(1)}, f32[136,256]{1,0:T(8,128)S(1)}, u32[]{:S(2)}, u32[]{:S(2)}) %collective-permute-start.8) | collective-permute-done | bytes 139296 | tf_op jit(solution)/shard_map/ppermute | solution.py:24
  155.1 5.3 %collective-permute-start.9 = (f32[136,256]{1,0:T(8,128)S(1)}, f32[136,256]{1,0:T(8,128)S(1)}, u32[]{:S(2)}, u32[]{:S(2)}) collective-permute-start(f32[136,256]{1,0:T(8,128)S(1)} %add.99), channel_id=1, source_target_pairs={{0,256},{8,264},{16,272},{24,280},{32,288},{40,296},{48,304},{56,3... | collective-permute-start | bytes 417800 | tf_op jit(solution)/shard_map/ppermute | solution.py:24
  160.4 0.6 fusion.15
  161.1 8.1 %collective-permute-done.9 = f32[136,256]{1,0:T(8,128)S(1)} collective-permute-done((f32[136,256]{1,0:T(8,128)S(1)}, f32[136,256]{1,0:T(8,128)S(1)}, u32[]{:S(2)}, u32[]{:S(2)}) %collective-permute-start.9) | collective-permute-done | bytes 139296 | tf_op jit(solution)/shard_map/ppermute | solution.py:24
  169.2 0.7 slice.78
  169.9 0.6 slice.79
  (51 shorter events, 0.4 us)
Async XLA Ops:
  0.6 103.3 %copy-start = (bf16[128,256]{1,0:T(8,128)(2,1)S(1)}, bf16[128,256]{1,0:T(8,128)(2,1)}, u32[]{:S(2)}) copy-start(bf16[128,256]{1,0:T(8,128)(2,1)} %param.17) | copy-start | bytes 196612
  0.6 1.1 copy-start.12
  1.7 0.9 copy-start.10
  1.7 0.9 copy-start.8
  1.8 0.9 copy-start.11
  1.8 1.0 collective-permute-start
  2.8 32.8 %copy-start.2 = (bf16[128,512]{1,0:T(8,128)(2,1)}, bf16[128,512]{1,0:T(8,128)(2,1)S(1)}, u32[]{:S(2)}) copy-start(bf16[128,512]{1,0:T(8,128)(2,1)S(1)} %collective-permute-done) | copy-start | bytes 393220
  2.8 16.5 %collective-permute-start.1 = (bf16[1,128,512]{2,1,0:T(8,128)(2,1)S(1)}, bf16[1,128,512]{2,1,0:T(8,128)(2,1)S(1)}, u32[]{:S(2)}, u32[]{:S(2)}) collective-permute-start(bf16[1,128,512]{2,1,0:T(8,128)(2,1)S(1)} %bitcast.34), channel_id=1, source_target_pairs={{0,480},{8,488},{16,496},{24,504},{32,0},{40,8},{48,16},{56,24},{6... | collective-permute-start | bytes 393224 | tf_op jit(solution)/shard_map/ppermute | solution.py:15
  17.8 12.7 %copy-start.14 = (s32[2]{0:T(128)S(1)}, s32[2]{0:T(128)}, u32[]{:S(2)}) copy-start(s32[2]{0:T(128)} %constant.168) | copy-start | bytes 28
  19.3 16.3 %copy-start.3 = (bf16[1,128,512]{2,1,0:T(8,128)(2,1)}, bf16[1,128,512]{2,1,0:T(8,128)(2,1)S(1)}, u32[]{:S(2)}) copy-start(bf16[1,128,512]{2,1,0:T(8,128)(2,1)S(1)} %collective-permute-done.1.bufT_ref) | copy-start | bytes 393220
  19.4 16.2 %collective-permute-start.2 = (bf16[2,128,512]{2,1,0:T(8,128)(2,1)S(1)}, bf16[2,128,512]{2,1,0:T(8,128)(2,1)S(1)}, u32[]{:S(2)}, u32[]{:S(2)}) collective-permute-start(bf16[2,128,512]{2,1,0:T(8,128)(2,1)S(1)} %pad_maximum_fusion.2), channel_id=1, source_target_pairs={{0,496},{8,504},{16,0},{24,8},{32,16},{40,24},{48,32},{56,40},{64,... | collective-permute-start | bytes 786440 | tf_op jit(solution)/shard_map/ppermute | solution.py:15
  32.3 7.9 %copy-start.13 = (s32[4]{0:T(128)S(1)}, s32[4]{0:T(128)}, u32[]{:S(2)}) copy-start(s32[4]{0:T(128)} %constant.170) | copy-start | bytes 52
  35.6 0.7 copy-start.7
  36.3 15.7 %collective-permute-start.3 = (bf16[4,128,512]{2,1,0:T(8,128)(2,1)S(1)}, bf16[4,128,512]{2,1,0:T(8,128)(2,1)S(1)}, u32[]{:S(2)}, u32[]{:S(2)}) collective-permute-start(bf16[4,128,512]{2,1,0:T(8,128)(2,1)S(1)} %pad_maximum_fusion.1), channel_id=1, source_target_pairs={{0,504},{8,0},{16,8},{24,16},{32,24},{40,32},{48,40},{56,48},{64,5... | collective-permute-start | bytes 1572872 | tf_op jit(solution)/shard_map/ppermute | solution.py:15
  52.1 0.8 copy-start.15
  52.9 6.1 %copy-start.4 = (f32[4,128,128]{2,1,0:T(8,128)S(1)}, f32[4,128,128]{2,1,0:T(8,128)}, u32[]{:S(2)}) copy-start(f32[4,128,128]{2,1,0:T(8,128)} %shard_map.139) | copy-start | bytes 786436
  52.9 6.1 %copy-start.5 = (f32[4,128,128]{2,1,0:T(8,128)S(1)}, f32[4,128,128]{2,1,0:T(8,128)}, u32[]{:S(2)}) copy-start(f32[4,128,128]{2,1,0:T(8,128)} %shard_map.140) | copy-start | bytes 786436
  52.9 6.1 %copy-start.6 = (f32[4,128,128]{2,1,0:T(8,128)S(1)}, f32[4,128,128]{2,1,0:T(8,128)}, u32[]{:S(2)}) copy-start(f32[4,128,128]{2,1,0:T(8,128)} %shard_map.141) | copy-start | bytes 786436
  59.0 1.0 copy-start.9
  93.4 4.2 %copy-start.1 = (f32[8,64,384]{2,1,0:T(8,128)}, f32[8,64,384]{2,1,0:T(8,128)S(1)}, u32[]{:S(2)}) copy-start(f32[8,64,384]{2,1,0:T(8,128)S(1)} %all_to_all.10) | copy-start | bytes 2359300
  94.2 9.5 %all-to-all-start.1 = ((f32[8,64,128]{2,1,0:T(8,128)}), f32[8,64,128]{2,1,0:T(8,128)S(1)}, u32[]{:S(2)}, u32[]{:S(2)}) async-start(f32[8,64,128]{2,1,0:T(8,128)} %broadcast_in_dim.24), calls=%async_computation.1 | async-start | bytes 524288 | tf_op jit(solution)/shard_map/all_to_all | solution.py:115
  103.7 1.0 slice-start
  103.9 0.9 copy-start.16
  105.6 5.3 %collective-permute-start.4 = (f32[136,256]{1,0:T(8,128)S(1)}, f32[136,256]{1,0:T(8,128)S(1)}, u32[]{:S(2)}, u32[]{:S(2)}) collective-permute-start(f32[136,256]{1,0:T(8,128)S(1)} %pad_maximum_fusion.3), channel_id=1, source_target_pairs={{0,8},{8,0},{16,24},{24,16},{32,40},{40,32},{48,56},{56,48},{64,72... | collective-permute-start | bytes 417800 | tf_op jit(solution)/shard_map/ppermute | solution.py:24
  110.9 6.8 %collective-permute-start.5 = (f32[136,256]{1,0:T(8,128)S(1)}, f32[136,256]{1,0:T(8,128)S(1)}, u32[]{:S(2)}, u32[]{:S(2)}) collective-permute-start(f32[136,256]{1,0:T(8,128)S(1)} %fusion.16), channel_id=1, source_target_pairs={{0,64},{8,72},{16,80},{24,88},{32,96},{40,104},{48,112},{56,120},{... | collective-permute-start | bytes 417800 | tf_op jit(solution)/shard_map/ppermute | solution.py:24
  117.7 11.1 %collective-permute-start.6 = (f32[136,256]{1,0:T(8,128)S(1)}, f32[136,256]{1,0:T(8,128)S(1)}, u32[]{:S(2)}, u32[]{:S(2)}) collective-permute-start(f32[136,256]{1,0:T(8,128)S(1)} %add.96), channel_id=1, source_target_pairs={{0,16},{8,24},{16,0},{24,8},{32,48},{40,56},{48,32},{56,40},{64,80... | collective-permute-start | bytes 417800 | tf_op jit(solution)/shard_map/ppermute | solution.py:24
  128.8 12.5 %collective-permute-start.7 = (f32[136,256]{1,0:T(8,128)S(1)}, f32[136,256]{1,0:T(8,128)S(1)}, u32[]{:S(2)}, u32[]{:S(2)}) collective-permute-start(f32[136,256]{1,0:T(8,128)S(1)} %add.97), channel_id=1, source_target_pairs={{0,128},{8,136},{16,144},{24,152},{32,160},{40,168},{48,176},{56,1... | collective-permute-start | bytes 417800 | tf_op jit(solution)/shard_map/ppermute | solution.py:24
  141.2 13.8 %collective-permute-start.8 = (f32[136,256]{1,0:T(8,128)S(1)}, f32[136,256]{1,0:T(8,128)S(1)}, u32[]{:S(2)}, u32[]{:S(2)}) collective-permute-start(f32[136,256]{1,0:T(8,128)S(1)} %add.98), channel_id=1, source_target_pairs={{0,32},{8,40},{16,48},{24,56},{32,0},{40,8},{48,16},{56,24},{64,96... | collective-permute-start | bytes 417800 | tf_op jit(solution)/shard_map/ppermute | solution.py:24
  155.1 14.1 %collective-permute-start.9 = (f32[136,256]{1,0:T(8,128)S(1)}, f32[136,256]{1,0:T(8,128)S(1)}, u32[]{:S(2)}, u32[]{:S(2)}) collective-permute-start(f32[136,256]{1,0:T(8,128)S(1)} %add.99), channel_id=1, source_target_pairs={{0,256},{8,264},{16,272},{24,280},{32,288},{40,296},{48,304},{56,3... | collective-permute-start | bytes 417800 | tf_op jit(solution)/shard_map/ppermute | solution.py:24

commit v11 on v10

--- a/solution.py
+++ b/solution.py
@@ -4,9 +4,6 @@
 from jax.experimental import pallas as pl
 from jax.experimental.pallas import tpu as pltpu
 from jax.sharding import PartitionSpec as P
-
-
-ROWS_BITS = (0, 3, 1, 4, 2, 5)
 
 
 def from_behind(value, axis, steps):
@@ -23,6 +20,25 @@
         pairs = [(source, source ^ (1 << bit)) for source in range(count)]
         value = value + lax.ppermute(value, axis, pairs)
     return value
+
+
+def split_sum(value, axis, outer_bits, inner_bits):
+    me = lax.axis_index(axis)
+    count = lax.axis_size(axis)
+    buf = value.reshape((2,) * len(outer_bits) + (-1,) + value.shape[1:])
+    for bit in outer_bits:
+        mine = (me >> bit) & 1
+        keep = lax.dynamic_index_in_dim(buf, mine, 0, keepdims=False)
+        send = lax.dynamic_index_in_dim(buf, 1 - mine, 0, keepdims=False)
+        pairs = [(source, source ^ (1 << bit)) for source in range(count)]
+        buf = keep + lax.ppermute(send, axis, pairs)
+    buf = butterfly_sum(buf, axis, inner_bits)
+    for bit in reversed(outer_bits):
+        mine = (me >> bit) & 1
+        pairs = [(source, source ^ (1 << bit)) for source in range(count)]
+        other = lax.ppermute(buf, axis, pairs)
+        buf = jnp.where(mine == 0, jnp.stack([buf, other]), jnp.stack([other, buf]))
+    return buf.reshape(value.shape)
 
 
 def gelu_tanh(values):
@@ -123,9 +139,9 @@
     local_bias = jnp.sum(delta_bf.astype(jnp.float32), axis=0)
     feat_rows = local_weight.shape[0]
     packed = jnp.concatenate(
-        [local_weight, jnp.broadcast_to(local_bias[None, :], (8, local_bias.shape[0]))], axis=0
+        [local_weight, jnp.broadcast_to(local_bias[None, :], (32, local_bias.shape[0]))], axis=0
     )
-    packed = butterfly_sum(packed, "rows", ROWS_BITS)
+    packed = split_sum(packed, "rows", (5, 2), (0, 3, 1, 4))
     grad_weight = packed[:feat_rows]
     grad_bias = packed[feat_rows]
     share_rows = cotangent.shape[0]

time: 171 us -> 174 us (1.018)
  the two profiles are of different devices: /device:TPU:1 before, /device:TPU:16 now
where the time goes in v11:
time: 174 us; the launch traced here: 173 us
  waiting for transfers between devices  60.2 us (35%)
  starting transfers between devices  52.2 us (30%)
  blocking collectives  30.6 us (18%)
  Pallas kernels  16.1 us (9%)
  local copies, waits for them, and re-layouts  9.8 us (6%)
  other arithmetic  2.11 us (1%)
    all_to_all x1, blocking collectives, layer(): lax.all_to_all(jnp.concatenate([pieces, cot_copies], axis=-1), 'rep', 0, 0)  30.6 us
    ppermute x3, starting transfers between devices, from_behind(): return lax.ppermute(value, axis, pairs)  23.8 us
    pallas_call x4, Pallas kernels, edge_sums_kernel(): pl.pallas_call(_edge_kernel, out_shape=jax.ShapeDtypeStruct((blocks, rows...  16.1 us
    ppermute x2, waiting for transfers between devices, split_sum(): buf = keep + lax.ppermute(send, axis, pairs)  14.1 us
    ppermute x3, waiting for transfers between devices, from_behind(): return lax.ppermute(value, axis, pairs)  13.1 us
    ppermute x4, waiting for transfers between devices, butterfly_sum(): value = value + lax.ppermute(value, axis, pairs)  12.5 us
    ppermute x2, waiting for transfers between devices, split_sum(): other = lax.ppermute(buf, axis, pairs)  12.2 us
    ppermute x4, starting transfers between devices, butterfly_sum(): value = value + lax.ppermute(value, axis, pairs)  10.1 us
  transfers between devices with their start and end apart: 13, of which 11 were waited for; matrix products, arithmetic and copies ran while one was open for 3% of the time, Pallas kernels for 6%

profile of v11, /device:TPU:16, one launch (start us, length us, event | category | flops | bytes accessed | tf_op | source)
XLA Modules:
  0.0 172.9 jit_solution(9698873329388664668)
XLA Ops:
  0.7 1.0 copy.16
  1.8 0.8 collective-permute-start
  2.7 0.1 fusion.11
  2.8 10.8 %collective-permute-start.1 = (bf16[1,128,512]{2,1,0:T(8,128)(2,1)S(1)}, bf16[1,128,512]{2,1,0:T(8,128)(2,1)S(1)}, u32[]{:S(2)}, u32[]{:S(2)}) collective-permute-start(bf16[1,128,512]{2,1,0:T(8,128)(2,1)S(1)} %bitcast.53), channel_id=1, source_target_pairs={{0,480},{8,488},{16,496},{24,504},{32,0},{40,8},{48,16},{56,24},{6... | collective-permute-start | bytes 393224 | tf_op jit(solution)/shard_map/ppermute | solution.py:12
  13.6 0.6 fusion.17
  14.3 3.0 %collective-permute-done.1.bufT_ref = bf16[1,128,512]{2,1,0:T(8,128)(2,1)S(1)} collective-permute-done((bf16[1,128,512]{2,1,0:T(8,128)(2,1)S(1)}, bf16[1,128,512]{2,1,0:T(8,128)(2,1)S(1)}, u32[]{:S(2)}, u32[]{:S(2)}) %collective-permute-start.1) | collective-permute-done | bytes 131104 | tf_op jit(solution)/shard_map/ppermute | solution.py:12
  17.4 11.0 %collective-permute-start.2 = (bf16[2,128,512]{2,1,0:T(8,128)(2,1)S(1)}, bf16[2,128,512]{2,1,0:T(8,128)(2,1)S(1)}, u32[]{:S(2)}, u32[]{:S(2)}) collective-permute-start(bf16[2,128,512]{2,1,0:T(8,128)(2,1)S(1)} %pad_maximum_fusion.2), channel_id=1, source_target_pairs={{0,496},{8,504},{16,0},{24,8},{32,16},{40,24},{48,32},{56,40},{64,... | collective-permute-start | bytes 786440 | tf_op jit(solution)/shard_map/ppermute | solution.py:12
  28.4 0.6 gather_fusion
  29.0 0.6 gather_fusion.1
  29.5 0.6 copy_bitcast_fusion.2
  30.2 10.0 %collective-permute-done.2.bufT_ref = bf16[2,128,512]{2,1,0:T(8,128)(2,1)S(1)} collective-permute-done((bf16[2,128,512]{2,1,0:T(8,128)(2,1)S(1)}, bf16[2,128,512]{2,1,0:T(8,128)(2,1)S(1)}, u32[]{:S(2)}, u32[]{:S(2)}) %collective-permute-start.2) | collective-permute-done | bytes 262176 | tf_op jit(solution)/shard_map/ppermute | solution.py:12
  40.3 0.6 copy-done.7
  40.9 1.9 %collective-permute-start.3 = (bf16[4,128,512]{2,1,0:T(8,128)(2,1)S(1)}, bf16[4,128,512]{2,1,0:T(8,128)(2,1)S(1)}, u32[]{:S(2)}, u32[]{:S(2)}) collective-permute-start(bf16[4,128,512]{2,1,0:T(8,128)(2,1)S(1)} %pad_maximum_fusion.1), channel_id=1, source_target_pairs={{0,504},{8,0},{16,8},{24,16},{32,24},{40,32},{48,40},{56,48},{64,5... | collective-permute-start | bytes 1572872 | tf_op jit(solution)/shard_map/ppermute | solution.py:12
  42.8 0.6 gather_fusion.2
  43.4 0.6 gather_fusion.3
  44.0 0.7 copy_bitcast_fusion
  44.6 3.0 %shard_map.139 = f32[4,128,128]{2,1,0:T(8,128)} custom-call(bf16[1,128,512]{2,1,0:T(8,128)(2,1)} %bitcast.56, s32[4,1,8,128]{3,2,1,0:T(8,128)} %get-tuple-element.57.far_ref, s32[4,1,8,128]{3,2,1,0:T(8,128)} %get-tuple-element.51.tgt_ref), custom_call_target="tpu_custom_call" | custom-call | flops 671088640 | bytes 425984 | tf_op jit(solution)/shard_map/pallas_call | solution.py:77
  47.6 3.0 %shard_map.140 = f32[4,128,128]{2,1,0:T(8,128)} custom-call(bf16[1,128,512]{2,1,0:T(8,128)(2,1)} %copy-done.3, s32[4,1,8,128]{3,2,1,0:T(8,128)} %get-tuple-element.58.far_ref, s32[4,1,8,128]{3,2,1,0:T(8,128)} %get-tuple-element.50.tgt_ref), custom_call_target="tpu_custom_call" | custom-call | flops 671088640 | bytes 425984 | tf_op jit(solution)/shard_map/pallas_call | solution.py:77
  50.6 4.0 %shard_map.141 = f32[4,128,128]{2,1,0:T(8,128)} custom-call(bf16[2,128,512]{2,1,0:T(8,128)(2,1)} %copy-done.7, s32[4,2,8,128]{3,2,1,0:T(8,128)} %get-tuple-element.62.far_ref, s32[4,2,8,128]{3,2,1,0:T(8,128)} %get-tuple-element.61.tgt_ref), custom_call_target="tpu_custom_call" | custom-call | flops 1342177280 | bytes 589824 | tf_op jit(solution)/shard_map/pallas_call | solution.py:77
  54.6 0.8 copy-done.15
  55.5 6.1 %shard_map.142 = f32[4,128,128]{2,1,0:T(8,128)} custom-call(bf16[4,128,512]{2,1,0:T(8,128)(2,1)} %copy-done.15, s32[4,4,8,128]{3,2,1,0:T(8,128)} %get-tuple-element.60.far_ref, s32[4,4,8,128]{3,2,1,0:T(8,128)} %get-tuple-element.59.tgt_ref), custom_call_target="tpu_custom_call" | custom-call | flops 2684354560 | bytes 917504 | tf_op jit(solution)/shard_map/pallas_call | solution.py:77
  61.6 1.0 add_add_fusion
  62.7 30.6 %all_to_all.10 = f32[8,64,384]{2,1,0:T(8,128)S(1)} all-to-all(f32[8,64,384]{2,1,0:T(8,128)S(1)} %pad_maximum_fusion), channel_id=1, replica_groups=mesh['rows'=64,'rep'=8] {'rep'}, dimensions={0} | all-to-all | bytes 1572864 | tf_op jit(solution)/shard_map/all_to_all | solution.py:127
  93.3 0.8 broadcast_in_dim.24
  94.1 3.4 %all-to-all-start.1 = ((f32[8,64,128]{2,1,0:T(8,128)}), f32[8,64,128]{2,1,0:T(8,128)S(1)}, u32[]{:S(2)}, u32[]{:S(2)}) async-start(f32[8,64,128]{2,1,0:T(8,128)} %broadcast_in_dim.24), calls=%async_computation.1 | async-start | bytes 524288 | tf_op jit(solution)/shard_map/all_to_all | solution.py:131
  97.6 8.4 %all-to-all-done.1 = f32[8,64,128]{2,1,0:T(8,128)S(1)} async-done(((f32[8,64,128]{2,1,0:T(8,128)}), f32[8,64,128]{2,1,0:T(8,128)S(1)}, u32[]{:S(2)}, u32[]{:S(2)}) %all-to-all-start.1) | async-done | bytes 262176 | tf_op jit(solution)/shard_map/all_to_all | solution.py:131
  106.2 0.8 slice-done
  107.0 0.6 convert_reduce_fusion
  107.6 0.2 fusion.19
  107.8 2.2 %collective-permute-start.4 = (f32[2,40,256]{2,1,0:T(8,128)S(1)}, f32[2,40,256]{2,1,0:T(8,128)S(1)}, u32[]{:S(2)}, u32[]{:S(2)}) collective-permute-start(f32[2,40,256]{2,1,0:T(8,128)S(1)} %dynamic-slice_bitcast_fusion), channel_id=1, source_target_pairs={{0,256},{8,264},{16,272},{24,280},{32,288},{40,296},{48,304},{56,3... | collective-permute-start | bytes 245768 | tf_op jit(solution)/shard_map/ppermute | solution.py:34
  110.1 8.4 %collective-permute-done.4 = f32[2,40,256]{2,1,0:T(8,128)S(1)} collective-permute-done((f32[2,40,256]{2,1,0:T(8,128)S(1)}, f32[2,40,256]{2,1,0:T(8,128)S(1)}, u32[]{:S(2)}, u32[]{:S(2)}) %collective-permute-start.4) | collective-permute-done | bytes 81952 | tf_op jit(solution)/shard_map/ppermute | solution.py:34
  118.5 4.1 %collective-permute-start.5 = (f32[40,256]{1,0:T(8,128)S(1)}, f32[40,256]{1,0:T(8,128)S(1)}, u32[]{:S(2)}, u32[]{:S(2)}) collective-permute-start(f32[40,256]{1,0:T(8,128)S(1)} %dynamic-slice_bitcast_fusion.1), channel_id=1, source_target_pairs={{0,32},{8,40},{16,48},{24,56},{32,0},{40,8},{48,16},{56,24},{64,96... | collective-permute-start | bytes 122888 | tf_op jit(solution)/shard_map/ppermute | solution.py:34
  122.6 5.7 %collective-permute-done.5 = f32[40,256]{1,0:T(8,128)S(1)} collective-permute-done((f32[40,256]{1,0:T(8,128)S(1)}, f32[40,256]{1,0:T(8,128)S(1)}, u32[]{:S(2)}, u32[]{:S(2)}) %collective-permute-start.5) | collective-permute-done | bytes 40992 | tf_op jit(solution)/shard_map/ppermute | solution.py:34
  128.3 1.9 %collective-permute-start.6 = (f32[40,256]{1,0:T(8,128)S(1)}, f32[40,256]{1,0:T(8,128)S(1)}, u32[]{:S(2)}, u32[]{:S(2)}) collective-permute-start(f32[40,256]{1,0:T(8,128)S(1)} %bitcast_add_fusion.1), channel_id=1, source_target_pairs={{0,8},{8,0},{16,24},{24,16},{32,40},{40,32},{48,56},{56,48},{64,72... | collective-permute-start | bytes 122888 | tf_op jit(solution)/shard_map/ppermute | solution.py:21
  130.3 1.2 collective-permute-done.6
  131.4 3.3 %collective-permute-start.7 = (f32[40,256]{1,0:T(8,128)S(1)}, f32[40,256]{1,0:T(8,128)S(1)}, u32[]{:S(2)}, u32[]{:S(2)}) collective-permute-start(f32[40,256]{1,0:T(8,128)S(1)} %add.117), channel_id=1, source_target_pairs={{0,64},{8,72},{16,80},{24,88},{32,96},{40,104},{48,112},{56,120},{... | collective-permute-start | bytes 122888 | tf_op jit(solution)/shard_map/ppermute | solution.py:21
  134.7 2.6 %collective-permute-done.7 = f32[40,256]{1,0:T(8,128)S(1)} collective-permute-done((f32[40,256]{1,0:T(8,128)S(1)}, f32[40,256]{1,0:T(8,128)S(1)}, u32[]{:S(2)}, u32[]{:S(2)}) %collective-permute-start.7) | collective-permute-done | bytes 40992 | tf_op jit(solution)/shard_map/ppermute | solution.py:21
  137.3 2.6 %collective-permute-start.8 = (f32[40,256]{1,0:T(8,128)S(1)}, f32[40,256]{1,0:T(8,128)S(1)}, u32[]{:S(2)}, u32[]{:S(2)}) collective-permute-start(f32[40,256]{1,0:T(8,128)S(1)} %add.118), channel_id=1, source_target_pairs={{0,16},{8,24},{16,0},{24,8},{32,48},{40,56},{48,32},{56,40},{64,80... | collective-permute-start | bytes 122888 | tf_op jit(solution)/shard_map/ppermute | solution.py:21
  140.0 4.2 %collective-permute-done.8 = f32[40,256]{1,0:T(8,128)S(1)} collective-permute-done((f32[40,256]{1,0:T(8,128)S(1)}, f32[40,256]{1,0:T(8,128)S(1)}, u32[]{:S(2)}, u32[]{:S(2)}) %collective-permute-start.8) | collective-permute-done | bytes 40992 | tf_op jit(solution)/shard_map/ppermute | solution.py:21
  144.1 2.3 %collective-permute-start.9 = (f32[40,256]{1,0:T(8,128)S(1)}, f32[40,256]{1,0:T(8,128)S(1)}, u32[]{:S(2)}, u32[]{:S(2)}) collective-permute-start(f32[40,256]{1,0:T(8,128)S(1)} %add.119), channel_id=1, source_target_pairs={{0,128},{8,136},{16,144},{24,152},{32,160},{40,168},{48,176},{56,1... | collective-permute-start | bytes 122888 | tf_op jit(solution)/shard_map/ppermute | solution.py:21
  146.4 4.5 %collective-permute-done.9 = f32[40,256]{1,0:T(8,128)S(1)} collective-permute-done((f32[40,256]{1,0:T(8,128)S(1)}, f32[40,256]{1,0:T(8,128)S(1)}, u32[]{:S(2)}, u32[]{:S(2)}) %collective-permute-start.9) | collective-permute-done | bytes 40992 | tf_op jit(solution)/shard_map/ppermute | solution.py:21
  151.0 4.5 %collective-permute-start.10 = (f32[40,256]{1,0:T(8,128)S(1)}, f32[40,256]{1,0:T(8,128)S(1)}, u32[]{:S(2)}, u32[]{:S(2)}) collective-permute-start(f32[40,256]{1,0:T(8,128)S(1)} %add.120), channel_id=1, source_target_pairs={{0,32},{8,40},{16,48},{24,56},{32,0},{40,8},{48,16},{56,24},{64,96... | collective-permute-start | bytes 122888 | tf_op jit(solution)/shard_map/ppermute | solution.py:39
  155.5 0.6 fusion.15
  156.1 4.7 %collective-permute-done.10 = f32[40,256]{1,0:T(8,128)S(1)} collective-permute-done((f32[40,256]{1,0:T(8,128)S(1)}, f32[40,256]{1,0:T(8,128)S(1)}, u32[]{:S(2)}, u32[]{:S(2)}) %collective-permute-start.10) | collective-permute-done | bytes 40992 | tf_op jit(solution)/shard_map/ppermute | solution.py:39
  160.8 3.4 %collective-permute-start.11 = (f32[2,40,256]{2,1,0:T(8,128)S(1)}, f32[2,40,256]{2,1,0:T(8,128)S(1)}, u32[]{:S(2)}, u32[]{:S(2)}) collective-permute-start(f32[2,40,256]{2,1,0:T(8,128)S(1)} %maximum_select_fusion.2), channel_id=1, source_target_pairs={{0,256},{8,264},{16,272},{24,280},{32,288},{40,296},{48,304},{56,3... | collective-permute-start | bytes 245768 | tf_op jit(solution)/shard_map/ppermute | solution.py:39
  164.2 7.5 %collective-permute-done.11 = f32[2,40,256]{2,1,0:T(8,128)S(1)} collective-permute-done((f32[2,40,256]{2,1,0:T(8,128)S(1)}, f32[2,40,256]{2,1,0:T(8,128)S(1)}, u32[]{:S(2)}, u32[]{:S(2)}) %collective-permute-start.11) | collective-permute-done | bytes 81952 | tf_op jit(solution)/shard_map/ppermute | solution.py:39
  171.7 0.7 slice.78
  172.4 0.6 slice.79
  (60 shorter events, 0.6 us)
Async XLA Ops:
  0.6 105.5 %copy-start = (bf16[128,256]{1,0:T(8,128)(2,1)S(1)}, bf16[128,256]{1,0:T(8,128)(2,1)}, u32[]{:S(2)}) copy-start(bf16[128,256]{1,0:T(8,128)(2,1)} %param.17) | copy-start | bytes 196612
  0.6 1.1 copy-start.12
  1.7 0.9 copy-start.10
  1.7 0.9 copy-start.8
  1.8 0.9 copy-start.11
  1.8 1.0 collective-permute-start
  2.8 37.4 %copy-start.2 = (bf16[128,512]{1,0:T(8,128)(2,1)}, bf16[128,512]{1,0:T(8,128)(2,1)S(1)}, u32[]{:S(2)}) copy-start(bf16[128,512]{1,0:T(8,128)(2,1)S(1)} %collective-permute-done) | copy-start | bytes 393220
  2.8 14.5 %collective-permute-start.1 = (bf16[1,128,512]{2,1,0:T(8,128)(2,1)S(1)}, bf16[1,128,512]{2,1,0:T(8,128)(2,1)S(1)}, u32[]{:S(2)}, u32[]{:S(2)}) collective-permute-start(bf16[1,128,512]{2,1,0:T(8,128)(2,1)S(1)} %bitcast.53), channel_id=1, source_target_pairs={{0,480},{8,488},{16,496},{24,504},{32,0},{40,8},{48,16},{56,24},{6... | collective-permute-start | bytes 393224 | tf_op jit(solution)/shard_map/ppermute | solution.py:12
  14.3 14.1 %copy-start.14 = (s32[2]{0:T(128)S(1)}, s32[2]{0:T(128)}, u32[]{:S(2)}) copy-start(s32[2]{0:T(128)} %constant.193) | copy-start | bytes 28
  17.3 22.9 %copy-start.3 = (bf16[1,128,512]{2,1,0:T(8,128)(2,1)}, bf16[1,128,512]{2,1,0:T(8,128)(2,1)S(1)}, u32[]{:S(2)}) copy-start(bf16[1,128,512]{2,1,0:T(8,128)(2,1)S(1)} %collective-permute-done.1.bufT_ref) | copy-start | bytes 393220
  17.4 22.8 %collective-permute-start.2 = (bf16[2,128,512]{2,1,0:T(8,128)(2,1)S(1)}, bf16[2,128,512]{2,1,0:T(8,128)(2,1)S(1)}, u32[]{:S(2)}, u32[]{:S(2)}) collective-permute-start(bf16[2,128,512]{2,1,0:T(8,128)(2,1)S(1)} %pad_maximum_fusion.2), channel_id=1, source_target_pairs={{0,496},{8,504},{16,0},{24,8},{32,16},{40,24},{48,32},{56,40},{64,... | collective-permute-start | bytes 786440 | tf_op jit(solution)/shard_map/ppermute | solution.py:12
  30.2 12.6 %copy-start.13 = (s32[4]{0:T(128)S(1)}, s32[4]{0:T(128)}, u32[]{:S(2)}) copy-start(s32[4]{0:T(128)} %constant.195) | copy-start | bytes 52
  40.2 0.7 copy-start.7
  40.9 13.7 %collective-permute-start.3 = (bf16[4,128,512]{2,1,0:T(8,128)(2,1)S(1)}, bf16[4,128,512]{2,1,0:T(8,128)(2,1)S(1)}, u32[]{:S(2)}, u32[]{:S(2)}) collective-permute-start(bf16[4,128,512]{2,1,0:T(8,128)(2,1)S(1)} %pad_maximum_fusion.1), channel_id=1, source_target_pairs={{0,504},{8,0},{16,8},{24,16},{32,24},{40,32},{48,40},{56,48},{64,5... | collective-permute-start | bytes 1572872 | tf_op jit(solution)/shard_map/ppermute | solution.py:12
  54.6 0.8 copy-start.15
  55.5 6.1 %copy-start.4 = (f32[4,128,128]{2,1,0:T(8,128)S(1)}, f32[4,128,128]{2,1,0:T(8,128)}, u32[]{:S(2)}) copy-start(f32[4,128,128]{2,1,0:T(8,128)} %shard_map.139) | copy-start | bytes 786436
  55.5 6.1 %copy-start.5 = (f32[4,128,128]{2,1,0:T(8,128)S(1)}, f32[4,128,128]{2,1,0:T(8,128)}, u32[]{:S(2)}) copy-start(f32[4,128,128]{2,1,0:T(8,128)} %shard_map.140) | copy-start | bytes 786436
  55.5 6.1 %copy-start.6 = (f32[4,128,128]{2,1,0:T(8,128)S(1)}, f32[4,128,128]{2,1,0:T(8,128)}, u32[]{:S(2)}) copy-start(f32[4,128,128]{2,1,0:T(8,128)} %shard_map.141) | copy-start | bytes 786436
  61.5 1.0 copy-start.9
  93.3 4.2 %copy-start.1 = (f32[8,64,384]{2,1,0:T(8,128)}, f32[8,64,384]{2,1,0:T(8,128)S(1)}, u32[]{:S(2)}) copy-start(f32[8,64,384]{2,1,0:T(8,128)S(1)} %all_to_all.10) | copy-start | bytes 2359300
  94.1 11.8 %all-to-all-start.1 = ((f32[8,64,128]{2,1,0:T(8,128)}), f32[8,64,128]{2,1,0:T(8,128)S(1)}, u32[]{:S(2)}, u32[]{:S(2)}) async-start(f32[8,64,128]{2,1,0:T(8,128)} %broadcast_in_dim.24), calls=%async_computation.1 | async-start | bytes 524288 | tf_op jit(solution)/shard_map/all_to_all | solution.py:131
  106.0 1.0 slice-start
  106.1 0.9 copy-start.16
  107.8 10.6 %collective-permute-start.4 = (f32[2,40,256]{2,1,0:T(8,128)S(1)}, f32[2,40,256]{2,1,0:T(8,128)S(1)}, u32[]{:S(2)}, u32[]{:S(2)}) collective-permute-start(f32[2,40,256]{2,1,0:T(8,128)S(1)} %dynamic-slice_bitcast_fusion), channel_id=1, source_target_pairs={{0,256},{8,264},{16,272},{24,280},{32,288},{40,296},{48,304},{56,3... | collective-permute-start | bytes 245768 | tf_op jit(solution)/shard_map/ppermute | solution.py:34
  118.5 9.8 %collective-permute-start.5 = (f32[40,256]{1,0:T(8,128)S(1)}, f32[40,256]{1,0:T(8,128)S(1)}, u32[]{:S(2)}, u32[]{:S(2)}) collective-permute-start(f32[40,256]{1,0:T(8,128)S(1)} %dynamic-slice_bitcast_fusion.1), channel_id=1, source_target_pairs={{0,32},{8,40},{16,48},{24,56},{32,0},{40,8},{48,16},{56,24},{64,96... | collective-permute-start | bytes 122888 | tf_op jit(solution)/shard_map/ppermute | solution.py:34
  128.3 3.1 %collective-permute-start.6 = (f32[40,256]{1,0:T(8,128)S(1)}, f32[40,256]{1,0:T(8,128)S(1)}, u32[]{:S(2)}, u32[]{:S(2)}) collective-permute-start(f32[40,256]{1,0:T(8,128)S(1)} %bitcast_add_fusion.1), channel_id=1, source_target_pairs={{0,8},{8,0},{16,24},{24,16},{32,40},{40,32},{48,56},{56,48},{64,72... | collective-permute-start | bytes 122888 | tf_op jit(solution)/shard_map/ppermute | solution.py:21
  131.4 5.9 %collective-permute-start.7 = (f32[40,256]{1,0:T(8,128)S(1)}, f32[40,256]{1,0:T(8,128)S(1)}, u32[]{:S(2)}, u32[]{:S(2)}) collective-permute-start(f32[40,256]{1,0:T(8,128)S(1)} %add.117), channel_id=1, source_target_pairs={{0,64},{8,72},{16,80},{24,88},{32,96},{40,104},{48,112},{56,120},{... | collective-permute-start | bytes 122888 | tf_op jit(solution)/shard_map/ppermute | solution.py:21
  137.3 6.8 %collective-permute-start.8 = (f32[40,256]{1,0:T(8,128)S(1)}, f32[40,256]{1,0:T(8,128)S(1)}, u32[]{:S(2)}, u32[]{:S(2)}) collective-permute-start(f32[40,256]{1,0:T(8,128)S(1)} %add.118), channel_id=1, source_target_pairs={{0,16},{8,24},{16,0},{24,8},{32,48},{40,56},{48,32},{56,40},{64,80... | collective-permute-start | bytes 122888 | tf_op jit(solution)/shard_map/ppermute | solution.py:21
  144.1 6.8 %collective-permute-start.9 = (f32[40,256]{1,0:T(8,128)S(1)}, f32[40,256]{1,0:T(8,128)S(1)}, u32[]{:S(2)}, u32[]{:S(2)}) collective-permute-start(f32[40,256]{1,0:T(8,128)S(1)} %add.119), channel_id=1, source_target_pairs={{0,128},{8,136},{16,144},{24,152},{32,160},{40,168},{48,176},{56,1... | collective-permute-start | bytes 122888 | tf_op jit(solution)/shard_map/ppermute | solution.py:21
  151.0 9.8 %collective-permute-start.10 = (f32[40,256]{1,0:T(8,128)S(1)}, f32[40,256]{1,0:T(8,128)S(1)}, u32[]{:S(2)}, u32[]{:S(2)}) collective-permute-start(f32[40,256]{1,0:T(8,128)S(1)} %add.120), channel_id=1, source_target_pairs={{0,32},{8,40},{16,48},{24,56},{32,0},{40,8},{48,16},{56,24},{64,96... | collective-permute-start | bytes 122888 | tf_op jit(solution)/shard_map/ppermute | solution.py:39
  160.8 10.9 %collective-permute-start.11 = (f32[2,40,256]{2,1,0:T(8,128)S(1)}, f32[2,40,256]{2,1,0:T(8,128)S(1)}, u32[]{:S(2)}, u32[]{:S(2)}) collective-permute-start(f32[2,40,256]{2,1,0:T(8,128)S(1)} %maximum_select_fusion.2), channel_id=1, source_target_pairs={{0,256},{8,264},{16,272},{24,280},{32,288},{40,296},{48,304},{56,3... | collective-permute-start | bytes 245768 | tf_op jit(solution)/shard_map/ppermute | solution.py:39

commit v12 on v10

--- a/solution.py
+++ b/solution.py
@@ -125,7 +125,14 @@
     packed = jnp.concatenate(
         [local_weight, jnp.broadcast_to(local_bias[None, :], (8, local_bias.shape[0]))], axis=0
     )
-    packed = butterfly_sum(packed, "rows", ROWS_BITS)
+    piece_rows = -(-packed.shape[0] // (8 * replicas)) * 8
+    padded = jnp.pad(packed, ((0, piece_rows * replicas - packed.shape[0]), (0, 0)))
+    mine = lax.dynamic_index_in_dim(
+        padded.reshape((replicas, piece_rows) + packed.shape[1:]), replica, 0, keepdims=False
+    )
+    mine = butterfly_sum(mine, "rows", ROWS_BITS)
+    spread = jnp.broadcast_to(mine[None], (replicas,) + mine.shape)
+    packed = lax.all_to_all(spread, "rep", 0, 0).reshape(-1, packed.shape[1])
     grad_weight = packed[:feat_rows]
     grad_bias = packed[feat_rows]
     share_rows = cotangent.shape[0]

time: 171 us -> 162 us (0.947)
  the two profiles are of different devices: /device:TPU:1 before, /device:TPU:6 now
where the time goes in v12:
time: 162 us; the launch traced here: 159 us
  starting transfers between devices  65.9 us (41%)
  waiting for transfers between devices  47.4 us (29%)
  Pallas kernels  16.1 us (10%)
  blocking collectives  15.5 us (10%)
  local copies, waits for them, and re-layouts  10.4 us (6%)
  other arithmetic  2.06 us (1%)
    ppermute x3, starting transfers between devices, from_behind(): return lax.ppermute(value, axis, pairs)  27.5 us
    ppermute x6, starting transfers between devices, butterfly_sum(): value = value + lax.ppermute(value, axis, pairs)  22.3 us
    ppermute x6, waiting for transfers between devices, butterfly_sum(): value = value + lax.ppermute(value, axis, pairs)  20 us
    pallas_call x4, Pallas kernels, edge_sums_kernel(): pl.pallas_call(_edge_kernel, out_shape=jax.ShapeDtypeStruct((blocks, rows...  16.1 us
    all_to_all x1, blocking collectives, layer(): lax.all_to_all(jnp.concatenate([pieces, cot_copies], axis=-1), 'rep', 0, 0)  15.5 us
    ppermute x3, waiting for transfers between devices, from_behind(): return lax.ppermute(value, axis, pairs)  12.7 us
    ppermute x1, waiting for transfers between devices, layer(): held = lax.ppermute(scaled.T, ('rows', 'rep'), pairs)[None]  5.9 us
    all_to_all x1, starting transfers between devices, layer(): edge_sums = lax.all_to_all(copies, 'rep', 0, 0).reshape(partial_total.shape)  5.73 us
  transfers between devices with their start and end apart: 12, of which 11 were waited for; matrix products, arithmetic and copies ran while one was open for 3% of the time, Pallas kernels for 6%

profile of v12, /device:TPU:6, one launch (start us, length us, event | category | flops | bytes accessed | tf_op | source)
XLA Modules:
  0.0 159.1 jit_solution(13575607985588569449)
XLA Ops:
  0.7 1.0 copy.16
  1.8 4.6 %collective-permute-start = (bf16[128,512]{1,0:T(8,128)(2,1)S(1)}, bf16[128,512]{1,0:T(8,128)(2,1)S(1)}, u32[]{:S(2)}, u32[]{:S(2)}) collective-permute-start(bf16[128,512]{1,0:T(8,128)(2,1)S(1)} %fusion.13), channel_id=1, source_target_pairs={{0,0},{8,8},{16,16},{24,24},{32,32},{40,40},{48,48},{56,56},{64,64... | collective-permute-start | bytes 393224 | tf_op jit(solution)/shard_map/ppermute | solution.py:94
  6.5 0.1 fusion.11
  6.6 5.9 %collective-permute-done = bf16[128,512]{1,0:T(8,128)(2,1)S(1)} collective-permute-done((bf16[128,512]{1,0:T(8,128)(2,1)S(1)}, bf16[128,512]{1,0:T(8,128)(2,1)S(1)}, u32[]{:S(2)}, u32[]{:S(2)}) %collective-permute-start) | collective-permute-done | bytes 131104 | tf_op jit(solution)/shard_map/ppermute | solution.py:94
  12.5 14.1 %collective-permute-start.1 = (bf16[1,128,512]{2,1,0:T(8,128)(2,1)S(1)}, bf16[1,128,512]{2,1,0:T(8,128)(2,1)S(1)}, u32[]{:S(2)}, u32[]{:S(2)}) collective-permute-start(bf16[1,128,512]{2,1,0:T(8,128)(2,1)S(1)} %bitcast.42), channel_id=1, source_target_pairs={{0,480},{8,488},{16,496},{24,504},{32,0},{40,8},{48,16},{56,24},{6... | collective-permute-start | bytes 393224 | tf_op jit(solution)/shard_map/ppermute | solution.py:15
  26.6 0.6 fusion.17
  27.2 1.9 %collective-permute-done.1.bufT_ref = bf16[1,128,512]{2,1,0:T(8,128)(2,1)S(1)} collective-permute-done((bf16[1,128,512]{2,1,0:T(8,128)(2,1)S(1)}, bf16[1,128,512]{2,1,0:T(8,128)(2,1)S(1)}, u32[]{:S(2)}, u32[]{:S(2)}) %collective-permute-start.1) | collective-permute-done | bytes 131104 | tf_op jit(solution)/shard_map/ppermute | solution.py:15
  29.1 11.6 %collective-permute-start.2 = (bf16[2,128,512]{2,1,0:T(8,128)(2,1)S(1)}, bf16[2,128,512]{2,1,0:T(8,128)(2,1)S(1)}, u32[]{:S(2)}, u32[]{:S(2)}) collective-permute-start(bf16[2,128,512]{2,1,0:T(8,128)(2,1)S(1)} %pad_maximum_fusion.2), channel_id=1, source_target_pairs={{0,496},{8,504},{16,0},{24,8},{32,16},{40,24},{48,32},{56,40},{64,... | collective-permute-start | bytes 786440 | tf_op jit(solution)/shard_map/ppermute | solution.py:15
  40.7 0.6 gather_fusion
  41.3 0.6 gather_fusion.1
  41.8 0.6 copy_bitcast_fusion.2
  42.5 10.8 %collective-permute-done.2.bufT_ref = bf16[2,128,512]{2,1,0:T(8,128)(2,1)S(1)} collective-permute-done((bf16[2,128,512]{2,1,0:T(8,128)(2,1)S(1)}, bf16[2,128,512]{2,1,0:T(8,128)(2,1)S(1)}, u32[]{:S(2)}, u32[]{:S(2)}) %collective-permute-start.2) | collective-permute-done | bytes 262176 | tf_op jit(solution)/shard_map/ppermute | solution.py:15
  53.3 0.6 copy-done.7
  54.0 1.9 %collective-permute-start.3 = (bf16[4,128,512]{2,1,0:T(8,128)(2,1)S(1)}, bf16[4,128,512]{2,1,0:T(8,128)(2,1)S(1)}, u32[]{:S(2)}, u32[]{:S(2)}) collective-permute-start(bf16[4,128,512]{2,1,0:T(8,128)(2,1)S(1)} %pad_maximum_fusion.1), channel_id=1, source_target_pairs={{0,504},{8,0},{16,8},{24,16},{32,24},{40,32},{48,40},{56,48},{64,5... | collective-permute-start | bytes 1572872 | tf_op jit(solution)/shard_map/ppermute | solution.py:15
  55.9 0.6 gather_fusion.2
  56.5 0.6 gather_fusion.3
  57.0 0.7 copy_bitcast_fusion
  57.7 3.0 %shard_map.139 = f32[4,128,128]{2,1,0:T(8,128)} custom-call(bf16[1,128,512]{2,1,0:T(8,128)(2,1)} %bitcast.45, s32[4,1,8,128]{3,2,1,0:T(8,128)} %get-tuple-element.57.far_ref, s32[4,1,8,128]{3,2,1,0:T(8,128)} %get-tuple-element.51.tgt_ref), custom_call_target="tpu_custom_call" | custom-call | flops 671088640 | bytes 425984 | tf_op jit(solution)/shard_map/pallas_call | solution.py:61
  60.7 3.0 %shard_map.140 = f32[4,128,128]{2,1,0:T(8,128)} custom-call(bf16[1,128,512]{2,1,0:T(8,128)(2,1)} %copy-done.3, s32[4,1,8,128]{3,2,1,0:T(8,128)} %get-tuple-element.58.far_ref, s32[4,1,8,128]{3,2,1,0:T(8,128)} %get-tuple-element.50.tgt_ref), custom_call_target="tpu_custom_call" | custom-call | flops 671088640 | bytes 425984 | tf_op jit(solution)/shard_map/pallas_call | solution.py:61
  63.6 4.0 %shard_map.141 = f32[4,128,128]{2,1,0:T(8,128)} custom-call(bf16[2,128,512]{2,1,0:T(8,128)(2,1)} %copy-done.7, s32[4,2,8,128]{3,2,1,0:T(8,128)} %get-tuple-element.62.far_ref, s32[4,2,8,128]{3,2,1,0:T(8,128)} %get-tuple-element.61.tgt_ref), custom_call_target="tpu_custom_call" | custom-call | flops 1342177280 | bytes 589824 | tf_op jit(solution)/shard_map/pallas_call | solution.py:61
  67.7 0.8 copy-done.15
  68.5 6.1 %shard_map.142 = f32[4,128,128]{2,1,0:T(8,128)} custom-call(bf16[4,128,512]{2,1,0:T(8,128)(2,1)} %copy-done.15, s32[4,4,8,128]{3,2,1,0:T(8,128)} %get-tuple-element.60.far_ref, s32[4,4,8,128]{3,2,1,0:T(8,128)} %get-tuple-element.59.tgt_ref), custom_call_target="tpu_custom_call" | custom-call | flops 2684354560 | bytes 917504 | tf_op jit(solution)/shard_map/pallas_call | solution.py:61
  74.6 1.0 add_add_fusion
  75.7 15.5 %all_to_all.15 = f32[8,64,384]{2,1,0:T(8,128)S(1)} all-to-all(f32[8,64,384]{2,1,0:T(8,128)S(1)} %pad_maximum_fusion), channel_id=1, replica_groups=mesh['rows'=64,'rep'=8] {'rep'}, dimensions={0} | all-to-all | bytes 1572864 | tf_op jit(solution)/shard_map/all_to_all | solution.py:111
  91.2 0.8 broadcast_in_dim.26
  92.0 5.7 %all-to-all-start.1 = ((f32[8,64,128]{2,1,0:T(8,128)}), f32[8,64,128]{2,1,0:T(8,128)S(1)}, u32[]{:S(2)}, u32[]{:S(2)}) async-start(f32[8,64,128]{2,1,0:T(8,128)} %broadcast_in_dim.26), calls=%async_computation.1 | async-start | bytes 524288 | tf_op jit(solution)/shard_map/all_to_all | solution.py:115
  97.8 4.9 %all-to-all-done.1 = f32[8,64,128]{2,1,0:T(8,128)S(1)} async-done(((f32[8,64,128]{2,1,0:T(8,128)}), f32[8,64,128]{2,1,0:T(8,128)S(1)}, u32[]{:S(2)}, u32[]{:S(2)}) %all-to-all-start.1) | async-done | bytes 262176 | tf_op jit(solution)/shard_map/all_to_all | solution.py:115
  102.9 0.8 slice-done
  103.7 0.6 convert_reduce_fusion
  104.3 0.2 fusion.19
  104.5 1.9 %collective-permute-start.4 = (f32[24,256]{1,0:T(8,128)S(1)}, f32[24,256]{1,0:T(8,128)S(1)}, u32[]{:S(2)}, u32[]{:S(2)}) collective-permute-start(f32[24,256]{1,0:T(8,128)S(1)} %dynamic-slice_bitcast_fusion), channel_id=1, source_target_pairs={{0,8},{8,0},{16,24},{24,16},{32,40},{40,32},{48,56},{56,48},{64,72... | collective-permute-start | bytes 73736 | tf_op jit(solution)/shard_map/ppermute | solution.py:24
  106.5 1.2 collective-permute-done.4
  107.6 2.4 %collective-permute-start.5 = (f32[24,256]{1,0:T(8,128)S(1)}, f32[24,256]{1,0:T(8,128)S(1)}, u32[]{:S(2)}, u32[]{:S(2)}) collective-permute-start(f32[24,256]{1,0:T(8,128)S(1)} %fusion.24), channel_id=1, source_target_pairs={{0,64},{8,72},{16,80},{24,88},{32,96},{40,104},{48,112},{56,120},{... | collective-permute-start | bytes 73736 | tf_op jit(solution)/shard_map/ppermute | solution.py:24
  110.1 3.3 %collective-permute-done.5 = f32[24,256]{1,0:T(8,128)S(1)} collective-permute-done((f32[24,256]{1,0:T(8,128)S(1)}, f32[24,256]{1,0:T(8,128)S(1)}, u32[]{:S(2)}, u32[]{:S(2)}) %collective-permute-start.5) | collective-permute-done | bytes 24608 | tf_op jit(solution)/shard_map/ppermute | solution.py:24
  113.3 1.9 %collective-permute-start.6 = (f32[24,256]{1,0:T(8,128)S(1)}, f32[24,256]{1,0:T(8,128)S(1)}, u32[]{:S(2)}, u32[]{:S(2)}) collective-permute-start(f32[24,256]{1,0:T(8,128)S(1)} %add.103), channel_id=1, source_target_pairs={{0,16},{8,24},{16,0},{24,8},{32,48},{40,56},{48,32},{56,40},{64,80... | collective-permute-start | bytes 73736 | tf_op jit(solution)/shard_map/ppermute | solution.py:24
  115.3 4.7 %collective-permute-done.6 = f32[24,256]{1,0:T(8,128)S(1)} collective-permute-done((f32[24,256]{1,0:T(8,128)S(1)}, f32[24,256]{1,0:T(8,128)S(1)}, u32[]{:S(2)}, u32[]{:S(2)}) %collective-permute-start.6) | collective-permute-done | bytes 24608 | tf_op jit(solution)/shard_map/ppermute | solution.py:24
  120.0 5.9 %collective-permute-start.7 = (f32[24,256]{1,0:T(8,128)S(1)}, f32[24,256]{1,0:T(8,128)S(1)}, u32[]{:S(2)}, u32[]{:S(2)}) collective-permute-start(f32[24,256]{1,0:T(8,128)S(1)} %add.104), channel_id=1, source_target_pairs={{0,128},{8,136},{16,144},{24,152},{32,160},{40,168},{48,176},{56,1... | collective-permute-start | bytes 73736 | tf_op jit(solution)/shard_map/ppermute | solution.py:24
  125.8 1.8 %collective-permute-done.7 = f32[24,256]{1,0:T(8,128)S(1)} collective-permute-done((f32[24,256]{1,0:T(8,128)S(1)}, f32[24,256]{1,0:T(8,128)S(1)}, u32[]{:S(2)}, u32[]{:S(2)}) %collective-permute-start.7) | collective-permute-done | bytes 24608 | tf_op jit(solution)/shard_map/ppermute | solution.py:24
  127.6 4.5 %collective-permute-start.8 = (f32[24,256]{1,0:T(8,128)S(1)}, f32[24,256]{1,0:T(8,128)S(1)}, u32[]{:S(2)}, u32[]{:S(2)}) collective-permute-start(f32[24,256]{1,0:T(8,128)S(1)} %add.105), channel_id=1, source_target_pairs={{0,32},{8,40},{16,48},{24,56},{32,0},{40,8},{48,16},{56,24},{64,96... | collective-permute-start | bytes 73736 | tf_op jit(solution)/shard_map/ppermute | solution.py:24
  132.1 5.1 %collective-permute-done.8 = f32[24,256]{1,0:T(8,128)S(1)} collective-permute-done((f32[24,256]{1,0:T(8,128)S(1)}, f32[24,256]{1,0:T(8,128)S(1)}, u32[]{:S(2)}, u32[]{:S(2)}) %collective-permute-start.8) | collective-permute-done | bytes 24608 | tf_op jit(solution)/shard_map/ppermute | solution.py:24
  137.3 5.7 %collective-permute-start.9 = (f32[24,256]{1,0:T(8,128)S(1)}, f32[24,256]{1,0:T(8,128)S(1)}, u32[]{:S(2)}, u32[]{:S(2)}) collective-permute-start(f32[24,256]{1,0:T(8,128)S(1)} %add.106), channel_id=1, source_target_pairs={{0,256},{8,264},{16,272},{24,280},{32,288},{40,296},{48,304},{56,3... | collective-permute-start | bytes 73736 | tf_op jit(solution)/shard_map/ppermute | solution.py:24
  143.0 3.9 %collective-permute-done.9 = f32[24,256]{1,0:T(8,128)S(1)} collective-permute-done((f32[24,256]{1,0:T(8,128)S(1)}, f32[24,256]{1,0:T(8,128)S(1)}, u32[]{:S(2)}, u32[]{:S(2)}) %collective-permute-start.9) | collective-permute-done | bytes 24608 | tf_op jit(solution)/shard_map/ppermute | solution.py:24
  146.9 0.7 broadcast_in_dim.28
  147.6 5.7 %all-to-all-start.2 = ((f32[8,24,256]{2,1,0:T(8,128)}), f32[8,24,256]{2,1,0:T(8,128)S(1)}, u32[]{:S(2)}, u32[]{:S(2)}) async-start(f32[8,24,256]{2,1,0:T(8,128)} %broadcast_in_dim.28), calls=%async_computation.2 | async-start | bytes 393216 | tf_op jit(solution)/shard_map/all_to_all | solution.py:135
  153.3 0.6 fusion.15
  153.9 4.0 %all-to-all-done.2 = f32[8,24,256]{2,1,0:T(8,128)S(1)} async-done(((f32[8,24,256]{2,1,0:T(8,128)}), f32[8,24,256]{2,1,0:T(8,128)S(1)}, u32[]{:S(2)}, u32[]{:S(2)}) %all-to-all-start.2) | async-done | bytes 196640 | tf_op jit(solution)/shard_map/all_to_all | solution.py:135
  157.9 0.7 slice.78
  158.6 0.6 slice.79
  (55 shorter events, 0.5 us)
Async XLA Ops:
  0.6 102.2 %copy-start = (bf16[128,256]{1,0:T(8,128)(2,1)S(1)}, bf16[128,256]{1,0:T(8,128)(2,1)}, u32[]{:S(2)}) copy-start(bf16[128,256]{1,0:T(8,128)(2,1)} %param.17) | copy-start | bytes 196612
  0.6 1.1 copy-start.12
  1.7 4.7 %copy-start.10 = (s32[4,8,8]{2,1,0:T(8,128)S(1)}, s32[4,8,8]{2,1,0:T(8,128)}, u32[]{:S(2)}) copy-start(s32[4,8,8]{2,1,0:T(8,128)} %param.14) | copy-start | bytes 3076
  1.7 4.7 %copy-start.8 = (s32[4,8,8,128]{3,2,1,0:T(8,128)S(1)}, s32[4,8,8,128]{3,2,1,0:T(8,128)}, u32[]{:S(2)}) copy-start(s32[4,8,8,128]{3,2,1,0:T(8,128)} %param.16) | copy-start | bytes 393220
  1.8 4.7 %copy-start.11 = (s32[4,8,8]{2,1,0:T(8,128)S(1)}, s32[4,8,8]{2,1,0:T(8,128)}, u32[]{:S(2)}) copy-start(s32[4,8,8]{2,1,0:T(8,128)} %param.15) | copy-start | bytes 3076
  1.8 10.7 %collective-permute-start = (bf16[128,512]{1,0:T(8,128)(2,1)S(1)}, bf16[128,512]{1,0:T(8,128)(2,1)S(1)}, u32[]{:S(2)}, u32[]{:S(2)}) collective-permute-start(bf16[128,512]{1,0:T(8,128)(2,1)S(1)} %fusion.13), channel_id=1, source_target_pairs={{0,0},{8,8},{16,16},{24,24},{32,32},{40,40},{48,48},{56,56},{64,64... | collective-permute-start | bytes 393224 | tf_op jit(solution)/shard_map/ppermute | solution.py:94
  12.5 40.7 %copy-start.2 = (bf16[128,512]{1,0:T(8,128)(2,1)}, bf16[128,512]{1,0:T(8,128)(2,1)S(1)}, u32[]{:S(2)}) copy-start(bf16[128,512]{1,0:T(8,128)(2,1)S(1)} %collective-permute-done) | copy-start | bytes 393220
  12.5 16.6 %collective-permute-start.1 = (bf16[1,128,512]{2,1,0:T(8,128)(2,1)S(1)}, bf16[1,128,512]{2,1,0:T(8,128)(2,1)S(1)}, u32[]{:S(2)}, u32[]{:S(2)}) collective-permute-start(bf16[1,128,512]{2,1,0:T(8,128)(2,1)S(1)} %bitcast.42), channel_id=1, source_target_pairs={{0,480},{8,488},{16,496},{24,504},{32,0},{40,8},{48,16},{56,24},{6... | collective-permute-start | bytes 393224 | tf_op jit(solution)/shard_map/ppermute | solution.py:15
  27.2 13.4 %copy-start.14 = (s32[2]{0:T(128)S(1)}, s32[2]{0:T(128)}, u32[]{:S(2)}) copy-start(s32[2]{0:T(128)} %constant.175) | copy-start | bytes 28
  29.1 24.2 %copy-start.3 = (bf16[1,128,512]{2,1,0:T(8,128)(2,1)}, bf16[1,128,512]{2,1,0:T(8,128)(2,1)S(1)}, u32[]{:S(2)}) copy-start(bf16[1,128,512]{2,1,0:T(8,128)(2,1)S(1)} %collective-permute-done.1.bufT_ref) | copy-start | bytes 393220
  29.1 24.1 %collective-permute-start.2 = (bf16[2,128,512]{2,1,0:T(8,128)(2,1)S(1)}, bf16[2,128,512]{2,1,0:T(8,128)(2,1)S(1)}, u32[]{:S(2)}, u32[]{:S(2)}) collective-permute-start(bf16[2,128,512]{2,1,0:T(8,128)(2,1)S(1)} %pad_maximum_fusion.2), channel_id=1, source_target_pairs={{0,496},{8,504},{16,0},{24,8},{32,16},{40,24},{48,32},{56,40},{64,... | collective-permute-start | bytes 786440 | tf_op jit(solution)/shard_map/ppermute | solution.py:15
  42.4 13.4 %copy-start.13 = (s32[4]{0:T(128)S(1)}, s32[4]{0:T(128)}, u32[]{:S(2)}) copy-start(s32[4]{0:T(128)} %constant.177) | copy-start | bytes 52
  53.3 0.7 copy-start.7
  54.0 13.7 %collective-permute-start.3 = (bf16[4,128,512]{2,1,0:T(8,128)(2,1)S(1)}, bf16[4,128,512]{2,1,0:T(8,128)(2,1)S(1)}, u32[]{:S(2)}, u32[]{:S(2)}) collective-permute-start(bf16[4,128,512]{2,1,0:T(8,128)(2,1)S(1)} %pad_maximum_fusion.1), channel_id=1, source_target_pairs={{0,504},{8,0},{16,8},{24,16},{32,24},{40,32},{48,40},{56,48},{64,5... | collective-permute-start | bytes 1572872 | tf_op jit(solution)/shard_map/ppermute | solution.py:15
  67.7 0.8 copy-start.15
  68.5 6.1 %copy-start.4 = (f32[4,128,128]{2,1,0:T(8,128)S(1)}, f32[4,128,128]{2,1,0:T(8,128)}, u32[]{:S(2)}) copy-start(f32[4,128,128]{2,1,0:T(8,128)} %shard_map.139) | copy-start | bytes 786436
  68.5 6.1 %copy-start.5 = (f32[4,128,128]{2,1,0:T(8,128)S(1)}, f32[4,128,128]{2,1,0:T(8,128)}, u32[]{:S(2)}) copy-start(f32[4,128,128]{2,1,0:T(8,128)} %shard_map.140) | copy-start | bytes 786436
  68.5 6.1 %copy-start.6 = (f32[4,128,128]{2,1,0:T(8,128)S(1)}, f32[4,128,128]{2,1,0:T(8,128)}, u32[]{:S(2)}) copy-start(f32[4,128,128]{2,1,0:T(8,128)} %shard_map.141) | copy-start | bytes 786436
  74.6 1.0 copy-start.9
  91.2 6.5 %copy-start.1 = (f32[8,64,384]{2,1,0:T(8,128)}, f32[8,64,384]{2,1,0:T(8,128)S(1)}, u32[]{:S(2)}) copy-start(f32[8,64,384]{2,1,0:T(8,128)S(1)} %all_to_all.15) | copy-start | bytes 2359300
  92.0 10.6 %all-to-all-start.1 = ((f32[8,64,128]{2,1,0:T(8,128)}), f32[8,64,128]{2,1,0:T(8,128)S(1)}, u32[]{:S(2)}, u32[]{:S(2)}) async-start(f32[8,64,128]{2,1,0:T(8,128)} %broadcast_in_dim.26), calls=%async_computation.1 | async-start | bytes 524288 | tf_op jit(solution)/shard_map/all_to_all | solution.py:115
  102.7 1.0 slice-start
  102.8 0.9 copy-start.16
  104.5 3.1 %collective-permute-start.4 = (f32[24,256]{1,0:T(8,128)S(1)}, f32[24,256]{1,0:T(8,128)S(1)}, u32[]{:S(2)}, u32[]{:S(2)}) collective-permute-start(f32[24,256]{1,0:T(8,128)S(1)} %dynamic-slice_bitcast_fusion), channel_id=1, source_target_pairs={{0,8},{8,0},{16,24},{24,16},{32,40},{40,32},{48,56},{56,48},{64,72... | collective-permute-start | bytes 73736 | tf_op jit(solution)/shard_map/ppermute | solution.py:24
  107.6 5.7 %collective-permute-start.5 = (f32[24,256]{1,0:T(8,128)S(1)}, f32[24,256]{1,0:T(8,128)S(1)}, u32[]{:S(2)}, u32[]{:S(2)}) collective-permute-start(f32[24,256]{1,0:T(8,128)S(1)} %fusion.24), channel_id=1, source_target_pairs={{0,64},{8,72},{16,80},{24,88},{32,96},{40,104},{48,112},{56,120},{... | collective-permute-start | bytes 73736 | tf_op jit(solution)/shard_map/ppermute | solution.py:24
  113.3 6.6 %collective-permute-start.6 = (f32[24,256]{1,0:T(8,128)S(1)}, f32[24,256]{1,0:T(8,128)S(1)}, u32[]{:S(2)}, u32[]{:S(2)}) collective-permute-start(f32[24,256]{1,0:T(8,128)S(1)} %add.103), channel_id=1, source_target_pairs={{0,16},{8,24},{16,0},{24,8},{32,48},{40,56},{48,32},{56,40},{64,80... | collective-permute-start | bytes 73736 | tf_op jit(solution)/shard_map/ppermute | solution.py:24
  120.0 7.7 %collective-permute-start.7 = (f32[24,256]{1,0:T(8,128)S(1)}, f32[24,256]{1,0:T(8,128)S(1)}, u32[]{:S(2)}, u32[]{:S(2)}) collective-permute-start(f32[24,256]{1,0:T(8,128)S(1)} %add.104), channel_id=1, source_target_pairs={{0,128},{8,136},{16,144},{24,152},{32,160},{40,168},{48,176},{56,1... | collective-permute-start | bytes 73736 | tf_op jit(solution)/shard_map/ppermute | solution.py:24
  127.6 9.6 %collective-permute-start.8 = (f32[24,256]{1,0:T(8,128)S(1)}, f32[24,256]{1,0:T(8,128)S(1)}, u32[]{:S(2)}, u32[]{:S(2)}) collective-permute-start(f32[24,256]{1,0:T(8,128)S(1)} %add.105), channel_id=1, source_target_pairs={{0,32},{8,40},{16,48},{24,56},{32,0},{40,8},{48,16},{56,24},{64,96... | collective-permute-start | bytes 73736 | tf_op jit(solution)/shard_map/ppermute | solution.py:24
  137.3 9.6 %collective-permute-start.9 = (f32[24,256]{1,0:T(8,128)S(1)}, f32[24,256]{1,0:T(8,128)S(1)}, u32[]{:S(2)}, u32[]{:S(2)}) collective-permute-start(f32[24,256]{1,0:T(8,128)S(1)} %add.106), channel_id=1, source_target_pairs={{0,256},{8,264},{16,272},{24,280},{32,288},{40,296},{48,304},{56,3... | collective-permute-start | bytes 73736 | tf_op jit(solution)/shard_map/ppermute | solution.py:24
  147.6 10.3 %all-to-all-start.2 = ((f32[8,24,256]{2,1,0:T(8,128)}), f32[8,24,256]{2,1,0:T(8,128)S(1)}, u32[]{:S(2)}, u32[]{:S(2)}) async-start(f32[8,24,256]{2,1,0:T(8,128)} %broadcast_in_dim.28), calls=%async_computation.2 | async-start | bytes 393216 | tf_op jit(solution)/shard_map/all_to_all | solution.py:135

commit v13 on v12

--- a/solution.py
+++ b/solution.py
@@ -104,19 +104,16 @@
         offsets = offsets + arrived_offsets
     partial_total = partial_total.reshape(-1, partial_total.shape[-1])
     pieces = partial_total.reshape((replicas, -1) + partial_total.shape[1:])
-    cot_copies = jnp.broadcast_to(
-        cotangent.astype(jnp.float32)[None], (replicas,) + cotangent.shape
-    )
-    feat_width = pieces.shape[-1]
-    pieces = lax.all_to_all(jnp.concatenate([pieces, cot_copies], axis=-1), "rep", 0, 0)
-    share = jnp.sum(pieces[..., :feat_width], axis=0)
-    cot_group = pieces[..., feat_width:].reshape(-1, cotangent.shape[1])
-    copies = jnp.broadcast_to(share[None], (replicas,) + share.shape)
-    edge_sums = lax.all_to_all(copies, "rep", 0, 0).reshape(partial_total.shape)
-    aggregate = (inv_deg[:, None] * (edge_sums + scaled.astype(jnp.float32))).astype(jnp.bfloat16)
+    pieces = lax.all_to_all(pieces.astype(jnp.bfloat16), "rep", 0, 0)
+    edge_sums = jnp.sum(pieces.astype(jnp.float32), axis=0)
+    share_rows = edge_sums.shape[0]
+    share_start = replica * share_rows
+    own_rows = lax.dynamic_slice_in_dim(scaled, share_start, share_rows, 0).astype(jnp.float32)
+    own_inv = lax.dynamic_slice_in_dim(inv_deg, share_start, share_rows, 0)
+    aggregate = (own_inv[:, None] * (edge_sums + own_rows)).astype(jnp.bfloat16)
     pre_act = jnp.dot(aggregate, weight, preferred_element_type=jnp.float32) + bias
     activated, pull_back = jax.vjp(gelu_tanh, pre_act)
-    delta_bf = pull_back(cot_group)[0].astype(jnp.bfloat16)
+    delta_bf = pull_back(cotangent.astype(jnp.float32))[0].astype(jnp.bfloat16)
     local_weight = lax.dot_general(
         aggregate, delta_bf, (((0,), (0,)), ((), ())), preferred_element_type=jnp.float32
     )
@@ -127,17 +124,15 @@
     )
     piece_rows = -(-packed.shape[0] // (8 * replicas)) * 8
     padded = jnp.pad(packed, ((0, piece_rows * replicas - packed.shape[0]), (0, 0)))
-    mine = lax.dynamic_index_in_dim(
-        padded.reshape((replicas, piece_rows) + packed.shape[1:]), replica, 0, keepdims=False
+    parts = lax.all_to_all(
+        padded.reshape((replicas, piece_rows) + packed.shape[1:]), "rep", 0, 0
     )
-    mine = butterfly_sum(mine, "rows", ROWS_BITS)
+    mine = butterfly_sum(jnp.sum(parts, axis=0), "rows", ROWS_BITS)
     spread = jnp.broadcast_to(mine[None], (replicas,) + mine.shape)
     packed = lax.all_to_all(spread, "rep", 0, 0).reshape(-1, packed.shape[1])
     grad_weight = packed[:feat_rows]
     grad_bias = packed[feat_rows]
-    share_rows = cotangent.shape[0]
-    own_act = lax.dynamic_slice_in_dim(activated, replica * share_rows, share_rows, 0)
-    return (own_act.astype(jnp.bfloat16), grad_weight, grad_bias)
+    return (activated.astype(jnp.bfloat16), grad_weight, grad_bias)
 
 
 def solution(mesh):

time: 162 us -> 153 us (0.944)
  the two profiles are of different devices: /device:TPU:6 before, /device:TPU:24 now
where the time goes in v13:
time: 153 us; the launch traced here: 152 us
  starting transfers between devices  61.1 us (40%)
  waiting for transfers between devices  42.8 us (28%)
  blocking collectives  18.8 us (12%)
  Pallas kernels  16 us (10%)
  local copies, waits for them, and re-layouts  8.71 us (6%)
  other arithmetic  2.83 us (2%)
    ppermute x6, waiting for transfers between devices, butterfly_sum(): value = value + lax.ppermute(value, axis, pairs)  27 us
    ppermute x3, starting transfers between devices, from_behind(): return lax.ppermute(value, axis, pairs)  23.8 us
    all_to_all x1, starting transfers between devices, layer(): pieces = lax.all_to_all(pieces.astype(jnp.bfloat16), 'rep', 0, 0)  22.1 us
    pallas_call x4, Pallas kernels, edge_sums_kernel(): pl.pallas_call(_edge_kernel, out_shape=jax.ShapeDtypeStruct((blocks, rows...  16 us
    ppermute x6, starting transfers between devices, butterfly_sum(): value = value + lax.ppermute(value, axis, pairs)  14.5 us
    all_to_all x1, blocking collectives, layer(): packed = lax.all_to_all(spread, 'rep', 0, 0).reshape(-1, packed.shape[1])  9.47 us
    all_to_all x1, blocking collectives, layer(): lax.all_to_all(padded.reshape((replicas, piece_rows) + packed.shape[1:]),...  9.38 us
    ppermute x3, waiting for transfers between devices, from_behind(): return lax.ppermute(value, axis, pairs)  9.12 us
  transfers between devices with their start and end apart: 11, of which 9 were waited for; matrix products, arithmetic and copies ran while one was open for 3% of the time, Pallas kernels for 7%

profile of v13, /device:TPU:24, one launch (start us, length us, event | category | flops | bytes accessed | tf_op | source)
XLA Modules:
  0.0 152.2 jit_solution(14247982736454718669)
XLA Ops:
  0.6 0.7 convert_rsqrt_fusion
  1.4 1.0 copy.21
  2.4 0.8 collective-permute-start
  3.3 0.1 fusion.1
  3.5 10.8 %collective-permute-start.1 = (bf16[1,128,512]{2,1,0:T(8,128)(2,1)S(1)}, bf16[1,128,512]{2,1,0:T(8,128)(2,1)S(1)}, u32[]{:S(2)}, u32[]{:S(2)}) collective-permute-start(bf16[1,128,512]{2,1,0:T(8,128)(2,1)S(1)} %bitcast.22), channel_id=1, source_target_pairs={{0,480},{8,488},{16,496},{24,504},{32,0},{40,8},{48,16},{56,24},{6... | collective-permute-start | bytes 393224 | tf_op jit(solution)/shard_map/ppermute | solution.py:15
  14.3 0.6 fusion.15
  14.9 3.1 %collective-permute-done.1.bufT_ref = bf16[1,128,512]{2,1,0:T(8,128)(2,1)S(1)} collective-permute-done((bf16[1,128,512]{2,1,0:T(8,128)(2,1)S(1)}, bf16[1,128,512]{2,1,0:T(8,128)(2,1)S(1)}, u32[]{:S(2)}, u32[]{:S(2)}) %collective-permute-start.1) | collective-permute-done | bytes 131104 | tf_op jit(solution)/shard_map/ppermute | solution.py:15
  18.0 11.0 %collective-permute-start.2 = (bf16[2,128,512]{2,1,0:T(8,128)(2,1)S(1)}, bf16[2,128,512]{2,1,0:T(8,128)(2,1)S(1)}, u32[]{:S(2)}, u32[]{:S(2)}) collective-permute-start(bf16[2,128,512]{2,1,0:T(8,128)(2,1)S(1)} %pad_maximum_fusion.1), channel_id=1, source_target_pairs={{0,496},{8,504},{16,0},{24,8},{32,16},{40,24},{48,32},{56,40},{64,... | collective-permute-start | bytes 786440 | tf_op jit(solution)/shard_map/ppermute | solution.py:15
  29.1 0.6 gather_fusion
  29.6 0.6 gather_fusion.1
  30.2 0.6 copy_bitcast_fusion.2
  30.8 6.1 %collective-permute-done.2.bufT_ref = bf16[2,128,512]{2,1,0:T(8,128)(2,1)S(1)} collective-permute-done((bf16[2,128,512]{2,1,0:T(8,128)(2,1)S(1)}, bf16[2,128,512]{2,1,0:T(8,128)(2,1)S(1)}, u32[]{:S(2)}, u32[]{:S(2)}) %collective-permute-start.2) | collective-permute-done | bytes 262176 | tf_op jit(solution)/shard_map/ppermute | solution.py:15
  36.9 0.1 pad_maximum_fusion
  36.9 0.6 copy-done.3
  37.6 1.9 %collective-permute-start.3 = (bf16[4,128,512]{2,1,0:T(8,128)(2,1)S(1)}, bf16[4,128,512]{2,1,0:T(8,128)(2,1)S(1)}, u32[]{:S(2)}, u32[]{:S(2)}) collective-permute-start(bf16[4,128,512]{2,1,0:T(8,128)(2,1)S(1)} %pad_maximum_fusion), channel_id=1, source_target_pairs={{0,504},{8,0},{16,8},{24,16},{32,24},{40,32},{48,40},{56,48},{64,5... | collective-permute-start | bytes 1572872 | tf_op jit(solution)/shard_map/ppermute | solution.py:15
  39.5 0.6 gather_fusion.2
  40.1 0.6 gather_fusion.3
  40.6 0.1 dynamic_slice.6
  40.7 0.7 copy_bitcast_fusion
  41.4 2.9 %shard_map.139 = f32[4,128,128]{2,1,0:T(8,128)} custom-call(bf16[1,128,512]{2,1,0:T(8,128)(2,1)} %bitcast.25, s32[4,1,8,128]{3,2,1,0:T(8,128)} %get-tuple-element.56.far_ref, s32[4,1,8,128]{3,2,1,0:T(8,128)} %get-tuple-element.50.tgt_ref), custom_call_target="tpu_custom_call" | custom-call | flops 671088640 | bytes 425984 | tf_op jit(solution)/shard_map/pallas_call | solution.py:61
  44.3 3.0 %shard_map.140 = f32[4,128,128]{2,1,0:T(8,128)} custom-call(bf16[1,128,512]{2,1,0:T(8,128)(2,1)} %copy-done.2, s32[4,1,8,128]{3,2,1,0:T(8,128)} %get-tuple-element.57.far_ref, s32[4,1,8,128]{3,2,1,0:T(8,128)} %get-tuple-element.49.tgt_ref), custom_call_target="tpu_custom_call" | custom-call | flops 671088640 | bytes 425984 | tf_op jit(solution)/shard_map/pallas_call | solution.py:61
  47.3 4.0 %shard_map.141 = f32[4,128,128]{2,1,0:T(8,128)} custom-call(bf16[2,128,512]{2,1,0:T(8,128)(2,1)} %copy-done.3, s32[4,2,8,128]{3,2,1,0:T(8,128)} %get-tuple-element.61.far_ref, s32[4,2,8,128]{3,2,1,0:T(8,128)} %get-tuple-element.60.tgt_ref), custom_call_target="tpu_custom_call" | custom-call | flops 1342177280 | bytes 589824 | tf_op jit(solution)/shard_map/pallas_call | solution.py:61
  51.3 0.8 copy-done.12
  52.1 6.0 %shard_map.142 = f32[4,128,128]{2,1,0:T(8,128)} custom-call(bf16[4,128,512]{2,1,0:T(8,128)(2,1)} %copy-done.12, s32[4,4,8,128]{3,2,1,0:T(8,128)} %get-tuple-element.59.far_ref, s32[4,4,8,128]{3,2,1,0:T(8,128)} %get-tuple-element.58.tgt_ref), custom_call_target="tpu_custom_call" | custom-call | flops 2684354560 | bytes 917504 | tf_op jit(solution)/shard_map/pallas_call | solution.py:61
  58.2 1.7 %add_convert_fusion = bf16[4,128,128]{2,1,0:T(8,128)(2,1)} fusion(f32[4,128,128]{2,1,0:T(8,128)} %shard_map.142, f32[4,128,128]{2,1,0:T(8,128)S(1)} %copy-done.6, f32[4,128,128]{2,1,0:T(8,128)S(1)} %copy-done.4, f32[4,128,128]{2,1,0:T(8,128)S(1)} %copy-done.5), kind=kLoop, calls=%fused_computation.8 | loop fusion | flops 262144 | bytes 1179648 | tf_op jit(solution)/shard_map/convert_element_type | solution.py:107
  59.9 22.1 %all-to-all-start = ((bf16[8,64,128]{2,1,0:T(8,128)(2,1)}), bf16[8,64,128]{2,1,0:T(8,128)(2,1)S(1)}, u32[]{:S(2)}, u32[]{:S(2)}) async-start(bf16[8,64,128]{2,1,0:T(8,128)(2,1)} %bitcast.6), calls=%async_computation | async-start | bytes 262144 | tf_op jit(solution)/shard_map/all_to_all | solution.py:107
  82.0 6.7 %all-to-all-done = bf16[8,64,128]{2,1,0:T(8,128)(2,1)S(1)} async-done(((bf16[8,64,128]{2,1,0:T(8,128)(2,1)}), bf16[8,64,128]{2,1,0:T(8,128)(2,1)S(1)}, u32[]{:S(2)}, u32[]{:S(2)}) %all-to-all-start) | async-done | bytes 131104 | tf_op jit(solution)/shard_map/all_to_all | solution.py:107
  88.7 0.1 copy.26
  88.8 0.1 multiply_convert_fusion.2
  88.9 0.6 copy-done.13
  89.6 0.8 convert_reduce_fusion.1
  90.4 0.1 fusion.17
  90.6 9.4 %all_to_all.15 = f32[8,24,256]{2,1,0:T(8,128)S(1)} all-to-all(f32[8,24,256]{2,1,0:T(8,128)S(1)} %bitcast.19), channel_id=1, replica_groups=mesh['rows'=64,'rep'=8] {'rep'}, dimensions={0} | all-to-all | bytes 393216 | tf_op jit(solution)/shard_map/all_to_all | solution.py:127
  100.0 1.9 %collective-permute-start.4 = (f32[24,256]{1,0:T(8,128)S(1)}, f32[24,256]{1,0:T(8,128)S(1)}, u32[]{:S(2)}, u32[]{:S(2)}) collective-permute-start(f32[24,256]{1,0:T(8,128)S(1)} %reduce_sum.29), channel_id=1, source_target_pairs={{0,8},{8,0},{16,24},{24,16},{32,40},{40,32},{48,56},{56,48},{64,72... | collective-permute-start | bytes 73736 | tf_op jit(solution)/shard_map/ppermute | solution.py:24
  101.9 1.2 collective-permute-done.4
  103.1 2.5 %collective-permute-start.5 = (f32[24,256]{1,0:T(8,128)S(1)}, f32[24,256]{1,0:T(8,128)S(1)}, u32[]{:S(2)}, u32[]{:S(2)}) collective-permute-start(f32[24,256]{1,0:T(8,128)S(1)} %add.98), channel_id=1, source_target_pairs={{0,64},{8,72},{16,80},{24,88},{32,96},{40,104},{48,112},{56,120},{... | collective-permute-start | bytes 73736 | tf_op jit(solution)/shard_map/ppermute | solution.py:24
  105.5 3.2 %collective-permute-done.5 = f32[24,256]{1,0:T(8,128)S(1)} collective-permute-done((f32[24,256]{1,0:T(8,128)S(1)}, f32[24,256]{1,0:T(8,128)S(1)}, u32[]{:S(2)}, u32[]{:S(2)}) %collective-permute-start.5) | collective-permute-done | bytes 24608 | tf_op jit(solution)/shard_map/ppermute | solution.py:24
  108.8 2.2 %collective-permute-start.6 = (f32[24,256]{1,0:T(8,128)S(1)}, f32[24,256]{1,0:T(8,128)S(1)}, u32[]{:S(2)}, u32[]{:S(2)}) collective-permute-start(f32[24,256]{1,0:T(8,128)S(1)} %add.99), channel_id=1, source_target_pairs={{0,16},{8,24},{16,0},{24,8},{32,48},{40,56},{48,32},{56,40},{64,80... | collective-permute-start | bytes 73736 | tf_op jit(solution)/shard_map/ppermute | solution.py:24
  111.0 4.4 %collective-permute-done.6 = f32[24,256]{1,0:T(8,128)S(1)} collective-permute-done((f32[24,256]{1,0:T(8,128)S(1)}, f32[24,256]{1,0:T(8,128)S(1)}, u32[]{:S(2)}, u32[]{:S(2)}) %collective-permute-start.6) | collective-permute-done | bytes 24608 | tf_op jit(solution)/shard_map/ppermute | solution.py:24
  115.4 1.9 %collective-permute-start.7 = (f32[24,256]{1,0:T(8,128)S(1)}, f32[24,256]{1,0:T(8,128)S(1)}, u32[]{:S(2)}, u32[]{:S(2)}) collective-permute-start(f32[24,256]{1,0:T(8,128)S(1)} %add.100), channel_id=1, source_target_pairs={{0,128},{8,136},{16,144},{24,152},{32,160},{40,168},{48,176},{56,1... | collective-permute-start | bytes 73736 | tf_op jit(solution)/shard_map/ppermute | solution.py:24
  117.3 4.9 %collective-permute-done.7 = f32[24,256]{1,0:T(8,128)S(1)} collective-permute-done((f32[24,256]{1,0:T(8,128)S(1)}, f32[24,256]{1,0:T(8,128)S(1)}, u32[]{:S(2)}, u32[]{:S(2)}) %collective-permute-start.7) | collective-permute-done | bytes 24608 | tf_op jit(solution)/shard_map/ppermute | solution.py:24
  122.3 2.7 %collective-permute-start.8 = (f32[24,256]{1,0:T(8,128)S(1)}, f32[24,256]{1,0:T(8,128)S(1)}, u32[]{:S(2)}, u32[]{:S(2)}) collective-permute-start(f32[24,256]{1,0:T(8,128)S(1)} %add.101), channel_id=1, source_target_pairs={{0,32},{8,40},{16,48},{24,56},{32,0},{40,8},{48,16},{56,24},{64,96... | collective-permute-start | bytes 73736 | tf_op jit(solution)/shard_map/ppermute | solution.py:24
  125.0 6.9 %collective-permute-done.8 = f32[24,256]{1,0:T(8,128)S(1)} collective-permute-done((f32[24,256]{1,0:T(8,128)S(1)}, f32[24,256]{1,0:T(8,128)S(1)}, u32[]{:S(2)}, u32[]{:S(2)}) %collective-permute-start.8) | collective-permute-done | bytes 24608 | tf_op jit(solution)/shard_map/ppermute | solution.py:24
  131.9 3.3 %collective-permute-start.9 = (f32[24,256]{1,0:T(8,128)S(1)}, f32[24,256]{1,0:T(8,128)S(1)}, u32[]{:S(2)}, u32[]{:S(2)}) collective-permute-start(f32[24,256]{1,0:T(8,128)S(1)} %add.102), channel_id=1, source_target_pairs={{0,256},{8,264},{16,272},{24,280},{32,288},{40,296},{48,304},{56,3... | collective-permute-start | bytes 73736 | tf_op jit(solution)/shard_map/ppermute | solution.py:24
  135.2 6.4 %collective-permute-done.9 = f32[24,256]{1,0:T(8,128)S(1)} collective-permute-done((f32[24,256]{1,0:T(8,128)S(1)}, f32[24,256]{1,0:T(8,128)S(1)}, u32[]{:S(2)}, u32[]{:S(2)}) %collective-permute-start.9) | collective-permute-done | bytes 24608 | tf_op jit(solution)/shard_map/ppermute | solution.py:24
  141.5 9.5 %all_to_all.16 = f32[8,24,256]{2,1,0:T(8,128)S(1)} all-to-all(f32[8,24,256]{2,1,0:T(8,128)S(1)} %broadcast_in_dim.22), channel_id=1, replica_groups=mesh['rows'=64,'rep'=8] {'rep'}, dimensions={0} | all-to-all | bytes 393216 | tf_op jit(solution)/shard_map/all_to_all | solution.py:132
  151.0 0.7 slice.68
  151.7 0.6 slice.69
  (46 shorter events, 0.3 us)
Async XLA Ops:
  0.6 88.3 %copy-start = (bf16[128,256]{1,0:T(8,128)(2,1)S(1)}, bf16[128,256]{1,0:T(8,128)(2,1)}, u32[]{:S(2)}) copy-start(bf16[128,256]{1,0:T(8,128)(2,1)} %param.17) | copy-start | bytes 196612
  2.4 0.9 copy-start.8
  2.4 0.9 copy-start.7
  2.4 0.9 copy-start.9
  2.4 1.0 collective-permute-start
  3.5 33.4 %copy-start.1 = (bf16[128,512]{1,0:T(8,128)(2,1)}, bf16[128,512]{1,0:T(8,128)(2,1)S(1)}, u32[]{:S(2)}) copy-start(bf16[128,512]{1,0:T(8,128)(2,1)S(1)} %collective-permute-done) | copy-start | bytes 393220
  3.5 14.5 %collective-permute-start.1 = (bf16[1,128,512]{2,1,0:T(8,128)(2,1)S(1)}, bf16[1,128,512]{2,1,0:T(8,128)(2,1)S(1)}, u32[]{:S(2)}, u32[]{:S(2)}) collective-permute-start(bf16[1,128,512]{2,1,0:T(8,128)(2,1)S(1)} %bitcast.22), channel_id=1, source_target_pairs={{0,480},{8,488},{16,496},{24,504},{32,0},{40,8},{48,16},{56,24},{6... | collective-permute-start | bytes 393224 | tf_op jit(solution)/shard_map/ppermute | solution.py:15
  14.9 14.2 %copy-start.11 = (s32[2]{0:T(128)S(1)}, s32[2]{0:T(128)}, u32[]{:S(2)}) copy-start(s32[2]{0:T(128)} %constant.171) | copy-start | bytes 28
  18.0 18.9 %copy-start.2 = (bf16[1,128,512]{2,1,0:T(8,128)(2,1)}, bf16[1,128,512]{2,1,0:T(8,128)(2,1)S(1)}, u32[]{:S(2)}) copy-start(bf16[1,128,512]{2,1,0:T(8,128)(2,1)S(1)} %collective-permute-done.1.bufT_ref) | copy-start | bytes 393220
  18.0 18.9 %collective-permute-start.2 = (bf16[2,128,512]{2,1,0:T(8,128)(2,1)S(1)}, bf16[2,128,512]{2,1,0:T(8,128)(2,1)S(1)}, u32[]{:S(2)}, u32[]{:S(2)}) collective-permute-start(bf16[2,128,512]{2,1,0:T(8,128)(2,1)S(1)} %pad_maximum_fusion.1), channel_id=1, source_target_pairs={{0,496},{8,504},{16,0},{24,8},{32,16},{40,24},{48,32},{56,40},{64,... | collective-permute-start | bytes 786440 | tf_op jit(solution)/shard_map/ppermute | solution.py:15
  30.8 8.7 %copy-start.10 = (s32[4]{0:T(128)S(1)}, s32[4]{0:T(128)}, u32[]{:S(2)}) copy-start(s32[4]{0:T(128)} %constant.173) | copy-start | bytes 52
  36.9 0.7 copy-start.3
  37.6 13.8 %collective-permute-start.3 = (bf16[4,128,512]{2,1,0:T(8,128)(2,1)S(1)}, bf16[4,128,512]{2,1,0:T(8,128)(2,1)S(1)}, u32[]{:S(2)}, u32[]{:S(2)}) collective-permute-start(bf16[4,128,512]{2,1,0:T(8,128)(2,1)S(1)} %pad_maximum_fusion), channel_id=1, source_target_pairs={{0,504},{8,0},{16,8},{24,16},{32,24},{40,32},{48,40},{56,48},{64,5... | collective-permute-start | bytes 1572872 | tf_op jit(solution)/shard_map/ppermute | solution.py:15
  51.3 0.8 copy-start.12
  52.1 6.1 %copy-start.4 = (f32[4,128,128]{2,1,0:T(8,128)S(1)}, f32[4,128,128]{2,1,0:T(8,128)}, u32[]{:S(2)}) copy-start(f32[4,128,128]{2,1,0:T(8,128)} %shard_map.139) | copy-start | bytes 786436
  52.1 6.1 %copy-start.5 = (f32[4,128,128]{2,1,0:T(8,128)S(1)}, f32[4,128,128]{2,1,0:T(8,128)}, u32[]{:S(2)}) copy-start(f32[4,128,128]{2,1,0:T(8,128)} %shard_map.140) | copy-start | bytes 786436
  52.1 6.1 %copy-start.6 = (f32[4,128,128]{2,1,0:T(8,128)S(1)}, f32[4,128,128]{2,1,0:T(8,128)}, u32[]{:S(2)}) copy-start(f32[4,128,128]{2,1,0:T(8,128)} %shard_map.141) | copy-start | bytes 786436
  59.9 28.8 %all-to-all-start = ((bf16[8,64,128]{2,1,0:T(8,128)(2,1)}), bf16[8,64,128]{2,1,0:T(8,128)(2,1)S(1)}, u32[]{:S(2)}, u32[]{:S(2)}) async-start(bf16[8,64,128]{2,1,0:T(8,128)(2,1)} %bitcast.6), calls=%async_computation | async-start | bytes 262144 | tf_op jit(solution)/shard_map/all_to_all | solution.py:107
  88.8 0.8 copy-start.13
  88.8 0.8 copy-start.14
  100.0 3.1 %collective-permute-start.4 = (f32[24,256]{1,0:T(8,128)S(1)}, f32[24,256]{1,0:T(8,128)S(1)}, u32[]{:S(2)}, u32[]{:S(2)}) collective-permute-start(f32[24,256]{1,0:T(8,128)S(1)} %reduce_sum.29), channel_id=1, source_target_pairs={{0,8},{8,0},{16,24},{24,16},{32,40},{40,32},{48,56},{56,48},{64,72... | collective-permute-start | bytes 73736 | tf_op jit(solution)/shard_map/ppermute | solution.py:24
  103.1 5.7 %collective-permute-start.5 = (f32[24,256]{1,0:T(8,128)S(1)}, f32[24,256]{1,0:T(8,128)S(1)}, u32[]{:S(2)}, u32[]{:S(2)}) collective-permute-start(f32[24,256]{1,0:T(8,128)S(1)} %add.98), channel_id=1, source_target_pairs={{0,64},{8,72},{16,80},{24,88},{32,96},{40,104},{48,112},{56,120},{... | collective-permute-start | bytes 73736 | tf_op jit(solution)/shard_map/ppermute | solution.py:24
  108.8 6.6 %collective-permute-start.6 = (f32[24,256]{1,0:T(8,128)S(1)}, f32[24,256]{1,0:T(8,128)S(1)}, u32[]{:S(2)}, u32[]{:S(2)}) collective-permute-start(f32[24,256]{1,0:T(8,128)S(1)} %add.99), channel_id=1, source_target_pairs={{0,16},{8,24},{16,0},{24,8},{32,48},{40,56},{48,32},{56,40},{64,80... | collective-permute-start | bytes 73736 | tf_op jit(solution)/shard_map/ppermute | solution.py:24
  115.4 6.9 %collective-permute-start.7 = (f32[24,256]{1,0:T(8,128)S(1)}, f32[24,256]{1,0:T(8,128)S(1)}, u32[]{:S(2)}, u32[]{:S(2)}) collective-permute-start(f32[24,256]{1,0:T(8,128)S(1)} %add.100), channel_id=1, source_target_pairs={{0,128},{8,136},{16,144},{24,152},{32,160},{40,168},{48,176},{56,1... | collective-permute-start | bytes 73736 | tf_op jit(solution)/shard_map/ppermute | solution.py:24
  122.3 9.6 %collective-permute-start.8 = (f32[24,256]{1,0:T(8,128)S(1)}, f32[24,256]{1,0:T(8,128)S(1)}, u32[]{:S(2)}, u32[]{:S(2)}) collective-permute-start(f32[24,256]{1,0:T(8,128)S(1)} %add.101), channel_id=1, source_target_pairs={{0,32},{8,40},{16,48},{24,56},{32,0},{40,8},{48,16},{56,24},{64,96... | collective-permute-start | bytes 73736 | tf_op jit(solution)/shard_map/ppermute | solution.py:24
  131.9 9.6 %collective-permute-start.9 = (f32[24,256]{1,0:T(8,128)S(1)}, f32[24,256]{1,0:T(8,128)S(1)}, u32[]{:S(2)}, u32[]{:S(2)}) collective-permute-start(f32[24,256]{1,0:T(8,128)S(1)} %add.102), channel_id=1, source_target_pairs={{0,256},{8,264},{16,272},{24,280},{32,288},{40,296},{48,304},{56,3... | collective-permute-start | bytes 73736 | tf_op jit(solution)/shard_map/ppermute | solution.py:24

commit v14 on v13

--- a/solution.py
+++ b/solution.py
@@ -6,7 +6,7 @@
 from jax.sharding import PartitionSpec as P
 
 
-ROWS_BITS = (0, 3, 1, 4, 2, 5)
+ROWS_BITS = (5, 2, 4, 1, 3, 0)
 
 
 def from_behind(value, axis, steps):
@@ -104,8 +104,8 @@
         offsets = offsets + arrived_offsets
     partial_total = partial_total.reshape(-1, partial_total.shape[-1])
     pieces = partial_total.reshape((replicas, -1) + partial_total.shape[1:])
-    pieces = lax.all_to_all(pieces.astype(jnp.bfloat16), "rep", 0, 0)
-    edge_sums = jnp.sum(pieces.astype(jnp.float32), axis=0)
+    pieces = lax.all_to_all(pieces, "rep", 0, 0)
+    edge_sums = jnp.sum(pieces, axis=0)
     share_rows = edge_sums.shape[0]
     share_start = replica * share_rows
     own_rows = lax.dynamic_slice_in_dim(scaled, share_start, share_rows, 0).astype(jnp.float32)

time: 153 us -> 154 us (level)
  waiting for transfers between devices: 42.8 us -> 44.5 us
    add x0 -> x1, other arithmetic: none -> 1.69 us  [layer(): partial_total = partial_total + local_sums(arrived, arrived_offsets)]
    convert_element_type x1 -> x0, other arithmetic: 1.66 us -> none  [layer(): pieces = lax.all_to_all(pieces.astype(jnp.bfloat16), 'rep', 0, 0)]
  transfers between devices with their start and end apart: 11 -> 11, of which waited for: 9 -> 9; matrix products, arithmetic and copies ran while one was open for 3% -> 3% of each run, Pallas kernels for 7% -> 6%
where the time goes in v14:
time: 154 us; the launch traced here: 153 us
  starting transfers between devices  60.4 us (39%)
  waiting for transfers between devices  44.5 us (29%)
  blocking collectives  19.1 us (12%)
  Pallas kernels  16 us (10%)
  local copies, waits for them, and re-layouts  8.71 us (6%)
  other arithmetic  2.86 us (2%)
    ppermute x6, waiting for transfers between devices, butterfly_sum(): value = value + lax.ppermute(value, axis, pairs)  27.9 us
    ppermute x3, starting transfers between devices, from_behind(): return lax.ppermute(value, axis, pairs)  23.8 us
    all_to_all x1, starting transfers between devices, layer(): pieces = lax.all_to_all(pieces, 'rep', 0, 0)  22.1 us
    pallas_call x4, Pallas kernels, edge_sums_kernel(): pl.pallas_call(_edge_kernel, out_shape=jax.ShapeDtypeStruct((blocks, rows...  16 us
    ppermute x6, starting transfers between devices, butterfly_sum(): value = value + lax.ppermute(value, axis, pairs)  13.7 us
    all_to_all x1, blocking collectives, layer(): packed = lax.all_to_all(spread, 'rep', 0, 0).reshape(-1, packed.shape[1])  9.61 us
    all_to_all x1, blocking collectives, layer(): lax.all_to_all(padded.reshape((replicas, piece_rows) + packed.shape[1:]),...  9.49 us
    ppermute x3, waiting for transfers between devices, from_behind(): return lax.ppermute(value, axis, pairs)  9.12 us
  transfers between devices with their start and end apart: 11, of which 9 were waited for; matrix products, arithmetic and copies ran while one was open for 3% of the time, Pallas kernels for 6%

profile of v14, /device:TPU:24, one launch (start us, length us, event | category | flops | bytes accessed | tf_op | source)
XLA Modules:
  0.0 153.4 jit_solution(10019454168353798140)
XLA Ops:
  0.6 0.7 convert_rsqrt_fusion
  1.4 1.0 copy.21
  2.4 0.8 collective-permute-start
  3.3 0.1 fusion.1
  3.5 10.8 %collective-permute-start.1 = (bf16[1,128,512]{2,1,0:T(8,128)(2,1)S(1)}, bf16[1,128,512]{2,1,0:T(8,128)(2,1)S(1)}, u32[]{:S(2)}, u32[]{:S(2)}) collective-permute-start(bf16[1,128,512]{2,1,0:T(8,128)(2,1)S(1)} %bitcast.22), channel_id=1, source_target_pairs={{0,480},{8,488},{16,496},{24,504},{32,0},{40,8},{48,16},{56,24},{6... | collective-permute-start | bytes 393224 | tf_op jit(solution)/shard_map/ppermute | solution.py:15
  14.3 0.6 fusion.15
  14.9 3.1 %collective-permute-done.1.bufT_ref = bf16[1,128,512]{2,1,0:T(8,128)(2,1)S(1)} collective-permute-done((bf16[1,128,512]{2,1,0:T(8,128)(2,1)S(1)}, bf16[1,128,512]{2,1,0:T(8,128)(2,1)S(1)}, u32[]{:S(2)}, u32[]{:S(2)}) %collective-permute-start.1) | collective-permute-done | bytes 131104 | tf_op jit(solution)/shard_map/ppermute | solution.py:15
  18.0 11.0 %collective-permute-start.2 = (bf16[2,128,512]{2,1,0:T(8,128)(2,1)S(1)}, bf16[2,128,512]{2,1,0:T(8,128)(2,1)S(1)}, u32[]{:S(2)}, u32[]{:S(2)}) collective-permute-start(bf16[2,128,512]{2,1,0:T(8,128)(2,1)S(1)} %pad_maximum_fusion.1), channel_id=1, source_target_pairs={{0,496},{8,504},{16,0},{24,8},{32,16},{40,24},{48,32},{56,40},{64,... | collective-permute-start | bytes 786440 | tf_op jit(solution)/shard_map/ppermute | solution.py:15
  29.1 0.6 gather_fusion
  29.6 0.6 gather_fusion.1
  30.2 0.6 copy_bitcast_fusion.2
  30.8 6.1 %collective-permute-done.2.bufT_ref = bf16[2,128,512]{2,1,0:T(8,128)(2,1)S(1)} collective-permute-done((bf16[2,128,512]{2,1,0:T(8,128)(2,1)S(1)}, bf16[2,128,512]{2,1,0:T(8,128)(2,1)S(1)}, u32[]{:S(2)}, u32[]{:S(2)}) %collective-permute-start.2) | collective-permute-done | bytes 262176 | tf_op jit(solution)/shard_map/ppermute | solution.py:15
  36.9 0.1 pad_maximum_fusion
  36.9 0.6 copy-done.6
  37.6 1.9 %collective-permute-start.3 = (bf16[4,128,512]{2,1,0:T(8,128)(2,1)S(1)}, bf16[4,128,512]{2,1,0:T(8,128)(2,1)S(1)}, u32[]{:S(2)}, u32[]{:S(2)}) collective-permute-start(bf16[4,128,512]{2,1,0:T(8,128)(2,1)S(1)} %pad_maximum_fusion), channel_id=1, source_target_pairs={{0,504},{8,0},{16,8},{24,16},{32,24},{40,32},{48,40},{56,48},{64,5... | collective-permute-start | bytes 1572872 | tf_op jit(solution)/shard_map/ppermute | solution.py:15
  39.5 0.6 gather_fusion.2
  40.1 0.6 gather_fusion.3
  40.6 0.7 copy_bitcast_fusion
  41.3 3.0 %shard_map.139 = f32[4,128,128]{2,1,0:T(8,128)} custom-call(bf16[1,128,512]{2,1,0:T(8,128)(2,1)} %bitcast.25, s32[4,1,8,128]{3,2,1,0:T(8,128)} %get-tuple-element.56.far_ref, s32[4,1,8,128]{3,2,1,0:T(8,128)} %get-tuple-element.50.tgt_ref), custom_call_target="tpu_custom_call" | custom-call | flops 671088640 | bytes 425984 | tf_op jit(solution)/shard_map/pallas_call | solution.py:61
  44.3 3.0 %shard_map.140 = f32[4,128,128]{2,1,0:T(8,128)} custom-call(bf16[1,128,512]{2,1,0:T(8,128)(2,1)} %copy-done.2, s32[4,1,8,128]{3,2,1,0:T(8,128)} %get-tuple-element.57.far_ref, s32[4,1,8,128]{3,2,1,0:T(8,128)} %get-tuple-element.49.tgt_ref), custom_call_target="tpu_custom_call" | custom-call | flops 671088640 | bytes 425984 | tf_op jit(solution)/shard_map/pallas_call | solution.py:61
  47.2 4.0 %shard_map.141 = f32[4,128,128]{2,1,0:T(8,128)} custom-call(bf16[2,128,512]{2,1,0:T(8,128)(2,1)} %copy-done.6, s32[4,2,8,128]{3,2,1,0:T(8,128)} %get-tuple-element.61.far_ref, s32[4,2,8,128]{3,2,1,0:T(8,128)} %get-tuple-element.60.tgt_ref), custom_call_target="tpu_custom_call" | custom-call | flops 1342177280 | bytes 589824 | tf_op jit(solution)/shard_map/pallas_call | solution.py:61
  51.3 0.8 copy-done.12
  52.1 6.0 %shard_map.142 = f32[4,128,128]{2,1,0:T(8,128)} custom-call(bf16[4,128,512]{2,1,0:T(8,128)(2,1)} %copy-done.12, s32[4,4,8,128]{3,2,1,0:T(8,128)} %get-tuple-element.59.far_ref, s32[4,4,8,128]{3,2,1,0:T(8,128)} %get-tuple-element.58.tgt_ref), custom_call_target="tpu_custom_call" | custom-call | flops 2684354560 | bytes 917504 | tf_op jit(solution)/shard_map/pallas_call | solution.py:61
  58.1 1.7 %add_add_fusion = f32[4,128,128]{2,1,0:T(8,128)} fusion(f32[4,128,128]{2,1,0:T(8,128)} %shard_map.142, f32[4,128,128]{2,1,0:T(8,128)S(1)} %copy-done.5, f32[4,128,128]{2,1,0:T(8,128)S(1)} %copy-done.3, f32[4,128,128]{2,1,0:T(8,128)S(1)} %copy-done.4), kind=kLoop, calls=%fused_computation.7 | loop fusion | flops 196608 | bytes 1310720 | tf_op jit(solution)/shard_map/add | solution.py:102
  59.8 22.1 %all-to-all-start = ((f32[8,64,128]{2,1,0:T(8,128)}), f32[8,64,128]{2,1,0:T(8,128)S(1)}, u32[]{:S(2)}, u32[]{:S(2)}) async-start(f32[8,64,128]{2,1,0:T(8,128)} %bitcast.6), calls=%async_computation | async-start | bytes 524288 | tf_op jit(solution)/shard_map/all_to_all | solution.py:107
  81.9 0.1 dynamic_slice.6
  82.0 7.4 %all-to-all-done = f32[8,64,128]{2,1,0:T(8,128)S(1)} async-done(((f32[8,64,128]{2,1,0:T(8,128)}), f32[8,64,128]{2,1,0:T(8,128)S(1)}, u32[]{:S(2)}, u32[]{:S(2)}) %all-to-all-start) | async-done | bytes 262176 | tf_op jit(solution)/shard_map/all_to_all | solution.py:107
  89.5 0.1 copy.26
  89.6 0.1 multiply_convert_fusion.2
  89.7 0.6 copy-done.13
  90.4 0.8 convert_reduce_fusion
  91.2 0.1 fusion.17
  91.4 9.5 %all_to_all.15 = f32[8,24,256]{2,1,0:T(8,128)S(1)} all-to-all(f32[8,24,256]{2,1,0:T(8,128)S(1)} %bitcast.19), channel_id=1, replica_groups=mesh['rows'=64,'rep'=8] {'rep'}, dimensions={0} | all-to-all | bytes 393216 | tf_op jit(solution)/shard_map/all_to_all | solution.py:127
  100.9 3.9 %collective-permute-start.4 = (f32[24,256]{1,0:T(8,128)S(1)}, f32[24,256]{1,0:T(8,128)S(1)}, u32[]{:S(2)}, u32[]{:S(2)}) collective-permute-start(f32[24,256]{1,0:T(8,128)S(1)} %reduce_sum.29), channel_id=1, source_target_pairs={{0,256},{8,264},{16,272},{24,280},{32,288},{40,296},{48,304},{56,3... | collective-permute-start | bytes 73736 | tf_op jit(solution)/shard_map/ppermute | solution.py:24
  104.7 6.0 %collective-permute-done.4 = f32[24,256]{1,0:T(8,128)S(1)} collective-permute-done((f32[24,256]{1,0:T(8,128)S(1)}, f32[24,256]{1,0:T(8,128)S(1)}, u32[]{:S(2)}, u32[]{:S(2)}) %collective-permute-start.4) | collective-permute-done | bytes 24608 | tf_op jit(solution)/shard_map/ppermute | solution.py:24
  110.7 1.9 %collective-permute-start.5 = (f32[24,256]{1,0:T(8,128)S(1)}, f32[24,256]{1,0:T(8,128)S(1)}, u32[]{:S(2)}, u32[]{:S(2)}) collective-permute-start(f32[24,256]{1,0:T(8,128)S(1)} %add.98), channel_id=1, source_target_pairs={{0,32},{8,40},{16,48},{24,56},{32,0},{40,8},{48,16},{56,24},{64,96... | collective-permute-start | bytes 73736 | tf_op jit(solution)/shard_map/ppermute | solution.py:24
  112.6 7.8 %collective-permute-done.5 = f32[24,256]{1,0:T(8,128)S(1)} collective-permute-done((f32[24,256]{1,0:T(8,128)S(1)}, f32[24,256]{1,0:T(8,128)S(1)}, u32[]{:S(2)}, u32[]{:S(2)}) %collective-permute-start.5) | collective-permute-done | bytes 24608 | tf_op jit(solution)/shard_map/ppermute | solution.py:24
  120.4 1.9 %collective-permute-start.6 = (f32[24,256]{1,0:T(8,128)S(1)}, f32[24,256]{1,0:T(8,128)S(1)}, u32[]{:S(2)}, u32[]{:S(2)}) collective-permute-start(f32[24,256]{1,0:T(8,128)S(1)} %add.99), channel_id=1, source_target_pairs={{0,128},{8,136},{16,144},{24,152},{32,160},{40,168},{48,176},{56,1... | collective-permute-start | bytes 73736 | tf_op jit(solution)/shard_map/ppermute | solution.py:24
  122.3 4.8 %collective-permute-done.6 = f32[24,256]{1,0:T(8,128)S(1)} collective-permute-done((f32[24,256]{1,0:T(8,128)S(1)}, f32[24,256]{1,0:T(8,128)S(1)}, u32[]{:S(2)}, u32[]{:S(2)}) %collective-permute-start.6) | collective-permute-done | bytes 24608 | tf_op jit(solution)/shard_map/ppermute | solution.py:24
  127.2 1.9 %collective-permute-start.7 = (f32[24,256]{1,0:T(8,128)S(1)}, f32[24,256]{1,0:T(8,128)S(1)}, u32[]{:S(2)}, u32[]{:S(2)}) collective-permute-start(f32[24,256]{1,0:T(8,128)S(1)} %add.100), channel_id=1, source_target_pairs={{0,16},{8,24},{16,0},{24,8},{32,48},{40,56},{48,32},{56,40},{64,80... | collective-permute-start | bytes 73736 | tf_op jit(solution)/shard_map/ppermute | solution.py:24
  129.1 4.7 %collective-permute-done.7 = f32[24,256]{1,0:T(8,128)S(1)} collective-permute-done((f32[24,256]{1,0:T(8,128)S(1)}, f32[24,256]{1,0:T(8,128)S(1)}, u32[]{:S(2)}, u32[]{:S(2)}) %collective-permute-start.7) | collective-permute-done | bytes 24608 | tf_op jit(solution)/shard_map/ppermute | solution.py:24
  133.8 2.2 %collective-permute-start.8 = (f32[24,256]{1,0:T(8,128)S(1)}, f32[24,256]{1,0:T(8,128)S(1)}, u32[]{:S(2)}, u32[]{:S(2)}) collective-permute-start(f32[24,256]{1,0:T(8,128)S(1)} %add.101), channel_id=1, source_target_pairs={{0,64},{8,72},{16,80},{24,88},{32,96},{40,104},{48,112},{56,120},{... | collective-permute-start | bytes 73736 | tf_op jit(solution)/shard_map/ppermute | solution.py:24
  136.0 3.5 %collective-permute-done.8 = f32[24,256]{1,0:T(8,128)S(1)} collective-permute-done((f32[24,256]{1,0:T(8,128)S(1)}, f32[24,256]{1,0:T(8,128)S(1)}, u32[]{:S(2)}, u32[]{:S(2)}) %collective-permute-start.8) | collective-permute-done | bytes 24608 | tf_op jit(solution)/shard_map/ppermute | solution.py:24
  139.5 1.9 %collective-permute-start.9 = (f32[24,256]{1,0:T(8,128)S(1)}, f32[24,256]{1,0:T(8,128)S(1)}, u32[]{:S(2)}, u32[]{:S(2)}) collective-permute-start(f32[24,256]{1,0:T(8,128)S(1)} %add.102), channel_id=1, source_target_pairs={{0,8},{8,0},{16,24},{24,16},{32,40},{40,32},{48,56},{56,48},{64,72... | collective-permute-start | bytes 73736 | tf_op jit(solution)/shard_map/ppermute | solution.py:24
  141.4 1.2 collective-permute-done.9
  142.6 9.6 %all_to_all.16 = f32[8,24,256]{2,1,0:T(8,128)S(1)} all-to-all(f32[8,24,256]{2,1,0:T(8,128)S(1)} %broadcast_in_dim.22), channel_id=1, replica_groups=mesh['rows'=64,'rep'=8] {'rep'}, dimensions={0} | all-to-all | bytes 393216 | tf_op jit(solution)/shard_map/all_to_all | solution.py:132
  152.2 0.7 slice.68
  152.9 0.6 slice.69
  (46 shorter events, 0.3 us)
Async XLA Ops:
  0.6 89.1 %copy-start = (bf16[128,256]{1,0:T(8,128)(2,1)S(1)}, bf16[128,256]{1,0:T(8,128)(2,1)}, u32[]{:S(2)}) copy-start(bf16[128,256]{1,0:T(8,128)(2,1)} %param.17) | copy-start | bytes 196612
  2.4 0.9 copy-start.8
  2.4 0.9 copy-start.7
  2.4 0.9 copy-start.9
  2.4 1.0 collective-permute-start
  3.5 33.4 %copy-start.1 = (bf16[128,512]{1,0:T(8,128)(2,1)}, bf16[128,512]{1,0:T(8,128)(2,1)S(1)}, u32[]{:S(2)}) copy-start(bf16[128,512]{1,0:T(8,128)(2,1)S(1)} %collective-permute-done) | copy-start | bytes 393220
  3.5 14.5 %collective-permute-start.1 = (bf16[1,128,512]{2,1,0:T(8,128)(2,1)S(1)}, bf16[1,128,512]{2,1,0:T(8,128)(2,1)S(1)}, u32[]{:S(2)}, u32[]{:S(2)}) collective-permute-start(bf16[1,128,512]{2,1,0:T(8,128)(2,1)S(1)} %bitcast.22), channel_id=1, source_target_pairs={{0,480},{8,488},{16,496},{24,504},{32,0},{40,8},{48,16},{56,24},{6... | collective-permute-start | bytes 393224 | tf_op jit(solution)/shard_map/ppermute | solution.py:15
  14.9 14.2 %copy-start.11 = (s32[2]{0:T(128)S(1)}, s32[2]{0:T(128)}, u32[]{:S(2)}) copy-start(s32[2]{0:T(128)} %constant.171) | copy-start | bytes 28
  18.0 18.9 %copy-start.2 = (bf16[1,128,512]{2,1,0:T(8,128)(2,1)}, bf16[1,128,512]{2,1,0:T(8,128)(2,1)S(1)}, u32[]{:S(2)}) copy-start(bf16[1,128,512]{2,1,0:T(8,128)(2,1)S(1)} %collective-permute-done.1.bufT_ref) | copy-start | bytes 393220
  18.0 18.9 %collective-permute-start.2 = (bf16[2,128,512]{2,1,0:T(8,128)(2,1)S(1)}, bf16[2,128,512]{2,1,0:T(8,128)(2,1)S(1)}, u32[]{:S(2)}, u32[]{:S(2)}) collective-permute-start(bf16[2,128,512]{2,1,0:T(8,128)(2,1)S(1)} %pad_maximum_fusion.1), channel_id=1, source_target_pairs={{0,496},{8,504},{16,0},{24,8},{32,16},{40,24},{48,32},{56,40},{64,... | collective-permute-start | bytes 786440 | tf_op jit(solution)/shard_map/ppermute | solution.py:15
  30.8 8.7 %copy-start.10 = (s32[4]{0:T(128)S(1)}, s32[4]{0:T(128)}, u32[]{:S(2)}) copy-start(s32[4]{0:T(128)} %constant.173) | copy-start | bytes 52
  36.9 0.7 copy-start.6
  37.6 13.7 %collective-permute-start.3 = (bf16[4,128,512]{2,1,0:T(8,128)(2,1)S(1)}, bf16[4,128,512]{2,1,0:T(8,128)(2,1)S(1)}, u32[]{:S(2)}, u32[]{:S(2)}) collective-permute-start(bf16[4,128,512]{2,1,0:T(8,128)(2,1)S(1)} %pad_maximum_fusion), channel_id=1, source_target_pairs={{0,504},{8,0},{16,8},{24,16},{32,24},{40,32},{48,40},{56,48},{64,5... | collective-permute-start | bytes 1572872 | tf_op jit(solution)/shard_map/ppermute | solution.py:15
  51.3 0.8 copy-start.12
  52.1 6.1 %copy-start.3 = (f32[4,128,128]{2,1,0:T(8,128)S(1)}, f32[4,128,128]{2,1,0:T(8,128)}, u32[]{:S(2)}) copy-start(f32[4,128,128]{2,1,0:T(8,128)} %shard_map.139) | copy-start | bytes 786436
  52.1 6.1 %copy-start.4 = (f32[4,128,128]{2,1,0:T(8,128)S(1)}, f32[4,128,128]{2,1,0:T(8,128)}, u32[]{:S(2)}) copy-start(f32[4,128,128]{2,1,0:T(8,128)} %shard_map.140) | copy-start | bytes 786436
  52.1 6.1 %copy-start.5 = (f32[4,128,128]{2,1,0:T(8,128)S(1)}, f32[4,128,128]{2,1,0:T(8,128)}, u32[]{:S(2)}) copy-start(f32[4,128,128]{2,1,0:T(8,128)} %shard_map.141) | copy-start | bytes 786436
  59.8 29.7 %all-to-all-start = ((f32[8,64,128]{2,1,0:T(8,128)}), f32[8,64,128]{2,1,0:T(8,128)S(1)}, u32[]{:S(2)}, u32[]{:S(2)}) async-start(f32[8,64,128]{2,1,0:T(8,128)} %bitcast.6), calls=%async_computation | async-start | bytes 524288 | tf_op jit(solution)/shard_map/all_to_all | solution.py:107
  89.6 0.8 copy-start.13
  89.6 0.8 copy-start.14
  100.9 9.8 %collective-permute-start.4 = (f32[24,256]{1,0:T(8,128)S(1)}, f32[24,256]{1,0:T(8,128)S(1)}, u32[]{:S(2)}, u32[]{:S(2)}) collective-permute-start(f32[24,256]{1,0:T(8,128)S(1)} %reduce_sum.29), channel_id=1, source_target_pairs={{0,256},{8,264},{16,272},{24,280},{32,288},{40,296},{48,304},{56,3... | collective-permute-start | bytes 73736 | tf_op jit(solution)/shard_map/ppermute | solution.py:24
  110.7 9.7 %collective-permute-start.5 = (f32[24,256]{1,0:T(8,128)S(1)}, f32[24,256]{1,0:T(8,128)S(1)}, u32[]{:S(2)}, u32[]{:S(2)}) collective-permute-start(f32[24,256]{1,0:T(8,128)S(1)} %add.98), channel_id=1, source_target_pairs={{0,32},{8,40},{16,48},{24,56},{32,0},{40,8},{48,16},{56,24},{64,96... | collective-permute-start | bytes 73736 | tf_op jit(solution)/shard_map/ppermute | solution.py:24
  120.4 6.7 %collective-permute-start.6 = (f32[24,256]{1,0:T(8,128)S(1)}, f32[24,256]{1,0:T(8,128)S(1)}, u32[]{:S(2)}, u32[]{:S(2)}) collective-permute-start(f32[24,256]{1,0:T(8,128)S(1)} %add.99), channel_id=1, source_target_pairs={{0,128},{8,136},{16,144},{24,152},{32,160},{40,168},{48,176},{56,1... | collective-permute-start | bytes 73736 | tf_op jit(solution)/shard_map/ppermute | solution.py:24
  127.2 6.6 %collective-permute-start.7 = (f32[24,256]{1,0:T(8,128)S(1)}, f32[24,256]{1,0:T(8,128)S(1)}, u32[]{:S(2)}, u32[]{:S(2)}) collective-permute-start(f32[24,256]{1,0:T(8,128)S(1)} %add.100), channel_id=1, source_target_pairs={{0,16},{8,24},{16,0},{24,8},{32,48},{40,56},{48,32},{56,40},{64,80... | collective-permute-start | bytes 73736 | tf_op jit(solution)/shard_map/ppermute | solution.py:24
  133.8 5.7 %collective-permute-start.8 = (f32[24,256]{1,0:T(8,128)S(1)}, f32[24,256]{1,0:T(8,128)S(1)}, u32[]{:S(2)}, u32[]{:S(2)}) collective-permute-start(f32[24,256]{1,0:T(8,128)S(1)} %add.101), channel_id=1, source_target_pairs={{0,64},{8,72},{16,80},{24,88},{32,96},{40,104},{48,112},{56,120},{... | collective-permute-start | bytes 73736 | tf_op jit(solution)/shard_map/ppermute | solution.py:24
  139.5 3.1 %collective-permute-start.9 = (f32[24,256]{1,0:T(8,128)S(1)}, f32[24,256]{1,0:T(8,128)S(1)}, u32[]{:S(2)}, u32[]{:S(2)}) collective-permute-start(f32[24,256]{1,0:T(8,128)S(1)} %add.102), channel_id=1, source_target_pairs={{0,8},{8,0},{16,24},{24,16},{32,40},{40,32},{48,56},{56,48},{64,72... | collective-permute-start | bytes 73736 | tf_op jit(solution)/shard_map/ppermute | solution.py:24
